TPU v7x, 32 devices: a whole 2x2x4 slice. The times are simulated.
32 devices in a mesh: rows: 8 (over y, x, core), rhs: 4 (over z).
Axes of the slice: x: 2, y: 2, z: 4, core: 2. Of those that a mesh axis runs over, the one named last changes fastest.
Arguments:
- win_rows: bfloat16 [4096, 4096], P('rows'), may hold values from -0.09375 to 0.09375
- anc_rows: bfloat16 [16384, 4096], P('rows'), may hold values from -0.09375 to 0.09375
- win_pattern: int32 [64, 64], replicated, may hold values 0 or 1
- anc_pattern: int32 [256, 64], P('rows'), may hold values 0 or 1
- window_owner: int32 [64], replicated, may hold values from 0 to 63, each once
- sn_order: int32 [8], replicated, may hold values from 0 to 7, each once
- diag_inv: bfloat16 [8, 512, 512], replicated, as said below
- rhs_win: bfloat16 [4096, 1024], P(('rows', 'rhs')), may hold values from -0.119628906 to 0.119628906
- rhs_anc: bfloat16 [16384, 1024], P(('rows', 'rhs')), may hold values from -6 to 6
Outputs:
- window_solution: bfloat16 [4096, 1024], P(None, 'rhs')
- anc_residual: bfloat16 [16384, 1024], P('rows', 'rhs')
Inputs may be any that keep to these rules, and one draw needn't show every extreme that they name: `window_owner`: each storage slot holds exactly one window block row. `sn_order`: each supernode label appears once. `diag_inv`: each block is lower triangular.
All inputs are finite; a program needn't handle non-finite values. No bound on the sum of `anc_pattern` on one device may be relied on, other than what follows from the above.
Results may differ from a plain program's by a relative error of at most 0.025.
Values may be sent and summed in bfloat16 or wider, within the bound.
No kernel may reach another device: no remote copies, remote signals or barrier semaphores. Data moves between devices by JAX's collectives and lax.ppermute only.
A program may use at most 256 MiB of HBM per device.

v0:
```python
import jax
import jax.numpy as jnp
from jax import lax
from jax.sharding import PartitionSpec as P

BS = 64
SB = 8
NSUP = 8
SN = 512
NW = 4096


def masked_columns(factor, pattern, node_label):
    blocks = pattern.shape[0]
    columns = lax.dynamic_slice_in_dim(factor, node_label * SN, SN, 1)
    chosen = lax.dynamic_slice_in_dim(pattern, node_label * SB, SB, 1)
    shaped = columns.reshape(blocks, BS, SB, BS) * chosen[:, None, :, None].astype(jnp.bfloat16)
    return shaped.reshape(blocks * BS, SN)


def split_product(matrix, values):
    high_part = lax.optimization_barrier(values.astype(jnp.bfloat16))
    low_part = (values - high_part.astype(jnp.float32)).astype(jnp.bfloat16)
    first_term = jnp.dot(matrix, high_part, preferred_element_type=jnp.float32)
    return first_term + jnp.dot(matrix, low_part, preferred_element_type=jnp.float32)


def local(
    win_rows, anc_rows, win_pattern, anc_pattern, window_owner, sn_order, diag_inv, rhs_win, rhs_anc
):
    win_rhs, anc_rhs = (
        lax.all_to_all(rhs_win, "rhs", split_axis=1, concat_axis=0, tiled=True),
        lax.all_to_all(rhs_anc, "rhs", split_axis=1, concat_axis=0, tiled=True),
    )
    columns_rhs = win_rhs.shape[1]
    slot_count = win_rows.shape[0] // BS
    solution = jnp.zeros((NW, columns_rhs), jnp.bfloat16)
    anc_resid = anc_rhs.astype(jnp.float32)
    win_resid = win_rhs.astype(jnp.float32)
    first_slot = lax.axis_index("rows") * slot_count
    local_pattern = lax.dynamic_slice_in_dim(win_pattern, first_slot, slot_count, 0)
    for position in range(NSUP):
        node_label = sn_order[position]
        owners = lax.dynamic_slice_in_dim(window_owner, node_label * SB, SB, 0)
        inverse = lax.dynamic_index_in_dim(diag_inv, node_label, 0, keepdims=False)
        local_place = owners - first_slot
        present = (local_place >= 0) & (local_place < slot_count)
        resid_blocks = win_resid.reshape(slot_count, BS, columns_rhs)
        taken = jnp.take(resid_blocks, jnp.clip(local_place, 0, slot_count - 1), axis=0)
        placed = jnp.where(present[:, None, None], taken, 0.0).reshape(SN, columns_rhs)
        panel = lax.psum(placed.astype(jnp.bfloat16), "rows").astype(jnp.float32)
        solved = split_product(inverse, panel).astype(jnp.bfloat16)
        solution = lax.dynamic_update_slice_in_dim(solution, solved, node_label * SN, 0)
        win_resid = win_resid - jnp.dot(
            masked_columns(win_rows, local_pattern, node_label),
            solved,
            preferred_element_type=jnp.float32,
        )
        anc_resid = anc_resid - jnp.dot(
            masked_columns(anc_rows, anc_pattern, node_label),
            solved,
            preferred_element_type=jnp.float32,
        )
    return (solution, anc_resid.astype(jnp.bfloat16))


def solution(mesh):
    return jax.shard_map(
        local,
        mesh=mesh,
        in_specs=(
            P("rows", None),
            P("rows", None),
            P(),
            P("rows", None),
            P(),
            P(),
            P(),
            P(("rows", "rhs"), None),
            P(("rows", "rhs"), None),
        ),
        out_specs=(P(None, "rhs"), P("rows", "rhs")),
        check_vma=False,
    )
```

profile of v0, /device:TPU:0, one launch (start us, length us, event | category | flops | bytes accessed | tf_op | source)
XLA Modules:
  0.0 546.8 jit_solution(15304940588658373823)
XLA Ops:
  8.8 6.3 %all-to-all-start = ((bf16[128,4,256]{2,0,1:T(8,128)(2,1)}), bf16[128,4,256]{2,0,1:T(8,128)(2,1)S(1)}, u32[]{:S(2)}, u32[]{:S(2)}) async-start(bf16[128,4,256]{2,0,1:T(8,128)(2,1)} %bitcast.147), calls=%async_computation | async-start | bytes 524288 | tf_op jit(solution)/shard_map/all_to_all | solution.py:32
  29.2 50.5 %all-reduce.9.cloned.1.call-done = bf16[512,256]{1,0:T(8,128)(2,1)} async-done(((bf16[512,256]{1,0:T(8,128)(2,1)}), bf16[512,256]{1,0:T(8,128)(2,1)}) %all-reduce.9.cloned.1.call-update) | async-done | bytes 262160 | tf_op jit(solution)/shard_map/psum | solution.py:51
  89.5 49.5 %all-reduce.11.cloned.1.call-done = bf16[512,256]{1,0:T(8,128)(2,1)} async-done(((bf16[512,256]{1,0:T(8,128)(2,1)}), bf16[512,256]{1,0:T(8,128)(2,1)}) %all-reduce.11.cloned.1.call-update) | async-done | bytes 262160 | tf_op jit(solution)/shard_map/psum | solution.py:51
  148.9 49.7 %all-reduce.13.cloned.1.call-done = bf16[512,256]{1,0:T(8,128)(2,1)} async-done(((bf16[512,256]{1,0:T(8,128)(2,1)}), bf16[512,256]{1,0:T(8,128)(2,1)}) %all-reduce.13.cloned.1.call-update) | async-done | bytes 262160 | tf_op jit(solution)/shard_map/psum | solution.py:51
  208.3 49.9 %all-reduce.15.cloned.1.call-done = bf16[512,256]{1,0:T(8,128)(2,1)} async-done(((bf16[512,256]{1,0:T(8,128)(2,1)}), bf16[512,256]{1,0:T(8,128)(2,1)}) %all-reduce.15.cloned.1.call-update) | async-done | bytes 262160 | tf_op jit(solution)/shard_map/psum | solution.py:51
  268.2 49.6 %all-reduce.17.cloned.1.call-done = bf16[512,256]{1,0:T(8,128)(2,1)} async-done(((bf16[512,256]{1,0:T(8,128)(2,1)}), bf16[512,256]{1,0:T(8,128)(2,1)}) %all-reduce.17.cloned.1.call-update) | async-done | bytes 262160 | tf_op jit(solution)/shard_map/psum | solution.py:51
  319.2 2.2 constant_dynamic-update-slice_fusion.3
  328.8 48.6 %all-reduce.19.cloned.1.call-done = bf16[512,256]{1,0:T(8,128)(2,1)} async-done(((bf16[512,256]{1,0:T(8,128)(2,1)}), bf16[512,256]{1,0:T(8,128)(2,1)}) %all-reduce.19.cloned.1.call-update) | async-done | bytes 262160 | tf_op jit(solution)/shard_map/psum | solution.py:51
  383.9 2.3 copy.17
  386.2 4.6 all-to-all-start.1
  395.2 41.8 %all-reduce.21.cloned.1.call-done = bf16[512,256]{1,0:T(8,128)(2,1)} async-done(((bf16[512,256]{1,0:T(8,128)(2,1)}), bf16[512,256]{1,0:T(8,128)(2,1)}) %all-reduce.21.cloned.1.call-update) | async-done | bytes 262160 | tf_op jit(solution)/shard_map/psum | solution.py:51
  445.4 2.6 mul.284
  447.9 6.5 %mul.285 = bf16[2048,512]{1,0:T(8,128)(2,1)} reshape(bf16[32,64,8,64]{3,2,1,0:T(8,128)(2,1)} %mul.284) | data formatting | bytes 4194304 | tf_op jit(solution)/shard_map/mul | solution.py:17
  454.4 2.6 mul.287
  457.0 6.5 %mul.288 = bf16[2048,512]{1,0:T(8,128)(2,1)} reshape(bf16[32,64,8,64]{3,2,1,0:T(8,128)(2,1)} %mul.287) | data formatting | bytes 4194304 | tf_op jit(solution)/shard_map/mul | solution.py:17
  463.5 2.6 mul.290
  466.0 6.5 %mul.291 = bf16[2048,512]{1,0:T(8,128)(2,1)} reshape(bf16[32,64,8,64]{3,2,1,0:T(8,128)(2,1)} %mul.290) | data formatting | bytes 4194304 | tf_op jit(solution)/shard_map/mul | solution.py:17
  472.5 2.6 mul.293
  475.1 6.5 %mul.294 = bf16[2048,512]{1,0:T(8,128)(2,1)} reshape(bf16[32,64,8,64]{3,2,1,0:T(8,128)(2,1)} %mul.293) | data formatting | bytes 4194304 | tf_op jit(solution)/shard_map/mul | solution.py:17
  481.6 2.6 mul.296
  484.1 6.5 %mul.297 = bf16[2048,512]{1,0:T(8,128)(2,1)} reshape(bf16[32,64,8,64]{3,2,1,0:T(8,128)(2,1)} %mul.296) | data formatting | bytes 4194304 | tf_op jit(solution)/shard_map/mul | solution.py:17
  490.6 2.6 mul.299
  493.2 6.5 %mul.300 = bf16[2048,512]{1,0:T(8,128)(2,1)} reshape(bf16[32,64,8,64]{3,2,1,0:T(8,128)(2,1)} %mul.299) | data formatting | bytes 4194304 | tf_op jit(solution)/shard_map/mul | solution.py:17
  499.7 2.6 mul.302
  502.2 5.4 mul.303
  507.6 2.6 mul.305
  510.2 6.5 %mul.306 = bf16[2048,512]{1,0:T(8,128)(2,1)} reshape(bf16[32,64,8,64]{3,2,1,0:T(8,128)(2,1)} %mul.305) | data formatting | bytes 4194304 | tf_op jit(solution)/shard_map/mul | solution.py:17
  518.7 2.3 constant_dynamic-update-slice_fusion
  522.6 2.5 convolution_subtract_fusion.7
  525.2 2.5 convolution_subtract_fusion.6
  527.8 2.5 convolution_subtract_fusion.5
  530.4 2.5 convolution_subtract_fusion.4
  (151 shorter events, 68.1 us)
Async XLA Ops:
  7.2 18.5 %copy-start.25 = (s32[64,64]{1,0:T(8,128)S(1)}, s32[64,64]{1,0:T(8,128)}, u32[]{:S(2)}) copy-start(s32[64,64]{1,0:T(8,128)} %param.13) | copy-start | bytes 49156
  8.8 15.2 %all-to-all-start = ((bf16[128,4,256]{2,0,1:T(8,128)(2,1)}), bf16[128,4,256]{2,0,1:T(8,128)(2,1)S(1)}, u32[]{:S(2)}, u32[]{:S(2)}) async-start(bf16[128,4,256]{2,0,1:T(8,128)(2,1)} %bitcast.147), calls=%async_computation | async-start | bytes 524288 | tf_op jit(solution)/shard_map/all_to_all | solution.py:32
  15.2 64.5 %all-reduce.9.cloned.1.call-start = ((), (), s32[]{:S(2)}) async-start(), calls=%async_computation.2 | async-start | bytes 524288 | tf_op jit(solution)/shard_map/psum | solution.py:51
  25.6 113.4 %all-reduce.11.cloned.1.call-start = ((), (), s32[]{:S(2)}) async-start(), calls=%async_computation.3 | async-start | bytes 524288 | tf_op jit(solution)/shard_map/psum | solution.py:51
  85.9 112.7 %all-reduce.13.cloned.1.call-start = ((), (), s32[]{:S(2)}) async-start(), calls=%async_computation.4 | async-start | bytes 524288 | tf_op jit(solution)/shard_map/psum | solution.py:51
  142.6 5.0 copy-start.7
  145.5 112.7 %all-reduce.15.cloned.1.call-start = ((), (), s32[]{:S(2)}) async-start(), calls=%async_computation.5 | async-start | bytes 524288 | tf_op jit(solution)/shard_map/psum | solution.py:51
  202.2 4.9 copy-start.9
  205.1 112.6 %all-reduce.17.cloned.1.call-start = ((), (), s32[]{:S(2)}) async-start(), calls=%async_computation.6 | async-start | bytes 524288 | tf_op jit(solution)/shard_map/psum | solution.py:51
  261.8 5.1 copy-start.11
  264.7 112.6 %all-reduce.19.cloned.1.call-start = ((), (), s32[]{:S(2)}) async-start(), calls=%async_computation.7 | async-start | bytes 524288 | tf_op jit(solution)/shard_map/psum | solution.py:51
  321.4 5.3 copy-start.13
  324.3 112.7 %all-reduce.21.cloned.1.call-start = ((), (), s32[]{:S(2)}) async-start(), calls=%async_computation.8 | async-start | bytes 524288 | tf_op jit(solution)/shard_map/psum | solution.py:51
  328.1 52.9 %copy-start.19 = (bf16[512,512]{1,0:T(8,128)(2,1)S(1)}, bf16[512,512]{1,0:T(8,128)(2,1)}, u32[]{:S(2)}) copy-start(bf16[512,512]{1,0:T(8,128)(2,1)} %mul.276) | copy-start | bytes 1572868
  381.0 5.2 copy-start.15
  386.2 134.8 %all-to-all-start.1 = ((bf16[512,4,256]{2,0,1:T(8,128)(2,1)}), bf16[512,4,256]{2,0,1:T(8,128)(2,1)S(1)}, u32[]{:S(2)}, u32[]{:S(2)}) async-start(bf16[512,4,256]{2,0,1:T(8,128)(2,1)} %bitcast.146), calls=%async_computation.1 | async-start | bytes 2097152 | tf_op jit(solution)/shard_map/all_to_all | solution.py:33
  390.8 126.4 %all-reduce.23.cloned.1.call-start = ((), (), s32[]{:S(2)}) async-start(), calls=%async_computation.9 | async-start | bytes 524288 | tf_op jit(solution)/shard_map/psum | solution.py:51
  394.5 46.2 %copy-start.20 = (bf16[512,512]{1,0:T(8,128)(2,1)S(1)}, bf16[512,512]{1,0:T(8,128)(2,1)}, u32[]{:S(2)}) copy-start(bf16[512,512]{1,0:T(8,128)(2,1)} %mul.281) | copy-start | bytes 1572868
  440.6 7.3 %copy-start.17 = (bf16[512,256]{1,0:T(8,128)(2,1)}, bf16[512,256]{1,0:T(8,128)(2,1)S(1)}, u32[]{:S(2)}) copy-start(bf16[512,256]{1,0:T(8,128)(2,1)S(1)} %get-tuple-element.79) | copy-start | bytes 786436
  440.6 4.6 copy-start.24
  522.6 2.6 copy-start.4
  522.6 2.6 copy-start.8
  522.6 10.3 %slice-start = ((s8[16777216]{0:T(1024)(128)(4,1)}), s8[4194304]{0:T(1024)(128)(4,1)S(1)}, s32[]{:S(2)}) async-start(s8[16777216]{0:T(1024)(128)(4,1)} %bitcast.148), calls=%async_computation.10 | async-start | bytes 8388608
  525.1 2.6 copy-start.3
  525.1 2.6 copy-start.10
  525.1 7.8 %slice-start.1 = ((s8[16777216]{0:T(1024)(128)(4,1)}), s8[4194304]{0:T(1024)(128)(4,1)S(1)}, s32[]{:S(2)}) async-start(s8[16777216]{0:T(1024)(128)(4,1)} %bitcast.148), calls=%async_computation.11 | async-start | bytes 8388608
  527.7 2.6 copy-start.2
  527.7 2.6 copy-start.12
  527.7 5.2 slice-start.2
  530.3 3.1 slice-start.3
  530.3 3.7 copy-start.1
  530.3 3.7 copy-start.14
  (8 other events, 12.3 us)
Sparse Core Ops, SparseCore 0:
  25.7 53.8 all-reduce.8
  86.0 52.9 all-reduce.10
  145.6 52.9 all-reduce.12
  205.3 52.8 all-reduce.14
  264.9 52.8 all-reduce.16
  324.5 52.8 all-reduce.18
  384.1 52.9 all-reduce.20
  443.7 52.9 all-reduce.22
where the time goes:
time: 549 us; the launch traced here: 547 us
  waiting for transfers between devices  341 us (62%)
  local copies, waits for them, and re-layouts  93.1 us (17%)
  matrix products  53 us (10%)
  between operations  40.1 us (7%)
  starting transfers between devices  11.4 us (2%)
  other arithmetic  8.4 us (2%)
    psum x8, waiting for transfers between devices, local(): panel = lax.psum(placed.astype(jnp.bfloat16), 'rows').astype(jnp.float32)  340 us
    mul x30, local copies, waits for them, and re-layouts, masked_columns(): columns.reshape(blocks, BS, SB, BS)  78.5 us
    dot_general x8, matrix products, split_product(): jnp.dot(matrix, low_part, preferred_element_type=jnp.float32)  17 us
    dot_general x8, matrix products, local(): jnp.dot(masked_columns(anc_rows, anc_pattern, node_label), solved, prefer...  14.3 us
    dot_general x8, matrix products, split_product(): first_term = jnp.dot(matrix, high_part, preferred_element_type=jnp.float32)  11.2 us
  transfers between devices with their start and end apart: 10, of which 8 were waited for; matrix products, arithmetic and copies ran while one was open for 17% of the time, Pallas kernels for 0%

commit v1 on v0

v1 whole, which is shorter than its diff:
```python
import jax
import jax.numpy as jnp
from jax import lax
from jax.experimental import pallas as pl
from jax.experimental.pallas import tpu as pltpu
from jax.sharding import PartitionSpec as P

BS = 64
SB = 8
NSUP = 8
SN = 512
NW = 4096
NWB = 64
GROUPS = 4
PAIR = 2 * SN
F32 = jnp.float32
BF16 = jnp.bfloat16


def masked_columns(factor, pattern, node_label):
    blocks = pattern.shape[0]
    columns = lax.dynamic_slice_in_dim(factor, node_label * SN, SN, 1)
    chosen = lax.dynamic_slice_in_dim(pattern, node_label * SB, SB, 1)
    shaped = columns.reshape(blocks, BS, SB, BS) * chosen[:, None, :, None].astype(BF16)
    return shaped.reshape(blocks * BS, SN)


def general_path(win_rows, anc_rows, win_pattern, anc_pattern, window_owner, sn_order, diag_inv, win_rhs, anc_rhs):
    columns_rhs = win_rhs.shape[1]
    slot_count = win_rows.shape[0] // BS
    first_slot = lax.axis_index("rows") * slot_count
    local_pattern = lax.dynamic_slice_in_dim(win_pattern, first_slot, slot_count, 0)

    def step(position, carry):
        solution, win_resid, anc_resid = carry
        node_label = sn_order[position]
        owners = lax.dynamic_slice_in_dim(window_owner, node_label * SB, SB, 0)
        inverse = lax.dynamic_index_in_dim(diag_inv, node_label, 0, keepdims=False)
        local_place = owners - first_slot
        present = (local_place >= 0) & (local_place < slot_count)
        resid_blocks = win_resid.reshape(slot_count, BS, columns_rhs)
        taken = jnp.take(resid_blocks, jnp.clip(local_place, 0, slot_count - 1), axis=0)
        placed = jnp.where(present[:, None, None], taken, 0.0).reshape(SN, columns_rhs)
        panel = lax.psum(placed.astype(BF16), "rows")
        solved = jnp.dot(inverse, panel, preferred_element_type=F32).astype(BF16)
        solution = lax.dynamic_update_slice_in_dim(solution, solved, node_label * SN, 0)
        win_part = jnp.dot(masked_columns(win_rows, local_pattern, node_label), solved, preferred_element_type=F32)
        anc_part = jnp.dot(masked_columns(anc_rows, anc_pattern, node_label), solved, preferred_element_type=F32)
        return solution, win_resid - win_part, anc_resid - anc_part

    first = (jnp.zeros((NW, columns_rhs), BF16), win_rhs.astype(F32), anc_rhs.astype(F32))
    solution, _, anc_resid = lax.fori_loop(0, NSUP, step, first)
    return solution, anc_resid.astype(BF16)


def expand_mask(rows_pattern, first_block, width):
    block_index = lax.broadcasted_iota(jnp.int32, (NWB, width), 0)
    lane_index = lax.broadcasted_iota(jnp.int32, (NWB, width), 1)
    spread = (block_index == first_block + lane_index // BS).astype(F32).astype(BF16)
    return jnp.dot(rows_pattern.astype(F32).astype(BF16), spread, preferred_element_type=F32).astype(BF16)


def masked_rows(block_of, mask, count):
    return jnp.concatenate([block_of(j) * mask[j:j + 1, :] for j in range(count)], axis=0)


def factor_pack_kernel(owner, order, pattern, win_ref, out_ref, buf, inv_sm, pos_sm, sem):
    row = lax.axis_index("rows")

    def note_slot(w, c):
        slot = owner[w]

        @pl.when(slot // SB == row)
        def _():
            inv_sm[slot % SB] = w

        return c

    lax.fori_loop(0, NWB, note_slot, 0)
    for k in range(NSUP):
        pos_sm[order[k]] = k
    labels = []
    for t in range(SB):
        label = order[(pos_sm[inv_sm[t] // SB] // 2) * 2]
        labels.append(label)
        pltpu.make_async_copy(
            win_ref.at[pl.ds(t * BS, BS), pl.ds(pl.multiple_of(label * SN, SN), SN)],
            buf.at[pl.ds(t * BS, BS), :], sem).start()
    pltpu.make_async_copy(win_ref.at[:, pl.ds(0, SN)], buf, sem).wait()
    own = pattern[pl.ds(pl.multiple_of(row * SB, SB), SB), :]
    for t in range(SB):
        mask = expand_mask(own, labels[t] * SB, SN)
        out_ref[t * BS:(t + 1) * BS, :] = buf[t * BS:(t + 1) * BS, :] * mask[t:t + 1, :]


def place_of(owner, order, i, group):
    w = order[2 * group + i // SB] * SB + i % SB
    return owner[w]


def pack_group(owner, order, resid_ref, p_ref, b_ref, cnt, group):
    row = lax.axis_index("rows")
    chip, core = row // 2, row % 2
    cnt[0] = 0

    def one(i, c):
        slot = place_of(owner, order, i, group)

        @pl.when(slot // (2 * SB) == chip)
        def _():
            rank = cnt[0]
            cnt[0] = rank + 1
            side = jnp.where((slot // SB) % 2 == core, 0, 1)
            at = pl.multiple_of((side * SB + slot % SB) * BS, BS)

            @pl.when(rank < SB)
            def _():
                block = resid_ref[pl.ds(at, BS), :].astype(BF16)
                p_ref[pl.ds(pl.multiple_of(rank * BS, BS), BS), :] = block

                @pl.when(rank // 4 == core)
                def _():
                    b_ref[pl.ds(pl.multiple_of((rank % 4) * BS, BS), BS), :] = block

        return c

    lax.fori_loop(0, 2 * SB, one, 0)


def first_pack_kernel(owner, order, own_ref, other_ref, resid_ref, p_ref, b_ref, cnt):
    half = SB * BS
    resid_ref[0:half, :] = own_ref[...].astype(F32)
    resid_ref[half:2 * half, :] = other_ref[...].astype(F32)
    pack_group(owner, order, resid_ref, p_ref, b_ref, cnt, 0)


def make_group_kernel(group):
    last = group == GROUPS - 1

    def kernel(*refs):
        owner, order, pattern, p_own, a_own, a_swap, b_own, b_swap = refs[:8]
        l_refs = refs[8:16]
        diag_ref = refs[16]
        refs = refs[17:]
        if last:
            x_ref, panel, lbuf, dbuf, cnt, lsem, dsem = refs
        else:
            (w_own, w_other, resid_in, x_ref, resid_ref, p_ref, b_ref,
             panel, lbuf, dbuf, wbuf, cnt, lsem, dsem, wsem) = refs
        row = lax.axis_index("rows")
        chip, core = row // 2, row % 2
        labels = (order[2 * group], order[2 * group + 1])
        for q in range(2):
            pltpu.make_async_copy(diag_ref.at[labels[q]], dbuf.at[q], dsem.at[q]).start()
        for i in range(SB):
            slot = place_of(owner, order, SB + i, group)
            source = jnp.bitwise_xor(slot // SB, row)
            at = pl.multiple_of((slot % SB) * BS, BS)
            for m in range(8):
                @pl.when(source == m)
                def _(m=m, at=at, i=i):
                    pltpu.make_async_copy(l_refs[m].at[pl.ds(at, BS), :], lbuf.at[pl.ds(i * BS, BS), :], lsem).start()
        if not last:
            for q in range(2):
                cols = pl.ds(pl.multiple_of(labels[q] * SN, SN), SN)
                pltpu.make_async_copy(w_own.at[:, cols], wbuf.at[0, q], wsem.at[0, q]).start()
                pltpu.make_async_copy(w_other.at[:, cols], wbuf.at[1, q], wsem.at[1, q]).start()
        for c in range(4):
            cnt[c] = 0

        def one(i, carry):
            slot = place_of(owner, order, i, group)
            where = slot // (2 * SB)
            rank = cnt[where]
            cnt[where] = rank + 1
            rank = jnp.minimum(rank, SB - 1)
            rel = jnp.bitwise_xor(where, chip)
            full = pl.ds(pl.multiple_of(rank * BS, BS), BS)
            half = pl.ds(pl.multiple_of((rank % 4) * BS, BS), BS)
            dst = pl.ds(pl.multiple_of(i * BS, BS), BS)
            direct = rel == 1 + core
            same_half = rank // 4 == core

            @pl.when(rel == 0)
            def _():
                panel[dst, :] = p_own[full, :]

            @pl.when((rel == 1 + core) & (rel != 3))
            def _():
                panel[dst, :] = a_own[full, :]

            @pl.when((rel == 2 - core) & (rel != 3))
            def _():
                panel[dst, :] = a_swap[full, :]

            @pl.when((rel == 3) & same_half)
            def _():
                panel[dst, :] = b_own[half, :]

            @pl.when((rel == 3) & jnp.logical_not(same_half))
            def _():
                panel[dst, :] = b_swap[half, :]

            return carry

        lax.fori_loop(0, 2 * SB, one, 0)
        pltpu.make_async_copy(diag_ref.at[0], dbuf.at[0], dsem.at[0]).wait()
        x_a = jnp.dot(dbuf[0], panel[0:SN, :], preferred_element_type=F32).astype(BF16)
        x_ref[0:SN, :] = x_a
        pltpu.make_async_copy(l_refs[0], lbuf, lsem).wait()
        rest = panel[SN:PAIR, :].astype(F32) - jnp.dot(lbuf[...], x_a, preferred_element_type=F32)
        pltpu.make_async_copy(diag_ref.at[0], dbuf.at[1], dsem.at[1]).wait()
        x_b = jnp.dot(dbuf[1], rest.astype(BF16), preferred_element_type=F32).astype(BF16)
        x_ref[SN:PAIR, :] = x_b
        if last:
            return
        for side in range(2):
            rows = pattern[pl.ds(pl.multiple_of(jnp.bitwise_xor(row, side) * SB, SB), SB), :]
            total = resid_in[side * SN:(side + 1) * SN, :]
            for q, solved in enumerate((x_a, x_b)):
                mask = expand_mask(rows, labels[q] * SB, SN)
                pltpu.make_async_copy(w_own.at[:, pl.ds(0, SN)], wbuf.at[side, q], wsem.at[side, q]).wait()
                part = masked_rows(lambda j: wbuf[side, q, j * BS:(j + 1) * BS, :], mask, SB)
                total = total - jnp.dot(part, solved, preferred_element_type=F32)
            resid_ref[side * SN:(side + 1) * SN, :] = total
        pack_group(owner, order, resid_ref, p_ref, b_ref, cnt, group + 1)

    return kernel


def anc_kernel(order, x0, x1, x2, x3, a_ref, pattern, rhs_ref, sol_ref, out_ref):
    @pl.when(pl.program_id(0) == 0)
    def _():
        for k, x in enumerate((x0, x1, x2, x3)):
            for q in range(2):
                at = pl.multiple_of(order[2 * k + q] * SN, SN)
                sol_ref[pl.ds(at, SN), :] = x[q * SN:(q + 1) * SN, :]

    total = rhs_ref[...].astype(F32)
    rows = pattern[...]
    for s in range(NSUP):
        mask = expand_mask(rows, s * SB, SN)
        part = masked_rows(lambda j: a_ref[j * BS:(j + 1) * BS, s * SN:(s + 1) * SN], mask, SB)
        total = total - jnp.dot(part, sol_ref[s * SN:(s + 1) * SN, :], preferred_element_type=F32)
    out_ref[...] = total.astype(BF16)


SMEM = pl.BlockSpec(memory_space=pltpu.SMEM)
VMEM = pl.BlockSpec(memory_space=pltpu.VMEM)
ANY = pl.BlockSpec(memory_space=pl.ANY)
PARAMS = pltpu.CompilerParams(vmem_limit_bytes=40 * 1024 * 1024)


def shape_of(dims, dtype=BF16):
    return jax.ShapeDtypeStruct(dims, dtype)


def local(win_rows, anc_rows, win_pattern, anc_pattern, window_owner, sn_order, diag_inv, rhs_win, rhs_anc):
    rows_size = lax.axis_size("rows")
    if rows_size != 8:
        win_rhs = lax.all_to_all(rhs_win, "rhs", split_axis=1, concat_axis=0, tiled=True)
        anc_rhs = lax.all_to_all(rhs_anc, "rhs", split_axis=1, concat_axis=0, tiled=True)
        return general_path(win_rows, anc_rows, win_pattern, anc_pattern, window_owner, sn_order, diag_inv, win_rhs, anc_rhs)

    def swap(x, m):
        return lax.ppermute(x, "rows", [(i, i ^ m) for i in range(8)])

    def neighbour(x):
        return lax.ppermute(x, "rows", [(i, i ^ (2 if i % 2 == 0 else 4)) for i in range(8)])

    columns = rhs_win.shape[1] // lax.axis_size("rhs")
    win_rhs = lax.all_to_all(rhs_win, "rhs", split_axis=1, concat_axis=0, tiled=True)
    win_other = swap(win_rhs, 1)
    l_own = pl.pallas_call(
        factor_pack_kernel,
        out_shape=shape_of((SB * BS, SN)),
        in_specs=[SMEM, SMEM, VMEM, ANY],
        out_specs=VMEM,
        scratch_shapes=[pltpu.VMEM((SB * BS, SN), BF16), pltpu.SMEM((SB,), jnp.int32),
                        pltpu.SMEM((NSUP,), jnp.int32), pltpu.SemaphoreType.DMA],
        compiler_params=PARAMS,
        name="factor_pack",
    )(window_owner, sn_order, win_pattern, win_rows)
    l_parts = [None] * 8
    l_parts[0] = l_own
    for m in (2, 4, 6):
        l_parts[m] = swap(l_own, m)
    for m in (0, 2, 4, 6):
        l_parts[m + 1] = swap(l_parts[m], 1)
    w_other = swap(win_rows, 1)
    resid, packed, part = pl.pallas_call(
        first_pack_kernel,
        out_shape=(shape_of((PAIR, columns), F32), shape_of((SN, columns)), shape_of((SN // 2, columns))),
        in_specs=[SMEM, SMEM, VMEM, VMEM],
        out_specs=(VMEM, VMEM, VMEM),
        scratch_shapes=[pltpu.SMEM((1,), jnp.int32)],
        compiler_params=PARAMS,
        name="first_pack",
    )(window_owner, sn_order, win_rhs, win_other)
    anc_rhs = lax.all_to_all(rhs_anc, "rhs", split_axis=1, concat_axis=0, tiled=True)
    solved = []
    for group in range(GROUPS):
        a_own = neighbour(packed)
        b_own = swap(part, 6)
        a_swap = swap(a_own, 1)
        b_swap = swap(b_own, 1)
        last = group == GROUPS - 1
        operands = [window_owner, sn_order, win_pattern, packed, a_own, a_swap, b_own, b_swap, *l_parts, diag_inv]
        in_specs = [SMEM, SMEM] + [VMEM] * 6 + [ANY] * 9
        scratch = [pltpu.VMEM((PAIR, columns), BF16), pltpu.VMEM((SN, SN), BF16), pltpu.VMEM((2, SN, SN), BF16)]
        sems = [pltpu.SMEM((4,), jnp.int32), pltpu.SemaphoreType.DMA, pltpu.SemaphoreType.DMA((2,))]
        if last:
            out_shape = (shape_of((PAIR, columns)),)
        else:
            operands += [win_rows, w_other, resid]
            in_specs += [ANY, ANY, VMEM]
            scratch += [pltpu.VMEM((2, 2, SN, SN), BF16)]
            sems += [pltpu.SemaphoreType.DMA((2, 2))]
            out_shape = (shape_of((PAIR, columns)), shape_of((PAIR, columns), F32),
                         shape_of((SN, columns)), shape_of((SN // 2, columns)))
        results = pl.pallas_call(
            make_group_kernel(group),
            out_shape=out_shape,
            in_specs=in_specs,
            out_specs=(VMEM,) * len(out_shape),
            scratch_shapes=scratch + sems,
            compiler_params=PARAMS,
            name="pair_solve",
        )(*operands)
        solved.append(results[0])
        if not last:
            resid, packed, part = results[1:]

    anc_local = anc_rows.shape[0]
    tile = SB * BS
    chip_of = window_owner // (2 * SB)
    place = jnp.argsort(sn_order)
    group_of = jnp.repeat(place // 2, SB, total_repeat_length=NWB)
    same = (group_of[:, None] == group_of[None, :]) & (chip_of[:, None] == chip_of[None, :])
    fits = jnp.max(jnp.sum(same.astype(jnp.int32), axis=1)) <= SB

    def packed_path(*xs):
        return pl.pallas_call(
            anc_kernel,
            out_shape=(shape_of((NW, columns)), shape_of((anc_local, columns))),
            grid=(anc_local // tile,),
            in_specs=[SMEM] + [pl.BlockSpec((PAIR, columns), lambda i: (0, 0))] * 4 + [
                pl.BlockSpec((tile, NW), lambda i: (i, 0)),
                pl.BlockSpec((SB, NWB), lambda i: (i, 0)),
                pl.BlockSpec((tile, columns), lambda i: (i, 0)),
            ],
            out_specs=(pl.BlockSpec((NW, columns), lambda i: (0, 0)), pl.BlockSpec((tile, columns), lambda i: (i, 0))),
            compiler_params=PARAMS,
            name="rows_below",
        )(sn_order, *xs, anc_rows, anc_pattern, anc_rhs)

    def other_path(*xs):
        return general_path(win_rows, anc_rows, win_pattern, anc_pattern, window_owner, sn_order, diag_inv, win_rhs, anc_rhs)

    return tuple(lax.cond(fits, packed_path, other_path, *solved))


def solution(mesh):
    return jax.shard_map(
        local,
        mesh=mesh,
        in_specs=(P("rows", None), P("rows", None), P(), P("rows", None), P(), P(), P(),
                  P(("rows", "rhs"), None), P(("rows", "rhs"), None)),
        out_specs=(P(None, "rhs"), P("rows", "rhs")),
        check_vma=False,
    )
```

time: 549 us -> 166 us (0.30)
  waiting for transfers between devices: 341 us -> 41.4 us
  local copies, waits for them, and re-layouts: 93.1 us -> 20.4 us
  matrix products: 53 us -> 0 us
  Pallas kernels: 0 us -> 45.1 us
  between operations: 40.1 us -> 15 us
  blocking collectives: 0 us -> 15.2 us
  starting transfers between devices: 11.4 us -> 21 us
    psum x8 -> x0, waiting for transfers between devices: 340 us -> none  [local(): panel = lax.psum(placed.astype(jnp.bfloat16), 'rows').astype(jnp.float32)]
    mul x30 -> x0, local copies, waits for them, and re-layouts: 78.5 us -> none  [masked_columns(): columns.reshape(blocks, BS, SB, BS)]
    dot_general x31 -> x0, matrix products: 53 us -> none  [the longest x8 17 us: split_product(): jnp.dot(matrix, low_part, preferred_element_type=jnp.float32)]
    pallas_call x0 -> x7, Pallas kernels: none -> 45.1 us  [the longest x4 28.4 us: local(): pl.pallas_call(make_group_kernel(group), out_shape=out_shape, in_specs=in...]
    ppermute x0 -> x25, waiting for transfers between devices: none -> 41.4 us  [the longest x21 31.9 us: swap(): return lax.ppermute(x, 'rows', [(i, i ^ m) for i in range(8)])]
    ppermute x0 -> x25, starting transfers between devices: none -> 16.7 us  [the longest x21 11.5 us: swap(): return lax.ppermute(x, 'rows', [(i, i ^ m) for i in range(8)])]
    all_to_all x0 -> x1, blocking collectives: none -> 15.2 us  [local(): lax.all_to_all(rhs_win, 'rhs', split_axis=1, concat_axis=0, tiled=True)]
    unnamed x60 -> x66, local copies, waits for them, and re-layouts: 4.3 us -> 17.7 us
  transfers between devices with their start and end apart: 10 -> 26, of which waited for: 8 -> 12; matrix products, arithmetic and copies ran while one was open for 17% -> 6% of each run, Pallas kernels for 0% -> 12%
where the time goes in v1:
time: 166 us; the launch traced here: 165 us
  Pallas kernels  45.1 us (27%)
  waiting for transfers between devices  41.4 us (25%)
  starting transfers between devices  21 us (13%)
  local copies, waits for them, and re-layouts  20.4 us (12%)
  blocking collectives  15.2 us (9%)
  between operations  15 us (9%)
  other arithmetic  6.78 us (4%)
    ppermute x21, waiting for transfers between devices, swap(): return lax.ppermute(x, 'rows', [(i, i ^ m) for i in range(8)])  31.9 us
    pallas_call x4, Pallas kernels, local(): pl.pallas_call(make_group_kernel(group), out_shape=out_shape, in_specs=in...  28.4 us
    unnamed x66, local copies, waits for them, and re-layouts  17.7 us
    all_to_all x1, blocking collectives, local(): lax.all_to_all(rhs_win, 'rhs', split_axis=1, concat_axis=0, tiled=True)  15.2 us
    pallas_call x1, Pallas kernels, packed_path(): pl.pallas_call(anc_kernel, out_shape=(shape_of((NW, columns)), shape_of((...  12.2 us
    ppermute x21, starting transfers between devices, swap(): return lax.ppermute(x, 'rows', [(i, i ^ m) for i in range(8)])  11.5 us
    ppermute x4, waiting for transfers between devices, neighbour(): lax.ppermute(x, 'rows', [(i, i ^ (2 if i % 2 == 0 else 4)) for i in range...  9.55 us
    ppermute x4, starting transfers between devices, neighbour(): lax.ppermute(x, 'rows', [(i, i ^ (2 if i % 2 == 0 else 4)) for i in range...  5.22 us
  transfers between devices with their start and end apart: 26, of which 12 were waited for; matrix products, arithmetic and copies ran while one was open for 6% of the time, Pallas kernels for 12%

profile of v1, /device:TPU:0, one launch (start us, length us, event | category | flops | bytes accessed | tf_op | source)
XLA Modules:
  0.0 164.8 jit_solution(3764717740776674355)
XLA Ops:
  8.7 15.2 %all_to_all.38 = bf16[128,4,256]{2,0,1:T(8,128)(2,1)S(1)} all-to-all(bf16[128,4,256]{2,0,1:T(8,128)(2,1)S(1)} %bitcast.61), channel_id=1, replica_groups=mesh['rows'=8,'rhs'=4] {'rhs'}, dimensions={1} | all-to-all | bytes 524288 | tf_op jit(solution)/shard_map/all_to_all | solution.py:272
  24.0 3.3 %factor_pack.1.refs_8_ = bf16[512,512]{1,0:T(8,128)(2,1)S(1)} custom-call(s32[64]{0:T(128)} %refs_0_.7, s32[8]{0:T(128)} %refs_1_.7, s32[64,64]{1,0:T(8,128)} %refs_2_.7, bf16[512,4096]{1,0:T(8,128)(2,1)} %refs_17_.5), custom_call_target="tpu_custom_call" | custom-call | tf_op jit(solution)/shard_map/factor_pack/pallas_call | solution.py:274
  27.3 2.5 %collective-permute-start.10 = (bf16[512,512]{1,0:T(8,128)(2,1)S(1)}, bf16[512,512]{1,0:T(8,128)(2,1)S(1)}, u32[]{:S(2)}, u32[]{:S(2)}) collective-permute-start(bf16[512,512]{1,0:T(8,128)(2,1)S(1)} %factor_pack.1.refs_8_), channel_id=1, source_target_pairs={{0,24},{4,28},{8,16},{12,20},{16,8},{20,12},{24,0},{28,4},{1,25},{... | collective-permute-start | bytes 1572872 | tf_op jit(solution)/shard_map/ppermute | solution.py:266
  30.9 1.2 first_pack.1
  32.0 11.0 %collective-permute-done.10.refs_14_ = bf16[512,512]{1,0:T(8,128)(2,1)S(1)} collective-permute-done((bf16[512,512]{1,0:T(8,128)(2,1)S(1)}, bf16[512,512]{1,0:T(8,128)(2,1)S(1)}, u32[]{:S(2)}, u32[]{:S(2)}) %collective-permute-start.10) | collective-permute-done | bytes 524320 | tf_op jit(solution)/shard_map/ppermute | solution.py:266
  43.0 2.4 %collective-permute-start.3 = (bf16[256,256]{1,0:T(8,128)(2,1)S(1)}, bf16[256,256]{1,0:T(8,128)(2,1)S(1)}, u32[]{:S(2)}, u32[]{:S(2)}) collective-permute-start(bf16[256,256]{1,0:T(8,128)(2,1)S(1)} %get-tuple-element.282), channel_id=1, source_target_pairs={{0,24},{4,28},{8,16},{12,20},{16,8},{20,12},{24,0},{28,4},{1,25},{... | collective-permute-start | bytes 393224 | tf_op jit(solution)/shard_map/ppermute | solution.py:266
  45.5 8.8 %collective-permute-done.6.refs_10_ = bf16[512,512]{1,0:T(8,128)(2,1)S(1)} collective-permute-done((bf16[512,512]{1,0:T(8,128)(2,1)S(1)}, bf16[512,512]{1,0:T(8,128)(2,1)S(1)}, u32[]{:S(2)}, u32[]{:S(2)}) %collective-permute-start.6) | collective-permute-done | bytes 524320 | tf_op jit(solution)/shard_map/ppermute | solution.py:266
  54.3 1.5 collective-permute-start.1
  56.6 4.1 %collective-permute-done.1.refs_4_ = bf16[512,256]{1,0:T(8,128)(2,1)S(1)} collective-permute-done((bf16[512,256]{1,0:T(8,128)(2,1)S(1)}, bf16[512,256]{1,0:T(8,128)(2,1)S(1)}, u32[]{:S(2)}, u32[]{:S(2)}) %collective-permute-start.1) | collective-permute-done | bytes 262176 | tf_op jit(solution)/shard_map/ppermute | solution.py:269
  60.7 1.3 collective-permute-done.4.refs_7_
  62.2 1.4 collective-permute-done.2.refs_5_
  63.6 7.4 %pair_solve.4 = (bf16[1024,256]{1,0:T(8,128)(2,1)}, f32[1024,256]{1,0:T(8,128)S(1)}, bf16[512,256]{1,0:T(8,128)(2,1)S(1)}, bf16[256,256]{1,0:T(8,128)(2,1)S(1)}) custom-call(s32[64]{0:T(128)S(1)} %copy-done.27, s32[8]{0:T(128)S(1)} %copy-done.29, s32[64,64]{1,0:T(8,128)S(1)} %copy-done.25, bf16[512,256]{1,0:T(8,128)(2,1)S(1)} %get-tuple-element.281.refs_3_, ...), custom_call_target="tpu_custom_call" | custom-call | tf_op jit(solution)/shard_map/pair_solve/pallas_call | solution.py:321
  72.0 1.4 collective-permute-start.13
  74.5 4.3 %all-to-all-start.1 = ((bf16[512,4,256]{2,0,1:T(8,128)(2,1)}), bf16[512,4,256]{2,0,1:T(8,128)(2,1)}, u32[]{:S(2)}, u32[]{:S(2)}) async-start(bf16[512,4,256]{2,0,1:T(8,128)(2,1)} %bitcast.56), calls=%async_computation.1 | async-start | bytes 2097152 | tf_op jit(solution)/shard_map/all_to_all | solution.py:300
  79.9 4.8 %collective-permute-done.15.refs_6_ = bf16[256,256]{1,0:T(8,128)(2,1)S(1)} collective-permute-done((bf16[256,256]{1,0:T(8,128)(2,1)S(1)}, bf16[256,256]{1,0:T(8,128)(2,1)S(1)}, u32[]{:S(2)}, u32[]{:S(2)}) %collective-permute-start.15) | collective-permute-done | bytes 131104 | tf_op jit(solution)/shard_map/ppermute | solution.py:266
  84.7 1.3 collective-permute-done.16.refs_7_
  86.0 2.2 %copy-done.1 = bf16[512,4096]{1,0:T(8,128)(2,1)S(1)} copy-done((bf16[512,4096]{1,0:T(8,128)(2,1)S(1)}, bf16[512,4096]{1,0:T(8,128)(2,1)}, u32[]{:S(2)}) %copy-start.1) | copy-done | bytes 4194328
  89.3 1.0 copy-done.8
  90.3 1.2 copy-done.14
  92.5 7.6 %pair_solve.5 = (bf16[1024,256]{1,0:T(8,128)(2,1)}, f32[1024,256]{1,0:T(8,128)S(1)}, bf16[512,256]{1,0:T(8,128)(2,1)S(1)}, bf16[256,256]{1,0:T(8,128)(2,1)}) custom-call(s32[64]{0:T(128)S(1)} %copy-done.27, s32[8]{0:T(128)S(1)} %copy-done.29, s32[64,64]{1,0:T(8,128)} %refs_2_.7, bf16[512,256]{1,0:T(8,128)(2,1)S(1)} %copy-done.16, ...), custom_call_target="tpu_custom_call" | custom-call | tf_op jit(solution)/shard_map/pair_solve/pallas_call | solution.py:321
  102.0 1.5 collective-permute-start.19
  103.6 5.4 %collective-permute-done.17.refs_4_ = bf16[512,256]{1,0:T(8,128)(2,1)} collective-permute-done((bf16[512,256]{1,0:T(8,128)(2,1)S(1)}, bf16[512,256]{1,0:T(8,128)(2,1)}, u32[]{:S(2)}, u32[]{:S(2)}) %collective-permute-start.17) | collective-permute-done | bytes 262176 | tf_op jit(solution)/shard_map/ppermute | solution.py:269
  110.7 1.3 collective-permute-done.20.refs_7_
  112.1 2.2 %copy-done.2 = bf16[512,4096]{1,0:T(8,128)(2,1)S(1)} copy-done((bf16[512,4096]{1,0:T(8,128)(2,1)S(1)}, bf16[512,4096]{1,0:T(8,128)(2,1)}, u32[]{:S(2)}) %copy-start.2) | copy-done | bytes 4194328
  116.3 1.2 copy-done.12
  117.6 8.1 %pair_solve.6 = (bf16[1024,256]{1,0:T(8,128)(2,1)}, f32[1024,256]{1,0:T(8,128)}, bf16[512,256]{1,0:T(8,128)(2,1)S(1)}, bf16[256,256]{1,0:T(8,128)(2,1)S(1)}) custom-call(s32[64]{0:T(128)S(1)} %copy-done.27, s32[8]{0:T(128)S(1)} %copy-done.29, s32[64,64]{1,0:T(8,128)} %refs_2_.7, bf16[512,256]{1,0:T(8,128)(2,1)S(1)} %get-tuple-element.289.refs_3_, ...), custom_call_target="tpu_custom_call" | custom-call | tf_op jit(solution)/shard_map/pair_solve/pallas_call | solution.py:321
  125.7 1.4 collective-permute-start.21
  128.5 1.1 collective-permute-start.23
  129.6 4.9 %select_select_fusion = s32[64]{0:T(128)S(1)} fusion(pred[64]{0:T(512)(128)(4,1)S(1)} %copy-done.31, pred[64]{0:T(512)(128)(4,1)S(1)} %copy-done.32, pred[64]{0:T(512)(128)(4,1)S(1)} %copy-done.33, pred[64]{0:T(512)(128)(4,1)S(1)} %copy-done.34, pred[64]{0:T(512)(128)(4,1)S(1)} %copy-done.35, pred[64]{0:T(512)(128)(4,1)S(1)} %copy-done.36, ...), kind=kLoop, calls=%fused_computation.36 | loop fusion | flops 448 | bytes 736 | tf_op jit(solution)/shard_map/jit(_take)/gather | solution.py:338
  140.4 5.3 %pair_solve.7 = bf16[1024,256]{1,0:T(8,128)(2,1)} custom-call(s32[64]{0:T(128)} %refs_0_.7, s32[8]{0:T(128)} %refs_1_.7, s32[64,64]{1,0:T(8,128)} %refs_2_.7, bf16[512,256]{1,0:T(8,128)(2,1)S(1)} %copy-done.18, bf16[512,256]{1,0:T(8,128)(2,1)S(1)} %collective-permute-done.21.refs_4_, bf16[512,256]{1,0:T(8,128)(2,1)} %collective-permute-done.22.refs_5_, ...), custom_call_target="tpu_custom_call" | custom-call | tf_op jit(solution)/shard_map/pair_solve/pallas_call | solution.py:321
  145.8 12.2 %conditional.1 = ((bf16[4096,256]{1,0:T(8,128)(2,1)}, bf16[2048,256]{1,0:T(8,128)(2,1)})) conditional(s32[]{:T(128)} %convert_element_type.46, (bf16[512,256]{1,0:T(8,128)(2,1)}, bf16[2048,256]{1,0:T(8,128)(2,1)}, s32[64,64]{1,0:T(8,128)}, s32[8]{0:T(128)}, bf16[8,512,512]{2,1,0:T(8,128)(2,1)}, /*index=5*/s32[64]{0:T(128)}, ...), branch_computations={%region_3.7_spmd, %region_7.8_spmd} | conditional | flops 812909952 | bytes 49824296 | solution.py:360
  145.8 12.2 %rows_below.1 = (bf16[4096,256]{1,0:T(8,128)(2,1)}, bf16[2048,256]{1,0:T(8,128)(2,1)}) custom-call(s32[8]{0:T(128)} %get-tuple-element.255.order, bf16[1024,256]{1,0:T(8,128)(2,1)} %get-tuple-element.256.x0, bf16[1024,256]{1,0:T(8,128)(2,1)} %get-tuple-element.257.x1, bf16[1024,256]{1,0:T(8,128)(2,1)} %get-tuple-element.258.x2, ...), custom_call_target="tpu_custom_call" | custom-call | tf_op jit(solution)/shard_map/cond/branch_1_fun/rows_below/pallas_call | solution.py:343
  (105 shorter events, 21.1 us)
Async XLA Ops:
  7.2 56.4 %collective-permute-start.12 = (bf16[512,4096]{1,0:T(8,128)(2,1)}, bf16[512,4096]{1,0:T(8,128)(2,1)S(1)}, u32[]{:S(2)}, u32[]{:S(2)}) collective-permute-start(bf16[512,4096]{1,0:T(8,128)(2,1)} %refs_17_.5), channel_id=1, source_target_pairs={{0,4},{4,0},{8,12},{12,8},{16,20},{20,16},{24,28},{28,24},{1,5},{5... | collective-permute-start | bytes 12582920 | tf_op jit(solution)/shard_map/ppermute | solution.py:266
  23.9 39.7 %copy-start.21 = (bf16[512,4096]{1,0:T(8,128)(2,1)S(1)}, bf16[512,4096]{1,0:T(8,128)(2,1)}, u32[]{:S(2)}) copy-start(bf16[512,4096]{1,0:T(8,128)(2,1)} %refs_17_.5) | copy-start | bytes 12582916
  23.9 39.7 %copy-start.25 = (s32[64,64]{1,0:T(8,128)S(1)}, s32[64,64]{1,0:T(8,128)}, u32[]{:S(2)}) copy-start(s32[64,64]{1,0:T(8,128)} %refs_2_.7) | copy-start | bytes 49156
  23.9 7.0 %collective-permute-start = (bf16[512,256]{1,0:T(8,128)(2,1)S(1)}, bf16[512,256]{1,0:T(8,128)(2,1)S(1)}, u32[]{:S(2)}, u32[]{:S(2)}) collective-permute-start(bf16[512,256]{1,0:T(8,128)(2,1)S(1)} %bitcast.57), channel_id=1, source_target_pairs={{0,4},{4,0},{8,12},{12,8},{16,20},{20,16},{24,28},{28,24},{1,5},{5... | collective-permute-start | bytes 786440 | tf_op jit(solution)/shard_map/ppermute | solution.py:266
  27.3 15.8 %collective-permute-start.10 = (bf16[512,512]{1,0:T(8,128)(2,1)S(1)}, bf16[512,512]{1,0:T(8,128)(2,1)S(1)}, u32[]{:S(2)}, u32[]{:S(2)}) collective-permute-start(bf16[512,512]{1,0:T(8,128)(2,1)S(1)} %factor_pack.1.refs_8_), channel_id=1, source_target_pairs={{0,24},{4,28},{8,16},{12,20},{16,8},{20,12},{24,0},{28,4},{1,25},{... | collective-permute-start | bytes 1572872 | tf_op jit(solution)/shard_map/ppermute | solution.py:266
  29.8 24.5 %collective-permute-start.6 = (bf16[512,512]{1,0:T(8,128)(2,1)S(1)}, bf16[512,512]{1,0:T(8,128)(2,1)S(1)}, u32[]{:S(2)}, u32[]{:S(2)}) collective-permute-start(bf16[512,512]{1,0:T(8,128)(2,1)S(1)} %factor_pack.1.refs_8_), channel_id=1, source_target_pairs={{0,8},{4,12},{8,0},{12,4},{16,24},{20,28},{24,16},{28,20},{1,9},{5... | collective-permute-start | bytes 1572872 | tf_op jit(solution)/shard_map/ppermute | solution.py:266
  30.3 25.5 %collective-permute-start.8 = (bf16[512,512]{1,0:T(8,128)(2,1)S(1)}, bf16[512,512]{1,0:T(8,128)(2,1)S(1)}, u32[]{:S(2)}, u32[]{:S(2)}) collective-permute-start(bf16[512,512]{1,0:T(8,128)(2,1)S(1)} %factor_pack.1.refs_8_), channel_id=1, source_target_pairs={{0,16},{4,20},{8,24},{12,28},{16,0},{20,4},{24,8},{28,12},{1,17},{... | collective-permute-start | bytes 1572872 | tf_op jit(solution)/shard_map/ppermute | solution.py:266
  30.8 25.0 %collective-permute-start.5 = (bf16[512,512]{1,0:T(8,128)(2,1)S(1)}, bf16[512,512]{1,0:T(8,128)(2,1)S(1)}, u32[]{:S(2)}, u32[]{:S(2)}) collective-permute-start(bf16[512,512]{1,0:T(8,128)(2,1)S(1)} %factor_pack.1.refs_8_), channel_id=1, source_target_pairs={{0,4},{4,0},{8,12},{12,8},{16,20},{20,16},{24,28},{28,24},{1,5},{5... | collective-permute-start | bytes 1572872 | tf_op jit(solution)/shard_map/ppermute | solution.py:266
  43.0 13.5 %collective-permute-start.3 = (bf16[256,256]{1,0:T(8,128)(2,1)S(1)}, bf16[256,256]{1,0:T(8,128)(2,1)S(1)}, u32[]{:S(2)}, u32[]{:S(2)}) collective-permute-start(bf16[256,256]{1,0:T(8,128)(2,1)S(1)} %get-tuple-element.282), channel_id=1, source_target_pairs={{0,24},{4,28},{8,16},{12,20},{16,8},{20,12},{24,0},{28,4},{1,25},{... | collective-permute-start | bytes 393224 | tf_op jit(solution)/shard_map/ppermute | solution.py:266
  54.3 6.4 %collective-permute-start.1 = (bf16[512,256]{1,0:T(8,128)(2,1)S(1)}, bf16[512,256]{1,0:T(8,128)(2,1)S(1)}, u32[]{:S(2)}, u32[]{:S(2)}) collective-permute-start(bf16[512,256]{1,0:T(8,128)(2,1)S(1)} %get-tuple-element.281.refs_3_), channel_id=1, source_target_pairs={{0,8},{4,20},{8,0},{12,28},{16,24},{20,4},{24,16},{28,12},{1,9},{5... | collective-permute-start | bytes 786440 | tf_op jit(solution)/shard_map/ppermute | solution.py:269
  55.8 6.4 %collective-permute-start.11 = (bf16[512,512]{1,0:T(8,128)(2,1)S(1)}, bf16[512,512]{1,0:T(8,128)(2,1)S(1)}, u32[]{:S(2)}, u32[]{:S(2)}) collective-permute-start(bf16[512,512]{1,0:T(8,128)(2,1)S(1)} %collective-permute-done.10.refs_14_), channel_id=1, source_target_pairs={{0,4},{4,0},{8,12},{12,8},{16,20},{20,16},{24,28},{28,24},{1,5},{5... | collective-permute-start | bytes 1572872 | tf_op jit(solution)/shard_map/ppermute | solution.py:266
  55.8 6.4 %collective-permute-start.7 = (bf16[512,512]{1,0:T(8,128)(2,1)S(1)}, bf16[512,512]{1,0:T(8,128)(2,1)S(1)}, u32[]{:S(2)}, u32[]{:S(2)}) collective-permute-start(bf16[512,512]{1,0:T(8,128)(2,1)S(1)} %collective-permute-done.6.refs_10_), channel_id=1, source_target_pairs={{0,4},{4,0},{8,12},{12,8},{16,20},{20,16},{24,28},{28,24},{1,5},{5... | collective-permute-start | bytes 1572872 | tf_op jit(solution)/shard_map/ppermute | solution.py:266
  56.6 5.7 %collective-permute-start.9 = (bf16[512,512]{1,0:T(8,128)(2,1)S(1)}, bf16[512,512]{1,0:T(8,128)(2,1)S(1)}, u32[]{:S(2)}, u32[]{:S(2)}) collective-permute-start(bf16[512,512]{1,0:T(8,128)(2,1)S(1)} %collective-permute-done.8.refs_12_), channel_id=1, source_target_pairs={{0,4},{4,0},{8,12},{12,8},{16,20},{20,16},{24,28},{28,24},{1,5},{5... | collective-permute-start | bytes 1572872 | tf_op jit(solution)/shard_map/ppermute | solution.py:266
  60.7 1.3 collective-permute-start.4
  62.1 1.5 collective-permute-start.2
  72.0 7.3 %collective-permute-start.13 = (bf16[512,256]{1,0:T(8,128)(2,1)S(1)}, bf16[512,256]{1,0:T(8,128)(2,1)}, u32[]{:S(2)}, u32[]{:S(2)}) collective-permute-start(bf16[512,256]{1,0:T(8,128)(2,1)S(1)} %get-tuple-element.285.refs_3_), channel_id=1, source_target_pairs={{0,8},{4,20},{8,0},{12,28},{16,24},{20,4},{24,16},{28,12},{1,9},{5... | collective-permute-start | bytes 786440 | tf_op jit(solution)/shard_map/ppermute | solution.py:269
  74.5 62.9 %all-to-all-start.1 = ((bf16[512,4,256]{2,0,1:T(8,128)(2,1)}), bf16[512,4,256]{2,0,1:T(8,128)(2,1)}, u32[]{:S(2)}, u32[]{:S(2)}) async-start(bf16[512,4,256]{2,0,1:T(8,128)(2,1)} %bitcast.56), calls=%async_computation.1 | async-start | bytes 2097152 | tf_op jit(solution)/shard_map/all_to_all | solution.py:300
  78.7 5.9 %collective-permute-start.15 = (bf16[256,256]{1,0:T(8,128)(2,1)S(1)}, bf16[256,256]{1,0:T(8,128)(2,1)S(1)}, u32[]{:S(2)}, u32[]{:S(2)}) collective-permute-start(bf16[256,256]{1,0:T(8,128)(2,1)S(1)} %get-tuple-element.286), channel_id=1, source_target_pairs={{0,24},{4,28},{8,16},{12,20},{16,8},{20,12},{24,0},{28,4},{1,25},{... | collective-permute-start | bytes 393224 | tf_op jit(solution)/shard_map/ppermute | solution.py:266
  79.4 6.7 %collective-permute-start.14 = (bf16[512,256]{1,0:T(8,128)(2,1)}, bf16[512,256]{1,0:T(8,128)(2,1)S(1)}, u32[]{:S(2)}, u32[]{:S(2)}) collective-permute-start(bf16[512,256]{1,0:T(8,128)(2,1)} %collective-permute-done.13.refs_4_), channel_id=1, source_target_pairs={{0,4},{4,0},{8,12},{12,8},{16,20},{20,16},{24,28},{28,24},{1,5},{5... | collective-permute-start | bytes 786440 | tf_op jit(solution)/shard_map/ppermute | solution.py:266
  84.7 1.3 collective-permute-start.16
  101.1 7.9 %collective-permute-start.17 = (bf16[512,256]{1,0:T(8,128)(2,1)S(1)}, bf16[512,256]{1,0:T(8,128)(2,1)}, u32[]{:S(2)}, u32[]{:S(2)}) collective-permute-start(bf16[512,256]{1,0:T(8,128)(2,1)S(1)} %get-tuple-element.289.refs_3_), channel_id=1, source_target_pairs={{0,8},{4,20},{8,0},{12,28},{16,24},{20,4},{24,16},{28,12},{1,9},{5... | collective-permute-start | bytes 786440 | tf_op jit(solution)/shard_map/ppermute | solution.py:269
  102.0 8.7 %collective-permute-start.19 = (bf16[256,256]{1,0:T(8,128)(2,1)}, bf16[256,256]{1,0:T(8,128)(2,1)S(1)}, u32[]{:S(2)}, u32[]{:S(2)}) collective-permute-start(bf16[256,256]{1,0:T(8,128)(2,1)} %get-tuple-element.290), channel_id=1, source_target_pairs={{0,24},{4,28},{8,16},{12,20},{16,8},{20,12},{24,0},{28,4},{1,25},{... | collective-permute-start | bytes 393224 | tf_op jit(solution)/shard_map/ppermute | solution.py:266
  109.0 3.1 %collective-permute-start.18 = (bf16[512,256]{1,0:T(8,128)(2,1)}, bf16[512,256]{1,0:T(8,128)(2,1)}, u32[]{:S(2)}, u32[]{:S(2)}) collective-permute-start(bf16[512,256]{1,0:T(8,128)(2,1)} %collective-permute-done.17.refs_4_), channel_id=1, source_target_pairs={{0,4},{4,0},{8,12},{12,8},{16,20},{20,16},{24,28},{28,24},{1,5},{5... | collective-permute-start | bytes 786440 | tf_op jit(solution)/shard_map/ppermute | solution.py:266
  110.7 1.3 collective-permute-start.20
  117.6 12.0 %copy-start.32 = (pred[64]{0:T(512)(128)(4,1)S(1)}, pred[64]{0:T(512)(128)(4,1)}, u32[]{:S(2)}) copy-start(pred[64]{0:T(512)(128)(4,1)} %constant.219) | copy-start | bytes 196
  117.6 12.0 %copy-start.33 = (pred[64]{0:T(512)(128)(4,1)S(1)}, pred[64]{0:T(512)(128)(4,1)}, u32[]{:S(2)}) copy-start(pred[64]{0:T(512)(128)(4,1)} %constant.220) | copy-start | bytes 196
  117.6 12.0 %copy-start.34 = (pred[64]{0:T(512)(128)(4,1)S(1)}, pred[64]{0:T(512)(128)(4,1)}, u32[]{:S(2)}) copy-start(pred[64]{0:T(512)(128)(4,1)} %constant.221) | copy-start | bytes 196
  117.6 12.0 %copy-start.35 = (pred[64]{0:T(512)(128)(4,1)S(1)}, pred[64]{0:T(512)(128)(4,1)}, u32[]{:S(2)}) copy-start(pred[64]{0:T(512)(128)(4,1)} %constant.222) | copy-start | bytes 196
  125.7 9.7 %collective-permute-start.21 = (bf16[512,256]{1,0:T(8,128)(2,1)S(1)}, bf16[512,256]{1,0:T(8,128)(2,1)S(1)}, u32[]{:S(2)}, u32[]{:S(2)}) collective-permute-start(bf16[512,256]{1,0:T(8,128)(2,1)S(1)} %get-tuple-element.293.refs_3_), channel_id=1, source_target_pairs={{0,8},{4,20},{8,0},{12,28},{16,24},{20,4},{24,16},{28,12},{1,9},{5... | collective-permute-start | bytes 786440 | tf_op jit(solution)/shard_map/ppermute | solution.py:269
  128.5 6.9 %collective-permute-start.23 = (bf16[256,256]{1,0:T(8,128)(2,1)S(1)}, bf16[256,256]{1,0:T(8,128)(2,1)S(1)}, u32[]{:S(2)}, u32[]{:S(2)}) collective-permute-start(bf16[256,256]{1,0:T(8,128)(2,1)S(1)} %get-tuple-element.294), channel_id=1, source_target_pairs={{0,24},{4,28},{8,16},{12,20},{16,8},{20,12},{24,0},{28,4},{1,25},{... | collective-permute-start | bytes 393224 | tf_op jit(solution)/shard_map/ppermute | solution.py:266
  135.4 2.0 %collective-permute-start.24 = (bf16[256,256]{1,0:T(8,128)(2,1)S(1)}, bf16[256,256]{1,0:T(8,128)(2,1)}, u32[]{:S(2)}, u32[]{:S(2)}) collective-permute-start(bf16[256,256]{1,0:T(8,128)(2,1)S(1)} %collective-permute-done.23.refs_6_), channel_id=1, source_target_pairs={{0,4},{4,0},{8,12},{12,8},{16,20},{20,16},{24,28},{28,24},{1,5},{5... | collective-permute-start | bytes 393224 | tf_op jit(solution)/shard_map/ppermute | solution.py:266
  135.4 2.0 %collective-permute-start.22 = (bf16[512,256]{1,0:T(8,128)(2,1)S(1)}, bf16[512,256]{1,0:T(8,128)(2,1)}, u32[]{:S(2)}, u32[]{:S(2)}) collective-permute-start(bf16[512,256]{1,0:T(8,128)(2,1)S(1)} %collective-permute-done.21.refs_4_), channel_id=1, source_target_pairs={{0,4},{4,0},{8,12},{12,8},{16,20},{20,16},{24,28},{28,24},{1,5},{5... | collective-permute-start | bytes 786440 | tf_op jit(solution)/shard_map/ppermute | solution.py:266
  (27 other events, 117.3 us)

commit v2 on v0

v2 whole, which is shorter than its diff:
```python
import jax
import jax.numpy as jnp
from jax import lax
from jax.experimental import pallas as pl
from jax.experimental.pallas import tpu as pltpu
from jax.sharding import PartitionSpec as P

BS = 64
SB = 8
NSUP = 8
SN = 512
NW = 4096
NWB = 64
GROUPS = 4
PAIR = 2 * SN
F32 = jnp.float32
BF16 = jnp.bfloat16


def masked_columns(factor, pattern, node_label):
    blocks = pattern.shape[0]
    columns = lax.dynamic_slice_in_dim(factor, node_label * SN, SN, 1)
    chosen = lax.dynamic_slice_in_dim(pattern, node_label * SB, SB, 1)
    shaped = columns.reshape(blocks, BS, SB, BS) * chosen[:, None, :, None].astype(BF16)
    return shaped.reshape(blocks * BS, SN)


def sum_over_rows(values):
    count = lax.axis_size("rows")
    if count & (count - 1):
        return lax.psum(values, "rows")
    step = 1
    while step < count:
        values = values + lax.ppermute(values, "rows", [(i, i ^ step) for i in range(count)])
        step *= 2
    return values


def general_path(win_rows, anc_rows, win_pattern, anc_pattern, window_owner, sn_order, diag_inv, win_rhs, anc_rhs):
    columns_rhs = win_rhs.shape[1]
    slot_count = win_rows.shape[0] // BS
    first_slot = lax.axis_index("rows") * slot_count
    local_pattern = lax.dynamic_slice_in_dim(win_pattern, first_slot, slot_count, 0)

    def step(position, carry):
        solution, win_resid, anc_resid = carry
        node_label = sn_order[position]
        owners = lax.dynamic_slice_in_dim(window_owner, node_label * SB, SB, 0)
        inverse = lax.dynamic_index_in_dim(diag_inv, node_label, 0, keepdims=False)
        local_place = owners - first_slot
        present = (local_place >= 0) & (local_place < slot_count)
        resid_blocks = win_resid.reshape(slot_count, BS, columns_rhs)
        taken = jnp.take(resid_blocks, jnp.clip(local_place, 0, slot_count - 1), axis=0)
        placed = jnp.where(present[:, None, None], taken, 0.0).reshape(SN, columns_rhs)
        panel = sum_over_rows(placed.astype(BF16))
        solved = jnp.dot(inverse, panel, preferred_element_type=F32).astype(BF16)
        solution = lax.dynamic_update_slice_in_dim(solution, solved, node_label * SN, 0)
        win_part = jnp.dot(masked_columns(win_rows, local_pattern, node_label), solved, preferred_element_type=F32)
        anc_part = jnp.dot(masked_columns(anc_rows, anc_pattern, node_label), solved, preferred_element_type=F32)
        return solution, win_resid - win_part, anc_resid - anc_part

    first = (jnp.zeros((NW, columns_rhs), BF16), win_rhs.astype(F32), anc_rhs.astype(F32))
    solution, _, anc_resid = lax.fori_loop(0, NSUP, step, first)
    return solution, anc_resid.astype(BF16)


def spread_matrix():
    block_index = lax.broadcasted_iota(jnp.int32, (NWB, SN), 0)
    lane_index = lax.broadcasted_iota(jnp.int32, (NWB, SN), 1)
    return (block_index % SB == lane_index // BS).astype(F32).astype(BF16)


def expand_mask(rows_pattern, label, spread):
    lane = lax.broadcasted_iota(jnp.int32, rows_pattern.shape, 1)
    chosen = jnp.where(lane // SB == label, rows_pattern, 0).astype(F32).astype(BF16)
    return jnp.dot(chosen, spread, preferred_element_type=F32).astype(BF16)


def masked_rows(block_of, mask, count):
    return jnp.concatenate([block_of(j) * mask[j:j + 1, :] for j in range(count)], axis=0)


def rows_at(index):
    return pl.ds(pl.multiple_of(index * BS, BS), BS)


def columns_at(label):
    return pl.ds(pl.multiple_of(label * SN, SN), SN)


SRC, LSRC, PACK, TABLE = 0, 64, 96, 128


def first_kernel(owner, order, pattern, rhs_ref, win_ref, tab, flag, l0, l1, r0, r1, r2, r3,
                 buf, pat, cnt, dcnt, lslot, llab, sem):
    row, depth = lax.axis_index("rows"), lax.axis_index("rhs")
    chip, core = row // 2, row % 2
    width = r0.shape[1]
    for s, r in enumerate((r0, r1, r2, r3)):
        at = pl.multiple_of(jnp.bitwise_xor(depth, s) * width, width)
        r[...] = rhs_ref[:, pl.ds(at, width)]
    flag[0] = 0
    for t in range(SB):
        dcnt[t] = 0
        lslot[t] = 0
        llab[t] = 0
    for t in range(GROUPS * SB):
        tab[PACK + t] = 0
    for group in range(GROUPS):
        for t in range(4):
            cnt[t] = 0

        def one(i, carry, group=group):
            slot = owner[order[2 * group + i // SB] * SB + i % SB]
            where, device = slot // (2 * SB), slot // SB
            rank = cnt[where]
            cnt[where] = rank + 1
            flag[0] = jnp.where(rank >= SB, 1, flag[0])
            rank = jnp.minimum(rank, SB - 1)
            rel = jnp.bitwise_xor(where, chip)
            diagonal = rel == 3
            source = jnp.where(rel == 0, 0, jnp.where(diagonal, jnp.where(rank // 4 == core, 3, 4),
                                                      jnp.where(rel == 1 + core, 1, 2)))
            tab[SRC + group * 16 + i] = source * SB + jnp.where(diagonal, rank % 4, rank)

            @pl.when(rel == 0)
            def _():
                tab[PACK + group * SB + rank] = jnp.bitwise_xor(device % 2, core) * SB + slot % SB

            @pl.when(i >= SB)
            def _():
                index = dcnt[device]
                dcnt[device] = index + 1
                tab[LSRC + group * SB + i - SB] = jnp.bitwise_xor(device, row) * SB + index
                if group == 0:
                    flag[0] = jnp.where(index >= 4, 1, flag[0])

                @pl.when(device == row)
                def _():
                    lslot[index] = slot % SB
                    llab[index] = order[2 * group]

            return carry

        lax.fori_loop(0, 2 * SB, one, 0)
    labels = jnp.zeros((SB, 1), jnp.int32)
    for t in range(SB):
        slot, label = lslot[t], llab[t]
        pltpu.make_async_copy(win_ref.at[rows_at(slot), columns_at(label)], buf.at[pl.ds(t * BS, BS), :], sem).start()
        pat[t:t + 1, :] = pattern[pl.ds(row * SB + slot, 1), :]
        labels = jnp.where(lax.broadcasted_iota(jnp.int32, (SB, 1), 0) == t, label, labels)
    mask = expand_mask(pat[...], labels, spread_matrix())
    pltpu.make_async_copy(win_ref.at[:, pl.ds(0, SN)], buf, sem).wait()
    l0[...] = masked_rows(lambda j: buf[j * BS:(j + 1) * BS, :], mask[0:4], 4)
    l1[...] = masked_rows(lambda j: buf[(j + 4) * BS:(j + 5) * BS, :], mask[4:8], 4)


def first_pack_kernel(tab, *refs):
    pieces, (chip_rhs, p_ref, b_ref) = refs[:8], refs[8:]
    depth, core = lax.axis_index("rhs"), lax.axis_index("rows") % 2
    tall = pieces[0].shape[0]
    for side in range(2):
        for s in range(4):
            at = pl.multiple_of(side * SB * BS + jnp.bitwise_xor(depth, s) * tall, tall)
            chip_rhs[pl.ds(at, tall), :] = pieces[side * 4 + s][...]
    for j in range(SB):
        block = chip_rhs[rows_at(tab[PACK + j]), :]
        p_ref[j * BS:(j + 1) * BS, :] = block
    b_ref[...] = p_ref[pl.ds(pl.multiple_of(core * SB // 2 * BS, SB // 2 * BS), SB // 2 * BS), :]


def make_prep_kernel(group):
    last = group == GROUPS - 1

    def kernel(*refs):
        tab, order = refs[:2]
        l_refs, diag_ref = refs[2:18], refs[18]
        refs = refs[19:]
        if last:
            d_out, l_out, dsem, lsem = refs
        else:
            pattern, w_own, w_other, chip_rhs = refs[:4]
            xs = refs[4:4 + group]
            d_out, l_out, wn_out, r_out, wrow, pat, dsem, lsem, wsem = refs[4 + group:]
        for q in range(2):
            pltpu.make_async_copy(diag_ref.at[order[2 * group + q]], d_out.at[q], dsem.at[q]).start()
        if not last:
            for j in range(SB):
                place = tab[PACK + (group + 1) * SB + j]
                for side, w_ref in enumerate((w_own, w_other)):
                    @pl.when(place // SB == side)
                    def _(j=j, place=place, w_ref=w_ref):
                        pltpu.make_async_copy(w_ref.at[rows_at(place % SB), :], wrow.at[pl.ds(j * BS, BS), :], wsem).start()
        for i in range(SB):
            code = tab[LSRC + group * SB + i]
            for m in range(8):
                for half in range(1 if group == 0 else 2):
                    @pl.when((code // SB == m) & ((code % SB) // 4 == half) if group else code // SB == m)
                    def _(m=m, half=half, i=i, code=code):
                        pltpu.make_async_copy(l_refs[2 * m + half].at[rows_at(code % 4), :], l_out.at[pl.ds(i * BS, BS), :], lsem).start()
        if not last:
            row = lax.axis_index("rows")
            for j in range(SB):
                place = tab[PACK + (group + 1) * SB + j]
                pat[j:j + 1, :] = pattern[pl.ds(jnp.bitwise_xor(row, place // SB) * SB + place % SB, 1), :]
            spread = spread_matrix()
            rows = pat[...]
            total = jnp.concatenate([chip_rhs[rows_at(tab[PACK + (group + 1) * SB + j]), :] for j in range(SB)], axis=0).astype(F32)
            pltpu.make_async_copy(w_own, wrow, wsem).wait()
            for k in range(group + 1):
                for q in range(2):
                    label = order[2 * k + q]
                    mask = expand_mask(rows, label, spread)
                    part = masked_rows(lambda j: wrow[j * BS:(j + 1) * BS, columns_at(label)], mask, SB)
                    if k == group:
                        wn_out[:, q * SN:(q + 1) * SN] = part
                    else:
                        total = total - jnp.dot(part, xs[k][q * SN:(q + 1) * SN, :], preferred_element_type=F32)
            r_out[...] = total
        for q in range(2):
            pltpu.make_async_copy(diag_ref.at[0], d_out.at[q], dsem.at[q]).wait()
        pltpu.make_async_copy(diag_ref.at[0], l_out, lsem).wait()

    return kernel


def make_solve_kernel(group):
    last = group == GROUPS - 1

    def kernel(*refs):
        tab, sources, d_ref, l_ref = refs[0], refs[1:6], refs[6], refs[7]
        if last:
            x_ref, panel = refs[8:]
        else:
            wn_ref, r_ref, x_ref, p_ref, b_ref, panel = refs[8:]

        def place(i):
            code = tab[SRC + group * 16 + i]
            for which, source in enumerate(sources):
                @pl.when(code // SB == which)
                def _(source=source):
                    panel[rows_at(i), :] = source[rows_at(code % SB), :]

        for i in range(2 * SB):
            place(i)
        x_a = jnp.dot(d_ref[0], panel[0:SN, :], preferred_element_type=F32).astype(BF16)
        x_ref[0:SN, :] = x_a
        rest = panel[SN:PAIR, :].astype(F32) - jnp.dot(l_ref[...], x_a, preferred_element_type=F32)
        x_b = jnp.dot(d_ref[1], rest.astype(BF16), preferred_element_type=F32).astype(BF16)
        x_ref[SN:PAIR, :] = x_b
        if last:
            return
        total = r_ref[...] - jnp.dot(wn_ref[:, 0:SN], x_a, preferred_element_type=F32)
        total = total - jnp.dot(wn_ref[:, SN:PAIR], x_b, preferred_element_type=F32)
        p_ref[...] = total.astype(BF16)
        core = lax.axis_index("rows") % 2
        b_ref[...] = p_ref[pl.ds(pl.multiple_of(core * SB // 2 * BS, SB // 2 * BS), SB // 2 * BS), :]

    return kernel


def pair_product(a0, a1, pattern, x_ref, order, group):
    spread = spread_matrix()
    rows = pattern[...]
    total = None
    for q, a_ref in enumerate((a0, a1)):
        mask = expand_mask(rows, order[2 * group + q], spread)
        part = masked_rows(lambda j: a_ref[j * BS:(j + 1) * BS, :], mask, a_ref.shape[0] // BS)
        term = jnp.dot(part, x_ref[q * SN:(q + 1) * SN, :], preferred_element_type=F32)
        total = term if total is None else total + term
    return total


def make_rows_kernel(group):
    def kernel(order, a0, a1, pattern, x_ref, *refs):
        total = pair_product(a0, a1, pattern, x_ref, order, group)
        refs[-1][...] = total if group == 0 else refs[0][...] + total

    return kernel


def last_rows_kernel(order, a0, a1, pattern, x0, x1, x2, x3, sums, h0, h1, h2, h3, sol_ref, out_ref, sems):
    step = pl.program_id(0)
    copies = []
    for k, x in enumerate((x0, x1, x2, x3)):
        for q in range(2):
            at = pl.multiple_of(order[2 * k + q] * SN, SN)
            copies.append(pltpu.make_async_copy(x.at[pl.ds(q * SN, SN), :], sol_ref.at[pl.ds(at, SN), :], sems.at[2 * k + q]))

    @pl.when(step == 0)
    def _():
        for c in copies:
            c.start()

    total = sums[...] + pair_product(a0, a1, pattern, x3, order, GROUPS - 1)
    which = jnp.bitwise_xor(lax.axis_index("rhs"), step)
    for s, h in enumerate((h0, h1, h2, h3)):
        @pl.when(which == s)
        def _(h=h):
            out_ref[...] = (h[...].astype(F32) - total).astype(BF16)

    @pl.when(step == pl.num_programs(0) - 1)
    def _():
        for c in copies:
            c.wait()


SMEM = pl.BlockSpec(memory_space=pltpu.SMEM)
VMEM = pl.BlockSpec(memory_space=pltpu.VMEM)
HBM = pl.BlockSpec(memory_space=pltpu.HBM)


def params(mib):
    return pltpu.CompilerParams(vmem_limit_bytes=mib * 1024 * 1024)


def shape_of(dims, dtype=BF16):
    return jax.ShapeDtypeStruct(dims, dtype)


def local(win_rows, anc_rows, win_pattern, anc_pattern, window_owner, sn_order, diag_inv, rhs_win, rhs_anc):
    if lax.axis_size("rows") != 8 or lax.axis_size("rhs") != 4 or anc_rows.shape[0] != 4 * SB * BS:
        win_rhs = lax.all_to_all(rhs_win, "rhs", split_axis=1, concat_axis=0, tiled=True)
        anc_rhs = lax.all_to_all(rhs_anc, "rhs", split_axis=1, concat_axis=0, tiled=True)
        return general_path(win_rows, anc_rows, win_pattern, anc_pattern, window_owner, sn_order, diag_inv, win_rhs, anc_rhs)

    def swap(x, m):
        return lax.ppermute(x, "rows", [(i, i ^ m) for i in range(8)])

    def deep(x, m):
        return lax.ppermute(x, "rhs", [(i, i ^ m) for i in range(4)])

    def neighbour(x):
        return lax.ppermute(x, "rows", [(i, i ^ (2 if i % 2 == 0 else 4)) for i in range(8)])

    columns = rhs_win.shape[1] // 4
    half = SN // 2
    w_other = swap(win_rows, 1)
    tall = rhs_win.shape[0]
    tab, flag, l_low, l_high, *sent = pl.pallas_call(
        first_kernel,
        out_shape=(shape_of((TABLE,), jnp.int32), shape_of((1,), jnp.int32), shape_of((half, SN)), shape_of((half, SN)))
        + (shape_of((tall, columns)),) * 4,
        in_specs=[SMEM, SMEM, VMEM, VMEM, HBM],
        out_specs=(SMEM, SMEM) + (VMEM,) * 6,
        scratch_shapes=[pltpu.VMEM((SN, SN), BF16), pltpu.VMEM((SB, NWB), jnp.int32), pltpu.SMEM((4,), jnp.int32),
                        pltpu.SMEM((SB,), jnp.int32), pltpu.SMEM((SB,), jnp.int32), pltpu.SMEM((SB,), jnp.int32),
                        pltpu.SemaphoreType.DMA],
        compiler_params=params(8),
        name="first",
    )(window_owner, sn_order, win_pattern, rhs_win, win_rows)

    low, high = {0: l_low}, {0: l_high}
    for m in (2, 4, 6):
        low[m] = swap(l_low, m)
    pieces = [sent[0]] + [deep(sent[s], s) for s in (1, 2, 3)]
    others = [swap(x, 1) for x in pieces]
    for m in (0, 2, 4, 6):
        low[m + 1] = swap(low[m], 1)
    chip_rhs, packed, part = pl.pallas_call(
        first_pack_kernel,
        out_shape=(shape_of((PAIR, columns)), shape_of((SN, columns)), shape_of((half, columns))),
        in_specs=[SMEM] + [VMEM] * 8,
        out_specs=(VMEM,) * 3,
        compiler_params=params(6),
        name="first_pack",
    )(tab, *pieces, *others)

    depth = lax.axis_index("rhs")
    tile = rhs_anc.shape[0]
    sums, anc_pieces, solved = None, None, []
    for group in range(GROUPS):
        last = group == GROUPS - 1
        a_own = neighbour(packed)
        b_own = swap(part, 6)
        if group == 0:
            for m in (2, 4, 6):
                high[m] = swap(l_high, m)
            for m in (0, 2, 4, 6):
                high[m + 1] = swap(high[m], 1)
            l_parts = [x for m in range(8) for x in (low[m], low[m])]
        else:
            l_parts = [x for m in range(8) for x in (low[m], high[m])]
        if group == 1:
            anc_pieces = [lax.dynamic_slice_in_dim(rhs_anc, (depth ^ s) * columns, columns, 1) for s in range(4)]
            anc_pieces = anc_pieces[:1] + [deep(anc_pieces[s], s) for s in (1, 2, 3)]
        a_swap = swap(a_own, 1)
        b_swap = swap(b_own, 1)

        operands = [tab, sn_order, *l_parts, diag_inv]
        in_specs = [SMEM, SMEM] + [HBM] * 17
        out_shape = [shape_of((2, SN, SN)), shape_of((SN, SN))]
        scratch = []
        sems = [pltpu.SemaphoreType.DMA((2,)), pltpu.SemaphoreType.DMA]
        if not last:
            operands += [win_pattern, win_rows, w_other, chip_rhs, *solved]
            in_specs += [VMEM, HBM, HBM] + [VMEM] * (1 + group)
            out_shape += [shape_of((SN, PAIR)), shape_of((SN, columns), F32)]
            scratch = [pltpu.VMEM((SN, NW), BF16), pltpu.VMEM((SB, NWB), jnp.int32)]
            sems += [pltpu.SemaphoreType.DMA]
        ready = pl.pallas_call(
            make_prep_kernel(group),
            out_shape=tuple(out_shape),
            in_specs=in_specs,
            out_specs=(VMEM,) * len(out_shape),
            scratch_shapes=scratch + sems,
            compiler_params=params(16),
            name="prep",
        )(*operands)
        if group > 0:
            k = group - 1
            more = [] if k == 0 else [sums]
            sums = pl.pallas_call(
                make_rows_kernel(k),
                out_shape=shape_of((anc_rows.shape[0], columns), F32),
                grid_spec=pltpu.PrefetchScalarGridSpec(
                    num_scalar_prefetch=1,
                    grid=(anc_rows.shape[0] // tile,),
                    in_specs=[pl.BlockSpec((tile, SN), lambda i, o, k=k: (i, o[2 * k])),
                              pl.BlockSpec((tile, SN), lambda i, o, k=k: (i, o[2 * k + 1])),
                              pl.BlockSpec((SB, NWB), lambda i, o: (i, 0)),
                              pl.BlockSpec((PAIR, columns), lambda i, o: (0, 0))]
                    + [pl.BlockSpec((tile, columns), lambda i, o: (i, 0))] * len(more),
                    out_specs=pl.BlockSpec((tile, columns), lambda i, o: (i, 0)),
                ),
                input_output_aliases={5: 0} if more else {},
                compiler_params=params(12),
                name="rows_below",
            )(sn_order, anc_rows, anc_rows, anc_pattern, solved[k], *more)

        out_shape = [shape_of((PAIR, columns))]
        if not last:
            out_shape += [shape_of((SN, columns)), shape_of((half, columns))]
        results = pl.pallas_call(
            make_solve_kernel(group),
            out_shape=tuple(out_shape),
            in_specs=[SMEM] + [VMEM] * (5 + len(ready)),
            out_specs=(VMEM,) * len(out_shape),
            scratch_shapes=[pltpu.VMEM((PAIR, columns), BF16)],
            compiler_params=params(12),
            name="pair_solve",
        )(tab, packed, a_own, a_swap, b_own, b_swap, *ready)
        solved.append(results[0])
        if not last:
            packed, part = results[1:]

    def packed_path(*xs):
        k = GROUPS - 1
        whole = [pl.BlockSpec((PAIR, columns), lambda i, o: (0, 0))] * 4
        return pl.pallas_call(
            last_rows_kernel,
            out_shape=(shape_of((NW, columns)), shape_of((anc_rows.shape[0], columns))),
            grid_spec=pltpu.PrefetchScalarGridSpec(
                num_scalar_prefetch=1,
                grid=(anc_rows.shape[0] // tile,),
                in_specs=[pl.BlockSpec((tile, SN), lambda i, o: (i, o[2 * k])),
                          pl.BlockSpec((tile, SN), lambda i, o: (i, o[2 * k + 1])),
                          pl.BlockSpec((SB, NWB), lambda i, o: (i, 0))] + whole
                + [pl.BlockSpec((tile, columns), lambda i, o: (i, 0))]
                + [pl.BlockSpec((tile, columns), lambda i, o: (0, 0))] * 4,
                out_specs=(HBM, pl.BlockSpec((tile, columns), lambda i, o: (i, 0))),
                scratch_shapes=[pltpu.SemaphoreType.DMA((2 * GROUPS,))],
            ),
            compiler_params=params(24),
            name="last_rows",
        )(sn_order, anc_rows, anc_rows, anc_pattern, *xs, sums, *anc_pieces)

    def other_path(*xs):
        back = depth ^ jnp.arange(4)
        win_rhs = jnp.take(jnp.stack(pieces), back, axis=0).reshape(4 * tall, columns)
        anc_rhs = jnp.take(jnp.stack(anc_pieces), back, axis=0).reshape(4 * tile, columns)
        return general_path(win_rows, anc_rows, win_pattern, anc_pattern, window_owner, sn_order, diag_inv, win_rhs, anc_rhs)

    return tuple(lax.cond(flag[0] == 0, packed_path, other_path, *solved))


def solution(mesh):
    return jax.shard_map(
        local,
        mesh=mesh,
        in_specs=(P("rows", None), P("rows", None), P(), P("rows", None), P(), P(), P(),
                  P(("rows", "rhs"), None), P(("rows", "rhs"), None)),
        out_specs=(P(None, "rhs"), P("rows", "rhs")),
        check_vma=False,
    )
```

time: 549 us -> 417 us (0.76)
  waiting for transfers between devices: 341 us -> 121 us
  Pallas kernels: 0 us -> 50 us
  starting transfers between devices: 11.4 us -> 51.8 us
  between operations: 40.1 us -> 1.69 us
  loops' own time: 0 us -> 26.6 us
  local copies, waits for them, and re-layouts: 93.1 us -> 101 us
    psum x8 -> x0, waiting for transfers between devices: 340 us -> none  [local(): panel = lax.psum(placed.astype(jnp.bfloat16), 'rows').astype(jnp.float32)]
    ppermute x0 -> x65, waiting for transfers between devices: none -> 121 us  [the longest x24 67.1 us: sum_over_rows(): lax.ppermute(values, 'rows', [(i, i ^ step) for i in range(count)])]
    ppermute x0 -> x65, starting transfers between devices: none -> 51.8 us  [the longest x24 21.6 us: sum_over_rows(): lax.ppermute(values, 'rows', [(i, i ^ step) for i in range(count)])]
    pallas_call x0 -> x13, Pallas kernels: none -> 50 us  [the longest x3 18.6 us: local(): pl.pallas_call(make_rows_kernel(k), out_shape=shape_of((anc_rows.shape[0]...]
    another operation x0 -> x2, loops' own time: none -> 26.6 us  [the longest x1 26.3 us: general_path(): solution, _, anc_resid = lax.fori_loop(0, NSUP, step, first)]
    all_to_all x2 -> x0, starting transfers between devices: 10.9 us -> none  [the longest x1 6.32 us: local(): lax.all_to_all(rhs_win, 'rhs', split_axis=1, concat_axis=0, tiled=True)]
    while x0 -> x32, local copies, waits for them, and re-layouts: none -> 10.6 us
    mul x30 -> x32, local copies, waits for them, and re-layouts: 78.5 us -> 70.7 us  [masked_columns(): columns.reshape(blocks, BS, SB, BS) * chosen[:, None, :, None].astype(BF16)]
  transfers between devices with their start and end apart: 10 -> 65, of which waited for: 8 -> 33; matrix products, arithmetic and copies ran while one was open for 17% -> 18% of each run, Pallas kernels for 0% -> 10%
where the time goes in v2:
time: 417 us; the launch traced here: 411 us
  waiting for transfers between devices  121 us (29%)
  local copies, waits for them, and re-layouts  101 us (24%)
  starting transfers between devices  51.8 us (12%)
  Pallas kernels  50 us (12%)
  matrix products  48.9 us (12%)
  loops' own time  26.6 us (6%)
  other arithmetic  10.5 us (3%)
    mul x32, local copies, waits for them, and re-layouts, masked_columns(): columns.reshape(blocks, BS, SB, BS) * chosen[:, None, :, None].astype(BF16)  70.7 us
    ppermute x24, waiting for transfers between devices, sum_over_rows(): lax.ppermute(values, 'rows', [(i, i ^ step) for i in range(count)])  67.1 us
    ppermute x31, waiting for transfers between devices, swap(): return lax.ppermute(x, 'rows', [(i, i ^ m) for i in range(8)])  28.6 us
    another operation x1, loops' own time, general_path(): solution, _, anc_resid = lax.fori_loop(0, NSUP, step, first)  26.3 us
    ppermute x24, starting transfers between devices, sum_over_rows(): lax.ppermute(values, 'rows', [(i, i ^ step) for i in range(count)])  21.6 us
    dot_general x8, matrix products, step(): jnp.dot(masked_columns(anc_rows, anc_pattern, node_label), solved, prefer...  19.9 us
    pallas_call x3, Pallas kernels, local(): pl.pallas_call(make_rows_kernel(k), out_shape=shape_of((anc_rows.shape[0]...  18.6 us
    dot_general x8, matrix products, step(): solved = jnp.dot(inverse, panel, preferred_element_type=F32).astype(BF16)  18.1 us
  transfers between devices with their start and end apart: 65, of which 33 were waited for; matrix products, arithmetic and copies ran while one was open for 18% of the time, Pallas kernels for 10%

profile of v2, /device:TPU:0, one launch (start us, length us, event | category | flops | bytes accessed | tf_op | source)
XLA Modules:
  0.0 410.9 jit_solution(6892555572222766373)
XLA Ops:
  2.1 5.6 %first.1 = (s32[128]{0:T(128)S(1)}, s32[1]{0:T(128)}, bf16[256,512]{1,0:T(8,128)(2,1)S(1)}, bf16[256,512]{1,0:T(8,128)(2,1)S(1)}, bf16[128,256]{1,0:T(8,128)(2,1...) custom-call(s32[64]{0:T(128)} %owner.1, s32[8]{0:T(128)} %order.7, ...), custom_call_target="tpu_custom_call" | custom-call | tf_op jit(solution)/shard_map/first/pallas_call | solution.py:340
  13.5 3.8 collective-permute-done.4.refs_2_
  24.7 3.7 collective-permute-done.15.refs_4_
  34.2 5.2 %collective-permute-done.20.refs_10_.refs_11_ = bf16[256,512]{1,0:T(8,128)(2,1)S(1)} collective-permute-done((bf16[256,512]{1,0:T(8,128)(2,1)S(1)}, bf16[256,512]{1,0:T(8,128)(2,1)S(1)}, u32[]{:S(2)}, u32[]{:S(2)}) %collective-permute-start.20) | collective-permute-done | bytes 262176 | tf_op jit(solution)/shard_map/ppermute | solution.py:328
  53.2 5.7 %collective-permute-done.32.refs_11_ = bf16[256,512]{1,0:T(8,128)(2,1)S(1)} collective-permute-done((bf16[256,512]{1,0:T(8,128)(2,1)S(1)}, bf16[256,512]{1,0:T(8,128)(2,1)S(1)}, u32[]{:S(2)}, u32[]{:S(2)}) %collective-permute-start.32) | collective-permute-done | bytes 262176 | tf_op jit(solution)/shard_map/ppermute | solution.py:328
  60.8 5.0 %collective-permute-done.27.refs_4_ = bf16[256,256]{1,0:T(8,128)(2,1)S(1)} collective-permute-done((bf16[256,256]{1,0:T(8,128)(2,1)S(1)}, bf16[256,256]{1,0:T(8,128)(2,1)S(1)}, u32[]{:S(2)}, u32[]{:S(2)}) %collective-permute-start.27) | collective-permute-done | bytes 131104 | tf_op jit(solution)/shard_map/ppermute | solution.py:328
  65.9 4.2 %prep.5 = (bf16[2,512,512]{2,1,0:T(8,128)(2,1)S(1)}, bf16[512,512]{1,0:T(8,128)(2,1)S(1)}, bf16[512,1024]{1,0:T(8,128)(2,1)S(1)}, f32[512,256]{1,0:T(8,128)S(1)}) custom-call(s32[128]{0:T(128)S(1)} %get-tuple-element.325.tab.refs_0_, s32[8]{0:T(128)S(1)} %copy-done.30, bf16[256,512]{1,0:T(8,128)(2,1)S(1)} %get-tuple-element.328.refs_2_.refs_3_, ...), custom_call_target="tpu_custom_call" | custom-call | tf_op jit(solution)/shard_map/prep/pallas_call | solution.py:401
  74.4 6.0 %collective-permute-done.36.refs_2_ = bf16[512,256]{1,0:T(8,128)(2,1)S(1)} collective-permute-done((bf16[512,256]{1,0:T(8,128)(2,1)S(1)}, bf16[512,256]{1,0:T(8,128)(2,1)S(1)}, u32[]{:S(2)}, u32[]{:S(2)}) %collective-permute-start.36) | collective-permute-done | bytes 262176 | tf_op jit(solution)/shard_map/ppermute | solution.py:334
  81.6 4.5 %prep.6 = (bf16[2,512,512]{2,1,0:T(8,128)(2,1)S(1)}, bf16[512,512]{1,0:T(8,128)(2,1)S(1)}, bf16[512,1024]{1,0:T(8,128)(2,1)S(1)}, f32[512,256]{1,0:T(8,128)S(1)}) custom-call(s32[128]{0:T(128)S(1)} %get-tuple-element.325.tab.refs_0_, s32[8]{0:T(128)S(1)} %copy-done.30, bf16[256,512]{1,0:T(8,128)(2,1)S(1)} %get-tuple-element.328.refs_2_.refs_3_, ...), custom_call_target="tpu_custom_call" | custom-call | tf_op jit(solution)/shard_map/prep/pallas_call | solution.py:401
  98.8 4.2 %collective-permute-done.42.refs_4_ = bf16[256,256]{1,0:T(8,128)(2,1)S(1)} collective-permute-done((bf16[256,256]{1,0:T(8,128)(2,1)S(1)}, bf16[256,256]{1,0:T(8,128)(2,1)S(1)}, u32[]{:S(2)}, u32[]{:S(2)}) %collective-permute-start.42) | collective-permute-done | bytes 131104 | tf_op jit(solution)/shard_map/ppermute | solution.py:328
  106.1 8.3 %collective-permute-done.7 = bf16[512,256]{1,0:T(8,128)(2,1)S(1)} collective-permute-done((bf16[512,256]{1,0:T(8,128)(2,1)S(1)}, bf16[512,256]{1,0:T(8,128)(2,1)S(1)}, u32[]{:S(2)}, u32[]{:S(2)}) %collective-permute-start.7) | collective-permute-done | bytes 262176 | tf_op jit(solution)/shard_map/ppermute | solution.py:331
  117.3 5.9 %rows_below.3.refs_0_ = f32[2048,256]{1,0:T(8,128)} custom-call(s32[8]{0:T(128)S(1)} %copy-done.30, bf16[2048,4096]{1,0:T(8,128)(2,1)} %a1.5, bf16[2048,4096]{1,0:T(8,128)(2,1)} %a1.5, s32[32,64]{1,0:T(8,128)S(1)} %copy-done.14, bf16[1024,256]{1,0:T(8,128)(2,1)} %get-tuple-element.334.refs_23_.x_ref), custom_call_target="tpu_custom_call" | custom-call | tf_op jit(solution)/shard_map/rows_below/pallas_call | solution.py:413
  123.2 6.2 %rows_below.4.refs_0_ = f32[2048,256]{1,0:T(8,128)} custom-call(s32[8]{0:T(128)S(1)} %copy-done.30, bf16[2048,4096]{1,0:T(8,128)(2,1)} %a1.5, bf16[2048,4096]{1,0:T(8,128)(2,1)} %a1.5, s32[32,64]{1,0:T(8,128)S(1)} %copy-done.14, bf16[1024,256]{1,0:T(8,128)(2,1)S(1)} %copy-done.12, f32[2048,256]{1,0:T(8,128)} %rows_below.3.refs_0_), custom_call_target="tpu_custom_call", output_to_operand_aliasing={{}: (5, {})} | custom-call | tf_op jit(solution)/shard_map/rows_below/pallas_call | solution.py:413
  129.4 6.5 %rows_below.5 = f32[2048,256]{1,0:T(8,128)} custom-call(s32[8]{0:T(128)S(1)} %copy-done.30, bf16[2048,4096]{1,0:T(8,128)(2,1)} %a1.5, bf16[2048,4096]{1,0:T(8,128)(2,1)} %a1.5, s32[32,64]{1,0:T(8,128)S(1)} %copy-done.14, bf16[1024,256]{1,0:T(8,128)(2,1)} %get-tuple-element.349.x_ref, f32[2048,256]{1,0:T(8,128)} %rows_below.4.refs_0_), custom_call_target="tpu_custom_call", output_to_operand_aliasing={{}: (5, {})} | custom-call | tf_op jit(solution)/shard_map/rows_below/pallas_call | solution.py:413
  139.5 271.4 %conditional.1 = ((bf16[4096,256]{1,0:T(8,128)(2,1)}, bf16[2048,256]{1,0:T(8,128)(2,1)})) conditional(s32[]{:T(128)} %bitcast.16, (s32[]{:T(128)}, bf16[128,256]{1,0:T(8,128)(2,1)S(1)}, bf16[128,256]{1,0:T(8,128)(2,1)S(1)}, bf16[128,256]{1,0:T(8,128)(2,1)S(1)}, bf16[128,256]{1,0:T(8,128)(2,1)S(1)}, /*index=5*/bf16[512,256]{1,0:T(8,128)(2,1)S(1)}, ...), branch_computations={%region_0.3_spmd, %region_3.4_spmd} | conditional | flops 816449984 | bytes 57439732 | solution.py:474
  145.3 263.0 %while.16 = (s32[]{:T(128)}, bf16[4096,256]{1,0:T(8,128)(2,1)}, f32[512,256]{1,0:T(8,128)S(1)}, f32[2048,256]{1,0:T(8,128)}, s32[8]{0:T(128)S(1)}, /*index=5*/bf...) while((s32[]{:T(128)}, bf16[4096,256]{1,0:T(8,128)(2,1)}, ...), condition=%wide.region_2.2_spmd, body=%wide.region_1.1_spmd.sunk | while | flops 812647808 | bytes 43004060 | solution.py:63
  150.9 7.1 %collective-permute-done.1 = bf16[512,256]{1,0:T(8,128)(2,1)S(1)} collective-permute-done((bf16[512,256]{1,0:T(8,128)(2,1)S(1)}, bf16[512,256]{1,0:T(8,128)(2,1)S(1)}, u32[]{:S(2)}, u32[]{:S(2)}) %collective-permute-start.1) | collective-permute-done | bytes 262176 | tf_op jit(solution)/shard_map/cond/branch_0_fun/while/body/eval_jaxpr/ppermute | solution.py:34
  164.9 5.4 %mul.98 = bf16[2048,512]{1,0:T(8,128)(2,1)S(1)} reshape(bf16[32,64,8,64]{3,2,1,0:T(8,128)(2,1)} %mul.97) | data formatting | bytes 4194304 | tf_op jit(solution)/shard_map/cond/branch_0_fun/while/body/eval_jaxpr/mul | solution.py:24
  184.5 6.6 %collective-permute-done.1 = bf16[512,256]{1,0:T(8,128)(2,1)S(1)} collective-permute-done((bf16[512,256]{1,0:T(8,128)(2,1)S(1)}, bf16[512,256]{1,0:T(8,128)(2,1)S(1)}, u32[]{:S(2)}, u32[]{:S(2)}) %collective-permute-start.1) | collective-permute-done | bytes 262176 | tf_op jit(solution)/shard_map/cond/branch_0_fun/while/body/eval_jaxpr/ppermute | solution.py:34
  197.5 5.4 %mul.98 = bf16[2048,512]{1,0:T(8,128)(2,1)S(1)} reshape(bf16[32,64,8,64]{3,2,1,0:T(8,128)(2,1)} %mul.97) | data formatting | bytes 4194304 | tf_op jit(solution)/shard_map/cond/branch_0_fun/while/body/eval_jaxpr/mul | solution.py:24
  216.6 7.1 %collective-permute-done.1 = bf16[512,256]{1,0:T(8,128)(2,1)S(1)} collective-permute-done((bf16[512,256]{1,0:T(8,128)(2,1)S(1)}, bf16[512,256]{1,0:T(8,128)(2,1)S(1)}, u32[]{:S(2)}, u32[]{:S(2)}) %collective-permute-start.1) | collective-permute-done | bytes 262176 | tf_op jit(solution)/shard_map/cond/branch_0_fun/while/body/eval_jaxpr/ppermute | solution.py:34
  230.7 5.4 %mul.98 = bf16[2048,512]{1,0:T(8,128)(2,1)S(1)} reshape(bf16[32,64,8,64]{3,2,1,0:T(8,128)(2,1)} %mul.97) | data formatting | bytes 4194304 | tf_op jit(solution)/shard_map/cond/branch_0_fun/while/body/eval_jaxpr/mul | solution.py:24
  250.3 6.6 %collective-permute-done.1 = bf16[512,256]{1,0:T(8,128)(2,1)S(1)} collective-permute-done((bf16[512,256]{1,0:T(8,128)(2,1)S(1)}, bf16[512,256]{1,0:T(8,128)(2,1)S(1)}, u32[]{:S(2)}, u32[]{:S(2)}) %collective-permute-start.1) | collective-permute-done | bytes 262176 | tf_op jit(solution)/shard_map/cond/branch_0_fun/while/body/eval_jaxpr/ppermute | solution.py:34
  263.3 5.4 %mul.98 = bf16[2048,512]{1,0:T(8,128)(2,1)S(1)} reshape(bf16[32,64,8,64]{3,2,1,0:T(8,128)(2,1)} %mul.97) | data formatting | bytes 4194304 | tf_op jit(solution)/shard_map/cond/branch_0_fun/while/body/eval_jaxpr/mul | solution.py:24
  282.4 7.1 %collective-permute-done.1 = bf16[512,256]{1,0:T(8,128)(2,1)S(1)} collective-permute-done((bf16[512,256]{1,0:T(8,128)(2,1)S(1)}, bf16[512,256]{1,0:T(8,128)(2,1)S(1)}, u32[]{:S(2)}, u32[]{:S(2)}) %collective-permute-start.1) | collective-permute-done | bytes 262176 | tf_op jit(solution)/shard_map/cond/branch_0_fun/while/body/eval_jaxpr/ppermute | solution.py:34
  296.4 5.4 %mul.98 = bf16[2048,512]{1,0:T(8,128)(2,1)S(1)} reshape(bf16[32,64,8,64]{3,2,1,0:T(8,128)(2,1)} %mul.97) | data formatting | bytes 4194304 | tf_op jit(solution)/shard_map/cond/branch_0_fun/while/body/eval_jaxpr/mul | solution.py:24
  316.0 6.6 %collective-permute-done.1 = bf16[512,256]{1,0:T(8,128)(2,1)S(1)} collective-permute-done((bf16[512,256]{1,0:T(8,128)(2,1)S(1)}, bf16[512,256]{1,0:T(8,128)(2,1)S(1)}, u32[]{:S(2)}, u32[]{:S(2)}) %collective-permute-start.1) | collective-permute-done | bytes 262176 | tf_op jit(solution)/shard_map/cond/branch_0_fun/while/body/eval_jaxpr/ppermute | solution.py:34
  329.0 5.4 %mul.98 = bf16[2048,512]{1,0:T(8,128)(2,1)S(1)} reshape(bf16[32,64,8,64]{3,2,1,0:T(8,128)(2,1)} %mul.97) | data formatting | bytes 4194304 | tf_op jit(solution)/shard_map/cond/branch_0_fun/while/body/eval_jaxpr/mul | solution.py:24
  348.1 7.1 %collective-permute-done.1 = bf16[512,256]{1,0:T(8,128)(2,1)S(1)} collective-permute-done((bf16[512,256]{1,0:T(8,128)(2,1)S(1)}, bf16[512,256]{1,0:T(8,128)(2,1)S(1)}, u32[]{:S(2)}, u32[]{:S(2)}) %collective-permute-start.1) | collective-permute-done | bytes 262176 | tf_op jit(solution)/shard_map/cond/branch_0_fun/while/body/eval_jaxpr/ppermute | solution.py:34
  362.2 5.4 %mul.98 = bf16[2048,512]{1,0:T(8,128)(2,1)S(1)} reshape(bf16[32,64,8,64]{3,2,1,0:T(8,128)(2,1)} %mul.97) | data formatting | bytes 4194304 | tf_op jit(solution)/shard_map/cond/branch_0_fun/while/body/eval_jaxpr/mul | solution.py:24
  381.8 6.6 %collective-permute-done.1 = bf16[512,256]{1,0:T(8,128)(2,1)S(1)} collective-permute-done((bf16[512,256]{1,0:T(8,128)(2,1)S(1)}, bf16[512,256]{1,0:T(8,128)(2,1)S(1)}, u32[]{:S(2)}, u32[]{:S(2)}) %collective-permute-start.1) | collective-permute-done | bytes 262176 | tf_op jit(solution)/shard_map/cond/branch_0_fun/while/body/eval_jaxpr/ppermute | solution.py:34
  394.8 5.4 %mul.98 = bf16[2048,512]{1,0:T(8,128)(2,1)S(1)} reshape(bf16[32,64,8,64]{3,2,1,0:T(8,128)(2,1)} %mul.97) | data formatting | bytes 4194304 | tf_op jit(solution)/shard_map/cond/branch_0_fun/while/body/eval_jaxpr/mul | solution.py:24
  (381 shorter events, 209.9 us)
Async XLA Ops:
  0.6 43.5 %collective-permute-start.24 = (bf16[512,4096]{1,0:T(8,128)(2,1)}, bf16[512,4096]{1,0:T(8,128)(2,1)S(1)}, u32[]{:S(2)}, u32[]{:S(2)}) collective-permute-start(bf16[512,4096]{1,0:T(8,128)(2,1)} %refs_20_.5), channel_id=1, source_target_pairs={{0,4},{4,0},{8,12},{12,8},{16,20},{20,16},{24,28},{28,24},{1,5},{5... | collective-permute-start | bytes 12582920 | tf_op jit(solution)/shard_map/ppermute | solution.py:328
  13.3 17.7 %collective-permute-start.17 = (bf16[256,512]{1,0:T(8,128)(2,1)S(1)}, bf16[256,512]{1,0:T(8,128)(2,1)S(1)}, u32[]{:S(2)}, u32[]{:S(2)}) collective-permute-start(bf16[256,512]{1,0:T(8,128)(2,1)S(1)} %get-tuple-element.328.refs_2_.refs_3_), channel_id=1, source_target_pairs={{0,4},{4,0},{8,12},{12,8},{16,20},{20,16},{24,28},{28,24},{1,5},{5... | collective-permute-start | bytes 786440 | tf_op jit(solution)/shard_map/ppermute | solution.py:328
  23.7 10.5 %collective-permute-start.18 = (bf16[256,512]{1,0:T(8,128)(2,1)S(1)}, bf16[256,512]{1,0:T(8,128)(2,1)S(1)}, u32[]{:S(2)}, u32[]{:S(2)}) collective-permute-start(bf16[256,512]{1,0:T(8,128)(2,1)S(1)} %get-tuple-element.328.refs_2_.refs_3_), channel_id=1, source_target_pairs={{0,8},{4,12},{8,0},{12,4},{16,24},{20,28},{24,16},{28,20},{1,9},{5... | collective-permute-start | bytes 786440 | tf_op jit(solution)/shard_map/ppermute | solution.py:328
  24.3 15.1 %collective-permute-start.20 = (bf16[256,512]{1,0:T(8,128)(2,1)S(1)}, bf16[256,512]{1,0:T(8,128)(2,1)S(1)}, u32[]{:S(2)}, u32[]{:S(2)}) collective-permute-start(bf16[256,512]{1,0:T(8,128)(2,1)S(1)} %get-tuple-element.328.refs_2_.refs_3_), channel_id=1, source_target_pairs={{0,16},{4,20},{8,24},{12,28},{16,0},{20,4},{24,8},{28,12},{1,17},{... | collective-permute-start | bytes 786440 | tf_op jit(solution)/shard_map/ppermute | solution.py:328
  28.4 10.9 %collective-permute-start.22 = (bf16[256,512]{1,0:T(8,128)(2,1)S(1)}, bf16[256,512]{1,0:T(8,128)(2,1)S(1)}, u32[]{:S(2)}, u32[]{:S(2)}) collective-permute-start(bf16[256,512]{1,0:T(8,128)(2,1)S(1)} %get-tuple-element.328.refs_2_.refs_3_), channel_id=1, source_target_pairs={{0,24},{4,28},{8,16},{12,20},{16,8},{20,12},{24,0},{28,4},{1,25},{... | collective-permute-start | bytes 786440 | tf_op jit(solution)/shard_map/ppermute | solution.py:328
  31.0 11.2 %collective-permute-start.13 = (bf16[512,256]{1,0:T(8,128)(2,1)S(1)}, bf16[512,256]{1,0:T(8,128)(2,1)S(1)}, u32[]{:S(2)}, u32[]{:S(2)}) collective-permute-start(bf16[512,256]{1,0:T(8,128)(2,1)S(1)} %get-tuple-element.326.refs_1_), channel_id=1, source_target_pairs={{0,8},{4,20},{8,0},{12,28},{16,24},{20,4},{24,16},{28,12},{1,9},{5... | collective-permute-start | bytes 786440 | tf_op jit(solution)/shard_map/ppermute | solution.py:334
  42.6 16.8 %collective-permute-start.29 = (bf16[256,512]{1,0:T(8,128)(2,1)S(1)}, bf16[256,512]{1,0:T(8,128)(2,1)S(1)}, u32[]{:S(2)}, u32[]{:S(2)}) collective-permute-start(bf16[256,512]{1,0:T(8,128)(2,1)S(1)} %get-tuple-element.337.refs_3_), channel_id=1, source_target_pairs={{0,4},{4,0},{8,12},{12,8},{16,20},{20,16},{24,28},{28,24},{1,5},{5... | collective-permute-start | bytes 786440 | tf_op jit(solution)/shard_map/ppermute | solution.py:328
  42.7 10.5 %collective-permute-start.30 = (bf16[256,512]{1,0:T(8,128)(2,1)S(1)}, bf16[256,512]{1,0:T(8,128)(2,1)S(1)}, u32[]{:S(2)}, u32[]{:S(2)}) collective-permute-start(bf16[256,512]{1,0:T(8,128)(2,1)S(1)} %get-tuple-element.337.refs_3_), channel_id=1, source_target_pairs={{0,8},{4,12},{8,0},{12,4},{16,24},{20,28},{24,16},{28,20},{1,9},{5... | collective-permute-start | bytes 786440 | tf_op jit(solution)/shard_map/ppermute | solution.py:328
  44.2 14.8 %collective-permute-start.32 = (bf16[256,512]{1,0:T(8,128)(2,1)S(1)}, bf16[256,512]{1,0:T(8,128)(2,1)S(1)}, u32[]{:S(2)}, u32[]{:S(2)}) collective-permute-start(bf16[256,512]{1,0:T(8,128)(2,1)S(1)} %get-tuple-element.337.refs_3_), channel_id=1, source_target_pairs={{0,16},{4,20},{8,24},{12,28},{16,0},{20,4},{24,8},{28,12},{1,17},{... | collective-permute-start | bytes 786440 | tf_op jit(solution)/shard_map/ppermute | solution.py:328
  47.9 11.1 %collective-permute-start.34 = (bf16[256,512]{1,0:T(8,128)(2,1)S(1)}, bf16[256,512]{1,0:T(8,128)(2,1)S(1)}, u32[]{:S(2)}, u32[]{:S(2)}) collective-permute-start(bf16[256,512]{1,0:T(8,128)(2,1)S(1)} %get-tuple-element.337.refs_3_), channel_id=1, source_target_pairs={{0,24},{4,28},{8,16},{12,20},{16,8},{20,12},{24,0},{28,4},{1,25},{... | collective-permute-start | bytes 786440 | tf_op jit(solution)/shard_map/ppermute | solution.py:328
  53.2 12.6 %collective-permute-start.31 = (bf16[256,512]{1,0:T(8,128)(2,1)S(1)}, bf16[256,512]{1,0:T(8,128)(2,1)S(1)}, u32[]{:S(2)}, u32[]{:S(2)}) collective-permute-start(bf16[256,512]{1,0:T(8,128)(2,1)S(1)} %collective-permute-done.30.refs_7_), channel_id=1, source_target_pairs={{0,4},{4,0},{8,12},{12,8},{16,20},{20,16},{24,28},{28,24},{1,5},{5... | collective-permute-start | bytes 786440 | tf_op jit(solution)/shard_map/ppermute | solution.py:328
  59.8 10.2 %collective-permute-start.26 = (bf16[512,256]{1,0:T(8,128)(2,1)S(1)}, bf16[512,256]{1,0:T(8,128)(2,1)S(1)}, u32[]{:S(2)}, u32[]{:S(2)}) collective-permute-start(bf16[512,256]{1,0:T(8,128)(2,1)S(1)} %collective-permute-done.25.refs_2_), channel_id=1, source_target_pairs={{0,4},{4,0},{8,12},{12,8},{16,20},{20,16},{24,28},{28,24},{1,5},{5... | collective-permute-start | bytes 786440 | tf_op jit(solution)/shard_map/ppermute | solution.py:328
  72.6 8.9 %collective-permute-start.38 = (bf16[256,256]{1,0:T(8,128)(2,1)S(1)}, bf16[256,256]{1,0:T(8,128)(2,1)S(1)}, u32[]{:S(2)}, u32[]{:S(2)}) collective-permute-start(bf16[256,256]{1,0:T(8,128)(2,1)S(1)} %get-tuple-element.344), channel_id=1, source_target_pairs={{0,24},{4,28},{8,16},{12,20},{16,8},{20,12},{24,0},{28,4},{1,25},{... | collective-permute-start | bytes 393224 | tf_op jit(solution)/shard_map/ppermute | solution.py:328
  89.2 9.6 %collective-permute-start.40 = (bf16[512,256]{1,0:T(8,128)(2,1)}, bf16[512,256]{1,0:T(8,128)(2,1)}, u32[]{:S(2)}, u32[]{:S(2)}) collective-permute-start(bf16[512,256]{1,0:T(8,128)(2,1)} %get-tuple-element.350.refs_1_), channel_id=1, source_target_pairs={{0,8},{4,20},{8,0},{12,28},{16,24},{20,4},{24,16},{28,12},{1,9},{5... | collective-permute-start | bytes 786440 | tf_op jit(solution)/shard_map/ppermute | solution.py:334
  91.9 14.1 %collective-permute-start.6 = (bf16[512,256]{1,0:T(8,128)(2,1)S(1)}, bf16[512,256]{1,0:T(8,128)(2,1)S(1)}, u32[]{:S(2)}, u32[]{:S(2)}) collective-permute-start(bf16[512,256]{1,0:T(8,128)(2,1)S(1)} %get-tuple-element.387), channel_id=1, source_target_pairs={{0,1},{1,0},{2,3},{3,2},{4,5},{5,4},{6,7},{7,6},{8,9},{9,8},{10,11... | collective-permute-start | bytes 786440 | tf_op jit(solution)/shard_map/ppermute | solution.py:331
  93.0 21.4 %collective-permute-start.7 = (bf16[512,256]{1,0:T(8,128)(2,1)S(1)}, bf16[512,256]{1,0:T(8,128)(2,1)S(1)}, u32[]{:S(2)}, u32[]{:S(2)}) collective-permute-start(bf16[512,256]{1,0:T(8,128)(2,1)S(1)} %get-tuple-element.389), channel_id=1, source_target_pairs={{0,2},{1,3},{2,0},{3,1},{4,6},{5,7},{6,4},{7,5},{8,10},{9,11},{10,... | collective-permute-start | bytes 786440 | tf_op jit(solution)/shard_map/ppermute | solution.py:331
  94.9 19.5 %collective-permute-start.8 = (bf16[512,256]{1,0:T(8,128)(2,1)S(1)}, bf16[512,256]{1,0:T(8,128)(2,1)S(1)}, u32[]{:S(2)}, u32[]{:S(2)}) collective-permute-start(bf16[512,256]{1,0:T(8,128)(2,1)S(1)} %get-tuple-element.386), channel_id=1, source_target_pairs={{0,3},{1,2},{2,1},{3,0},{4,7},{5,6},{6,5},{7,4},{8,11},{9,10},{10,... | collective-permute-start | bytes 786440 | tf_op jit(solution)/shard_map/ppermute | solution.py:331
  98.8 37.2 %collective-permute-start.41 = (bf16[512,256]{1,0:T(8,128)(2,1)}, bf16[512,256]{1,0:T(8,128)(2,1)S(1)}, u32[]{:S(2)}, u32[]{:S(2)}) collective-permute-start(bf16[512,256]{1,0:T(8,128)(2,1)} %collective-permute-done.40.refs_2_), channel_id=1, source_target_pairs={{0,4},{4,0},{8,12},{12,8},{16,20},{20,16},{24,28},{28,24},{1,5},{5... | collective-permute-start | bytes 786440 | tf_op jit(solution)/shard_map/ppermute | solution.py:328
  103.0 33.0 %collective-permute-start.43 = (bf16[256,256]{1,0:T(8,128)(2,1)S(1)}, bf16[256,256]{1,0:T(8,128)(2,1)S(1)}, u32[]{:S(2)}, u32[]{:S(2)}) collective-permute-start(bf16[256,256]{1,0:T(8,128)(2,1)S(1)} %collective-permute-done.42.refs_4_), channel_id=1, source_target_pairs={{0,4},{4,0},{8,12},{12,8},{16,20},{20,16},{24,28},{28,24},{1,5},{5... | collective-permute-start | bytes 393224 | tf_op jit(solution)/shard_map/ppermute | solution.py:328
  149.6 8.4 %collective-permute-start.1 = (bf16[512,256]{1,0:T(8,128)(2,1)S(1)}, bf16[512,256]{1,0:T(8,128)(2,1)S(1)}, u32[]{:S(2)}, u32[]{:S(2)}) collective-permute-start(bf16[512,256]{1,0:T(8,128)(2,1)S(1)} %fusion.29), channel_id=1, source_target_pairs={{0,8},{4,12},{8,0},{12,4},{16,24},{20,28},{24,16},{28,20},{1,9},{5... | collective-permute-start | bytes 786440 | tf_op jit(solution)/shard_map/cond/branch_0_fun/while/body/eval_jaxpr/ppermute | solution.py:34
  158.1 12.9 %collective-permute-start.2 = (bf16[512,256]{1,0:T(8,128)(2,1)S(1)}, bf16[512,256]{1,0:T(8,128)(2,1)}, u32[]{:S(2)}, u32[]{:S(2)}) collective-permute-start(bf16[512,256]{1,0:T(8,128)(2,1)S(1)} %add.137), channel_id=1, source_target_pairs={{0,16},{4,20},{8,24},{12,28},{16,0},{20,4},{24,8},{28,12},{1,17},{... | collective-permute-start | bytes 786440 | tf_op jit(solution)/shard_map/cond/branch_0_fun/while/body/eval_jaxpr/ppermute | solution.py:34
  182.7 8.4 %collective-permute-start.1 = (bf16[512,256]{1,0:T(8,128)(2,1)S(1)}, bf16[512,256]{1,0:T(8,128)(2,1)S(1)}, u32[]{:S(2)}, u32[]{:S(2)}) collective-permute-start(bf16[512,256]{1,0:T(8,128)(2,1)S(1)} %fusion.29), channel_id=1, source_target_pairs={{0,8},{4,12},{8,0},{12,4},{16,24},{20,28},{24,16},{28,20},{1,9},{5... | collective-permute-start | bytes 786440 | tf_op jit(solution)/shard_map/cond/branch_0_fun/while/body/eval_jaxpr/ppermute | solution.py:34
  191.2 12.4 %collective-permute-start.2 = (bf16[512,256]{1,0:T(8,128)(2,1)S(1)}, bf16[512,256]{1,0:T(8,128)(2,1)}, u32[]{:S(2)}, u32[]{:S(2)}) collective-permute-start(bf16[512,256]{1,0:T(8,128)(2,1)S(1)} %add.137), channel_id=1, source_target_pairs={{0,16},{4,20},{8,24},{12,28},{16,0},{20,4},{24,8},{28,12},{1,17},{... | collective-permute-start | bytes 786440 | tf_op jit(solution)/shard_map/cond/branch_0_fun/while/body/eval_jaxpr/ppermute | solution.py:34
  223.8 12.9 %collective-permute-start.2 = (bf16[512,256]{1,0:T(8,128)(2,1)S(1)}, bf16[512,256]{1,0:T(8,128)(2,1)}, u32[]{:S(2)}, u32[]{:S(2)}) collective-permute-start(bf16[512,256]{1,0:T(8,128)(2,1)S(1)} %add.137), channel_id=1, source_target_pairs={{0,16},{4,20},{8,24},{12,28},{16,0},{20,4},{24,8},{28,12},{1,17},{... | collective-permute-start | bytes 786440 | tf_op jit(solution)/shard_map/cond/branch_0_fun/while/body/eval_jaxpr/ppermute | solution.py:34
  248.5 8.4 %collective-permute-start.1 = (bf16[512,256]{1,0:T(8,128)(2,1)S(1)}, bf16[512,256]{1,0:T(8,128)(2,1)S(1)}, u32[]{:S(2)}, u32[]{:S(2)}) collective-permute-start(bf16[512,256]{1,0:T(8,128)(2,1)S(1)} %fusion.29), channel_id=1, source_target_pairs={{0,8},{4,12},{8,0},{12,4},{16,24},{20,28},{24,16},{28,20},{1,9},{5... | collective-permute-start | bytes 786440 | tf_op jit(solution)/shard_map/cond/branch_0_fun/while/body/eval_jaxpr/ppermute | solution.py:34
  256.9 12.4 %collective-permute-start.2 = (bf16[512,256]{1,0:T(8,128)(2,1)S(1)}, bf16[512,256]{1,0:T(8,128)(2,1)}, u32[]{:S(2)}, u32[]{:S(2)}) collective-permute-start(bf16[512,256]{1,0:T(8,128)(2,1)S(1)} %add.137), channel_id=1, source_target_pairs={{0,16},{4,20},{8,24},{12,28},{16,0},{20,4},{24,8},{28,12},{1,17},{... | collective-permute-start | bytes 786440 | tf_op jit(solution)/shard_map/cond/branch_0_fun/while/body/eval_jaxpr/ppermute | solution.py:34
  289.5 12.9 %collective-permute-start.2 = (bf16[512,256]{1,0:T(8,128)(2,1)S(1)}, bf16[512,256]{1,0:T(8,128)(2,1)}, u32[]{:S(2)}, u32[]{:S(2)}) collective-permute-start(bf16[512,256]{1,0:T(8,128)(2,1)S(1)} %add.137), channel_id=1, source_target_pairs={{0,16},{4,20},{8,24},{12,28},{16,0},{20,4},{24,8},{28,12},{1,17},{... | collective-permute-start | bytes 786440 | tf_op jit(solution)/shard_map/cond/branch_0_fun/while/body/eval_jaxpr/ppermute | solution.py:34
  314.2 8.4 %collective-permute-start.1 = (bf16[512,256]{1,0:T(8,128)(2,1)S(1)}, bf16[512,256]{1,0:T(8,128)(2,1)S(1)}, u32[]{:S(2)}, u32[]{:S(2)}) collective-permute-start(bf16[512,256]{1,0:T(8,128)(2,1)S(1)} %fusion.29), channel_id=1, source_target_pairs={{0,8},{4,12},{8,0},{12,4},{16,24},{20,28},{24,16},{28,20},{1,9},{5... | collective-permute-start | bytes 786440 | tf_op jit(solution)/shard_map/cond/branch_0_fun/while/body/eval_jaxpr/ppermute | solution.py:34
  322.7 12.4 %collective-permute-start.2 = (bf16[512,256]{1,0:T(8,128)(2,1)S(1)}, bf16[512,256]{1,0:T(8,128)(2,1)}, u32[]{:S(2)}, u32[]{:S(2)}) collective-permute-start(bf16[512,256]{1,0:T(8,128)(2,1)S(1)} %add.137), channel_id=1, source_target_pairs={{0,16},{4,20},{8,24},{12,28},{16,0},{20,4},{24,8},{28,12},{1,17},{... | collective-permute-start | bytes 786440 | tf_op jit(solution)/shard_map/cond/branch_0_fun/while/body/eval_jaxpr/ppermute | solution.py:34
  355.3 12.9 %collective-permute-start.2 = (bf16[512,256]{1,0:T(8,128)(2,1)S(1)}, bf16[512,256]{1,0:T(8,128)(2,1)}, u32[]{:S(2)}, u32[]{:S(2)}) collective-permute-start(bf16[512,256]{1,0:T(8,128)(2,1)S(1)} %add.137), channel_id=1, source_target_pairs={{0,16},{4,20},{8,24},{12,28},{16,0},{20,4},{24,8},{28,12},{1,17},{... | collective-permute-start | bytes 786440 | tf_op jit(solution)/shard_map/cond/branch_0_fun/while/body/eval_jaxpr/ppermute | solution.py:34
  380.0 8.4 %collective-permute-start.1 = (bf16[512,256]{1,0:T(8,128)(2,1)S(1)}, bf16[512,256]{1,0:T(8,128)(2,1)S(1)}, u32[]{:S(2)}, u32[]{:S(2)}) collective-permute-start(bf16[512,256]{1,0:T(8,128)(2,1)S(1)} %fusion.29), channel_id=1, source_target_pairs={{0,8},{4,12},{8,0},{12,4},{16,24},{20,28},{24,16},{28,20},{1,9},{5... | collective-permute-start | bytes 786440 | tf_op jit(solution)/shard_map/cond/branch_0_fun/while/body/eval_jaxpr/ppermute | solution.py:34
  388.4 12.4 %collective-permute-start.2 = (bf16[512,256]{1,0:T(8,128)(2,1)S(1)}, bf16[512,256]{1,0:T(8,128)(2,1)}, u32[]{:S(2)}, u32[]{:S(2)}) collective-permute-start(bf16[512,256]{1,0:T(8,128)(2,1)S(1)} %add.137), channel_id=1, source_target_pairs={{0,16},{4,20},{8,24},{12,28},{16,0},{20,4},{24,8},{28,12},{1,17},{... | collective-permute-start | bytes 786440 | tf_op jit(solution)/shard_map/cond/branch_0_fun/while/body/eval_jaxpr/ppermute | solution.py:34
  (79 other events, 657.0 us)

commit v3 on v2

--- a/solution.py
+++ b/solution.py
@@ -91,19 +91,41 @@
 SRC, LSRC, PACK, TABLE = 0, 64, 96, 128
 
 
-def first_kernel(owner, order, pattern, rhs_ref, win_ref, tab, flag, l0, l1, r0, r1, r2, r3,
-                 buf, pat, cnt, dcnt, lslot, llab, sem):
+def first_kernel(owner, order, pattern, rhs_ref, win_ref, l0, l1, r0, r1, r2, r3, buf, pat, inv, pos, sem):
     row, depth = lax.axis_index("rows"), lax.axis_index("rhs")
-    chip, core = row // 2, row % 2
     width = r0.shape[1]
+
+    def note_slot(w, carry):
+        slot = owner[w]
+
+        @pl.when(slot // SB == row)
+        def _():
+            inv[slot % SB] = w
+
+        return carry
+
+    lax.fori_loop(0, NWB, note_slot, 0)
+    for k in range(NSUP):
+        pos[order[k]] = k
+    labels = jnp.zeros((SB, 1), jnp.int32)
+    for t in range(SB):
+        label = order[(pos[inv[t] // SB] // 2) * 2]
+        pltpu.make_async_copy(win_ref.at[pl.ds(t * BS, BS), columns_at(label)], buf.at[pl.ds(t * BS, BS), :], sem).start()
+        labels = jnp.where(lax.broadcasted_iota(jnp.int32, (SB, 1), 0) == t, label, labels)
     for s, r in enumerate((r0, r1, r2, r3)):
         at = pl.multiple_of(jnp.bitwise_xor(depth, s) * width, width)
         r[...] = rhs_ref[:, pl.ds(at, width)]
+    pat[...] = pattern[pl.ds(pl.multiple_of(row * SB, SB), SB), :]
+    mask = expand_mask(pat[...], labels, spread_matrix())
+    pltpu.make_async_copy(win_ref.at[:, pl.ds(0, SN)], buf, sem).wait()
+    l0[...] = masked_rows(lambda j: buf[j * BS:(j + 1) * BS, :], mask[0:4], 4)
+    l1[...] = masked_rows(lambda j: buf[(j + 4) * BS:(j + 5) * BS, :], mask[4:8], 4)
+
+
+def table_kernel(owner, order, tab, flag, cnt):
+    row = lax.axis_index("rows")
+    chip, core = row // 2, row % 2
     flag[0] = 0
-    for t in range(SB):
-        dcnt[t] = 0
-        lslot[t] = 0
-        llab[t] = 0
     for t in range(GROUPS * SB):
         tab[PACK + t] = 0
     for group in range(GROUPS):
@@ -129,30 +151,11 @@
 
             @pl.when(i >= SB)
             def _():
-                index = dcnt[device]
-                dcnt[device] = index + 1
-                tab[LSRC + group * SB + i - SB] = jnp.bitwise_xor(device, row) * SB + index
-                if group == 0:
-                    flag[0] = jnp.where(index >= 4, 1, flag[0])
-
-                @pl.when(device == row)
-                def _():
-                    lslot[index] = slot % SB
-                    llab[index] = order[2 * group]
+                tab[LSRC + group * SB + i - SB] = jnp.bitwise_xor(device, row) * SB + slot % SB
 
             return carry
 
         lax.fori_loop(0, 2 * SB, one, 0)
-    labels = jnp.zeros((SB, 1), jnp.int32)
-    for t in range(SB):
-        slot, label = lslot[t], llab[t]
-        pltpu.make_async_copy(win_ref.at[rows_at(slot), columns_at(label)], buf.at[pl.ds(t * BS, BS), :], sem).start()
-        pat[t:t + 1, :] = pattern[pl.ds(row * SB + slot, 1), :]
-        labels = jnp.where(lax.broadcasted_iota(jnp.int32, (SB, 1), 0) == t, label, labels)
-    mask = expand_mask(pat[...], labels, spread_matrix())
-    pltpu.make_async_copy(win_ref.at[:, pl.ds(0, SN)], buf, sem).wait()
-    l0[...] = masked_rows(lambda j: buf[j * BS:(j + 1) * BS, :], mask[0:4], 4)
-    l1[...] = masked_rows(lambda j: buf[(j + 4) * BS:(j + 5) * BS, :], mask[4:8], 4)
 
 
 def first_pack_kernel(tab, *refs):
@@ -169,6 +172,28 @@
     b_ref[...] = p_ref[pl.ds(pl.multiple_of(core * SB // 2 * BS, SB // 2 * BS), SB // 2 * BS), :]
 
 
+def make_mask_kernel(group):
+    def kernel(tab, order, pattern, w_own, w_other, out, wrow, pat, sem):
+        row = lax.axis_index("rows")
+        for j in range(SB):
+            place = tab[PACK + (group + 1) * SB + j]
+            for side, w_ref in enumerate((w_own, w_other)):
+                @pl.when(place // SB == side)
+                def _(j=j, place=place, w_ref=w_ref):
+                    pltpu.make_async_copy(w_ref.at[rows_at(place % SB), :], wrow.at[pl.ds(j * BS, BS), :], sem).start()
+            pat[j:j + 1, :] = pattern[pl.ds(jnp.bitwise_xor(row, place // SB) * SB + place % SB, 1), :]
+        spread = spread_matrix()
+        rows = pat[...]
+        masks = [expand_mask(rows, order[k], spread) for k in range(2 * group + 2)]
+        pltpu.make_async_copy(w_own, wrow, sem).wait()
+        for k in range(2 * group + 2):
+            for j in range(SB):
+                at = slice(j * BS, (j + 1) * BS)
+                out[at, k * SN:(k + 1) * SN] = wrow[at, columns_at(order[k])] * masks[k][j:j + 1, :]
+
+    return kernel
+
+
 def make_prep_kernel(group):
     last = group == GROUPS - 1
 
@@ -179,43 +204,24 @@
         if last:
             d_out, l_out, dsem, lsem = refs
         else:
-            pattern, w_own, w_other, chip_rhs = refs[:4]
-            xs = refs[4:4 + group]
-            d_out, l_out, wn_out, r_out, wrow, pat, dsem, lsem, wsem = refs[4 + group:]
+            w_ref, chip_rhs = refs[:2]
+            xs = refs[2:2 + group]
+            d_out, l_out, r_out, dsem, lsem = refs[2 + group:]
         for q in range(2):
             pltpu.make_async_copy(diag_ref.at[order[2 * group + q]], d_out.at[q], dsem.at[q]).start()
-        if not last:
-            for j in range(SB):
-                place = tab[PACK + (group + 1) * SB + j]
-                for side, w_ref in enumerate((w_own, w_other)):
-                    @pl.when(place // SB == side)
-                    def _(j=j, place=place, w_ref=w_ref):
-                        pltpu.make_async_copy(w_ref.at[rows_at(place % SB), :], wrow.at[pl.ds(j * BS, BS), :], wsem).start()
         for i in range(SB):
             code = tab[LSRC + group * SB + i]
             for m in range(8):
-                for half in range(1 if group == 0 else 2):
-                    @pl.when((code // SB == m) & ((code % SB) // 4 == half) if group else code // SB == m)
-                    def _(m=m, half=half, i=i, code=code):
-                        pltpu.make_async_copy(l_refs[2 * m + half].at[rows_at(code % 4), :], l_out.at[pl.ds(i * BS, BS), :], lsem).start()
+                @pl.when(code // SB == m)
+                def _(m=m, i=i, code=code):
+                    for half in range(2):
+                        @pl.when((code % SB) // 4 == half)
+                        def _(half=half):
+                            pltpu.make_async_copy(l_refs[2 * m + half].at[rows_at(code % 4), :], l_out.at[pl.ds(i * BS, BS), :], lsem).start()
         if not last:
-            row = lax.axis_index("rows")
-            for j in range(SB):
-                place = tab[PACK + (group + 1) * SB + j]
-                pat[j:j + 1, :] = pattern[pl.ds(jnp.bitwise_xor(row, place // SB) * SB + place % SB, 1), :]
-            spread = spread_matrix()
-            rows = pat[...]
             total = jnp.concatenate([chip_rhs[rows_at(tab[PACK + (group + 1) * SB + j]), :] for j in range(SB)], axis=0).astype(F32)
-            pltpu.make_async_copy(w_own, wrow, wsem).wait()
-            for k in range(group + 1):
-                for q in range(2):
-                    label = order[2 * k + q]
-                    mask = expand_mask(rows, label, spread)
-                    part = masked_rows(lambda j: wrow[j * BS:(j + 1) * BS, columns_at(label)], mask, SB)
-                    if k == group:
-                        wn_out[:, q * SN:(q + 1) * SN] = part
-                    else:
-                        total = total - jnp.dot(part, xs[k][q * SN:(q + 1) * SN, :], preferred_element_type=F32)
+            for k in range(group):
+                total = total - jnp.dot(w_ref[:, k * PAIR:(k + 1) * PAIR], xs[k][...], preferred_element_type=F32)
             r_out[...] = total
         for q in range(2):
             pltpu.make_async_copy(diag_ref.at[0], d_out.at[q], dsem.at[q]).wait()
@@ -232,7 +238,7 @@
         if last:
             x_ref, panel = refs[8:]
         else:
-            wn_ref, r_ref, x_ref, p_ref, b_ref, panel = refs[8:]
+            r_ref, wn_ref, x_ref, p_ref, b_ref, panel = refs[8:]
 
         def place(i):
             code = tab[SRC + group * 16 + i]
@@ -250,8 +256,7 @@
         x_ref[SN:PAIR, :] = x_b
         if last:
             return
-        total = r_ref[...] - jnp.dot(wn_ref[:, 0:SN], x_a, preferred_element_type=F32)
-        total = total - jnp.dot(wn_ref[:, SN:PAIR], x_b, preferred_element_type=F32)
+        total = r_ref[...] - jnp.dot(wn_ref[:, group * PAIR:(group + 1) * PAIR], x_ref[...], preferred_element_type=F32)
         p_ref[...] = total.astype(BF16)
         core = lax.axis_index("rows") % 2
         b_ref[...] = p_ref[pl.ds(pl.multiple_of(core * SB // 2 * BS, SB // 2 * BS), SB // 2 * BS), :]
@@ -314,6 +319,10 @@
     return pltpu.CompilerParams(vmem_limit_bytes=mib * 1024 * 1024)
 
 
+def cost(micros):
+    return pl.CostEstimate(flops=micros * 10 ** 8, bytes_accessed=micros * 3 * 10 ** 6, transcendentals=0)
+
+
 def shape_of(dims, dtype=BF16):
     return jax.ShapeDtypeStruct(dims, dtype)
 
@@ -337,74 +346,95 @@
     half = SN // 2
     w_other = swap(win_rows, 1)
     tall = rhs_win.shape[0]
-    tab, flag, l_low, l_high, *sent = pl.pallas_call(
+    l_low, l_high, *sent = pl.pallas_call(
         first_kernel,
-        out_shape=(shape_of((TABLE,), jnp.int32), shape_of((1,), jnp.int32), shape_of((half, SN)), shape_of((half, SN)))
-        + (shape_of((tall, columns)),) * 4,
+        out_shape=(shape_of((half, SN)), shape_of((half, SN))) + (shape_of((tall, columns)),) * 4,
         in_specs=[SMEM, SMEM, VMEM, VMEM, HBM],
-        out_specs=(SMEM, SMEM) + (VMEM,) * 6,
-        scratch_shapes=[pltpu.VMEM((SN, SN), BF16), pltpu.VMEM((SB, NWB), jnp.int32), pltpu.SMEM((4,), jnp.int32),
-                        pltpu.SMEM((SB,), jnp.int32), pltpu.SMEM((SB,), jnp.int32), pltpu.SMEM((SB,), jnp.int32),
-                        pltpu.SemaphoreType.DMA],
+        out_specs=(VMEM,) * 6,
+        scratch_shapes=[pltpu.VMEM((SN, SN), BF16), pltpu.VMEM((SB, NWB), jnp.int32),
+                        pltpu.SMEM((SB,), jnp.int32), pltpu.SMEM((SB,), jnp.int32), pltpu.SemaphoreType.DMA],
         compiler_params=params(8),
+        cost_estimate=cost(2),
         name="first",
     )(window_owner, sn_order, win_pattern, rhs_win, win_rows)
-
     low, high = {0: l_low}, {0: l_high}
-    for m in (2, 4, 6):
+    for m in (2, 4):
         low[m] = swap(l_low, m)
     pieces = [sent[0]] + [deep(sent[s], s) for s in (1, 2, 3)]
+    for m in (2, 4):
+        high[m] = swap(l_high, m)
+    tab, flag = pl.pallas_call(
+        table_kernel,
+        out_shape=(shape_of((TABLE,), jnp.int32), shape_of((1,), jnp.int32)),
+        in_specs=[SMEM, SMEM],
+        out_specs=(SMEM, SMEM),
+        scratch_shapes=[pltpu.SMEM((4,), jnp.int32)],
+        compiler_params=params(4),
+        cost_estimate=cost(2),
+        name="tables",
+    )(window_owner, sn_order)
     others = [swap(x, 1) for x in pieces]
-    for m in (0, 2, 4, 6):
-        low[m + 1] = swap(low[m], 1)
     chip_rhs, packed, part = pl.pallas_call(
         first_pack_kernel,
         out_shape=(shape_of((PAIR, columns)), shape_of((SN, columns)), shape_of((half, columns))),
         in_specs=[SMEM] + [VMEM] * 8,
         out_specs=(VMEM,) * 3,
         compiler_params=params(6),
+        cost_estimate=cost(1),
         name="first_pack",
     )(tab, *pieces, *others)
+    low[6], high[6] = swap(low[2], 4), swap(high[4], 2)
+    for m in (0, 2, 4, 6):
+        low[m + 1] = swap(low[m], 1)
+        high[m + 1] = swap(high[m], 1)
+    l_parts = [x for m in range(8) for x in (low[m], high[m])]
 
     depth = lax.axis_index("rhs")
     tile = rhs_anc.shape[0]
-    sums, anc_pieces, solved = None, None, []
+    sums, solved, masked = None, [], []
+    anc_order, anc_pieces = (2, 3, 1), [None] * 4
+    tab_later, rhs_later = tab, rhs_anc
     for group in range(GROUPS):
         last = group == GROUPS - 1
         a_own = neighbour(packed)
         b_own = swap(part, 6)
+        hold = [a_own, b_own]
         if group == 0:
-            for m in (2, 4, 6):
-                high[m] = swap(l_high, m)
-            for m in (0, 2, 4, 6):
-                high[m + 1] = swap(high[m], 1)
-            l_parts = [x for m in range(8) for x in (low[m], low[m])]
-        else:
-            l_parts = [x for m in range(8) for x in (low[m], high[m])]
-        if group == 1:
-            anc_pieces = [lax.dynamic_slice_in_dim(rhs_anc, (depth ^ s) * columns, columns, 1) for s in range(4)]
-            anc_pieces = anc_pieces[:1] + [deep(anc_pieces[s], s) for s in (1, 2, 3)]
-        a_swap = swap(a_own, 1)
-        b_swap = swap(b_own, 1)
+            tab_later, _ = lax.optimization_barrier((tab, packed))
+            for k in range(GROUPS - 1):
+                masked.append(pl.pallas_call(
+                    make_mask_kernel(k),
+                    out_shape=shape_of((SN, (k + 1) * PAIR)),
+                    in_specs=[SMEM, SMEM, VMEM, HBM, HBM],
+                    out_specs=VMEM,
+                    scratch_shapes=[pltpu.VMEM((SN, NW), BF16), pltpu.VMEM((SB, NWB), jnp.int32), pltpu.SemaphoreType.DMA],
+                    compiler_params=params(10),
+                    cost_estimate=cost(3),
+                    name="mask_rows",
+                )(tab_later, sn_order, win_pattern, win_rows, w_other))
+            hold += masked
+        if not last:
+            rhs_later, _ = lax.optimization_barrier((rhs_later, packed))
+            s = anc_order[group]
+            anc_pieces[s] = deep(lax.dynamic_slice_in_dim(rhs_later, (depth ^ s) * columns, columns, 1), s)
+            if group == 2:
+                anc_pieces[0] = lax.dynamic_slice_in_dim(rhs_later, depth * columns, columns, 1)
 
         operands = [tab, sn_order, *l_parts, diag_inv]
         in_specs = [SMEM, SMEM] + [HBM] * 17
         out_shape = [shape_of((2, SN, SN)), shape_of((SN, SN))]
-        scratch = []
-        sems = [pltpu.SemaphoreType.DMA((2,)), pltpu.SemaphoreType.DMA]
         if not last:
-            operands += [win_pattern, win_rows, w_other, chip_rhs, *solved]
-            in_specs += [VMEM, HBM, HBM] + [VMEM] * (1 + group)
-            out_shape += [shape_of((SN, PAIR)), shape_of((SN, columns), F32)]
-            scratch = [pltpu.VMEM((SN, NW), BF16), pltpu.VMEM((SB, NWB), jnp.int32)]
-            sems += [pltpu.SemaphoreType.DMA]
+            operands += [masked[group], chip_rhs, *solved]
+            in_specs += [VMEM] * (2 + group)
+            out_shape += [shape_of((SN, columns), F32)]
         ready = pl.pallas_call(
             make_prep_kernel(group),
             out_shape=tuple(out_shape),
             in_specs=in_specs,
             out_specs=(VMEM,) * len(out_shape),
-            scratch_shapes=scratch + sems,
-            compiler_params=params(16),
+            scratch_shapes=[pltpu.SemaphoreType.DMA((2,)), pltpu.SemaphoreType.DMA],
+            compiler_params=params(8),
+            cost_estimate=cost(2),
             name="prep",
         )(*operands)
         if group > 0:
@@ -415,18 +445,27 @@
                 out_shape=shape_of((anc_rows.shape[0], columns), F32),
                 grid_spec=pltpu.PrefetchScalarGridSpec(
                     num_scalar_prefetch=1,
-                    grid=(anc_rows.shape[0] // tile,),
-                    in_specs=[pl.BlockSpec((tile, SN), lambda i, o, k=k: (i, o[2 * k])),
-                              pl.BlockSpec((tile, SN), lambda i, o, k=k: (i, o[2 * k + 1])),
-                              pl.BlockSpec((SB, NWB), lambda i, o: (i, 0)),
+                    grid=(anc_rows.shape[0] // (2 * tile),),
+                    in_specs=[pl.BlockSpec((2 * tile, SN), lambda i, o, k=k: (i, o[2 * k])),
+                              pl.BlockSpec((2 * tile, SN), lambda i, o, k=k: (i, o[2 * k + 1])),
+                              pl.BlockSpec((2 * SB, NWB), lambda i, o: (i, 0)),
                               pl.BlockSpec((PAIR, columns), lambda i, o: (0, 0))]
-                    + [pl.BlockSpec((tile, columns), lambda i, o: (i, 0))] * len(more),
-                    out_specs=pl.BlockSpec((tile, columns), lambda i, o: (i, 0)),
+                    + [pl.BlockSpec((2 * tile, columns), lambda i, o: (i, 0))] * len(more),
+                    out_specs=pl.BlockSpec((2 * tile, columns), lambda i, o: (i, 0)),
                 ),
                 input_output_aliases={5: 0} if more else {},
-                compiler_params=params(12),
+                compiler_params=params(14),
+                cost_estimate=cost(5),
                 name="rows_below",
             )(sn_order, anc_rows, anc_rows, anc_pattern, solved[k], *more)
+            previous = anc_pieces[anc_order[k]]
+            a_own, b_own, sums, previous, *ready = lax.optimization_barrier((a_own, b_own, sums, previous, *ready))
+            anc_pieces[anc_order[k]] = previous
+        else:
+            a_own, b_own, *masked = lax.optimization_barrier((a_own, b_own, *masked))
+        a_swap = swap(a_own, 1)
+        b_swap = swap(b_own, 1)
+        ready = list(ready) if last else list(ready) + [masked[group]]
 
         out_shape = [shape_of((PAIR, columns))]
         if not last:
@@ -437,7 +476,8 @@
             in_specs=[SMEM] + [VMEM] * (5 + len(ready)),
             out_specs=(VMEM,) * len(out_shape),
             scratch_shapes=[pltpu.VMEM((PAIR, columns), BF16)],
-            compiler_params=params(12),
+            compiler_params=params(8),
+            cost_estimate=cost(3),
             name="pair_solve",
         )(tab, packed, a_own, a_swap, b_own, b_swap, *ready)
         solved.append(results[0])
@@ -461,7 +501,8 @@
                 out_specs=(HBM, pl.BlockSpec((tile, columns), lambda i, o: (i, 0))),
                 scratch_shapes=[pltpu.SemaphoreType.DMA((2 * GROUPS,))],
             ),
-            compiler_params=params(24),
+            compiler_params=params(20),
+            cost_estimate=cost(6),
             name="last_rows",
         )(sn_order, anc_rows, anc_rows, anc_pattern, *xs, sums, *anc_pieces)
 

time: 417 us -> 144 us (0.35); the launches traced: 411 us -> 143 us
  waiting for transfers between devices: 121 us -> 20.2 us
  local copies, waits for them, and re-layouts: 101 us -> 30.1 us
  matrix products: 48.9 us -> 0 us
  loops' own time: 26.6 us -> 0.24 us
  starting transfers between devices: 51.8 us -> 33.4 us
  other arithmetic: 10.5 us -> 0 us
  Pallas kernels: 50 us -> 56.6 us
    mul x32 -> x0, local copies, waits for them, and re-layouts: 70.7 us -> none  [masked_columns(): columns.reshape(blocks, BS, SB, BS) * chosen[:, None, :, None].astype(BF16)]
    ppermute x24 -> x0, waiting for transfers between devices: 67.1 us -> none  [sum_over_rows(): lax.ppermute(values, 'rows', [(i, i ^ step) for i in range(count)])]
    dot_general x24 -> x0, matrix products: 48.9 us -> none  [the longest x8 19.9 us: step(): jnp.dot(masked_columns(anc_rows, anc_pattern, node_label), solved, prefer...]
    another operation x1 -> x0, loops' own time: 26.3 us -> none  [general_path(): solution, _, anc_resid = lax.fori_loop(0, NSUP, step, first)]
    unnamed x60 -> x174, local copies, waits for them, and re-layouts: 1.84 us -> 26.3 us
    ppermute x24 -> x0, starting transfers between devices: 21.6 us -> none  [sum_over_rows(): lax.ppermute(values, 'rows', [(i, i ^ step) for i in range(count)])]
    ppermute x31, waiting for transfers between devices: 28.6 us -> 14.5 us  [swap(): return lax.ppermute(x, 'rows', [(i, i ^ m) for i in range(8)])]
    pallas_call x1 -> x6, Pallas kernels: 5.62 us -> 18.8 us  [the longest x1 7.6 us: packed_path(): pl.pallas_call(last_rows_kernel, out_shape=(shape_of((NW, columns)), shap...]
  transfers between devices with their start and end apart: 65 -> 41, of which waited for: 33 -> 8; matrix products, arithmetic and copies ran while one was open for 18% -> 3% of each run, Pallas kernels for 10% -> 32%
where the time goes in v3:
time: 144 us; the launch traced here: 143 us
  Pallas kernels  56.6 us (39%)
  starting transfers between devices  33.4 us (23%)
  local copies, waits for them, and re-layouts  30.1 us (21%)
  waiting for transfers between devices  20.2 us (14%)
  between operations  2.39 us (2%)
    unnamed x174, local copies, waits for them, and re-layouts  26.3 us
    ppermute x31, starting transfers between devices, swap(): return lax.ppermute(x, 'rows', [(i, i ^ m) for i in range(8)])  18.3 us
    pallas_call x3, Pallas kernels, local(): pl.pallas_call(make_rows_kernel(k), out_shape=shape_of((anc_rows.shape[0]...  16 us
    ppermute x31, waiting for transfers between devices, swap(): return lax.ppermute(x, 'rows', [(i, i ^ m) for i in range(8)])  14.5 us
    pallas_call x4, Pallas kernels, local(): pl.pallas_call(make_solve_kernel(group), out_shape=tuple(out_shape), in_s...  12.8 us
    ppermute x6, starting transfers between devices, deep(): return lax.ppermute(x, 'rhs', [(i, i ^ m) for i in range(4)])  9.04 us
    pallas_call x4, Pallas kernels, local(): pl.pallas_call(make_prep_kernel(group), out_shape=tuple(out_shape), in_sp...  8.37 us
    pallas_call x1, Pallas kernels, packed_path(): pl.pallas_call(last_rows_kernel, out_shape=(shape_of((NW, columns)), shap...  7.6 us
  transfers between devices with their start and end apart: 41, of which 8 were waited for; matrix products, arithmetic and copies ran while one was open for 3% of the time, Pallas kernels for 32%

profile of v3, /device:TPU:0, one launch (start us, length us, event | category | flops | bytes accessed | tf_op | source)
XLA Modules:
  0.0 142.9 jit_solution(15017167757117063318)
XLA Ops:
  2.1 3.2 %first.1 = (bf16[256,512]{1,0:T(8,128)(2,1)S(1)}, bf16[256,512]{1,0:T(8,128)(2,1)S(1)}, bf16[128,256]{1,0:T(8,128)(2,1)S(1)}, bf16[128,256]{1,0:T(8,128)(2,1)S(1...) custom-call(s32[64]{0:T(128)} %owner.3, s32[8]{0:T(128)} %refs_1_.7, s32[64,64]{1,0:T(8,128)} %pattern.10, ...), custom_call_target="tpu_custom_call" | custom-call | flops 200000000 | bytes 6000000 | tf_op jit(solution)/shard_map/first/pallas_call | solution.py:349
  5.3 2.7 %collective-permute-start.3 = (bf16[128,256]{1,0:T(8,128)(2,1)S(1)}, bf16[128,256]{1,0:T(8,128)(2,1)S(1)}, u32[]{:S(2)}, u32[]{:S(2)}) collective-permute-start(bf16[128,256]{1,0:T(8,128)(2,1)S(1)} %get-tuple-element.348), channel_id=1, source_target_pairs={{0,1},{1,0},{2,3},{3,2},{4,5},{5,4},{6,7},{7,6},{8,9},{9,8},{10,11... | collective-permute-start | bytes 196616 | tf_op jit(solution)/shard_map/ppermute | solution.py:340
  8.0 2.6 %collective-permute-start.4 = (bf16[128,256]{1,0:T(8,128)(2,1)S(1)}, bf16[128,256]{1,0:T(8,128)(2,1)S(1)}, u32[]{:S(2)}, u32[]{:S(2)}) collective-permute-start(bf16[128,256]{1,0:T(8,128)(2,1)S(1)} %get-tuple-element.349), channel_id=1, source_target_pairs={{0,2},{1,3},{2,0},{3,1},{4,6},{5,7},{6,4},{7,5},{8,10},{9,11},{10,... | collective-permute-start | bytes 196616 | tf_op jit(solution)/shard_map/ppermute | solution.py:340
  11.1 3.9 %collective-permute-done.4.refs_2_ = bf16[128,256]{1,0:T(8,128)(2,1)S(1)} collective-permute-done((bf16[128,256]{1,0:T(8,128)(2,1)S(1)}, bf16[128,256]{1,0:T(8,128)(2,1)S(1)}, u32[]{:S(2)}, u32[]{:S(2)}) %collective-permute-start.4) | collective-permute-done | bytes 65568 | tf_op jit(solution)/shard_map/ppermute | solution.py:340
  15.0 1.7 %collective-permute-done.5.refs_3_ = bf16[128,256]{1,0:T(8,128)(2,1)S(1)} collective-permute-done((bf16[128,256]{1,0:T(8,128)(2,1)S(1)}, bf16[128,256]{1,0:T(8,128)(2,1)S(1)}, u32[]{:S(2)}, u32[]{:S(2)}) %collective-permute-start.5) | collective-permute-done | bytes 65568 | tf_op jit(solution)/shard_map/ppermute | solution.py:340
  18.7 4.0 %tables.1 = (s32[128]{0:T(128)S(1)}, s32[1]{0:T(128)}) custom-call(s32[64]{0:T(128)S(1)} %copy-done.90, s32[8]{0:T(128)S(1)} %copy-done.86), custom_call_target="tpu_custom_call" | custom-call | flops 200000000 | bytes 6000000 | tf_op jit(solution)/shard_map/tables/pallas_call | solution.py:366
  25.7 5.3 %collective-permute-done.11.refs_4_ = bf16[256,256]{1,0:T(8,128)(2,1)S(1)} collective-permute-done((bf16[256,256]{1,0:T(8,128)(2,1)S(1)}, bf16[256,256]{1,0:T(8,128)(2,1)S(1)}, u32[]{:S(2)}, u32[]{:S(2)}) %collective-permute-start.11) | collective-permute-done | bytes 131104 | tf_op jit(solution)/shard_map/ppermute | solution.py:337
  32.2 1.5 %collective-permute-start.21 = (bf16[256,512]{1,0:T(8,128)(2,1)S(1)}, bf16[256,512]{1,0:T(8,128)(2,1)}, u32[]{:S(2)}, u32[]{:S(2)}) collective-permute-start(bf16[256,512]{1,0:T(8,128)(2,1)S(1)} %get-tuple-element.358.refs_2_), channel_id=1, source_target_pairs={{0,16},{4,20},{8,24},{12,28},{16,0},{20,4},{24,8},{28,12},{1,17},{... | collective-permute-start | bytes 786440 | tf_op jit(solution)/shard_map/ppermute | solution.py:337
  37.2 1.7 %collective-permute-done.18.refs_7_ = bf16[256,512]{1,0:T(8,128)(2,1)S(1)} collective-permute-done((bf16[256,512]{1,0:T(8,128)(2,1)S(1)}, bf16[256,512]{1,0:T(8,128)(2,1)S(1)}, u32[]{:S(2)}, u32[]{:S(2)}) %collective-permute-start.18) | collective-permute-done | bytes 262176 | tf_op jit(solution)/shard_map/ppermute | solution.py:337
  38.9 2.7 %collective-permute-done.21.refs_10_ = bf16[256,512]{1,0:T(8,128)(2,1)} collective-permute-done((bf16[256,512]{1,0:T(8,128)(2,1)S(1)}, bf16[256,512]{1,0:T(8,128)(2,1)}, u32[]{:S(2)}, u32[]{:S(2)}) %collective-permute-start.21) | collective-permute-done | bytes 262176 | tf_op jit(solution)/shard_map/ppermute | solution.py:337
  41.6 1.5 %collective-permute-start.25 = (bf16[256,512]{1,0:T(8,128)(2,1)S(1)}, bf16[256,512]{1,0:T(8,128)(2,1)}, u32[]{:S(2)}, u32[]{:S(2)}) collective-permute-start(bf16[256,512]{1,0:T(8,128)(2,1)S(1)} %collective-permute-done.17.refs_6_), channel_id=1, source_target_pairs={{0,16},{4,20},{8,24},{12,28},{16,0},{20,4},{24,8},{28,12},{1,17},{... | collective-permute-start | bytes 786440 | tf_op jit(solution)/shard_map/ppermute | solution.py:337
  43.1 4.1 %collective-permute-done.22.refs_11_ = bf16[256,512]{1,0:T(8,128)(2,1)} collective-permute-done((bf16[256,512]{1,0:T(8,128)(2,1)S(1)}, bf16[256,512]{1,0:T(8,128)(2,1)}, u32[]{:S(2)}, u32[]{:S(2)}) %collective-permute-start.22) | collective-permute-done | bytes 262176 | tf_op jit(solution)/shard_map/ppermute | solution.py:337
  58.3 2.3 %collective-permute-start.31 = (bf16[512,256]{1,0:T(8,128)(2,1)S(1)}, bf16[512,256]{1,0:T(8,128)(2,1)S(1)}, u32[]{:S(2)}, u32[]{:S(2)}) collective-permute-start(bf16[512,256]{1,0:T(8,128)(2,1)S(1)} %constant_dynamic-slice_fusion.4), channel_id=1, source_target_pairs={{0,2},{1,3},{2,0},{3,1},{4,6},{5,7},{6,4},{7,5},{8,10},{9,11},{10,... | collective-permute-start | bytes 786440 | tf_op jit(solution)/shard_map/ppermute | solution.py:340
  69.5 2.2 %prep.4 = (bf16[2,512,512]{2,1,0:T(8,128)(2,1)S(1)}, bf16[512,512]{1,0:T(8,128)(2,1)S(1)}, f32[512,256]{1,0:T(8,128)S(1)}) custom-call(s32[128]{0:T(128)S(1)} %get-tuple-element.355.tab.refs_0_, s32[8]{0:T(128)S(1)} %copy-done.86, bf16[256,512]{1,0:T(8,128)(2,1)S(1)} %get-tuple-element.358.refs_2_, bf16[256,512]{1,0:T(8,128)(2,1)S(1)} %copy-done.10, ...), custom_call_target="tpu_custom_call" | custom-call | flops 200000000 | bytes 6000000 | tf_op jit(solution)/shard_map/prep/pallas_call | solution.py:430
  71.8 3.1 %pair_solve.4 = (bf16[1024,256]{1,0:T(8,128)(2,1)S(1)}, bf16[512,256]{1,0:T(8,128)(2,1)S(1)}, bf16[256,256]{1,0:T(8,128)(2,1)S(1)}) custom-call(s32[128]{0:T(128)S(1)} %get-tuple-element.355.tab.refs_0_, bf16[512,256]{1,0:T(8,128)(2,1)S(1)} %copy-done.58, bf16[512,256]{1,0:T(8,128)(2,1)} %collective-permute-done.10.refs_2_, ...), custom_call_target="tpu_custom_call" | custom-call | flops 300000000 | bytes 9000000 | tf_op jit(solution)/shard_map/pair_solve/pallas_call | solution.py:473
  74.9 1.6 %collective-permute-start.29 = (bf16[512,256]{1,0:T(8,128)(2,1)S(1)}, bf16[512,256]{1,0:T(8,128)(2,1)}, u32[]{:S(2)}, u32[]{:S(2)}) collective-permute-start(bf16[512,256]{1,0:T(8,128)(2,1)S(1)} %get-tuple-element.365.refs_1_), channel_id=1, source_target_pairs={{0,8},{4,20},{8,0},{12,28},{16,24},{20,4},{24,16},{28,12},{1,9},{5... | collective-permute-start | bytes 786440 | tf_op jit(solution)/shard_map/ppermute | solution.py:343
  76.5 1.5 %collective-permute-start.30 = (bf16[256,256]{1,0:T(8,128)(2,1)S(1)}, bf16[256,256]{1,0:T(8,128)(2,1)S(1)}, u32[]{:S(2)}, u32[]{:S(2)}) collective-permute-start(bf16[256,256]{1,0:T(8,128)(2,1)S(1)} %get-tuple-element.367), channel_id=1, source_target_pairs={{0,24},{4,28},{8,16},{12,20},{16,8},{20,12},{24,0},{28,4},{1,25},{... | collective-permute-start | bytes 393224 | tf_op jit(solution)/shard_map/ppermute | solution.py:337
  78.1 2.1 %prep.5 = (bf16[2,512,512]{2,1,0:T(8,128)(2,1)S(1)}, bf16[512,512]{1,0:T(8,128)(2,1)S(1)}, f32[512,256]{1,0:T(8,128)S(1)}) custom-call(s32[128]{0:T(128)S(1)} %get-tuple-element.355.tab.refs_0_, s32[8]{0:T(128)S(1)} %copy-done.86, bf16[256,512]{1,0:T(8,128)(2,1)S(1)} %get-tuple-element.358.refs_2_, bf16[256,512]{1,0:T(8,128)(2,1)S(1)} %copy-done.11, ...), custom_call_target="tpu_custom_call" | custom-call | flops 200000000 | bytes 6000000 | tf_op jit(solution)/shard_map/prep/pallas_call | solution.py:430
  80.2 5.0 %rows_below.3.refs_0_ = f32[2048,256]{1,0:T(8,128)} custom-call(s32[8]{0:T(128)S(1)} %copy-done.86, bf16[2048,4096]{1,0:T(8,128)(2,1)} %a1.5, bf16[2048,4096]{1,0:T(8,128)(2,1)} %a1.5, s32[32,64]{1,0:T(8,128)S(1)} %copy-done.70, bf16[1024,256]{1,0:T(8,128)(2,1)S(1)} %get-tuple-element.368.x_ref.refs_21_), custom_call_target="tpu_custom_call" | custom-call | flops 500000000 | bytes 15000000 | tf_op jit(solution)/shard_map/rows_below/pallas_call | solution.py:443
  88.9 1.6 %copy-done.2 = bf16[512,2048]{1,0:T(8,128)(2,1)S(1)} copy-done((bf16[512,2048]{1,0:T(8,128)(2,1)S(1)}, bf16[512,2048]{1,0:T(8,128)(2,1)}, u32[]{:S(2)}) %copy-start.2) | copy-done | bytes 2097176
  94.8 3.3 %pair_solve.5 = (bf16[1024,256]{1,0:T(8,128)(2,1)S(1)}, bf16[512,256]{1,0:T(8,128)(2,1)S(1)}, bf16[256,256]{1,0:T(8,128)(2,1)S(1)}) custom-call(s32[128]{0:T(128)S(1)} %get-tuple-element.355.tab.refs_0_, bf16[512,256]{1,0:T(8,128)(2,1)S(1)} %copy-done.62, bf16[512,256]{1,0:T(8,128)(2,1)} %collective-permute-done.29.refs_2_, ...), custom_call_target="tpu_custom_call" | custom-call | flops 300000000 | bytes 9000000 | tf_op jit(solution)/shard_map/pair_solve/pallas_call | solution.py:473
  98.2 1.6 %collective-permute-start.34 = (bf16[512,256]{1,0:T(8,128)(2,1)S(1)}, bf16[512,256]{1,0:T(8,128)(2,1)}, u32[]{:S(2)}, u32[]{:S(2)}) collective-permute-start(bf16[512,256]{1,0:T(8,128)(2,1)S(1)} %get-tuple-element.378.refs_1_), channel_id=1, source_target_pairs={{0,8},{4,20},{8,0},{12,28},{16,24},{20,4},{24,16},{28,12},{1,9},{5... | collective-permute-start | bytes 786440 | tf_op jit(solution)/shard_map/ppermute | solution.py:343
  100.9 2.2 %prep.6 = (bf16[2,512,512]{2,1,0:T(8,128)(2,1)S(1)}, bf16[512,512]{1,0:T(8,128)(2,1)S(1)}, f32[512,256]{1,0:T(8,128)S(1)}) custom-call(s32[128]{0:T(128)S(1)} %get-tuple-element.355.tab.refs_0_, s32[8]{0:T(128)S(1)} %copy-done.86, bf16[256,512]{1,0:T(8,128)(2,1)S(1)} %get-tuple-element.358.refs_2_, bf16[256,512]{1,0:T(8,128)(2,1)S(1)} %copy-done.12, ...), custom_call_target="tpu_custom_call" | custom-call | flops 200000000 | bytes 6000000 | tf_op jit(solution)/shard_map/prep/pallas_call | solution.py:430
  103.1 5.4 %rows_below.4.refs_0_ = f32[2048,256]{1,0:T(8,128)} custom-call(s32[8]{0:T(128)S(1)} %copy-done.86, bf16[2048,4096]{1,0:T(8,128)(2,1)} %a1.5, bf16[2048,4096]{1,0:T(8,128)(2,1)} %a1.5, s32[32,64]{1,0:T(8,128)S(1)} %copy-done.71, bf16[1024,256]{1,0:T(8,128)(2,1)S(1)} %get-tuple-element.381.x_ref.refs_22_, ...), custom_call_target="tpu_custom_call", output_to_operand_aliasing={{}: (5, {})} | custom-call | flops 500000000 | bytes 15000000 | tf_op jit(solution)/shard_map/rows_below/pallas_call | solution.py:443
  109.7 1.8 %constant_dynamic-slice_fusion.1 = (bf16[512,256]{1,0:T(8,128)(2,1)S(1)}, bf16[512,256]{1,0:T(8,128)(2,1)}) fusion(bf16[512,1024]{1,0:T(8,128)(2,1)} %param.21, s32[]{:T(128)S(6)} %select_n.104, s32[]{:T(128)S(6)} %select_n.102), kind=kLoop, calls=%fused_computation.41 | loop fusion | bytes 1048584 | tf_op jit(solution)/shard_map/dynamic_slice | solution.py:419
  116.0 3.5 %pair_solve.6 = (bf16[1024,256]{1,0:T(8,128)(2,1)}, bf16[512,256]{1,0:T(8,128)(2,1)S(1)}, bf16[256,256]{1,0:T(8,128)(2,1)S(1)}) custom-call(s32[128]{0:T(128)S(1)} %get-tuple-element.355.tab.refs_0_, bf16[512,256]{1,0:T(8,128)(2,1)S(1)} %copy-done.60, bf16[512,256]{1,0:T(8,128)(2,1)} %collective-permute-done.34.refs_2_, ...), custom_call_target="tpu_custom_call" | custom-call | flops 300000000 | bytes 9000000 | tf_op jit(solution)/shard_map/pair_solve/pallas_call | solution.py:473
  120.9 1.5 %collective-permute-start.40 = (bf16[256,256]{1,0:T(8,128)(2,1)S(1)}, bf16[256,256]{1,0:T(8,128)(2,1)S(1)}, u32[]{:S(2)}, u32[]{:S(2)}) collective-permute-start(bf16[256,256]{1,0:T(8,128)(2,1)S(1)} %get-tuple-element.393), channel_id=1, source_target_pairs={{0,24},{4,28},{8,16},{12,20},{16,8},{20,12},{24,0},{28,4},{1,25},{... | collective-permute-start | bytes 393224 | tf_op jit(solution)/shard_map/ppermute | solution.py:337
  122.5 2.0 %prep.7 = (bf16[2,512,512]{2,1,0:T(8,128)(2,1)S(1)}, bf16[512,512]{1,0:T(8,128)(2,1)S(1)}) custom-call(s32[128]{0:T(128)S(1)} %get-tuple-element.355.tab.refs_0_, s32[8]{0:T(128)S(1)} %copy-done.86, bf16[256,512]{1,0:T(8,128)(2,1)S(1)} %get-tuple-element.358.refs_2_, bf16[256,512]{1,0:T(8,128)(2,1)S(1)} %copy-done.13, bf16[256,512]{1,0:T(8,128)(2,1)S(1)} %copy-done.18, ...), custom_call_target="tpu_custom_call" | custom-call | flops 200000000 | bytes 6000000 | tf_op jit(solution)/shard_map/prep/pallas_call | solution.py:430
  124.5 5.6 %rows_below.5 = f32[2048,256]{1,0:T(8,128)} custom-call(s32[8]{0:T(128)S(1)} %copy-done.86, bf16[2048,4096]{1,0:T(8,128)(2,1)} %a1.5, bf16[2048,4096]{1,0:T(8,128)(2,1)} %a1.5, s32[32,64]{1,0:T(8,128)S(1)} %copy-done.72, bf16[1024,256]{1,0:T(8,128)(2,1)} %get-tuple-element.394.x_ref, f32[2048,256]{1,0:T(8,128)} %rows_below.4.refs_0_), custom_call_target="tpu_custom_call", output_to_operand_aliasing={{}: (5, {})} | custom-call | flops 500000000 | bytes 15000000 | tf_op jit(solution)/shard_map/rows_below/pallas_call | solution.py:443
  132.0 2.9 %pair_solve.7 = bf16[1024,256]{1,0:T(8,128)(2,1)} custom-call(s32[128]{0:T(128)S(1)} %get-tuple-element.355.tab.refs_0_, bf16[512,256]{1,0:T(8,128)(2,1)S(1)} %get-tuple-element.392.refs_1_, bf16[512,256]{1,0:T(8,128)(2,1)S(1)} %collective-permute-done.39.refs_2_, bf16[512,256]{1,0:T(8,128)(2,1)S(1)} %collective-permute-done.42.refs_3_, ...), custom_call_target="tpu_custom_call" | custom-call | flops 300000000 | bytes 9000000 | tf_op jit(solution)/shard_map/pair_solve/pallas_call | solution.py:473
  134.9 7.8 %conditional.1 = ((bf16[4096,256]{1,0:T(8,128)(2,1)}, bf16[2048,256]{1,0:T(8,128)(2,1)})) conditional(s32[]{:T(128)} %bitcast.16, (s32[]{:T(128)}, bf16[128,256]{1,0:T(8,128)(2,1)S(1)}, bf16[128,256]{1,0:T(8,128)(2,1)S(1)}, bf16[128,256]{1,0:T(8,128)(2,1)S(1)}, bf16[128,256]{1,0:T(8,128)(2,1)S(1)}, /*index=5*/bf16[512,256]{1,0:T(8,128)(2,1)S(1)}, ...), branch_computations={%region_0.3_spmd, %region_3.4_spmd} | conditional | flops 816449984 | bytes 57440044 | solution.py:515
  135.2 7.6 %last_rows.1 = (bf16[4096,256]{1,0:T(8,128)(2,1)}, bf16[2048,256]{1,0:T(8,128)(2,1)}) custom-call(s32[8]{0:T(128)S(1)} %get-tuple-element.272.order, bf16[2048,4096]{1,0:T(8,128)(2,1)} %get-tuple-element.273.a0.a1, bf16[2048,4096]{1,0:T(8,128)(2,1)} %get-tuple-element.273.a0.a1, s32[32,64]{1,0:T(8,128)S(1)} %get-tuple-element.274.pattern, ...), custom_call_target="tpu_custom_call" | custom-call | flops 600000000 | bytes 18000000 | tf_op jit(solution)/shard_map/cond/branch_1_fun/last_rows/pallas_call | solution.py:490
  (246 shorter events, 49.0 us)
Async XLA Ops:
  0.6 49.1 %collective-permute-start.12 = (bf16[512,4096]{1,0:T(8,128)(2,1)}, bf16[512,4096]{1,0:T(8,128)(2,1)S(1)}, u32[]{:S(2)}, u32[]{:S(2)}) collective-permute-start(bf16[512,4096]{1,0:T(8,128)(2,1)} %w_own.5), channel_id=1, source_target_pairs={{0,4},{4,0},{8,12},{12,8},{16,20},{20,16},{24,28},{28,24},{1,5},{5... | collective-permute-start | bytes 12582920 | tf_op jit(solution)/shard_map/ppermute | solution.py:337
  5.3 5.4 %collective-permute-start.3 = (bf16[128,256]{1,0:T(8,128)(2,1)S(1)}, bf16[128,256]{1,0:T(8,128)(2,1)S(1)}, u32[]{:S(2)}, u32[]{:S(2)}) collective-permute-start(bf16[128,256]{1,0:T(8,128)(2,1)S(1)} %get-tuple-element.348), channel_id=1, source_target_pairs={{0,1},{1,0},{2,3},{3,2},{4,5},{5,4},{6,7},{7,6},{8,9},{9,8},{10,11... | collective-permute-start | bytes 196616 | tf_op jit(solution)/shard_map/ppermute | solution.py:340
  8.0 7.0 %collective-permute-start.4 = (bf16[128,256]{1,0:T(8,128)(2,1)S(1)}, bf16[128,256]{1,0:T(8,128)(2,1)S(1)}, u32[]{:S(2)}, u32[]{:S(2)}) collective-permute-start(bf16[128,256]{1,0:T(8,128)(2,1)S(1)} %get-tuple-element.349), channel_id=1, source_target_pairs={{0,2},{1,3},{2,0},{3,1},{4,6},{5,7},{6,4},{7,5},{8,10},{9,11},{10,... | collective-permute-start | bytes 196616 | tf_op jit(solution)/shard_map/ppermute | solution.py:340
  10.6 6.1 %collective-permute-start.5 = (bf16[128,256]{1,0:T(8,128)(2,1)S(1)}, bf16[128,256]{1,0:T(8,128)(2,1)S(1)}, u32[]{:S(2)}, u32[]{:S(2)}) collective-permute-start(bf16[128,256]{1,0:T(8,128)(2,1)S(1)} %get-tuple-element.350), channel_id=1, source_target_pairs={{0,3},{1,2},{2,1},{3,0},{4,7},{5,6},{6,5},{7,4},{8,11},{9,10},{10,... | collective-permute-start | bytes 196616 | tf_op jit(solution)/shard_map/ppermute | solution.py:340
  10.6 6.1 %collective-permute-start.6 = (bf16[128,256]{1,0:T(8,128)(2,1)S(1)}, bf16[128,256]{1,0:T(8,128)(2,1)S(1)}, u32[]{:S(2)}, u32[]{:S(2)}) collective-permute-start(bf16[128,256]{1,0:T(8,128)(2,1)S(1)} %get-tuple-element.347.refs_0_), channel_id=1, source_target_pairs={{0,4},{4,0},{8,12},{12,8},{16,20},{20,16},{24,28},{28,24},{1,5},{5... | collective-permute-start | bytes 196616 | tf_op jit(solution)/shard_map/ppermute | solution.py:337
  10.7 6.5 %collective-permute-start.7 = (bf16[128,256]{1,0:T(8,128)(2,1)S(1)}, bf16[128,256]{1,0:T(8,128)(2,1)S(1)}, u32[]{:S(2)}, u32[]{:S(2)}) collective-permute-start(bf16[128,256]{1,0:T(8,128)(2,1)S(1)} %collective-permute-done.3.refs_1_), channel_id=1, source_target_pairs={{0,4},{4,0},{8,12},{12,8},{16,20},{20,16},{24,28},{28,24},{1,5},{5... | collective-permute-start | bytes 196616 | tf_op jit(solution)/shard_map/ppermute | solution.py:337
  16.7 14.8 %collective-permute-start.15 = (bf16[256,512]{1,0:T(8,128)(2,1)S(1)}, bf16[256,512]{1,0:T(8,128)(2,1)S(1)}, u32[]{:S(2)}, u32[]{:S(2)}) collective-permute-start(bf16[256,512]{1,0:T(8,128)(2,1)S(1)} %get-tuple-element.358.refs_2_), channel_id=1, source_target_pairs={{0,4},{4,0},{8,12},{12,8},{16,20},{20,16},{24,28},{28,24},{1,5},{5... | collective-permute-start | bytes 786440 | tf_op jit(solution)/shard_map/ppermute | solution.py:337
  16.7 17.1 %collective-permute-start.16 = (bf16[256,512]{1,0:T(8,128)(2,1)S(1)}, bf16[256,512]{1,0:T(8,128)(2,1)S(1)}, u32[]{:S(2)}, u32[]{:S(2)}) collective-permute-start(bf16[256,512]{1,0:T(8,128)(2,1)S(1)} %get-tuple-element.359.refs_3_), channel_id=1, source_target_pairs={{0,4},{4,0},{8,12},{12,8},{16,20},{20,16},{24,28},{28,24},{1,5},{5... | collective-permute-start | bytes 786440 | tf_op jit(solution)/shard_map/ppermute | solution.py:337
  17.2 17.7 %collective-permute-start.17 = (bf16[256,512]{1,0:T(8,128)(2,1)S(1)}, bf16[256,512]{1,0:T(8,128)(2,1)S(1)}, u32[]{:S(2)}, u32[]{:S(2)}) collective-permute-start(bf16[256,512]{1,0:T(8,128)(2,1)S(1)} %get-tuple-element.358.refs_2_), channel_id=1, source_target_pairs={{0,8},{4,12},{8,0},{12,4},{16,24},{20,28},{24,16},{28,20},{1,9},{5... | collective-permute-start | bytes 786440 | tf_op jit(solution)/shard_map/ppermute | solution.py:337
  24.2 6.8 %collective-permute-start.11 = (bf16[256,256]{1,0:T(8,128)(2,1)S(1)}, bf16[256,256]{1,0:T(8,128)(2,1)S(1)}, u32[]{:S(2)}, u32[]{:S(2)}) collective-permute-start(bf16[256,256]{1,0:T(8,128)(2,1)S(1)} %get-tuple-element.354), channel_id=1, source_target_pairs={{0,24},{4,28},{8,16},{12,20},{16,8},{20,12},{24,0},{28,4},{1,25},{... | collective-permute-start | bytes 393224 | tf_op jit(solution)/shard_map/ppermute | solution.py:337
  31.0 7.9 %collective-permute-start.18 = (bf16[256,512]{1,0:T(8,128)(2,1)S(1)}, bf16[256,512]{1,0:T(8,128)(2,1)S(1)}, u32[]{:S(2)}, u32[]{:S(2)}) collective-permute-start(bf16[256,512]{1,0:T(8,128)(2,1)S(1)} %get-tuple-element.359.refs_3_), channel_id=1, source_target_pairs={{0,8},{4,12},{8,0},{12,4},{16,24},{20,28},{24,16},{28,20},{1,9},{5... | collective-permute-start | bytes 786440 | tf_op jit(solution)/shard_map/ppermute | solution.py:337
  32.2 9.3 %collective-permute-start.21 = (bf16[256,512]{1,0:T(8,128)(2,1)S(1)}, bf16[256,512]{1,0:T(8,128)(2,1)}, u32[]{:S(2)}, u32[]{:S(2)}) collective-permute-start(bf16[256,512]{1,0:T(8,128)(2,1)S(1)} %get-tuple-element.358.refs_2_), channel_id=1, source_target_pairs={{0,16},{4,20},{8,24},{12,28},{16,0},{20,4},{24,8},{28,12},{1,17},{... | collective-permute-start | bytes 786440 | tf_op jit(solution)/shard_map/ppermute | solution.py:337
  34.5 12.7 %collective-permute-start.22 = (bf16[256,512]{1,0:T(8,128)(2,1)S(1)}, bf16[256,512]{1,0:T(8,128)(2,1)}, u32[]{:S(2)}, u32[]{:S(2)}) collective-permute-start(bf16[256,512]{1,0:T(8,128)(2,1)S(1)} %get-tuple-element.359.refs_3_), channel_id=1, source_target_pairs={{0,16},{4,20},{8,24},{12,28},{16,0},{20,4},{24,8},{28,12},{1,17},{... | collective-permute-start | bytes 786440 | tf_op jit(solution)/shard_map/ppermute | solution.py:337
  34.9 13.7 %collective-permute-start.10 = (bf16[512,256]{1,0:T(8,128)(2,1)S(1)}, bf16[512,256]{1,0:T(8,128)(2,1)}, u32[]{:S(2)}, u32[]{:S(2)}) collective-permute-start(bf16[512,256]{1,0:T(8,128)(2,1)S(1)} %get-tuple-element.352.refs_1_), channel_id=1, source_target_pairs={{0,8},{4,20},{8,0},{12,28},{16,24},{20,4},{24,16},{28,12},{1,9},{5... | collective-permute-start | bytes 786440 | tf_op jit(solution)/shard_map/ppermute | solution.py:343
  38.9 14.6 %collective-permute-start.19 = (bf16[256,512]{1,0:T(8,128)(2,1)S(1)}, bf16[256,512]{1,0:T(8,128)(2,1)S(1)}, u32[]{:S(2)}, u32[]{:S(2)}) collective-permute-start(bf16[256,512]{1,0:T(8,128)(2,1)S(1)} %collective-permute-done.17.refs_6_), channel_id=1, source_target_pairs={{0,4},{4,0},{8,12},{12,8},{16,20},{20,16},{24,28},{28,24},{1,5},{5... | collective-permute-start | bytes 786440 | tf_op jit(solution)/shard_map/ppermute | solution.py:337
  41.6 12.5 %collective-permute-start.25 = (bf16[256,512]{1,0:T(8,128)(2,1)S(1)}, bf16[256,512]{1,0:T(8,128)(2,1)}, u32[]{:S(2)}, u32[]{:S(2)}) collective-permute-start(bf16[256,512]{1,0:T(8,128)(2,1)S(1)} %collective-permute-done.17.refs_6_), channel_id=1, source_target_pairs={{0,16},{4,20},{8,24},{12,28},{16,0},{20,4},{24,8},{28,12},{1,17},{... | collective-permute-start | bytes 786440 | tf_op jit(solution)/shard_map/ppermute | solution.py:337
  47.2 7.0 %collective-permute-start.26 = (bf16[256,512]{1,0:T(8,128)(2,1)}, bf16[256,512]{1,0:T(8,128)(2,1)}, u32[]{:S(2)}, u32[]{:S(2)}) collective-permute-start(bf16[256,512]{1,0:T(8,128)(2,1)} %collective-permute-done.22.refs_11_), channel_id=1, source_target_pairs={{0,8},{4,12},{8,0},{12,4},{16,24},{20,28},{24,16},{28,20},{1,9},{5... | collective-permute-start | bytes 786440 | tf_op jit(solution)/shard_map/ppermute | solution.py:337
  48.7 7.4 %collective-permute-start.20 = (bf16[256,512]{1,0:T(8,128)(2,1)S(1)}, bf16[256,512]{1,0:T(8,128)(2,1)S(1)}, u32[]{:S(2)}, u32[]{:S(2)}) collective-permute-start(bf16[256,512]{1,0:T(8,128)(2,1)S(1)} %collective-permute-done.18.refs_7_), channel_id=1, source_target_pairs={{0,4},{4,0},{8,12},{12,8},{16,20},{20,16},{24,28},{28,24},{1,5},{5... | collective-permute-start | bytes 786440 | tf_op jit(solution)/shard_map/ppermute | solution.py:337
  49.8 7.1 %collective-permute-start.23 = (bf16[256,512]{1,0:T(8,128)(2,1)}, bf16[256,512]{1,0:T(8,128)(2,1)}, u32[]{:S(2)}, u32[]{:S(2)}) collective-permute-start(bf16[256,512]{1,0:T(8,128)(2,1)} %collective-permute-done.21.refs_10_), channel_id=1, source_target_pairs={{0,4},{4,0},{8,12},{12,8},{16,20},{20,16},{24,28},{28,24},{1,5},{5... | collective-permute-start | bytes 786440 | tf_op jit(solution)/shard_map/ppermute | solution.py:337
  54.0 6.5 %collective-permute-start.27 = (bf16[256,512]{1,0:T(8,128)(2,1)}, bf16[256,512]{1,0:T(8,128)(2,1)}, u32[]{:S(2)}, u32[]{:S(2)}) collective-permute-start(bf16[256,512]{1,0:T(8,128)(2,1)} %collective-permute-done.25.refs_14_), channel_id=1, source_target_pairs={{0,4},{4,0},{8,12},{12,8},{16,20},{20,16},{24,28},{28,24},{1,5},{5... | collective-permute-start | bytes 786440 | tf_op jit(solution)/shard_map/ppermute | solution.py:337
  54.1 6.4 %collective-permute-start.28 = (bf16[256,512]{1,0:T(8,128)(2,1)}, bf16[256,512]{1,0:T(8,128)(2,1)}, u32[]{:S(2)}, u32[]{:S(2)}) collective-permute-start(bf16[256,512]{1,0:T(8,128)(2,1)} %collective-permute-done.26.refs_15_), channel_id=1, source_target_pairs={{0,4},{4,0},{8,12},{12,8},{16,20},{20,16},{24,28},{28,24},{1,5},{5... | collective-permute-start | bytes 786440 | tf_op jit(solution)/shard_map/ppermute | solution.py:337
  56.8 14.9 %collective-permute-start.13 = (bf16[512,256]{1,0:T(8,128)(2,1)}, bf16[512,256]{1,0:T(8,128)(2,1)}, u32[]{:S(2)}, u32[]{:S(2)}) collective-permute-start(bf16[512,256]{1,0:T(8,128)(2,1)} %collective-permute-done.10.refs_2_), channel_id=1, source_target_pairs={{0,4},{4,0},{8,12},{12,8},{16,20},{20,16},{24,28},{28,24},{1,5},{5... | collective-permute-start | bytes 786440 | tf_op jit(solution)/shard_map/ppermute | solution.py:337
  56.9 14.8 %collective-permute-start.14 = (bf16[256,256]{1,0:T(8,128)(2,1)S(1)}, bf16[256,256]{1,0:T(8,128)(2,1)S(1)}, u32[]{:S(2)}, u32[]{:S(2)}) collective-permute-start(bf16[256,256]{1,0:T(8,128)(2,1)S(1)} %collective-permute-done.11.refs_4_), channel_id=1, source_target_pairs={{0,4},{4,0},{8,12},{12,8},{16,20},{20,16},{24,28},{28,24},{1,5},{5... | collective-permute-start | bytes 393224 | tf_op jit(solution)/shard_map/ppermute | solution.py:337
  58.3 26.9 %collective-permute-start.31 = (bf16[512,256]{1,0:T(8,128)(2,1)S(1)}, bf16[512,256]{1,0:T(8,128)(2,1)S(1)}, u32[]{:S(2)}, u32[]{:S(2)}) collective-permute-start(bf16[512,256]{1,0:T(8,128)(2,1)S(1)} %constant_dynamic-slice_fusion.4), channel_id=1, source_target_pairs={{0,2},{1,3},{2,0},{3,1},{4,6},{5,7},{6,4},{7,5},{8,10},{9,11},{10,... | collective-permute-start | bytes 786440 | tf_op jit(solution)/shard_map/ppermute | solution.py:340
  74.9 10.3 %collective-permute-start.29 = (bf16[512,256]{1,0:T(8,128)(2,1)S(1)}, bf16[512,256]{1,0:T(8,128)(2,1)}, u32[]{:S(2)}, u32[]{:S(2)}) collective-permute-start(bf16[512,256]{1,0:T(8,128)(2,1)S(1)} %get-tuple-element.365.refs_1_), channel_id=1, source_target_pairs={{0,8},{4,20},{8,0},{12,28},{16,24},{20,4},{24,16},{28,12},{1,9},{5... | collective-permute-start | bytes 786440 | tf_op jit(solution)/shard_map/ppermute | solution.py:343
  76.5 8.7 %collective-permute-start.30 = (bf16[256,256]{1,0:T(8,128)(2,1)S(1)}, bf16[256,256]{1,0:T(8,128)(2,1)S(1)}, u32[]{:S(2)}, u32[]{:S(2)}) collective-permute-start(bf16[256,256]{1,0:T(8,128)(2,1)S(1)} %get-tuple-element.367), channel_id=1, source_target_pairs={{0,24},{4,28},{8,16},{12,20},{16,8},{20,12},{24,0},{28,4},{1,25},{... | collective-permute-start | bytes 393224 | tf_op jit(solution)/shard_map/ppermute | solution.py:337
  87.5 21.1 %collective-permute-start.36 = (bf16[512,256]{1,0:T(8,128)(2,1)S(1)}, bf16[512,256]{1,0:T(8,128)(2,1)S(1)}, u32[]{:S(2)}, u32[]{:S(2)}) collective-permute-start(bf16[512,256]{1,0:T(8,128)(2,1)S(1)} %constant_dynamic-slice_fusion.2), channel_id=1, source_target_pairs={{0,3},{1,2},{2,1},{3,0},{4,7},{5,6},{6,5},{7,4},{8,11},{9,10},{10,... | collective-permute-start | bytes 786440 | tf_op jit(solution)/shard_map/ppermute | solution.py:340
  98.2 10.4 %collective-permute-start.34 = (bf16[512,256]{1,0:T(8,128)(2,1)S(1)}, bf16[512,256]{1,0:T(8,128)(2,1)}, u32[]{:S(2)}, u32[]{:S(2)}) collective-permute-start(bf16[512,256]{1,0:T(8,128)(2,1)S(1)} %get-tuple-element.378.refs_1_), channel_id=1, source_target_pairs={{0,8},{4,20},{8,0},{12,28},{16,24},{20,4},{24,16},{28,12},{1,9},{5... | collective-permute-start | bytes 786440 | tf_op jit(solution)/shard_map/ppermute | solution.py:343
  99.7 8.8 %collective-permute-start.35 = (bf16[256,256]{1,0:T(8,128)(2,1)S(1)}, bf16[256,256]{1,0:T(8,128)(2,1)S(1)}, u32[]{:S(2)}, u32[]{:S(2)}) collective-permute-start(bf16[256,256]{1,0:T(8,128)(2,1)S(1)} %get-tuple-element.380), channel_id=1, source_target_pairs={{0,24},{4,28},{8,16},{12,20},{16,8},{20,12},{24,0},{28,4},{1,25},{... | collective-permute-start | bytes 393224 | tf_op jit(solution)/shard_map/ppermute | solution.py:337
  111.5 18.6 %collective-permute-start.41 = (bf16[512,256]{1,0:T(8,128)(2,1)S(1)}, bf16[512,256]{1,0:T(8,128)(2,1)}, u32[]{:S(2)}, u32[]{:S(2)}) collective-permute-start(bf16[512,256]{1,0:T(8,128)(2,1)S(1)} %get-tuple-element.438), channel_id=1, source_target_pairs={{0,1},{1,0},{2,3},{3,2},{4,5},{5,4},{6,7},{7,6},{8,9},{9,8},{10,11... | collective-permute-start | bytes 786440 | tf_op jit(solution)/shard_map/ppermute | solution.py:340
  119.5 10.7 %collective-permute-start.39 = (bf16[512,256]{1,0:T(8,128)(2,1)S(1)}, bf16[512,256]{1,0:T(8,128)(2,1)S(1)}, u32[]{:S(2)}, u32[]{:S(2)}) collective-permute-start(bf16[512,256]{1,0:T(8,128)(2,1)S(1)} %get-tuple-element.392.refs_1_), channel_id=1, source_target_pairs={{0,8},{4,20},{8,0},{12,28},{16,24},{20,4},{24,16},{28,12},{1,9},{5... | collective-permute-start | bytes 786440 | tf_op jit(solution)/shard_map/ppermute | solution.py:343
  120.9 9.2 %collective-permute-start.40 = (bf16[256,256]{1,0:T(8,128)(2,1)S(1)}, bf16[256,256]{1,0:T(8,128)(2,1)S(1)}, u32[]{:S(2)}, u32[]{:S(2)}) collective-permute-start(bf16[256,256]{1,0:T(8,128)(2,1)S(1)} %get-tuple-element.393), channel_id=1, source_target_pairs={{0,24},{4,28},{8,16},{12,20},{16,8},{20,12},{24,0},{28,4},{1,25},{... | collective-permute-start | bytes 393224 | tf_op jit(solution)/shard_map/ppermute | solution.py:337
  (96 other events, 702.3 us)

commit v4 on v3

--- a/solution.py
+++ b/solution.py
@@ -91,9 +91,8 @@
 SRC, LSRC, PACK, TABLE = 0, 64, 96, 128
 
 
-def first_kernel(owner, order, pattern, rhs_ref, win_ref, l0, l1, r0, r1, r2, r3, buf, pat, inv, pos, sem):
-    row, depth = lax.axis_index("rows"), lax.axis_index("rhs")
-    width = r0.shape[1]
+def factor_kernel(owner, order, pattern, win_ref, out, buf, pat, inv, pos, sem):
+    row = lax.axis_index("rows")
 
     def note_slot(w, carry):
         slot = owner[w]
@@ -104,7 +103,7 @@
 
         return carry
 
-    lax.fori_loop(0, NWB, note_slot, 0)
+    lax.fori_loop(0, NWB, note_slot, 0, unroll=8)
     for k in range(NSUP):
         pos[order[k]] = k
     labels = jnp.zeros((SB, 1), jnp.int32)
@@ -112,14 +111,20 @@
         label = order[(pos[inv[t] // SB] // 2) * 2]
         pltpu.make_async_copy(win_ref.at[pl.ds(t * BS, BS), columns_at(label)], buf.at[pl.ds(t * BS, BS), :], sem).start()
         labels = jnp.where(lax.broadcasted_iota(jnp.int32, (SB, 1), 0) == t, label, labels)
-    for s, r in enumerate((r0, r1, r2, r3)):
-        at = pl.multiple_of(jnp.bitwise_xor(depth, s) * width, width)
-        r[...] = rhs_ref[:, pl.ds(at, width)]
     pat[...] = pattern[pl.ds(pl.multiple_of(row * SB, SB), SB), :]
     mask = expand_mask(pat[...], labels, spread_matrix())
     pltpu.make_async_copy(win_ref.at[:, pl.ds(0, SN)], buf, sem).wait()
-    l0[...] = masked_rows(lambda j: buf[j * BS:(j + 1) * BS, :], mask[0:4], 4)
-    l1[...] = masked_rows(lambda j: buf[(j + 4) * BS:(j + 5) * BS, :], mask[4:8], 4)
+    for j in range(SB):
+        out[j * BS:(j + 1) * BS, :] = buf[j * BS:(j + 1) * BS, :] * mask[j:j + 1, :]
+
+
+def rhs_kernel(own_ref, other_ref, *sent):
+    depth = lax.axis_index("rhs")
+    tall, width = own_ref.shape[0], sent[0].shape[1]
+    for s, out in enumerate(sent):
+        at = pl.multiple_of(jnp.bitwise_xor(depth, s) * width, width)
+        out[0:tall, :] = own_ref[:, pl.ds(at, width)]
+        out[tall:2 * tall, :] = other_ref[:, pl.ds(at, width)]
 
 
 def table_kernel(owner, order, tab, flag, cnt):
@@ -151,24 +156,37 @@
 
             @pl.when(i >= SB)
             def _():
-                tab[LSRC + group * SB + i - SB] = jnp.bitwise_xor(device, row) * SB + slot % SB
+                kind = jnp.where(rel == 0, 0, jnp.where(diagonal, 3, jnp.where(rel == 1 + core, 1, 2)))
+                tab[LSRC + group * SB + i - SB] = (2 * kind + jnp.where(device % 2 == core, 0, 1)) * SB + slot % SB
 
             return carry
 
-        lax.fori_loop(0, 2 * SB, one, 0)
+        lax.fori_loop(0, 2 * SB, one, 0, unroll=True)
+
+
+def below_rhs_kernel(rhs_ref, *refs):
+    outs, sems = refs[:-1], refs[-1]
+    depth = lax.axis_index("rhs")
+    width = outs[0].shape[1]
+    copies = []
+    for s, out in enumerate(outs):
+        at = pl.multiple_of(jnp.bitwise_xor(depth, s) * width, width)
+        copies.append(pltpu.make_async_copy(rhs_ref.at[:, pl.ds(at, width)], out, sems.at[s]))
+        copies[-1].start()
+    for c in copies:
+        c.wait()
 
 
 def first_pack_kernel(tab, *refs):
-    pieces, (chip_rhs, p_ref, b_ref) = refs[:8], refs[8:]
+    pieces, (chip_rhs, p_ref, b_ref) = refs[:4], refs[4:]
     depth, core = lax.axis_index("rhs"), lax.axis_index("rows") % 2
-    tall = pieces[0].shape[0]
-    for side in range(2):
-        for s in range(4):
+    tall = pieces[0].shape[0] // 2
+    for s in range(4):
+        for side in range(2):
             at = pl.multiple_of(side * SB * BS + jnp.bitwise_xor(depth, s) * tall, tall)
-            chip_rhs[pl.ds(at, tall), :] = pieces[side * 4 + s][...]
+            chip_rhs[pl.ds(at, tall), :] = pieces[s][side * tall:(side + 1) * tall, :]
     for j in range(SB):
-        block = chip_rhs[rows_at(tab[PACK + j]), :]
-        p_ref[j * BS:(j + 1) * BS, :] = block
+        p_ref[j * BS:(j + 1) * BS, :] = chip_rhs[rows_at(tab[PACK + j]), :]
     b_ref[...] = p_ref[pl.ds(pl.multiple_of(core * SB // 2 * BS, SB // 2 * BS), SB // 2 * BS), :]
 
 
@@ -199,8 +217,8 @@
 
     def kernel(*refs):
         tab, order = refs[:2]
-        l_refs, diag_ref = refs[2:18], refs[18]
-        refs = refs[19:]
+        l_refs, diag_ref = refs[2:10], refs[10]
+        refs = refs[11:]
         if last:
             d_out, l_out, dsem, lsem = refs
         else:
@@ -214,10 +232,7 @@
             for m in range(8):
                 @pl.when(code // SB == m)
                 def _(m=m, i=i, code=code):
-                    for half in range(2):
-                        @pl.when((code % SB) // 4 == half)
-                        def _(half=half):
-                            pltpu.make_async_copy(l_refs[2 * m + half].at[rows_at(code % 4), :], l_out.at[pl.ds(i * BS, BS), :], lsem).start()
+                    pltpu.make_async_copy(l_refs[m].at[rows_at(code % SB), :], l_out.at[pl.ds(i * BS, BS), :], lsem).start()
         if not last:
             total = jnp.concatenate([chip_rhs[rows_at(tab[PACK + (group + 1) * SB + j]), :] for j in range(SB)], axis=0).astype(F32)
             for k in range(group):
@@ -264,50 +279,67 @@
     return kernel
 
 
-def pair_product(a0, a1, pattern, x_ref, order, group):
-    spread = spread_matrix()
-    rows = pattern[...]
-    total = None
-    for q, a_ref in enumerate((a0, a1)):
-        mask = expand_mask(rows, order[2 * group + q], spread)
-        part = masked_rows(lambda j: a_ref[j * BS:(j + 1) * BS, :], mask, a_ref.shape[0] // BS)
-        term = jnp.dot(part, x_ref[q * SN:(q + 1) * SN, :], preferred_element_type=F32)
-        total = term if total is None else total + term
-    return total
-
-
-def make_rows_kernel(group):
-    def kernel(order, a0, a1, pattern, x_ref, *refs):
-        total = pair_product(a0, a1, pattern, x_ref, order, group)
-        refs[-1][...] = total if group == 0 else refs[0][...] + total
+def make_below_mask_kernel(group):
+    def kernel(order, pattern, a_ref, out, sems):
+        tiles = sems.shape[0]
+        tall = out.shape[0] // tiles
+        copies = []
+        for i in range(tiles):
+            for q in range(2):
+                c = pltpu.make_async_copy(a_ref.at[pl.ds(i * tall, tall), columns_at(order[2 * group + q])],
+                                          out.at[pl.ds(i * tall, tall), pl.ds(q * SN, SN)], sems.at[i, q])
+                c.start()
+                copies.append(c)
+        spread = spread_matrix()
+        rows = pattern[...]
+        masks = [expand_mask(rows, order[2 * group + q], spread) for q in range(2)]
+        for i in range(tiles):
+            for q in range(2):
+                copies[2 * i + q].wait()
+                for j in range(i * tall // BS, (i + 1) * tall // BS):
+                    at = (slice(j * BS, (j + 1) * BS), slice(q * SN, (q + 1) * SN))
+                    out[at] = out[at] * masks[q][j:j + 1, :]
 
     return kernel
 
 
-def last_rows_kernel(order, a0, a1, pattern, x0, x1, x2, x3, sums, h0, h1, h2, h3, sol_ref, out_ref, sems):
-    step = pl.program_id(0)
+def first_rows_kernel(a_ref, x_ref, out):
+    out[...] = jnp.dot(a_ref[...], x_ref[...], preferred_element_type=F32)
+
+
+def next_rows_kernel(a_ref, x_ref, sums, out):
+    out[...] = sums[...] + jnp.dot(a_ref[...], x_ref[...], preferred_element_type=F32)
+
+
+def base_rows_kernel(a_ref, x_ref, sums, h0, h1, h2, h3, out):
+    depth = lax.axis_index("rhs")
+    tall = h0.shape[0]
+    for s, h in enumerate((h0, h1, h2, h3)):
+        at = pl.ds(pl.multiple_of(jnp.bitwise_xor(depth, s) * tall, tall), tall)
+        part = jnp.dot(a_ref[at, :], x_ref[...], preferred_element_type=F32)
+        out[at, :] = h[...].astype(F32) - (sums[at, :] + part)
+
+
+def last_rows_kernel(order, a_ref, x0, x1, x2, x3, base, sol_ref, out_ref, done, sems, osem):
     copies = []
     for k, x in enumerate((x0, x1, x2, x3)):
         for q in range(2):
             at = pl.multiple_of(order[2 * k + q] * SN, SN)
             copies.append(pltpu.make_async_copy(x.at[pl.ds(q * SN, SN), :], sol_ref.at[pl.ds(at, SN), :], sems.at[2 * k + q]))
-
-    @pl.when(step == 0)
-    def _():
-        for c in copies:
-            c.start()
-
-    total = sums[...] + pair_product(a0, a1, pattern, x3, order, GROUPS - 1)
-    which = jnp.bitwise_xor(lax.axis_index("rhs"), step)
-    for s, h in enumerate((h0, h1, h2, h3)):
-        @pl.when(which == s)
-        def _(h=h):
-            out_ref[...] = (h[...].astype(F32) - total).astype(BF16)
-
-    @pl.when(step == pl.num_programs(0) - 1)
-    def _():
-        for c in copies:
-            c.wait()
+            copies[-1].start()
+    tiles = osem.shape[0]
+    tall = done.shape[0] // tiles
+    for i in range(tiles):
+        at = slice(i * tall, (i + 1) * tall)
+        done[at, :] = (base[at, :] - jnp.dot(a_ref[at, :], x3[...], preferred_element_type=F32)).astype(BF16)
+        copies.append(pltpu.make_async_copy(done.at[pl.ds(i * tall, tall), :], out_ref.at[pl.ds(i * tall, tall), :], osem.at[i]))
+        copies[-1].start()
+    for c in copies:
+        c.wait()
+
+
+def in_hbm(x):
+    return pltpu.with_memory_space_constraint(x, pltpu.HBM)
 
 
 SMEM = pl.BlockSpec(memory_space=pltpu.SMEM)
@@ -342,27 +374,37 @@
     def neighbour(x):
         return lax.ppermute(x, "rows", [(i, i ^ (2 if i % 2 == 0 else 4)) for i in range(8)])
 
+    def forward(x):
+        return lax.ppermute(x, "rows", [(i, i ^ (4 if i % 2 == 0 else 2)) for i in range(8)])
+
     columns = rhs_win.shape[1] // 4
     half = SN // 2
-    w_other = swap(win_rows, 1)
     tall = rhs_win.shape[0]
-    l_low, l_high, *sent = pl.pallas_call(
-        first_kernel,
-        out_shape=(shape_of((half, SN)), shape_of((half, SN))) + (shape_of((tall, columns)),) * 4,
-        in_specs=[SMEM, SMEM, VMEM, VMEM, HBM],
-        out_specs=(VMEM,) * 6,
+    rhs_other = swap(rhs_win, 1)
+    w_own = in_hbm(win_rows)
+    l_own = pl.pallas_call(
+        factor_kernel,
+        out_shape=shape_of((SN, SN)),
+        in_specs=[SMEM, SMEM, VMEM, HBM],
+        out_specs=VMEM,
         scratch_shapes=[pltpu.VMEM((SN, SN), BF16), pltpu.VMEM((SB, NWB), jnp.int32),
                         pltpu.SMEM((SB,), jnp.int32), pltpu.SMEM((SB,), jnp.int32), pltpu.SemaphoreType.DMA],
-        compiler_params=params(8),
+        compiler_params=params(4),
         cost_estimate=cost(2),
-        name="first",
-    )(window_owner, sn_order, win_pattern, rhs_win, win_rows)
-    low, high = {0: l_low}, {0: l_high}
-    for m in (2, 4):
-        low[m] = swap(l_low, m)
+        name="factor_pack",
+    )(window_owner, sn_order, win_pattern, w_own)
+    near = neighbour(l_own)
+    sent = pl.pallas_call(
+        rhs_kernel,
+        out_shape=(shape_of((2 * tall, columns)),) * 4,
+        in_specs=[VMEM] * 2,
+        out_specs=(VMEM,) * 4,
+        compiler_params=params(4),
+        cost_estimate=cost(1),
+        name="rhs_pack",
+    )(rhs_win, rhs_other)
     pieces = [sent[0]] + [deep(sent[s], s) for s in (1, 2, 3)]
-    for m in (2, 4):
-        high[m] = swap(l_high, m)
+    owner_later, _ = lax.optimization_barrier((window_owner, l_own))
     tab, flag = pl.pallas_call(
         table_kernel,
         out_shape=(shape_of((TABLE,), jnp.int32), shape_of((1,), jnp.int32)),
@@ -370,37 +412,50 @@
         out_specs=(SMEM, SMEM),
         scratch_shapes=[pltpu.SMEM((4,), jnp.int32)],
         compiler_params=params(4),
-        cost_estimate=cost(2),
+        cost_estimate=cost(3),
         name="tables",
-    )(window_owner, sn_order)
-    others = [swap(x, 1) for x in pieces]
+    )(owner_later, sn_order)
     chip_rhs, packed, part = pl.pallas_call(
         first_pack_kernel,
         out_shape=(shape_of((PAIR, columns)), shape_of((SN, columns)), shape_of((half, columns))),
-        in_specs=[SMEM] + [VMEM] * 8,
+        in_specs=[SMEM] + [VMEM] * 4,
         out_specs=(VMEM,) * 3,
-        compiler_params=params(6),
+        compiler_params=params(4),
         cost_estimate=cost(1),
         name="first_pack",
-    )(tab, *pieces, *others)
-    low[6], high[6] = swap(low[2], 4), swap(high[4], 2)
-    for m in (0, 2, 4, 6):
-        low[m + 1] = swap(low[m], 1)
-        high[m + 1] = swap(high[m], 1)
-    l_parts = [x for m in range(8) for x in (low[m], high[m])]
+    )(tab, *pieces)
+    l_other = swap(l_own, 1)
+    near_other = neighbour(l_other)
+    far = forward(near)
+    l_parts = [in_hbm(x) for x in (l_own, l_other, near, near_other, swap(near_other, 1), swap(near, 1), far, swap(far, 1))]
+    w_other = in_hbm(swap(win_rows, 1))
 
     depth = lax.axis_index("rhs")
     tile = rhs_anc.shape[0]
-    sums, solved, masked = None, [], []
+    sums, solved, masked, below = None, [], [], []
+    anc_hbm = in_hbm(anc_rows)
+    diag_hbm = in_hbm(diag_inv)
+    below_rows = anc_rows.shape[0]
+
+    def mask_below(k, order):
+        below.append(pl.pallas_call(
+            make_below_mask_kernel(k),
+            out_shape=shape_of((below_rows, PAIR)),
+            in_specs=[SMEM, VMEM, HBM],
+            out_specs=VMEM,
+            scratch_shapes=[pltpu.SemaphoreType.DMA((4, 2))],
+            compiler_params=params(4),
+            cost_estimate=cost(3),
+            name="mask_below",
+        )(order, anc_pattern, anc_hbm))
+
     anc_order, anc_pieces = (2, 3, 1), [None] * 4
-    tab_later, rhs_later = tab, rhs_anc
     for group in range(GROUPS):
         last = group == GROUPS - 1
         a_own = neighbour(packed)
         b_own = swap(part, 6)
-        hold = [a_own, b_own]
         if group == 0:
-            tab_later, _ = lax.optimization_barrier((tab, packed))
+            tab_later, order_later, _ = lax.optimization_barrier((tab, sn_order, packed))
             for k in range(GROUPS - 1):
                 masked.append(pl.pallas_call(
                     make_mask_kernel(k),
@@ -408,20 +463,31 @@
                     in_specs=[SMEM, SMEM, VMEM, HBM, HBM],
                     out_specs=VMEM,
                     scratch_shapes=[pltpu.VMEM((SN, NW), BF16), pltpu.VMEM((SB, NWB), jnp.int32), pltpu.SemaphoreType.DMA],
-                    compiler_params=params(10),
-                    cost_estimate=cost(3),
+                    compiler_params=params(6),
+                    cost_estimate=cost(2),
                     name="mask_rows",
-                )(tab_later, sn_order, win_pattern, win_rows, w_other))
-            hold += masked
+                )(tab_later, order_later, win_pattern, w_own, w_other))
+            mask_below(0, order_later)
+            mask_below(1, order_later)
+        if group == 0:
+            rhs_later, _ = lax.optimization_barrier((rhs_anc, packed))
+            anc_pieces = list(pl.pallas_call(
+                below_rhs_kernel,
+                out_shape=(shape_of((tile, columns)),) * 4,
+                in_specs=[HBM],
+                out_specs=(VMEM,) * 4,
+                scratch_shapes=[pltpu.SemaphoreType.DMA((4,))],
+                compiler_params=params(4),
+                cost_estimate=cost(1),
+                name="below_rhs",
+            )(in_hbm(rhs_later)))
         if not last:
-            rhs_later, _ = lax.optimization_barrier((rhs_later, packed))
             s = anc_order[group]
-            anc_pieces[s] = deep(lax.dynamic_slice_in_dim(rhs_later, (depth ^ s) * columns, columns, 1), s)
-            if group == 2:
-                anc_pieces[0] = lax.dynamic_slice_in_dim(rhs_later, depth * columns, columns, 1)
-
-        operands = [tab, sn_order, *l_parts, diag_inv]
-        in_specs = [SMEM, SMEM] + [HBM] * 17
+            moved, _ = lax.optimization_barrier((anc_pieces[s], packed))
+            anc_pieces[s] = deep(moved, s)
+
+        operands = [tab, sn_order, *l_parts, diag_hbm]
+        in_specs = [SMEM, SMEM] + [HBM] * 9
         out_shape = [shape_of((2, SN, SN)), shape_of((SN, SN))]
         if not last:
             operands += [masked[group], chip_rhs, *solved]
@@ -439,30 +505,30 @@
         )(*operands)
         if group > 0:
             k = group - 1
-            more = [] if k == 0 else [sums]
+            previous = anc_pieces[anc_order[k]]
+            if k < 2:
+                more, kernel = ([], first_rows_kernel) if k == 0 else ([sums], next_rows_kernel)
+            else:
+                more, kernel = [sums, *anc_pieces], base_rows_kernel
             sums = pl.pallas_call(
-                make_rows_kernel(k),
-                out_shape=shape_of((anc_rows.shape[0], columns), F32),
-                grid_spec=pltpu.PrefetchScalarGridSpec(
-                    num_scalar_prefetch=1,
-                    grid=(anc_rows.shape[0] // (2 * tile),),
-                    in_specs=[pl.BlockSpec((2 * tile, SN), lambda i, o, k=k: (i, o[2 * k])),
-                              pl.BlockSpec((2 * tile, SN), lambda i, o, k=k: (i, o[2 * k + 1])),
-                              pl.BlockSpec((2 * SB, NWB), lambda i, o: (i, 0)),
-                              pl.BlockSpec((PAIR, columns), lambda i, o: (0, 0))]
-                    + [pl.BlockSpec((2 * tile, columns), lambda i, o: (i, 0))] * len(more),
-                    out_specs=pl.BlockSpec((2 * tile, columns), lambda i, o: (i, 0)),
-                ),
-                input_output_aliases={5: 0} if more else {},
-                compiler_params=params(14),
-                cost_estimate=cost(5),
+                kernel,
+                out_shape=shape_of((below_rows, columns), F32),
+                in_specs=[VMEM] * (2 + len(more)),
+                out_specs=VMEM,
+                input_output_aliases={2: 0} if more else {},
+                compiler_params=params(6),
+                cost_estimate=cost(3),
                 name="rows_below",
-            )(sn_order, anc_rows, anc_rows, anc_pattern, solved[k], *more)
-            previous = anc_pieces[anc_order[k]]
-            a_own, b_own, sums, previous, *ready = lax.optimization_barrier((a_own, b_own, sums, previous, *ready))
+            )(below[k], solved[k], *more)
+            if k < 2:
+                order_later, _ = lax.optimization_barrier((sn_order, packed))
+                mask_below(k + 2, order_later)
+            a_own, b_own, sums, below[-1], previous, *ready = lax.optimization_barrier(
+                (a_own, b_own, sums, below[-1], previous, *ready))
             anc_pieces[anc_order[k]] = previous
         else:
-            a_own, b_own, *masked = lax.optimization_barrier((a_own, b_own, *masked))
+            a_own, b_own, masked[0], masked[1], masked[2], below[0], below[1] = lax.optimization_barrier(
+                (a_own, b_own, *masked, *below))
         a_swap = swap(a_own, 1)
         b_swap = swap(b_own, 1)
         ready = list(ready) if last else list(ready) + [masked[group]]
@@ -485,30 +551,21 @@
             packed, part = results[1:]
 
     def packed_path(*xs):
-        k = GROUPS - 1
-        whole = [pl.BlockSpec((PAIR, columns), lambda i, o: (0, 0))] * 4
         return pl.pallas_call(
             last_rows_kernel,
-            out_shape=(shape_of((NW, columns)), shape_of((anc_rows.shape[0], columns))),
-            grid_spec=pltpu.PrefetchScalarGridSpec(
-                num_scalar_prefetch=1,
-                grid=(anc_rows.shape[0] // tile,),
-                in_specs=[pl.BlockSpec((tile, SN), lambda i, o: (i, o[2 * k])),
-                          pl.BlockSpec((tile, SN), lambda i, o: (i, o[2 * k + 1])),
-                          pl.BlockSpec((SB, NWB), lambda i, o: (i, 0))] + whole
-                + [pl.BlockSpec((tile, columns), lambda i, o: (i, 0))]
-                + [pl.BlockSpec((tile, columns), lambda i, o: (0, 0))] * 4,
-                out_specs=(HBM, pl.BlockSpec((tile, columns), lambda i, o: (i, 0))),
-                scratch_shapes=[pltpu.SemaphoreType.DMA((2 * GROUPS,))],
-            ),
-            compiler_params=params(20),
-            cost_estimate=cost(6),
+            out_shape=(shape_of((NW, columns)), shape_of((below_rows, columns))),
+            in_specs=[SMEM] + [VMEM] * 6,
+            out_specs=(HBM, HBM),
+            scratch_shapes=[pltpu.VMEM((below_rows, columns), BF16), pltpu.SemaphoreType.DMA((2 * GROUPS,)),
+                            pltpu.SemaphoreType.DMA((4,))],
+            compiler_params=params(16),
+            cost_estimate=cost(3),
             name="last_rows",
-        )(sn_order, anc_rows, anc_rows, anc_pattern, *xs, sums, *anc_pieces)
+        )(sn_order, below[-1], *xs, sums)
 
     def other_path(*xs):
         back = depth ^ jnp.arange(4)
-        win_rhs = jnp.take(jnp.stack(pieces), back, axis=0).reshape(4 * tall, columns)
+        win_rhs = jnp.take(jnp.stack([x[:tall] for x in pieces]), back, axis=0).reshape(4 * tall, columns)
         anc_rhs = jnp.take(jnp.stack(anc_pieces), back, axis=0).reshape(4 * tile, columns)
         return general_path(win_rows, anc_rows, win_pattern, anc_pattern, window_owner, sn_order, diag_inv, win_rhs, anc_rhs)
 

time: 144 us -> 113 us (0.78)
  local copies, waits for them, and re-layouts: 30.1 us -> 1.1 us
  waiting for transfers between devices: 20.2 us -> 16 us
  Pallas kernels: 56.6 us -> 60.5 us
    unnamed x174 -> x44, local copies, waits for them, and re-layouts: 26.3 us -> 1.1 us
    ppermute x31 -> x18, starting transfers between devices: 18.3 us -> 7.74 us  [swap(): return lax.ppermute(x, 'rows', [(i, i ^ m) for i in range(8)])]
    pallas_call x3, Pallas kernels: 4.09 us -> 9.67 us  [local(): pl.pallas_call(make_mask_kernel(k), out_shape=shape_of((SN, (k + 1) * PAI...]
    ppermute x4 -> x6, starting transfers between devices: 6.07 us -> 11.3 us  [neighbour(): lax.ppermute(x, 'rows', [(i, i ^ (2 if i % 2 == 0 else 4)) for i in range...]
    ppermute x31 -> x18, waiting for transfers between devices: 14.5 us -> 9.33 us  [swap(): return lax.ppermute(x, 'rows', [(i, i ^ m) for i in range(8)])]
    dynamic_slice x3 -> x0, local copies, waits for them, and re-layouts: 3.75 us -> none  [local(): lax.dynamic_slice_in_dim(rhs_later, (depth ^ s) * columns, columns, 1)]
    pallas_call x4 -> x10, Pallas kernels: 19.2 us -> 21.9 us  [the longest x4 14.1 us: mask_below(): pl.pallas_call(make_below_mask_kernel(k), out_shape=shape_of((below_rows,...]
    ppermute x6, starting transfers between devices: 9.04 us -> 11.6 us  [deep(): return lax.ppermute(x, 'rhs', [(i, i ^ m) for i in range(4)])]
  transfers between devices with their start and end apart: 41 -> 31, of which waited for: 8 -> 9; matrix products, arithmetic and copies ran while one was open for 3% -> 0% of each run, Pallas kernels for 32% -> 46%
where the time goes in v4:
time: 113 us; the launch traced here: 112 us
  Pallas kernels  60.5 us (54%)
  starting transfers between devices  32.7 us (29%)
  waiting for transfers between devices  16 us (14%)
  between operations  1.98 us (2%)
    pallas_call x4, Pallas kernels, mask_below(): pl.pallas_call(make_below_mask_kernel(k), out_shape=shape_of((below_rows,...  14.1 us
    ppermute x6, starting transfers between devices, deep(): return lax.ppermute(x, 'rhs', [(i, i ^ m) for i in range(4)])  11.6 us
    ppermute x6, starting transfers between devices, neighbour(): lax.ppermute(x, 'rows', [(i, i ^ (2 if i % 2 == 0 else 4)) for i in range...  11.3 us
    pallas_call x4, Pallas kernels, local(): pl.pallas_call(make_solve_kernel(group), out_shape=tuple(out_shape), in_s...  10.5 us
    pallas_call x3, Pallas kernels, local(): pl.pallas_call(make_mask_kernel(k), out_shape=shape_of((SN, (k + 1) * PAI...  9.67 us
    ppermute x18, waiting for transfers between devices, swap(): return lax.ppermute(x, 'rows', [(i, i ^ m) for i in range(8)])  9.33 us
    pallas_call x4, Pallas kernels, local(): pl.pallas_call(make_prep_kernel(group), out_shape=tuple(out_shape), in_sp...  9.18 us
    ppermute x18, starting transfers between devices, swap(): return lax.ppermute(x, 'rows', [(i, i ^ m) for i in range(8)])  7.74 us
  transfers between devices with their start and end apart: 31, of which 9 were waited for; matrix products, arithmetic and copies ran while one was open for 0% of the time, Pallas kernels for 46%

profile of v4, /device:TPU:0, one launch (start us, length us, event | category | flops | bytes accessed | tf_op | source)
XLA Modules:
  0.0 112.3 jit_solution(18391172422449141974)
XLA Ops:
  1.2 2.4 %factor_pack.1.refs_2_ = bf16[512,512]{1,0:T(8,128)(2,1)S(1)} custom-call(s32[64]{0:T(128)} %owner.2, s32[8]{0:T(128)} %refs_1_.7, s32[64,64]{1,0:T(8,128)} %pattern.11, bf16[512,4096]{1,0:T(8,128)(2,1)} %w_own.5), custom_call_target="tpu_custom_call" | custom-call | flops 200000000 | bytes 6000000 | tf_op jit(solution)/shard_map/factor_pack/pallas_call | solution.py:385
  3.7 2.9 %collective-permute-start.13 = (bf16[512,512]{1,0:T(8,128)(2,1)S(1)}, bf16[512,512]{1,0:T(8,128)(2,1)S(1)}, u32[]{:S(2)}, u32[]{:S(2)}) collective-permute-start(bf16[512,512]{1,0:T(8,128)(2,1)S(1)} %factor_pack.1.refs_2_), channel_id=1, source_target_pairs={{0,8},{4,20},{8,0},{12,28},{16,24},{20,4},{24,16},{28,12},{1,9},{5... | collective-permute-start | bytes 1572872 | tf_op jit(solution)/shard_map/ppermute | solution.py:375
  6.7 2.1 %collective-permute-done.12.refs_3_ = bf16[512,512]{1,0:T(8,128)(2,1)S(1)} collective-permute-done((bf16[512,512]{1,0:T(8,128)(2,1)S(1)}, bf16[512,512]{1,0:T(8,128)(2,1)S(1)}, u32[]{:S(2)}, u32[]{:S(2)}) %collective-permute-start.12) | collective-permute-done | bytes 524320 | tf_op jit(solution)/shard_map/ppermute | solution.py:369
  8.7 2.9 %collective-permute-start.14 = (bf16[512,512]{1,0:T(8,128)(2,1)S(1)}, bf16[512,512]{1,0:T(8,128)(2,1)S(1)}, u32[]{:S(2)}, u32[]{:S(2)}) collective-permute-start(bf16[512,512]{1,0:T(8,128)(2,1)S(1)} %collective-permute-done.12.refs_3_), channel_id=1, source_target_pairs={{0,8},{4,20},{8,0},{12,28},{16,24},{20,4},{24,16},{28,12},{1,9},{5... | collective-permute-start | bytes 1572872 | tf_op jit(solution)/shard_map/ppermute | solution.py:375
  11.6 2.2 %collective-permute-done.13.refs_4_ = bf16[512,512]{1,0:T(8,128)(2,1)S(1)} collective-permute-done((bf16[512,512]{1,0:T(8,128)(2,1)S(1)}, bf16[512,512]{1,0:T(8,128)(2,1)S(1)}, u32[]{:S(2)}, u32[]{:S(2)}) %collective-permute-start.13) | collective-permute-done | bytes 524320 | tf_op jit(solution)/shard_map/ppermute | solution.py:375
  13.8 2.1 %collective-permute-start.17 = (bf16[512,512]{1,0:T(8,128)(2,1)S(1)}, bf16[512,512]{1,0:T(8,128)(2,1)S(1)}, u32[]{:S(2)}, u32[]{:S(2)}) collective-permute-start(bf16[512,512]{1,0:T(8,128)(2,1)S(1)} %collective-permute-done.13.refs_4_), channel_id=1, source_target_pairs={{0,16},{4,12},{8,24},{12,4},{16,0},{20,28},{24,8},{28,20},{1,17},{... | collective-permute-start | bytes 1572872 | tf_op jit(solution)/shard_map/ppermute | solution.py:378
  17.5 1.6 %collective-permute-start.4 = (bf16[256,256]{1,0:T(8,128)(2,1)S(1)}, bf16[256,256]{1,0:T(8,128)(2,1)S(1)}, u32[]{:S(2)}, u32[]{:S(2)}) collective-permute-start(bf16[256,256]{1,0:T(8,128)(2,1)S(1)} %get-tuple-element.346), channel_id=1, source_target_pairs={{0,1},{1,0},{2,3},{3,2},{4,5},{5,4},{6,7},{7,6},{8,9},{9,8},{10,11... | collective-permute-start | bytes 393224 | tf_op jit(solution)/shard_map/ppermute | solution.py:372
  19.1 2.6 %collective-permute-start.5 = (bf16[256,256]{1,0:T(8,128)(2,1)S(1)}, bf16[256,256]{1,0:T(8,128)(2,1)S(1)}, u32[]{:S(2)}, u32[]{:S(2)}) collective-permute-start(bf16[256,256]{1,0:T(8,128)(2,1)S(1)} %get-tuple-element.347), channel_id=1, source_target_pairs={{0,2},{1,3},{2,0},{3,1},{4,6},{5,7},{6,4},{7,5},{8,10},{9,11},{10,... | collective-permute-start | bytes 393224 | tf_op jit(solution)/shard_map/ppermute | solution.py:372
  21.7 3.7 %collective-permute-done.4.refs_1_ = bf16[256,256]{1,0:T(8,128)(2,1)S(1)} collective-permute-done((bf16[256,256]{1,0:T(8,128)(2,1)S(1)}, bf16[256,256]{1,0:T(8,128)(2,1)S(1)}, u32[]{:S(2)}, u32[]{:S(2)}) %collective-permute-start.4) | collective-permute-done | bytes 131104 | tf_op jit(solution)/shard_map/ppermute | solution.py:372
  25.4 2.8 %collective-permute-start.6 = (bf16[256,256]{1,0:T(8,128)(2,1)S(1)}, bf16[256,256]{1,0:T(8,128)(2,1)S(1)}, u32[]{:S(2)}, u32[]{:S(2)}) collective-permute-start(bf16[256,256]{1,0:T(8,128)(2,1)S(1)} %get-tuple-element.348), channel_id=1, source_target_pairs={{0,3},{1,2},{2,1},{3,0},{4,7},{5,6},{6,5},{7,4},{8,11},{9,10},{10,... | collective-permute-start | bytes 393224 | tf_op jit(solution)/shard_map/ppermute | solution.py:372
  28.9 2.8 %tables.1 = (s32[128]{0:T(128)S(1)}, s32[1]{0:T(128)}) custom-call(s32[64]{0:T(128)S(1)} %copy-done.27, s32[8]{0:T(128)S(1)} %copy-done.26), custom_call_target="tpu_custom_call" | custom-call | flops 300000000 | bytes 9000000 | tf_op jit(solution)/shard_map/tables/pallas_call | solution.py:408
  34.6 3.6 %mask_below.4.a_ref = bf16[2048,1024]{1,0:T(8,128)(2,1)S(1)} custom-call(s32[8]{0:T(128)S(1)} %copy-done.26, s32[32,64]{1,0:T(8,128)S(1)} %copy-done.16, bf16[2048,4096]{1,0:T(8,128)(2,1)} %a_ref.7), custom_call_target="tpu_custom_call" | custom-call | flops 300000000 | bytes 9000000 | tf_op jit(solution)/shard_map/mask_below/pallas_call | solution.py:441
  38.3 2.8 %mask_below.5.a_ref = bf16[2048,1024]{1,0:T(8,128)(2,1)S(1)} custom-call(s32[8]{0:T(128)S(1)} %copy-done.26, s32[32,64]{1,0:T(8,128)S(1)} %copy-done.16, bf16[2048,4096]{1,0:T(8,128)(2,1)} %a_ref.7), custom_call_target="tpu_custom_call" | custom-call | flops 300000000 | bytes 9000000 | tf_op jit(solution)/shard_map/mask_below/pallas_call | solution.py:441
  41.2 3.4 %mask_rows.3.refs_11_.refs_9_ = bf16[512,1024]{1,0:T(8,128)(2,1)S(1)} custom-call(s32[128]{0:T(128)S(1)} %get-tuple-element.354.tab.refs_0_, s32[8]{0:T(128)S(1)} %copy-done.26, s32[64,64]{1,0:T(8,128)S(1)} %copy-done.25, bf16[512,4096]{1,0:T(8,128)(2,1)} %w_own.5, bf16[512,4096]{1,0:T(8,128)(2,1)} %copy-done.4), custom_call_target="tpu_custom_call" | custom-call | flops 200000000 | bytes 6000000 | tf_op jit(solution)/shard_map/mask_rows/pallas_call | solution.py:460
  44.6 3.2 %mask_rows.4.refs_11_.refs_9_ = bf16[512,2048]{1,0:T(8,128)(2,1)S(1)} custom-call(s32[128]{0:T(128)S(1)} %get-tuple-element.354.tab.refs_0_, s32[8]{0:T(128)S(1)} %copy-done.26, s32[64,64]{1,0:T(8,128)S(1)} %copy-done.25, bf16[512,4096]{1,0:T(8,128)(2,1)} %w_own.5, bf16[512,4096]{1,0:T(8,128)(2,1)} %copy-done.4), custom_call_target="tpu_custom_call" | custom-call | flops 200000000 | bytes 6000000 | tf_op jit(solution)/shard_map/mask_rows/pallas_call | solution.py:460
  47.7 3.1 %mask_rows.5.refs_11_.refs_9_ = bf16[512,3072]{1,0:T(8,128)(2,1)S(1)} custom-call(s32[128]{0:T(128)S(1)} %get-tuple-element.354.tab.refs_0_, s32[8]{0:T(128)S(1)} %copy-done.26, s32[64,64]{1,0:T(8,128)S(1)} %copy-done.25, bf16[512,4096]{1,0:T(8,128)(2,1)} %w_own.5, bf16[512,4096]{1,0:T(8,128)(2,1)} %copy-done.4), custom_call_target="tpu_custom_call" | custom-call | flops 200000000 | bytes 6000000 | tf_op jit(solution)/shard_map/mask_rows/pallas_call | solution.py:460
  52.7 3.0 %collective-permute-start.21 = (bf16[512,256]{1,0:T(8,128)(2,1)S(1)}, bf16[512,256]{1,0:T(8,128)(2,1)S(1)}, u32[]{:S(2)}, u32[]{:S(2)}) collective-permute-start(bf16[512,256]{1,0:T(8,128)(2,1)S(1)} %get-tuple-element.369), channel_id=1, source_target_pairs={{0,2},{1,3},{2,0},{3,1},{4,6},{5,7},{6,4},{7,5},{8,10},{9,11},{10,... | collective-permute-start | bytes 786440 | tf_op jit(solution)/shard_map/ppermute | solution.py:372
  56.8 2.1 %prep.4 = (bf16[2,512,512]{2,1,0:T(8,128)(2,1)S(1)}, bf16[512,512]{1,0:T(8,128)(2,1)S(1)}, f32[512,256]{1,0:T(8,128)S(1)}) custom-call(s32[128]{0:T(128)S(1)} %get-tuple-element.354.tab.refs_0_, s32[8]{0:T(128)S(1)} %copy-done.26, bf16[512,512]{1,0:T(8,128)(2,1)} %copy-done, bf16[512,512]{1,0:T(8,128)(2,1)} %copy-done.6, bf16[512,512]{1,0:T(8,128)(2,1)} %copy-done.7, ...), custom_call_target="tpu_custom_call" | custom-call | flops 200000000 | bytes 6000000 | tf_op jit(solution)/shard_map/prep/pallas_call | solution.py:496
  58.9 2.5 %pair_solve.4 = (bf16[1024,256]{1,0:T(8,128)(2,1)S(1)}, bf16[512,256]{1,0:T(8,128)(2,1)S(1)}, bf16[256,256]{1,0:T(8,128)(2,1)S(1)}) custom-call(s32[128]{0:T(128)S(1)} %get-tuple-element.354.tab.refs_0_, bf16[512,256]{1,0:T(8,128)(2,1)S(1)} %get-tuple-element.350.refs_1_, bf16[512,256]{1,0:T(8,128)(2,1)S(1)} %collective-permute-done.7.refs_2_, ...), custom_call_target="tpu_custom_call" | custom-call | flops 300000000 | bytes 9000000 | tf_op jit(solution)/shard_map/pair_solve/pallas_call | solution.py:539
  62.8 1.7 %collective-permute-start.20 = (bf16[256,256]{1,0:T(8,128)(2,1)S(1)}, bf16[256,256]{1,0:T(8,128)(2,1)S(1)}, u32[]{:S(2)}, u32[]{:S(2)}) collective-permute-start(bf16[256,256]{1,0:T(8,128)(2,1)S(1)} %get-tuple-element.364), channel_id=1, source_target_pairs={{0,24},{4,28},{8,16},{12,20},{16,8},{20,12},{24,0},{28,4},{1,25},{... | collective-permute-start | bytes 393224 | tf_op jit(solution)/shard_map/ppermute | solution.py:369
  64.5 2.4 %prep.5 = (bf16[2,512,512]{2,1,0:T(8,128)(2,1)S(1)}, bf16[512,512]{1,0:T(8,128)(2,1)S(1)}, f32[512,256]{1,0:T(8,128)S(1)}) custom-call(s32[128]{0:T(128)S(1)} %get-tuple-element.354.tab.refs_0_, s32[8]{0:T(128)S(1)} %copy-done.26, bf16[512,512]{1,0:T(8,128)(2,1)} %copy-done, bf16[512,512]{1,0:T(8,128)(2,1)} %copy-done.6, bf16[512,512]{1,0:T(8,128)(2,1)} %copy-done.7, ...), custom_call_target="tpu_custom_call" | custom-call | flops 200000000 | bytes 6000000 | tf_op jit(solution)/shard_map/prep/pallas_call | solution.py:496
  68.1 2.8 %mask_below.6.a_ref = bf16[2048,1024]{1,0:T(8,128)(2,1)S(1)} custom-call(s32[8]{0:T(128)S(1)} %copy-done.26, s32[32,64]{1,0:T(8,128)S(1)} %copy-done.16, bf16[2048,4096]{1,0:T(8,128)(2,1)} %a_ref.7), custom_call_target="tpu_custom_call" | custom-call | flops 300000000 | bytes 9000000 | tf_op jit(solution)/shard_map/mask_below/pallas_call | solution.py:441
  73.5 2.7 %pair_solve.5 = (bf16[1024,256]{1,0:T(8,128)(2,1)S(1)}, bf16[512,256]{1,0:T(8,128)(2,1)S(1)}, bf16[256,256]{1,0:T(8,128)(2,1)S(1)}) custom-call(s32[128]{0:T(128)S(1)} %get-tuple-element.354.tab.refs_0_, bf16[512,256]{1,0:T(8,128)(2,1)S(1)} %get-tuple-element.363.refs_1_, bf16[512,256]{1,0:T(8,128)(2,1)S(1)} %collective-permute-done.19.refs_2_, ...), custom_call_target="tpu_custom_call" | custom-call | flops 300000000 | bytes 9000000 | tf_op jit(solution)/shard_map/pair_solve/pallas_call | solution.py:539
  78.2 2.7 %prep.6 = (bf16[2,512,512]{2,1,0:T(8,128)(2,1)S(1)}, bf16[512,512]{1,0:T(8,128)(2,1)S(1)}, f32[512,256]{1,0:T(8,128)S(1)}) custom-call(s32[128]{0:T(128)S(1)} %get-tuple-element.354.tab.refs_0_, s32[8]{0:T(128)S(1)} %copy-done.26, bf16[512,512]{1,0:T(8,128)(2,1)} %copy-done, bf16[512,512]{1,0:T(8,128)(2,1)} %copy-done.6, bf16[512,512]{1,0:T(8,128)(2,1)} %copy-done.7, ...), custom_call_target="tpu_custom_call" | custom-call | flops 200000000 | bytes 6000000 | tf_op jit(solution)/shard_map/prep/pallas_call | solution.py:496
  80.9 4.8 %mask_below.7 = bf16[2048,1024]{1,0:T(8,128)(2,1)} custom-call(s32[8]{0:T(128)S(1)} %copy-done.26, s32[32,64]{1,0:T(8,128)S(1)} %copy-done.16, bf16[2048,4096]{1,0:T(8,128)(2,1)} %a_ref.7), custom_call_target="tpu_custom_call" | custom-call | flops 300000000 | bytes 9000000 | tf_op jit(solution)/shard_map/mask_below/pallas_call | solution.py:441
  88.9 2.5 %pair_solve.6 = (bf16[1024,256]{1,0:T(8,128)(2,1)S(1)}, bf16[512,256]{1,0:T(8,128)(2,1)S(1)}, bf16[256,256]{1,0:T(8,128)(2,1)S(1)}) custom-call(s32[128]{0:T(128)S(1)} %get-tuple-element.354.tab.refs_0_, bf16[512,256]{1,0:T(8,128)(2,1)S(1)} %get-tuple-element.379.refs_1_, bf16[512,256]{1,0:T(8,128)(2,1)S(1)} %collective-permute-done.24.refs_2_, ...), custom_call_target="tpu_custom_call" | custom-call | flops 300000000 | bytes 9000000 | tf_op jit(solution)/shard_map/pair_solve/pallas_call | solution.py:539
  92.8 1.7 %collective-permute-start.30 = (bf16[256,256]{1,0:T(8,128)(2,1)S(1)}, bf16[256,256]{1,0:T(8,128)(2,1)S(1)}, u32[]{:S(2)}, u32[]{:S(2)}) collective-permute-start(bf16[256,256]{1,0:T(8,128)(2,1)S(1)} %get-tuple-element.397), channel_id=1, source_target_pairs={{0,24},{4,28},{8,16},{12,20},{16,8},{20,12},{24,0},{28,4},{1,25},{... | collective-permute-start | bytes 393224 | tf_op jit(solution)/shard_map/ppermute | solution.py:369
  94.4 2.1 %prep.7 = (bf16[2,512,512]{2,1,0:T(8,128)(2,1)S(1)}, bf16[512,512]{1,0:T(8,128)(2,1)S(1)}) custom-call(s32[128]{0:T(128)S(1)} %get-tuple-element.354.tab.refs_0_, s32[8]{0:T(128)S(1)} %copy-done.26, bf16[512,512]{1,0:T(8,128)(2,1)} %copy-done, bf16[512,512]{1,0:T(8,128)(2,1)} %copy-done.6, bf16[512,512]{1,0:T(8,128)(2,1)} %copy-done.7, ...), custom_call_target="tpu_custom_call" | custom-call | flops 200000000 | bytes 6000000 | tf_op jit(solution)/shard_map/prep/pallas_call | solution.py:496
  98.2 3.4 %collective-permute-done.30.refs_4_ = bf16[256,256]{1,0:T(8,128)(2,1)S(1)} collective-permute-done((bf16[256,256]{1,0:T(8,128)(2,1)S(1)}, bf16[256,256]{1,0:T(8,128)(2,1)S(1)}, u32[]{:S(2)}, u32[]{:S(2)}) %collective-permute-start.30) | collective-permute-done | bytes 131104 | tf_op jit(solution)/shard_map/ppermute | solution.py:369
  103.3 2.9 %pair_solve.7 = bf16[1024,256]{1,0:T(8,128)(2,1)} custom-call(s32[128]{0:T(128)S(1)} %get-tuple-element.354.tab.refs_0_, bf16[512,256]{1,0:T(8,128)(2,1)S(1)} %get-tuple-element.396.refs_1_, bf16[512,256]{1,0:T(8,128)(2,1)S(1)} %collective-permute-done.29.refs_2_, bf16[512,256]{1,0:T(8,128)(2,1)S(1)} %collective-permute-done.32.refs_3_, ...), custom_call_target="tpu_custom_call" | custom-call | flops 300000000 | bytes 9000000 | tf_op jit(solution)/shard_map/pair_solve/pallas_call | solution.py:539
  106.2 5.9 %conditional.1 = ((bf16[4096,256]{1,0:T(8,128)(2,1)}, bf16[2048,256]{1,0:T(8,128)(2,1)})) conditional(s32[]{:T(128)} %bitcast.16, (s32[]{:T(128)}, bf16[256,256]{1,0:T(8,128)(2,1)S(1)}, bf16[256,256]{1,0:T(8,128)(2,1)S(1)}, bf16[256,256]{1,0:T(8,128)(2,1)S(1)}, bf16[256,256]{1,0:T(8,128)(2,1)S(1)}, /*index=5*/bf16[512,256]{1,0:T(8,128)(2,1)}, ...), branch_computations={%region_0.3_spmd, %region_3.4_spmd} | conditional | flops 816449984 | bytes 62158436 | solution.py:572
  106.2 5.9 %last_rows.1 = (bf16[4096,256]{1,0:T(8,128)(2,1)}, bf16[2048,256]{1,0:T(8,128)(2,1)}) custom-call(s32[8]{0:T(128)S(1)} %get-tuple-element.262.order, bf16[2048,1024]{1,0:T(8,128)(2,1)} %get-tuple-element.263.a_ref, bf16[1024,256]{1,0:T(8,128)(2,1)} %get-tuple-element.264.x0, bf16[1024,256]{1,0:T(8,128)(2,1)} %get-tuple-element.265.x1, ...), custom_call_target="tpu_custom_call" | custom-call | flops 300000000 | bytes 9000000 | tf_op jit(solution)/shard_map/cond/branch_1_fun/last_rows/pallas_call | solution.py:554
  (99 shorter events, 23.1 us)
Async XLA Ops:
  0.7 33.8 %collective-permute-start.9 = (bf16[512,4096]{1,0:T(8,128)(2,1)}, bf16[512,4096]{1,0:T(8,128)(2,1)S(1)}, u32[]{:S(2)}, u32[]{:S(2)}) collective-permute-start(bf16[512,4096]{1,0:T(8,128)(2,1)} %w_own.5), channel_id=1, source_target_pairs={{0,4},{4,0},{8,12},{12,8},{16,20},{20,16},{24,28},{28,24},{1,5},{5... | collective-permute-start | bytes 12582920 | tf_op jit(solution)/shard_map/ppermute | solution.py:369
  3.6 5.1 %collective-permute-start.12 = (bf16[512,512]{1,0:T(8,128)(2,1)S(1)}, bf16[512,512]{1,0:T(8,128)(2,1)S(1)}, u32[]{:S(2)}, u32[]{:S(2)}) collective-permute-start(bf16[512,512]{1,0:T(8,128)(2,1)S(1)} %factor_pack.1.refs_2_), channel_id=1, source_target_pairs={{0,4},{4,0},{8,12},{12,8},{16,20},{20,16},{24,28},{28,24},{1,5},{5... | collective-permute-start | bytes 1572872 | tf_op jit(solution)/shard_map/ppermute | solution.py:369
  3.7 10.1 %collective-permute-start.13 = (bf16[512,512]{1,0:T(8,128)(2,1)S(1)}, bf16[512,512]{1,0:T(8,128)(2,1)S(1)}, u32[]{:S(2)}, u32[]{:S(2)}) collective-permute-start(bf16[512,512]{1,0:T(8,128)(2,1)S(1)} %factor_pack.1.refs_2_), channel_id=1, source_target_pairs={{0,8},{4,20},{8,0},{12,28},{16,24},{20,4},{24,16},{28,12},{1,9},{5... | collective-permute-start | bytes 1572872 | tf_op jit(solution)/shard_map/ppermute | solution.py:375
  8.7 19.6 %collective-permute-start.14 = (bf16[512,512]{1,0:T(8,128)(2,1)S(1)}, bf16[512,512]{1,0:T(8,128)(2,1)S(1)}, u32[]{:S(2)}, u32[]{:S(2)}) collective-permute-start(bf16[512,512]{1,0:T(8,128)(2,1)S(1)} %collective-permute-done.12.refs_3_), channel_id=1, source_target_pairs={{0,8},{4,20},{8,0},{12,28},{16,24},{20,4},{24,16},{28,12},{1,9},{5... | collective-permute-start | bytes 1572872 | tf_op jit(solution)/shard_map/ppermute | solution.py:375
  13.8 15.0 %collective-permute-start.17 = (bf16[512,512]{1,0:T(8,128)(2,1)S(1)}, bf16[512,512]{1,0:T(8,128)(2,1)S(1)}, u32[]{:S(2)}, u32[]{:S(2)}) collective-permute-start(bf16[512,512]{1,0:T(8,128)(2,1)S(1)} %collective-permute-done.13.refs_4_), channel_id=1, source_target_pairs={{0,16},{4,12},{8,24},{12,4},{16,0},{20,28},{24,8},{28,20},{1,17},{... | collective-permute-start | bytes 1572872 | tf_op jit(solution)/shard_map/ppermute | solution.py:378
  15.9 1.5 %collective-permute-start.3 = (bf16[128,1024]{1,0:T(8,128)(2,1)S(1)}, bf16[128,1024]{1,0:T(8,128)(2,1)S(1)}, u32[]{:S(2)}, u32[]{:S(2)}) collective-permute-start(bf16[128,1024]{1,0:T(8,128)(2,1)S(1)} %copy-done.1), channel_id=1, source_target_pairs={{0,4},{4,0},{8,12},{12,8},{16,20},{20,16},{24,28},{28,24},{1,5},{5... | collective-permute-start | bytes 786440 | tf_op jit(solution)/shard_map/ppermute | solution.py:369
  17.5 8.0 %collective-permute-start.4 = (bf16[256,256]{1,0:T(8,128)(2,1)S(1)}, bf16[256,256]{1,0:T(8,128)(2,1)S(1)}, u32[]{:S(2)}, u32[]{:S(2)}) collective-permute-start(bf16[256,256]{1,0:T(8,128)(2,1)S(1)} %get-tuple-element.346), channel_id=1, source_target_pairs={{0,1},{1,0},{2,3},{3,2},{4,5},{5,4},{6,7},{7,6},{8,9},{9,8},{10,11... | collective-permute-start | bytes 393224 | tf_op jit(solution)/shard_map/ppermute | solution.py:372
  19.1 9.1 %collective-permute-start.5 = (bf16[256,256]{1,0:T(8,128)(2,1)S(1)}, bf16[256,256]{1,0:T(8,128)(2,1)S(1)}, u32[]{:S(2)}, u32[]{:S(2)}) collective-permute-start(bf16[256,256]{1,0:T(8,128)(2,1)S(1)} %get-tuple-element.347), channel_id=1, source_target_pairs={{0,2},{1,3},{2,0},{3,1},{4,6},{5,7},{6,4},{7,5},{8,10},{9,11},{10,... | collective-permute-start | bytes 393224 | tf_op jit(solution)/shard_map/ppermute | solution.py:372
  25.4 6.9 %collective-permute-start.6 = (bf16[256,256]{1,0:T(8,128)(2,1)S(1)}, bf16[256,256]{1,0:T(8,128)(2,1)S(1)}, u32[]{:S(2)}, u32[]{:S(2)}) collective-permute-start(bf16[256,256]{1,0:T(8,128)(2,1)S(1)} %get-tuple-element.348), channel_id=1, source_target_pairs={{0,3},{1,2},{2,1},{3,0},{4,7},{5,6},{6,5},{7,4},{8,11},{9,10},{10,... | collective-permute-start | bytes 393224 | tf_op jit(solution)/shard_map/ppermute | solution.py:372
  28.3 24.5 %collective-permute-start.16 = (bf16[512,512]{1,0:T(8,128)(2,1)S(1)}, bf16[512,512]{1,0:T(8,128)(2,1)S(1)}, u32[]{:S(2)}, u32[]{:S(2)}) collective-permute-start(bf16[512,512]{1,0:T(8,128)(2,1)S(1)} %collective-permute-done.13.refs_4_), channel_id=1, source_target_pairs={{0,4},{4,0},{8,12},{12,8},{16,20},{20,16},{24,28},{28,24},{1,5},{5... | collective-permute-start | bytes 1572872 | tf_op jit(solution)/shard_map/ppermute | solution.py:369
  28.3 27.5 %collective-permute-start.15 = (bf16[512,512]{1,0:T(8,128)(2,1)S(1)}, bf16[512,512]{1,0:T(8,128)(2,1)S(1)}, u32[]{:S(2)}, u32[]{:S(2)}) collective-permute-start(bf16[512,512]{1,0:T(8,128)(2,1)S(1)} %collective-permute-done.14.refs_5_), channel_id=1, source_target_pairs={{0,4},{4,0},{8,12},{12,8},{16,20},{20,16},{24,28},{28,24},{1,5},{5... | collective-permute-start | bytes 1572872 | tf_op jit(solution)/shard_map/ppermute | solution.py:369
  28.8 27.0 %collective-permute-start.18 = (bf16[512,512]{1,0:T(8,128)(2,1)S(1)}, bf16[512,512]{1,0:T(8,128)(2,1)S(1)}, u32[]{:S(2)}, u32[]{:S(2)}) collective-permute-start(bf16[512,512]{1,0:T(8,128)(2,1)S(1)} %collective-permute-done.17.refs_8_), channel_id=1, source_target_pairs={{0,4},{4,0},{8,12},{12,8},{16,20},{20,16},{24,28},{28,24},{1,5},{5... | collective-permute-start | bytes 1572872 | tf_op jit(solution)/shard_map/ppermute | solution.py:369
  32.9 17.9 %collective-permute-start.7 = (bf16[512,256]{1,0:T(8,128)(2,1)S(1)}, bf16[512,256]{1,0:T(8,128)(2,1)S(1)}, u32[]{:S(2)}, u32[]{:S(2)}) collective-permute-start(bf16[512,256]{1,0:T(8,128)(2,1)S(1)} %get-tuple-element.350.refs_1_), channel_id=1, source_target_pairs={{0,8},{4,20},{8,0},{12,28},{16,24},{20,4},{24,16},{28,12},{1,9},{5... | collective-permute-start | bytes 786440 | tf_op jit(solution)/shard_map/ppermute | solution.py:375
  34.5 16.4 %collective-permute-start.8 = (bf16[256,256]{1,0:T(8,128)(2,1)S(1)}, bf16[256,256]{1,0:T(8,128)(2,1)S(1)}, u32[]{:S(2)}, u32[]{:S(2)}) collective-permute-start(bf16[256,256]{1,0:T(8,128)(2,1)S(1)} %get-tuple-element.353), channel_id=1, source_target_pairs={{0,24},{4,28},{8,16},{12,20},{16,8},{20,12},{24,0},{28,4},{1,25},{... | collective-permute-start | bytes 393224 | tf_op jit(solution)/shard_map/ppermute | solution.py:369
  50.9 8.0 %collective-permute-start.10 = (bf16[512,256]{1,0:T(8,128)(2,1)S(1)}, bf16[512,256]{1,0:T(8,128)(2,1)S(1)}, u32[]{:S(2)}, u32[]{:S(2)}) collective-permute-start(bf16[512,256]{1,0:T(8,128)(2,1)S(1)} %collective-permute-done.7.refs_2_), channel_id=1, source_target_pairs={{0,4},{4,0},{8,12},{12,8},{16,20},{20,16},{24,28},{28,24},{1,5},{5... | collective-permute-start | bytes 786440 | tf_op jit(solution)/shard_map/ppermute | solution.py:369
  51.0 7.9 %collective-permute-start.11 = (bf16[256,256]{1,0:T(8,128)(2,1)S(1)}, bf16[256,256]{1,0:T(8,128)(2,1)S(1)}, u32[]{:S(2)}, u32[]{:S(2)}) collective-permute-start(bf16[256,256]{1,0:T(8,128)(2,1)S(1)} %collective-permute-done.8.refs_4_), channel_id=1, source_target_pairs={{0,4},{4,0},{8,12},{12,8},{16,20},{20,16},{24,28},{28,24},{1,5},{5... | collective-permute-start | bytes 393224 | tf_op jit(solution)/shard_map/ppermute | solution.py:369
  52.7 43.8 %copy-start.17 = (bf16[512,256]{1,0:T(8,128)(2,1)}, bf16[512,256]{1,0:T(8,128)(2,1)S(1)}, u32[]{:S(2)}) copy-start(bf16[512,256]{1,0:T(8,128)(2,1)S(1)} %get-tuple-element.352.h0) | copy-start | bytes 786436
  52.7 18.2 %collective-permute-start.21 = (bf16[512,256]{1,0:T(8,128)(2,1)S(1)}, bf16[512,256]{1,0:T(8,128)(2,1)S(1)}, u32[]{:S(2)}, u32[]{:S(2)}) collective-permute-start(bf16[512,256]{1,0:T(8,128)(2,1)S(1)} %get-tuple-element.369), channel_id=1, source_target_pairs={{0,2},{1,3},{2,0},{3,1},{4,6},{5,7},{6,4},{7,5},{8,10},{9,11},{10,... | collective-permute-start | bytes 786440 | tf_op jit(solution)/shard_map/ppermute | solution.py:372
  61.4 10.2 %collective-permute-start.19 = (bf16[512,256]{1,0:T(8,128)(2,1)S(1)}, bf16[512,256]{1,0:T(8,128)(2,1)S(1)}, u32[]{:S(2)}, u32[]{:S(2)}) collective-permute-start(bf16[512,256]{1,0:T(8,128)(2,1)S(1)} %get-tuple-element.363.refs_1_), channel_id=1, source_target_pairs={{0,8},{4,20},{8,0},{12,28},{16,24},{20,4},{24,16},{28,12},{1,9},{5... | collective-permute-start | bytes 786440 | tf_op jit(solution)/shard_map/ppermute | solution.py:375
  62.8 8.9 %collective-permute-start.20 = (bf16[256,256]{1,0:T(8,128)(2,1)S(1)}, bf16[256,256]{1,0:T(8,128)(2,1)S(1)}, u32[]{:S(2)}, u32[]{:S(2)}) collective-permute-start(bf16[256,256]{1,0:T(8,128)(2,1)S(1)} %get-tuple-element.364), channel_id=1, source_target_pairs={{0,24},{4,28},{8,16},{12,20},{16,8},{20,12},{24,0},{28,4},{1,25},{... | collective-permute-start | bytes 393224 | tf_op jit(solution)/shard_map/ppermute | solution.py:369
  71.6 1.9 %collective-permute-start.22 = (bf16[512,256]{1,0:T(8,128)(2,1)S(1)}, bf16[512,256]{1,0:T(8,128)(2,1)S(1)}, u32[]{:S(2)}, u32[]{:S(2)}) collective-permute-start(bf16[512,256]{1,0:T(8,128)(2,1)S(1)} %collective-permute-done.19.refs_2_), channel_id=1, source_target_pairs={{0,4},{4,0},{8,12},{12,8},{16,20},{20,16},{24,28},{28,24},{1,5},{5... | collective-permute-start | bytes 786440 | tf_op jit(solution)/shard_map/ppermute | solution.py:369
  71.6 1.9 %collective-permute-start.23 = (bf16[256,256]{1,0:T(8,128)(2,1)S(1)}, bf16[256,256]{1,0:T(8,128)(2,1)S(1)}, u32[]{:S(2)}, u32[]{:S(2)}) collective-permute-start(bf16[256,256]{1,0:T(8,128)(2,1)S(1)} %collective-permute-done.20.refs_4_), channel_id=1, source_target_pairs={{0,4},{4,0},{8,12},{12,8},{16,20},{20,16},{24,28},{28,24},{1,5},{5... | collective-permute-start | bytes 393224 | tf_op jit(solution)/shard_map/ppermute | solution.py:369
  72.1 14.9 %collective-permute-start.26 = (bf16[512,256]{1,0:T(8,128)(2,1)S(1)}, bf16[512,256]{1,0:T(8,128)(2,1)S(1)}, u32[]{:S(2)}, u32[]{:S(2)}) collective-permute-start(bf16[512,256]{1,0:T(8,128)(2,1)S(1)} %get-tuple-element.386), channel_id=1, source_target_pairs={{0,3},{1,2},{2,1},{3,0},{4,7},{5,6},{6,5},{7,4},{8,11},{9,10},{10,... | collective-permute-start | bytes 786440 | tf_op jit(solution)/shard_map/ppermute | solution.py:372
  76.2 10.9 %collective-permute-start.24 = (bf16[512,256]{1,0:T(8,128)(2,1)S(1)}, bf16[512,256]{1,0:T(8,128)(2,1)S(1)}, u32[]{:S(2)}, u32[]{:S(2)}) collective-permute-start(bf16[512,256]{1,0:T(8,128)(2,1)S(1)} %get-tuple-element.379.refs_1_), channel_id=1, source_target_pairs={{0,8},{4,20},{8,0},{12,28},{16,24},{20,4},{24,16},{28,12},{1,9},{5... | collective-permute-start | bytes 786440 | tf_op jit(solution)/shard_map/ppermute | solution.py:375
  77.4 9.7 %collective-permute-start.25 = (bf16[256,256]{1,0:T(8,128)(2,1)S(1)}, bf16[256,256]{1,0:T(8,128)(2,1)S(1)}, u32[]{:S(2)}, u32[]{:S(2)}) collective-permute-start(bf16[256,256]{1,0:T(8,128)(2,1)S(1)} %get-tuple-element.380), channel_id=1, source_target_pairs={{0,24},{4,28},{8,16},{12,20},{16,8},{20,12},{24,0},{28,4},{1,25},{... | collective-permute-start | bytes 393224 | tf_op jit(solution)/shard_map/ppermute | solution.py:369
  87.1 1.8 %collective-permute-start.27 = (bf16[512,256]{1,0:T(8,128)(2,1)S(1)}, bf16[512,256]{1,0:T(8,128)(2,1)S(1)}, u32[]{:S(2)}, u32[]{:S(2)}) collective-permute-start(bf16[512,256]{1,0:T(8,128)(2,1)S(1)} %collective-permute-done.24.refs_2_), channel_id=1, source_target_pairs={{0,4},{4,0},{8,12},{12,8},{16,20},{20,16},{24,28},{28,24},{1,5},{5... | collective-permute-start | bytes 786440 | tf_op jit(solution)/shard_map/ppermute | solution.py:369
  87.3 1.6 %collective-permute-start.28 = (bf16[256,256]{1,0:T(8,128)(2,1)S(1)}, bf16[256,256]{1,0:T(8,128)(2,1)S(1)}, u32[]{:S(2)}, u32[]{:S(2)}) collective-permute-start(bf16[256,256]{1,0:T(8,128)(2,1)S(1)} %collective-permute-done.25.refs_4_), channel_id=1, source_target_pairs={{0,4},{4,0},{8,12},{12,8},{16,20},{20,16},{24,28},{28,24},{1,5},{5... | collective-permute-start | bytes 393224 | tf_op jit(solution)/shard_map/ppermute | solution.py:369
  87.7 8.8 %collective-permute-start.31 = (bf16[512,256]{1,0:T(8,128)(2,1)S(1)}, bf16[512,256]{1,0:T(8,128)(2,1)S(1)}, u32[]{:S(2)}, u32[]{:S(2)}) collective-permute-start(bf16[512,256]{1,0:T(8,128)(2,1)S(1)} %get-tuple-element.402), channel_id=1, source_target_pairs={{0,1},{1,0},{2,3},{3,2},{4,5},{5,4},{6,7},{7,6},{8,9},{9,8},{10,11... | collective-permute-start | bytes 786440 | tf_op jit(solution)/shard_map/ppermute | solution.py:372
  91.4 10.2 %collective-permute-start.29 = (bf16[512,256]{1,0:T(8,128)(2,1)S(1)}, bf16[512,256]{1,0:T(8,128)(2,1)S(1)}, u32[]{:S(2)}, u32[]{:S(2)}) collective-permute-start(bf16[512,256]{1,0:T(8,128)(2,1)S(1)} %get-tuple-element.396.refs_1_), channel_id=1, source_target_pairs={{0,8},{4,20},{8,0},{12,28},{16,24},{20,4},{24,16},{28,12},{1,9},{5... | collective-permute-start | bytes 786440 | tf_op jit(solution)/shard_map/ppermute | solution.py:375
  92.8 8.8 %collective-permute-start.30 = (bf16[256,256]{1,0:T(8,128)(2,1)S(1)}, bf16[256,256]{1,0:T(8,128)(2,1)S(1)}, u32[]{:S(2)}, u32[]{:S(2)}) collective-permute-start(bf16[256,256]{1,0:T(8,128)(2,1)S(1)} %get-tuple-element.397), channel_id=1, source_target_pairs={{0,24},{4,28},{8,16},{12,20},{16,8},{20,12},{24,0},{28,4},{1,25},{... | collective-permute-start | bytes 393224 | tf_op jit(solution)/shard_map/ppermute | solution.py:369
  101.6 1.7 %collective-permute-start.32 = (bf16[512,256]{1,0:T(8,128)(2,1)S(1)}, bf16[512,256]{1,0:T(8,128)(2,1)S(1)}, u32[]{:S(2)}, u32[]{:S(2)}) collective-permute-start(bf16[512,256]{1,0:T(8,128)(2,1)S(1)} %collective-permute-done.29.refs_2_), channel_id=1, source_target_pairs={{0,4},{4,0},{8,12},{12,8},{16,20},{20,16},{24,28},{28,24},{1,5},{5... | collective-permute-start | bytes 786440 | tf_op jit(solution)/shard_map/ppermute | solution.py:369
  101.6 1.7 %collective-permute-start.33 = (bf16[256,256]{1,0:T(8,128)(2,1)S(1)}, bf16[256,256]{1,0:T(8,128)(2,1)S(1)}, u32[]{:S(2)}, u32[]{:S(2)}) collective-permute-start(bf16[256,256]{1,0:T(8,128)(2,1)S(1)} %collective-permute-done.30.refs_4_), channel_id=1, source_target_pairs={{0,4},{4,0},{8,12},{12,8},{16,20},{20,16},{24,28},{28,24},{1,5},{5... | collective-permute-start | bytes 393224 | tf_op jit(solution)/shard_map/ppermute | solution.py:369
  (21 other events, 294.2 us)

commit v5 on v4

--- a/solution.py
+++ b/solution.py
@@ -131,6 +131,7 @@
     row = lax.axis_index("rows")
     chip, core = row // 2, row % 2
     flag[0] = 0
+    flag[1] = lax.axis_index("rhs")
     for t in range(GROUPS * SB):
         tab[PACK + t] = 0
     for group in range(GROUPS):
@@ -191,23 +192,22 @@
 
 
 def make_mask_kernel(group):
-    def kernel(tab, order, pattern, w_own, w_other, out, wrow, pat, sem):
+    def kernel(tab, order, pattern, w_own, w_other, out, pat):
         row = lax.axis_index("rows")
-        for j in range(SB):
-            place = tab[PACK + (group + 1) * SB + j]
-            for side, w_ref in enumerate((w_own, w_other)):
-                @pl.when(place // SB == side)
-                def _(j=j, place=place, w_ref=w_ref):
-                    pltpu.make_async_copy(w_ref.at[rows_at(place % SB), :], wrow.at[pl.ds(j * BS, BS), :], sem).start()
+        places = [tab[PACK + (group + 1) * SB + j] for j in range(SB)]
+        for j, place in enumerate(places):
             pat[j:j + 1, :] = pattern[pl.ds(jnp.bitwise_xor(row, place // SB) * SB + place % SB, 1), :]
         spread = spread_matrix()
         rows = pat[...]
         masks = [expand_mask(rows, order[k], spread) for k in range(2 * group + 2)]
-        pltpu.make_async_copy(w_own, wrow, sem).wait()
-        for k in range(2 * group + 2):
-            for j in range(SB):
-                at = slice(j * BS, (j + 1) * BS)
-                out[at, k * SN:(k + 1) * SN] = wrow[at, columns_at(order[k])] * masks[k][j:j + 1, :]
+        for j, place in enumerate(places):
+            at = slice(j * BS, (j + 1) * BS)
+            for side, w_ref in enumerate((w_own, w_other)):
+                @pl.when(place // SB == side)
+                def _(w_ref=w_ref, at=at, j=j, place=place):
+                    for k in range(2 * group + 2):
+                        block = w_ref[rows_at(place % SB), columns_at(order[k])]
+                        out[at, k * SN:(k + 1) * SN] = block * masks[k][j:j + 1, :]
 
     return kernel
 
@@ -215,32 +215,25 @@
 def make_prep_kernel(group):
     last = group == GROUPS - 1
 
-    def kernel(*refs):
-        tab, order = refs[:2]
-        l_refs, diag_ref = refs[2:10], refs[10]
-        refs = refs[11:]
+    def kernel(tab, *refs):
+        l_refs, refs = refs[:8], refs[8:]
         if last:
-            d_out, l_out, dsem, lsem = refs
+            l_out = refs[0]
         else:
             w_ref, chip_rhs = refs[:2]
             xs = refs[2:2 + group]
-            d_out, l_out, r_out, dsem, lsem = refs[2 + group:]
-        for q in range(2):
-            pltpu.make_async_copy(diag_ref.at[order[2 * group + q]], d_out.at[q], dsem.at[q]).start()
+            l_out, r_out = refs[2 + group:]
         for i in range(SB):
             code = tab[LSRC + group * SB + i]
             for m in range(8):
                 @pl.when(code // SB == m)
                 def _(m=m, i=i, code=code):
-                    pltpu.make_async_copy(l_refs[m].at[rows_at(code % SB), :], l_out.at[pl.ds(i * BS, BS), :], lsem).start()
+                    l_out[i * BS:(i + 1) * BS, :] = l_refs[m][rows_at(code % SB), :]
         if not last:
             total = jnp.concatenate([chip_rhs[rows_at(tab[PACK + (group + 1) * SB + j]), :] for j in range(SB)], axis=0).astype(F32)
             for k in range(group):
                 total = total - jnp.dot(w_ref[:, k * PAIR:(k + 1) * PAIR], xs[k][...], preferred_element_type=F32)
             r_out[...] = total
-        for q in range(2):
-            pltpu.make_async_copy(diag_ref.at[0], d_out.at[q], dsem.at[q]).wait()
-        pltpu.make_async_copy(diag_ref.at[0], l_out, lsem).wait()
 
     return kernel
 
@@ -249,11 +242,11 @@
     last = group == GROUPS - 1
 
     def kernel(*refs):
-        tab, sources, d_ref, l_ref = refs[0], refs[1:6], refs[6], refs[7]
+        tab, order, sources, d_ref, l_ref = refs[0], refs[1], refs[2:7], refs[7], refs[8]
         if last:
-            x_ref, panel = refs[8:]
+            x_ref, panel = refs[9:]
         else:
-            r_ref, wn_ref, x_ref, p_ref, b_ref, panel = refs[8:]
+            r_ref, wn_ref, x_ref, p_ref, b_ref, panel = refs[9:]
 
         def place(i):
             code = tab[SRC + group * 16 + i]
@@ -264,10 +257,10 @@
 
         for i in range(2 * SB):
             place(i)
-        x_a = jnp.dot(d_ref[0], panel[0:SN, :], preferred_element_type=F32).astype(BF16)
+        x_a = jnp.dot(d_ref[order[2 * group]], panel[0:SN, :], preferred_element_type=F32).astype(BF16)
         x_ref[0:SN, :] = x_a
         rest = panel[SN:PAIR, :].astype(F32) - jnp.dot(l_ref[...], x_a, preferred_element_type=F32)
-        x_b = jnp.dot(d_ref[1], rest.astype(BF16), preferred_element_type=F32).astype(BF16)
+        x_b = jnp.dot(d_ref[order[2 * group + 1]], rest.astype(BF16), preferred_element_type=F32).astype(BF16)
         x_ref[SN:PAIR, :] = x_b
         if last:
             return
@@ -279,45 +272,50 @@
     return kernel
 
 
-def make_below_mask_kernel(group):
-    def kernel(order, pattern, a_ref, out, sems):
-        tiles = sems.shape[0]
-        tall = out.shape[0] // tiles
-        copies = []
-        for i in range(tiles):
-            for q in range(2):
-                c = pltpu.make_async_copy(a_ref.at[pl.ds(i * tall, tall), columns_at(order[2 * group + q])],
-                                          out.at[pl.ds(i * tall, tall), pl.ds(q * SN, SN)], sems.at[i, q])
-                c.start()
-                copies.append(c)
-        spread = spread_matrix()
-        rows = pattern[...]
-        masks = [expand_mask(rows, order[2 * group + q], spread) for q in range(2)]
-        for i in range(tiles):
-            for q in range(2):
-                copies[2 * i + q].wait()
-                for j in range(i * tall // BS, (i + 1) * tall // BS):
-                    at = (slice(j * BS, (j + 1) * BS), slice(q * SN, (q + 1) * SN))
-                    out[at] = out[at] * masks[q][j:j + 1, :]
-
-    return kernel
-
-
-def first_rows_kernel(a_ref, x_ref, out):
-    out[...] = jnp.dot(a_ref[...], x_ref[...], preferred_element_type=F32)
-
-
-def next_rows_kernel(a_ref, x_ref, sums, out):
-    out[...] = sums[...] + jnp.dot(a_ref[...], x_ref[...], preferred_element_type=F32)
-
-
-def base_rows_kernel(a_ref, x_ref, sums, h0, h1, h2, h3, out):
+def below_part(order, pattern, a_ref, buf, sems, group):
+    tiles = sems.shape[0]
+    tall = buf.shape[0] // tiles
+    copies = []
+    for i in range(tiles):
+        for q in range(2):
+            c = pltpu.make_async_copy(a_ref.at[pl.ds(i * tall, tall), columns_at(order[2 * group + q])],
+                                      buf.at[pl.ds(i * tall, tall), pl.ds(q * SN, SN)], sems.at[i, q])
+            c.start()
+            copies.append(c)
+    spread = spread_matrix()
+    rows = pattern[...]
+    masks = [expand_mask(rows, order[2 * group + q], spread) for q in range(2)]
+    for i in range(tiles):
+        halves = []
+        for q in range(2):
+            copies[2 * i + q].wait()
+            halves.append(jnp.concatenate([buf[j * BS:(j + 1) * BS, q * SN:(q + 1) * SN] * masks[q][j:j + 1, :]
+                                           for j in range(i * tall // BS, (i + 1) * tall // BS)], axis=0))
+        yield slice(i * tall, (i + 1) * tall), jnp.concatenate(halves, axis=1)
+
+
+def last_mask_kernel(order, pattern, a_ref, out, sems):
+    for at, part in below_part(order, pattern, a_ref, out, sems, GROUPS - 1):
+        out[at, :] = part
+
+
+def first_rows_kernel(order, pattern, a_ref, x_ref, out, buf, sems):
+    for at, part in below_part(order, pattern, a_ref, buf, sems, 0):
+        out[at, :] = jnp.dot(part, x_ref[...], preferred_element_type=F32)
+
+
+def next_rows_kernel(order, pattern, a_ref, x_ref, sums, out, buf, sems):
+    for at, part in below_part(order, pattern, a_ref, buf, sems, 1):
+        out[at, :] = sums[at, :] + jnp.dot(part, x_ref[...], preferred_element_type=F32)
+
+
+def base_rows_kernel(order, pattern, a_ref, x_ref, sums, h0, h1, h2, h3, out, buf, sems, rhs):
     depth = lax.axis_index("rhs")
     tall = h0.shape[0]
     for s, h in enumerate((h0, h1, h2, h3)):
-        at = pl.ds(pl.multiple_of(jnp.bitwise_xor(depth, s) * tall, tall), tall)
-        part = jnp.dot(a_ref[at, :], x_ref[...], preferred_element_type=F32)
-        out[at, :] = h[...].astype(F32) - (sums[at, :] + part)
+        rhs[pl.ds(pl.multiple_of(jnp.bitwise_xor(depth, s) * tall, tall), tall), :] = h[...]
+    for at, part in below_part(order, pattern, a_ref, buf, sems, 2):
+        out[at, :] = rhs[at, :].astype(F32) - (sums[at, :] + jnp.dot(part, x_ref[...], preferred_element_type=F32))
 
 
 def last_rows_kernel(order, a_ref, x0, x1, x2, x3, base, sol_ref, out_ref, done, sems, osem):
@@ -338,6 +336,10 @@
         c.wait()
 
 
+def in_vmem(x):
+    return pltpu.with_memory_space_constraint(x, pltpu.VMEM)
+
+
 def in_hbm(x):
     return pltpu.with_memory_space_constraint(x, pltpu.HBM)
 
@@ -393,7 +395,8 @@
         cost_estimate=cost(2),
         name="factor_pack",
     )(window_owner, sn_order, win_pattern, w_own)
-    near = neighbour(l_own)
+    l_other = swap(l_own, 1)
+    rhs_late, _ = lax.optimization_barrier((rhs_win, l_own))
     sent = pl.pallas_call(
         rhs_kernel,
         out_shape=(shape_of((2 * tall, columns)),) * 4,
@@ -402,12 +405,14 @@
         compiler_params=params(4),
         cost_estimate=cost(1),
         name="rhs_pack",
-    )(rhs_win, rhs_other)
+    )(rhs_late, rhs_other)
+    l_own, l_other, *sent = lax.optimization_barrier((l_own, l_other, *sent))
+    near, near_other = neighbour(l_own), neighbour(l_other)
     pieces = [sent[0]] + [deep(sent[s], s) for s in (1, 2, 3)]
     owner_later, _ = lax.optimization_barrier((window_owner, l_own))
     tab, flag = pl.pallas_call(
         table_kernel,
-        out_shape=(shape_of((TABLE,), jnp.int32), shape_of((1,), jnp.int32)),
+        out_shape=(shape_of((TABLE,), jnp.int32), shape_of((2,), jnp.int32)),
         in_specs=[SMEM, SMEM],
         out_specs=(SMEM, SMEM),
         scratch_shapes=[pltpu.SMEM((4,), jnp.int32)],
@@ -424,30 +429,17 @@
         cost_estimate=cost(1),
         name="first_pack",
     )(tab, *pieces)
-    l_other = swap(l_own, 1)
-    near_other = neighbour(l_other)
-    far = forward(near)
-    l_parts = [in_hbm(x) for x in (l_own, l_other, near, near_other, swap(near_other, 1), swap(near, 1), far, swap(far, 1))]
-    w_other = in_hbm(swap(win_rows, 1))
-
-    depth = lax.axis_index("rhs")
+    near_late, near_other, w_late, *_ = lax.optimization_barrier((near, near_other, win_rows, *pieces[1:]))
+    far = forward(near_late)
+    l_parts = [in_vmem(x) for x in (l_own, l_other, near, near_other, swap(near_other, 1), swap(near, 1), far, swap(far, 1))]
+    w_other = in_vmem(swap(w_late, 1))
+    w_own = in_vmem(win_rows)
+
     tile = rhs_anc.shape[0]
-    sums, solved, masked, below = None, [], [], []
+    sums, solved, masked = None, [], []
     anc_hbm = in_hbm(anc_rows)
-    diag_hbm = in_hbm(diag_inv)
+    diag_vmem = in_vmem(diag_inv)
     below_rows = anc_rows.shape[0]
-
-    def mask_below(k, order):
-        below.append(pl.pallas_call(
-            make_below_mask_kernel(k),
-            out_shape=shape_of((below_rows, PAIR)),
-            in_specs=[SMEM, VMEM, HBM],
-            out_specs=VMEM,
-            scratch_shapes=[pltpu.SemaphoreType.DMA((4, 2))],
-            compiler_params=params(4),
-            cost_estimate=cost(3),
-            name="mask_below",
-        )(order, anc_pattern, anc_hbm))
 
     anc_order, anc_pieces = (2, 3, 1), [None] * 4
     for group in range(GROUPS):
@@ -460,15 +452,25 @@
                 masked.append(pl.pallas_call(
                     make_mask_kernel(k),
                     out_shape=shape_of((SN, (k + 1) * PAIR)),
-                    in_specs=[SMEM, SMEM, VMEM, HBM, HBM],
+                    in_specs=[SMEM, SMEM, VMEM, VMEM, VMEM],
                     out_specs=VMEM,
-                    scratch_shapes=[pltpu.VMEM((SN, NW), BF16), pltpu.VMEM((SB, NWB), jnp.int32), pltpu.SemaphoreType.DMA],
+                    scratch_shapes=[pltpu.VMEM((SB, NWB), jnp.int32)],
                     compiler_params=params(6),
                     cost_estimate=cost(2),
                     name="mask_rows",
                 )(tab_later, order_later, win_pattern, w_own, w_other))
-            mask_below(0, order_later)
-            mask_below(1, order_later)
+        if group == 1:
+            order_later, _ = lax.optimization_barrier((sn_order, packed))
+            last_below = pl.pallas_call(
+                last_mask_kernel,
+                out_shape=shape_of((below_rows, PAIR)),
+                in_specs=[SMEM, VMEM, HBM],
+                out_specs=VMEM,
+                scratch_shapes=[pltpu.SemaphoreType.DMA((4, 2))],
+                compiler_params=params(4),
+                cost_estimate=cost(3),
+                name="last_mask",
+            )(order_later, anc_pattern, anc_hbm)
         if group == 0:
             rhs_later, _ = lax.optimization_barrier((rhs_anc, packed))
             anc_pieces = list(pl.pallas_call(
@@ -486,20 +488,17 @@
             moved, _ = lax.optimization_barrier((anc_pieces[s], packed))
             anc_pieces[s] = deep(moved, s)
 
-        operands = [tab, sn_order, *l_parts, diag_hbm]
-        in_specs = [SMEM, SMEM] + [HBM] * 9
-        out_shape = [shape_of((2, SN, SN)), shape_of((SN, SN))]
+        operands = [tab, *l_parts]
+        out_shape = [shape_of((SN, SN))]
         if not last:
             operands += [masked[group], chip_rhs, *solved]
-            in_specs += [VMEM] * (2 + group)
             out_shape += [shape_of((SN, columns), F32)]
         ready = pl.pallas_call(
             make_prep_kernel(group),
             out_shape=tuple(out_shape),
-            in_specs=in_specs,
+            in_specs=[SMEM] + [VMEM] * (len(operands) - 1),
             out_specs=(VMEM,) * len(out_shape),
-            scratch_shapes=[pltpu.SemaphoreType.DMA((2,)), pltpu.SemaphoreType.DMA],
-            compiler_params=params(8),
+            compiler_params=params(6),
             cost_estimate=cost(2),
             name="prep",
         )(*operands)
@@ -513,22 +512,21 @@
             sums = pl.pallas_call(
                 kernel,
                 out_shape=shape_of((below_rows, columns), F32),
-                in_specs=[VMEM] * (2 + len(more)),
+                in_specs=[SMEM, VMEM, HBM] + [VMEM] * (1 + len(more)),
                 out_specs=VMEM,
-                input_output_aliases={2: 0} if more else {},
-                compiler_params=params(6),
+                scratch_shapes=[pltpu.VMEM((below_rows, PAIR), BF16), pltpu.SemaphoreType.DMA((4, 2))]
+                + ([pltpu.VMEM((below_rows, columns), BF16)] if k == 2 else []),
+                input_output_aliases={4: 0} if more else {},
+                compiler_params=params(10),
                 cost_estimate=cost(3),
                 name="rows_below",
-            )(below[k], solved[k], *more)
-            if k < 2:
-                order_later, _ = lax.optimization_barrier((sn_order, packed))
-                mask_below(k + 2, order_later)
-            a_own, b_own, sums, below[-1], previous, *ready = lax.optimization_barrier(
-                (a_own, b_own, sums, below[-1], previous, *ready))
+            )(sn_order, anc_pattern, anc_hbm, solved[k], *more)
+            if k == 2:
+                a_own, last_below = lax.optimization_barrier((a_own, last_below))
+            a_own, b_own, sums, previous, *ready = lax.optimization_barrier((a_own, b_own, sums, previous, *ready))
             anc_pieces[anc_order[k]] = previous
         else:
-            a_own, b_own, masked[0], masked[1], masked[2], below[0], below[1] = lax.optimization_barrier(
-                (a_own, b_own, *masked, *below))
+            a_own, b_own, *masked = lax.optimization_barrier((a_own, b_own, *masked))
         a_swap = swap(a_own, 1)
         b_swap = swap(b_own, 1)
         ready = list(ready) if last else list(ready) + [masked[group]]
@@ -539,37 +537,38 @@
         results = pl.pallas_call(
             make_solve_kernel(group),
             out_shape=tuple(out_shape),
-            in_specs=[SMEM] + [VMEM] * (5 + len(ready)),
+            in_specs=[SMEM, SMEM] + [VMEM] * (6 + len(ready)),
             out_specs=(VMEM,) * len(out_shape),
             scratch_shapes=[pltpu.VMEM((PAIR, columns), BF16)],
             compiler_params=params(8),
             cost_estimate=cost(3),
             name="pair_solve",
-        )(tab, packed, a_own, a_swap, b_own, b_swap, *ready)
+        )(tab, sn_order, packed, a_own, a_swap, b_own, b_swap, diag_vmem, *ready)
         solved.append(results[0])
         if not last:
             packed, part = results[1:]
 
-    def packed_path(*xs):
-        return pl.pallas_call(
-            last_rows_kernel,
-            out_shape=(shape_of((NW, columns)), shape_of((below_rows, columns))),
-            in_specs=[SMEM] + [VMEM] * 6,
-            out_specs=(HBM, HBM),
-            scratch_shapes=[pltpu.VMEM((below_rows, columns), BF16), pltpu.SemaphoreType.DMA((2 * GROUPS,)),
-                            pltpu.SemaphoreType.DMA((4,))],
-            compiler_params=params(16),
-            cost_estimate=cost(3),
-            name="last_rows",
-        )(sn_order, below[-1], *xs, sums)
-
-    def other_path(*xs):
-        back = depth ^ jnp.arange(4)
-        win_rhs = jnp.take(jnp.stack([x[:tall] for x in pieces]), back, axis=0).reshape(4 * tall, columns)
-        anc_rhs = jnp.take(jnp.stack(anc_pieces), back, axis=0).reshape(4 * tile, columns)
-        return general_path(win_rows, anc_rows, win_pattern, anc_pattern, window_owner, sn_order, diag_inv, win_rhs, anc_rhs)
-
-    return tuple(lax.cond(flag[0] == 0, packed_path, other_path, *solved))
+    outputs = pl.pallas_call(
+        last_rows_kernel,
+        out_shape=(shape_of((NW, columns)), shape_of((below_rows, columns))),
+        in_specs=[SMEM] + [VMEM] * 6,
+        out_specs=(HBM, HBM),
+        scratch_shapes=[pltpu.VMEM((below_rows, columns), BF16), pltpu.SemaphoreType.DMA((2 * GROUPS,)),
+                        pltpu.SemaphoreType.DMA((4,))],
+        compiler_params=params(6),
+        cost_estimate=cost(3),
+        name="last_rows",
+    )(sn_order, last_below, *solved, sums)
+
+    def again(carry):
+        carry, own_pieces, below_pieces = lax.optimization_barrier((carry, pieces, anc_pieces))
+        back = carry[0][1] ^ jnp.arange(4)
+        win_rhs = jnp.take(jnp.stack([x[:tall] for x in own_pieces]), back, axis=0).reshape(4 * tall, columns)
+        anc_rhs = jnp.take(jnp.stack(below_pieces), back, axis=0).reshape(4 * tile, columns)
+        return jnp.zeros_like(carry[0]), *general_path(
+            win_rows, anc_rows, win_pattern, anc_pattern, window_owner, sn_order, diag_inv, win_rhs, anc_rhs)
+
+    return tuple(lax.while_loop(lambda carry: carry[0][0] != 0, again, (flag, *outputs))[1:])
 
 
 def solution(mesh):

time: 113 us -> 109 us (0.965)
  waiting for transfers between devices: 16 us -> 27.3 us
  Pallas kernels: 60.5 us -> 52.2 us
  starting transfers between devices: 32.7 us -> 27.2 us
    pallas_call x5 -> x2, Pallas kernels: 19.9 us -> 5.86 us  [the longest x1 3 us: local(): pl.pallas_call(last_rows_kernel, out_shape=(shape_of((NW, columns)), shap...]
    pallas_call x3, Pallas kernels: 4.17 us -> 14.7 us  [local(): pl.pallas_call(kernel, out_shape=shape_of((below_rows, columns), F32), in...]
    ppermute x1, waiting for transfers between devices: 0.01 us -> 7.15 us  [forward(): lax.ppermute(x, 'rows', [(i, i ^ (4 if i % 2 == 0 else 2)) for i in range...]
    pallas_call x3, Pallas kernels: 9.67 us -> 2.98 us  [local(): pl.pallas_call(make_mask_kernel(k), out_shape=shape_of((SN, (k + 1) * PAI...]
    pallas_call x4, Pallas kernels: 10.5 us -> 16.3 us  [local(): pl.pallas_call(make_solve_kernel(group), out_shape=tuple(out_shape), in_s...]
    ppermute x6, waiting for transfers between devices: 4.4 us -> 10.1 us  [deep(): return lax.ppermute(x, 'rhs', [(i, i ^ m) for i in range(4)])]
    pallas_call x4, Pallas kernels: 9.18 us -> 5.13 us  [local(): pl.pallas_call(make_prep_kernel(group), out_shape=tuple(out_shape), in_sp...]
    ppermute x6, starting transfers between devices: 11.6 us -> 9.01 us  [deep(): return lax.ppermute(x, 'rhs', [(i, i ^ m) for i in range(4)])]
  transfers between devices with their start and end apart: 31 -> 31, of which waited for: 9 -> 9; matrix products, arithmetic and copies ran while one was open for 0% -> 0% of each run, Pallas kernels for 46% -> 39%
where the time goes in v5:
time: 109 us
  Pallas kernels  52.2 us (48%)
  waiting for transfers between devices  27.3 us (25%)
  starting transfers between devices  27.2 us (25%)
  between operations  1.14 us (1%)
    pallas_call x4, Pallas kernels, local(): pl.pallas_call(make_solve_kernel(group), out_shape=tuple(out_shape), in_s...  16.3 us
    pallas_call x3, Pallas kernels, local(): pl.pallas_call(kernel, out_shape=shape_of((below_rows, columns), F32), in...  14.7 us
    ppermute x6, waiting for transfers between devices, deep(): return lax.ppermute(x, 'rhs', [(i, i ^ m) for i in range(4)])  10.1 us
    ppermute x18, waiting for transfers between devices, swap(): return lax.ppermute(x, 'rows', [(i, i ^ m) for i in range(8)])  10 us
    ppermute x6, starting transfers between devices, neighbour(): lax.ppermute(x, 'rows', [(i, i ^ (2 if i % 2 == 0 else 4)) for i in range...  9.25 us
    ppermute x6, starting transfers between devices, deep(): return lax.ppermute(x, 'rhs', [(i, i ^ m) for i in range(4)])  9.01 us
    ppermute x18, starting transfers between devices, swap(): return lax.ppermute(x, 'rows', [(i, i ^ m) for i in range(8)])  7.36 us
    ppermute x1, waiting for transfers between devices, forward(): lax.ppermute(x, 'rows', [(i, i ^ (4 if i % 2 == 0 else 2)) for i in range...  7.15 us
  transfers between devices with their start and end apart: 31, of which 9 were waited for; matrix products, arithmetic and copies ran while one was open for 0% of the time, Pallas kernels for 39%

profile of v5, /device:TPU:0, one launch (start us, length us, event | category | flops | bytes accessed | tf_op | source)
XLA Modules:
  0.0 108.7 jit_solution(3269416820455074422)
XLA Ops:
  0.7 2.6 %factor_pack.1.refs_0_ = bf16[512,512]{1,0:T(8,128)(2,1)S(1)} custom-call(s32[64]{0:T(128)} %owner.2, s32[8]{0:T(128)} %order.15, s32[64,64]{1,0:T(8,128)} %pattern.11, bf16[512,4096]{1,0:T(8,128)(2,1)} %w_own.5), custom_call_target="tpu_custom_call" | custom-call | flops 200000000 | bytes 6000000 | tf_op jit(solution)/shard_map/factor_pack/pallas_call | solution.py:387
  3.9 1.8 %collective-permute-done.4.other_ref = bf16[128,1024]{1,0:T(8,128)(2,1)S(1)} collective-permute-done((bf16[128,1024]{1,0:T(8,128)(2,1)S(1)}, bf16[128,1024]{1,0:T(8,128)(2,1)S(1)}, u32[]{:S(2)}, u32[]{:S(2)}) %collective-permute-start.4) | collective-permute-done | bytes 262176 | tf_op jit(solution)/shard_map/ppermute | solution.py:371
  5.8 2.9 %collective-permute-start.10 = (bf16[512,512]{1,0:T(8,128)(2,1)S(1)}, bf16[512,512]{1,0:T(8,128)(2,1)S(1)}, u32[]{:S(2)}, u32[]{:S(2)}) collective-permute-start(bf16[512,512]{1,0:T(8,128)(2,1)S(1)} %factor_pack.1.refs_0_), channel_id=1, source_target_pairs={{0,8},{4,20},{8,0},{12,28},{16,24},{20,4},{24,16},{28,12},{1,9},{5... | collective-permute-start | bytes 1572872 | tf_op jit(solution)/shard_map/ppermute | solution.py:377
  8.8 2.0 %collective-permute-start.5 = (bf16[256,256]{1,0:T(8,128)(2,1)S(1)}, bf16[256,256]{1,0:T(8,128)(2,1)S(1)}, u32[]{:S(2)}, u32[]{:S(2)}) collective-permute-start(bf16[256,256]{1,0:T(8,128)(2,1)S(1)} %get-tuple-element.384), channel_id=1, source_target_pairs={{0,1},{1,0},{2,3},{3,2},{4,5},{5,4},{6,7},{7,6},{8,9},{9,8},{10,11... | collective-permute-start | bytes 393224 | tf_op jit(solution)/shard_map/ppermute | solution.py:374
  10.8 2.6 %collective-permute-start.6 = (bf16[256,256]{1,0:T(8,128)(2,1)S(1)}, bf16[256,256]{1,0:T(8,128)(2,1)S(1)}, u32[]{:S(2)}, u32[]{:S(2)}) collective-permute-start(bf16[256,256]{1,0:T(8,128)(2,1)S(1)} %get-tuple-element.385), channel_id=1, source_target_pairs={{0,2},{1,3},{2,0},{3,1},{4,6},{5,7},{6,4},{7,5},{8,10},{9,11},{10,... | collective-permute-start | bytes 393224 | tf_op jit(solution)/shard_map/ppermute | solution.py:374
  13.4 2.1 %collective-permute-done.5.refs_1_ = bf16[256,256]{1,0:T(8,128)(2,1)S(1)} collective-permute-done((bf16[256,256]{1,0:T(8,128)(2,1)S(1)}, bf16[256,256]{1,0:T(8,128)(2,1)S(1)}, u32[]{:S(2)}, u32[]{:S(2)}) %collective-permute-start.5) | collective-permute-done | bytes 131104 | tf_op jit(solution)/shard_map/ppermute | solution.py:374
  15.5 8.0 %collective-permute-done.6.refs_2_ = bf16[256,256]{1,0:T(8,128)(2,1)S(1)} collective-permute-done((bf16[256,256]{1,0:T(8,128)(2,1)S(1)}, bf16[256,256]{1,0:T(8,128)(2,1)S(1)}, u32[]{:S(2)}, u32[]{:S(2)}) %collective-permute-start.6) | collective-permute-done | bytes 131104 | tf_op jit(solution)/shard_map/ppermute | solution.py:374
  23.6 1.6 %collective-permute-start.17 = (bf16[512,512]{1,0:T(8,128)(2,1)S(1)}, bf16[512,512]{1,0:T(8,128)(2,1)S(1)}, u32[]{:S(2)}, u32[]{:S(2)}) collective-permute-start(bf16[512,512]{1,0:T(8,128)(2,1)S(1)} %collective-permute-done.10.refs_2_), channel_id=1, source_target_pairs={{0,16},{4,12},{8,24},{12,4},{16,0},{20,28},{24,8},{28,20},{1,17},{... | collective-permute-start | bytes 1572872 | tf_op jit(solution)/shard_map/ppermute | solution.py:380
  25.7 7.2 %collective-permute-done.17.refs_6_ = bf16[512,512]{1,0:T(8,128)(2,1)S(1)} collective-permute-done((bf16[512,512]{1,0:T(8,128)(2,1)S(1)}, bf16[512,512]{1,0:T(8,128)(2,1)S(1)}, u32[]{:S(2)}, u32[]{:S(2)}) %collective-permute-start.17) | collective-permute-done | bytes 524320 | tf_op jit(solution)/shard_map/ppermute | solution.py:380
  32.8 2.8 %tables.1 = (s32[128]{0:T(128)S(1)}, s32[2]{0:T(128)}) custom-call(s32[64]{0:T(128)S(1)} %copy-done.22, s32[8]{0:T(128)S(1)} %copy-done.23), custom_call_target="tpu_custom_call" | custom-call | flops 300000000 | bytes 9000000 | tf_op jit(solution)/shard_map/tables/pallas_call | solution.py:413
  36.2 1.6 %collective-permute-start.8 = (bf16[512,256]{1,0:T(8,128)(2,1)S(1)}, bf16[512,256]{1,0:T(8,128)(2,1)S(1)}, u32[]{:S(2)}, u32[]{:S(2)}) collective-permute-start(bf16[512,256]{1,0:T(8,128)(2,1)S(1)} %get-tuple-element.387.refs_2_), channel_id=1, source_target_pairs={{0,8},{4,20},{8,0},{12,28},{16,24},{20,4},{24,16},{28,12},{1,9},{5... | collective-permute-start | bytes 786440 | tf_op jit(solution)/shard_map/ppermute | solution.py:377
  37.8 1.5 %collective-permute-start.9 = (bf16[256,256]{1,0:T(8,128)(2,1)S(1)}, bf16[256,256]{1,0:T(8,128)(2,1)S(1)}, u32[]{:S(2)}, u32[]{:S(2)}) collective-permute-start(bf16[256,256]{1,0:T(8,128)(2,1)S(1)} %get-tuple-element.388), channel_id=1, source_target_pairs={{0,24},{4,28},{8,16},{12,20},{16,8},{20,12},{24,0},{28,4},{1,25},{... | collective-permute-start | bytes 393224 | tf_op jit(solution)/shard_map/ppermute | solution.py:371
  42.3 4.1 %collective-permute-done.9.refs_5_ = bf16[256,256]{1,0:T(8,128)(2,1)S(1)} collective-permute-done((bf16[256,256]{1,0:T(8,128)(2,1)S(1)}, bf16[256,256]{1,0:T(8,128)(2,1)S(1)}, u32[]{:S(2)}, u32[]{:S(2)}) %collective-permute-start.9) | collective-permute-done | bytes 131104 | tf_op jit(solution)/shard_map/ppermute | solution.py:371
  46.9 1.2 %below_rhs.1 = (bf16[512,256]{1,0:T(8,128)(2,1)S(1)}, bf16[512,256]{1,0:T(8,128)(2,1)S(1)}, bf16[512,256]{1,0:T(8,128)(2,1)S(1)}, bf16[512,256]{1,0:T(8,128)(2,1)S(1)}) custom-call(bf16[512,1024]{1,0:T(8,128)(2,1)} %rhs_ref), custom_call_target="tpu_custom_call" | custom-call | flops 100000000 | bytes 3000000 | tf_op jit(solution)/shard_map/below_rhs/pallas_call | solution.py:476
  48.2 3.0 %collective-permute-start.21 = (bf16[512,256]{1,0:T(8,128)(2,1)S(1)}, bf16[512,256]{1,0:T(8,128)(2,1)S(1)}, u32[]{:S(2)}, u32[]{:S(2)}) collective-permute-start(bf16[512,256]{1,0:T(8,128)(2,1)S(1)} %get-tuple-element.406), channel_id=1, source_target_pairs={{0,2},{1,3},{2,0},{3,1},{4,6},{5,7},{6,4},{7,5},{8,10},{9,11},{10,... | collective-permute-start | bytes 786440 | tf_op jit(solution)/shard_map/ppermute | solution.py:374
  52.3 4.1 %pair_solve.4 = (bf16[1024,256]{1,0:T(8,128)(2,1)S(1)}, bf16[512,256]{1,0:T(8,128)(2,1)S(1)}, bf16[256,256]{1,0:T(8,128)(2,1)S(1)}) custom-call(s32[128]{0:T(128)S(1)} %get-tuple-element.389.tab.refs_0_, s32[8]{0:T(128)S(1)} %copy-done.23, bf16[512,256]{1,0:T(8,128)(2,1)S(1)} %get-tuple-element.387.refs_2_, ...), custom_call_target="tpu_custom_call" | custom-call | flops 300000000 | bytes 9000000 | tf_op jit(solution)/shard_map/pair_solve/pallas_call | solution.py:537
  56.4 1.6 %collective-permute-start.19 = (bf16[512,256]{1,0:T(8,128)(2,1)S(1)}, bf16[512,256]{1,0:T(8,128)(2,1)S(1)}, u32[]{:S(2)}, u32[]{:S(2)}) collective-permute-start(bf16[512,256]{1,0:T(8,128)(2,1)S(1)} %get-tuple-element.401.refs_2_), channel_id=1, source_target_pairs={{0,8},{4,20},{8,0},{12,28},{16,24},{20,4},{24,16},{28,12},{1,9},{5... | collective-permute-start | bytes 786440 | tf_op jit(solution)/shard_map/ppermute | solution.py:377
  58.5 1.4 %prep.5 = (bf16[512,512]{1,0:T(8,128)(2,1)S(1)}, f32[512,256]{1,0:T(8,128)S(1)}) custom-call(s32[128]{0:T(128)S(1)} %get-tuple-element.389.tab.refs_0_, bf16[512,512]{1,0:T(8,128)(2,1)S(1)} %factor_pack.1.refs_0_, bf16[512,512]{1,0:T(8,128)(2,1)S(1)} %collective-permute-done.3.refs_1_, bf16[512,512]{1,0:T(8,128)(2,1)S(1)} %collective-permute-done.10.refs_2_, ...), custom_call_target="tpu_custom_call" | custom-call | flops 200000000 | bytes 6000000 | tf_op jit(solution)/shard_map/prep/pallas_call | solution.py:496
  59.9 4.7 %rows_below.3.sums = f32[2048,256]{1,0:T(8,128)S(1)} custom-call(s32[8]{0:T(128)S(1)} %copy-done.23, s32[32,64]{1,0:T(8,128)S(1)} %copy-done.4, bf16[2048,4096]{1,0:T(8,128)(2,1)} %a_ref.7, bf16[1024,256]{1,0:T(8,128)(2,1)S(1)} %get-tuple-element.403.x_ref.refs_10_.x0), custom_call_target="tpu_custom_call" | custom-call | flops 300000000 | bytes 9000000 | tf_op jit(solution)/shard_map/rows_below/pallas_call | solution.py:512
  66.1 1.3 %collective-permute-start.26 = (bf16[512,256]{1,0:T(8,128)(2,1)S(1)}, bf16[512,256]{1,0:T(8,128)(2,1)S(1)}, u32[]{:S(2)}, u32[]{:S(2)}) collective-permute-start(bf16[512,256]{1,0:T(8,128)(2,1)S(1)} %get-tuple-element.419), channel_id=1, source_target_pairs={{0,3},{1,2},{2,1},{3,0},{4,7},{5,6},{6,5},{7,4},{8,11},{9,10},{10,... | collective-permute-start | bytes 786440 | tf_op jit(solution)/shard_map/ppermute | solution.py:374
  67.4 4.3 %pair_solve.5 = (bf16[1024,256]{1,0:T(8,128)(2,1)S(1)}, bf16[512,256]{1,0:T(8,128)(2,1)S(1)}, bf16[256,256]{1,0:T(8,128)(2,1)S(1)}) custom-call(s32[128]{0:T(128)S(1)} %get-tuple-element.389.tab.refs_0_, s32[8]{0:T(128)S(1)} %copy-done.23, bf16[512,256]{1,0:T(8,128)(2,1)S(1)} %get-tuple-element.401.refs_2_, ...), custom_call_target="tpu_custom_call" | custom-call | flops 300000000 | bytes 9000000 | tf_op jit(solution)/shard_map/pair_solve/pallas_call | solution.py:537
  71.7 1.6 %collective-permute-start.24 = (bf16[512,256]{1,0:T(8,128)(2,1)S(1)}, bf16[512,256]{1,0:T(8,128)(2,1)S(1)}, u32[]{:S(2)}, u32[]{:S(2)}) collective-permute-start(bf16[512,256]{1,0:T(8,128)(2,1)S(1)} %get-tuple-element.414.refs_2_), channel_id=1, source_target_pairs={{0,8},{4,20},{8,0},{12,28},{16,24},{20,4},{24,16},{28,12},{1,9},{5... | collective-permute-start | bytes 786440 | tf_op jit(solution)/shard_map/ppermute | solution.py:377
  73.3 1.5 %collective-permute-start.25 = (bf16[256,256]{1,0:T(8,128)(2,1)S(1)}, bf16[256,256]{1,0:T(8,128)(2,1)S(1)}, u32[]{:S(2)}, u32[]{:S(2)}) collective-permute-start(bf16[256,256]{1,0:T(8,128)(2,1)S(1)} %get-tuple-element.415), channel_id=1, source_target_pairs={{0,24},{4,28},{8,16},{12,20},{16,8},{20,12},{24,0},{28,4},{1,25},{... | collective-permute-start | bytes 393224 | tf_op jit(solution)/shard_map/ppermute | solution.py:371
  74.8 1.7 %prep.6 = (bf16[512,512]{1,0:T(8,128)(2,1)S(1)}, f32[512,256]{1,0:T(8,128)S(1)}) custom-call(s32[128]{0:T(128)S(1)} %get-tuple-element.389.tab.refs_0_, bf16[512,512]{1,0:T(8,128)(2,1)S(1)} %factor_pack.1.refs_0_, bf16[512,512]{1,0:T(8,128)(2,1)S(1)} %collective-permute-done.3.refs_1_, bf16[512,512]{1,0:T(8,128)(2,1)S(1)} %collective-permute-done.10.refs_2_, ...), custom_call_target="tpu_custom_call" | custom-call | flops 200000000 | bytes 6000000 | tf_op jit(solution)/shard_map/prep/pallas_call | solution.py:496
  76.5 4.8 %rows_below.4.sums = f32[2048,256]{1,0:T(8,128)S(1)} custom-call(s32[8]{0:T(128)S(1)} %copy-done.23, s32[32,64]{1,0:T(8,128)S(1)} %copy-done.4, bf16[2048,4096]{1,0:T(8,128)(2,1)} %a_ref.7, bf16[1024,256]{1,0:T(8,128)(2,1)S(1)} %get-tuple-element.416.x_ref.refs_11_.x1, f32[2048,256]{1,0:T(8,128)S(1)} %rows_below.3.sums), custom_call_target="tpu_custom_call", output_to_operand_aliasing={{}: (4, {})} | custom-call | flops 300000000 | bytes 9000000 | tf_op jit(solution)/shard_map/rows_below/pallas_call | solution.py:512
  83.7 4.1 %pair_solve.6 = (bf16[1024,256]{1,0:T(8,128)(2,1)S(1)}, bf16[512,256]{1,0:T(8,128)(2,1)S(1)}, bf16[256,256]{1,0:T(8,128)(2,1)S(1)}) custom-call(s32[128]{0:T(128)S(1)} %get-tuple-element.389.tab.refs_0_, s32[8]{0:T(128)S(1)} %copy-done.23, bf16[512,256]{1,0:T(8,128)(2,1)S(1)} %get-tuple-element.414.refs_2_, ...), custom_call_target="tpu_custom_call" | custom-call | flops 300000000 | bytes 9000000 | tf_op jit(solution)/shard_map/pair_solve/pallas_call | solution.py:537
  87.8 1.6 %collective-permute-start.29 = (bf16[512,256]{1,0:T(8,128)(2,1)S(1)}, bf16[512,256]{1,0:T(8,128)(2,1)S(1)}, u32[]{:S(2)}, u32[]{:S(2)}) collective-permute-start(bf16[512,256]{1,0:T(8,128)(2,1)S(1)} %get-tuple-element.427.refs_2_), channel_id=1, source_target_pairs={{0,8},{4,20},{8,0},{12,28},{16,24},{20,4},{24,16},{28,12},{1,9},{5... | collective-permute-start | bytes 786440 | tf_op jit(solution)/shard_map/ppermute | solution.py:377
  90.8 2.9 %last_mask.1.a_ref = bf16[2048,1024]{1,0:T(8,128)(2,1)S(1)} custom-call(s32[8]{0:T(128)S(1)} %copy-done.23, s32[32,64]{1,0:T(8,128)S(1)} %copy-done.4, bf16[2048,4096]{1,0:T(8,128)(2,1)} %a_ref.7), custom_call_target="tpu_custom_call" | custom-call | flops 300000000 | bytes 9000000 | tf_op jit(solution)/shard_map/last_mask/pallas_call | solution.py:464
  93.7 5.2 %rows_below.5.base = f32[2048,256]{1,0:T(8,128)S(1)} custom-call(s32[8]{0:T(128)S(1)} %copy-done.23, s32[32,64]{1,0:T(8,128)S(1)} %copy-done.4, bf16[2048,4096]{1,0:T(8,128)(2,1)} %a_ref.7, bf16[1024,256]{1,0:T(8,128)(2,1)S(1)} %get-tuple-element.430.x_ref.x2, f32[2048,256]{1,0:T(8,128)S(1)} %rows_below.4.sums, ...), custom_call_target="tpu_custom_call", output_to_operand_aliasing={{}: (4, {})} | custom-call | flops 300000000 | bytes 9000000 | tf_op jit(solution)/shard_map/rows_below/pallas_call | solution.py:512
  99.6 1.3 %collective-permute-done.33.refs_6_ = bf16[256,256]{1,0:T(8,128)(2,1)S(1)} collective-permute-done((bf16[256,256]{1,0:T(8,128)(2,1)S(1)}, bf16[256,256]{1,0:T(8,128)(2,1)S(1)}, u32[]{:S(2)}, u32[]{:S(2)}) %collective-permute-start.33) | collective-permute-done | bytes 131104 | tf_op jit(solution)/shard_map/ppermute | solution.py:371
  100.9 3.7 %pair_solve.7.x3 = bf16[1024,256]{1,0:T(8,128)(2,1)S(1)} custom-call(s32[128]{0:T(128)S(1)} %get-tuple-element.389.tab.refs_0_, s32[8]{0:T(128)S(1)} %copy-done.23, bf16[512,256]{1,0:T(8,128)(2,1)S(1)} %get-tuple-element.427.refs_2_, bf16[512,256]{1,0:T(8,128)(2,1)S(1)} %collective-permute-done.29.refs_3_, ...), custom_call_target="tpu_custom_call" | custom-call | flops 300000000 | bytes 9000000 | tf_op jit(solution)/shard_map/pair_solve/pallas_call | solution.py:537
  104.7 3.0 %last_rows.1 = (bf16[4096,256]{1,0:T(8,128)(2,1)}, bf16[2048,256]{1,0:T(8,128)(2,1)}) custom-call(s32[8]{0:T(128)S(1)} %copy-done.23, bf16[2048,1024]{1,0:T(8,128)(2,1)S(1)} %last_mask.1.a_ref, bf16[1024,256]{1,0:T(8,128)(2,1)S(1)} %get-tuple-element.403.x_ref.refs_10_.x0, bf16[1024,256]{1,0:T(8,128)(2,1)S(1)} %get-tuple-element.416.x_ref.refs_11_.x1, ...), custom_call_target="tpu_custom_call" | custom-call | flops 300000000 | bytes 9000000 | tf_op jit(solution)/shard_map/last_rows/pallas_call | solution.py:551
  (64 shorter events, 13.8 us)
Async XLA Ops:
  3.2 36.0 %copy-start.21 = (s32[64,64]{1,0:T(8,128)S(1)}, s32[64,64]{1,0:T(8,128)}, u32[]{:S(2)}) copy-start(s32[64,64]{1,0:T(8,128)} %pattern.11) | copy-start | bytes 49156
  3.2 2.5 %collective-permute-start.3 = (bf16[512,512]{1,0:T(8,128)(2,1)S(1)}, bf16[512,512]{1,0:T(8,128)(2,1)S(1)}, u32[]{:S(2)}, u32[]{:S(2)}) collective-permute-start(bf16[512,512]{1,0:T(8,128)(2,1)S(1)} %factor_pack.1.refs_0_), channel_id=1, source_target_pairs={{0,4},{4,0},{8,12},{12,8},{16,20},{20,16},{24,28},{28,24},{1,5},{5... | collective-permute-start | bytes 1572872 | tf_op jit(solution)/shard_map/ppermute | solution.py:371
  3.8 1.9 %collective-permute-start.4 = (bf16[128,1024]{1,0:T(8,128)(2,1)S(1)}, bf16[128,1024]{1,0:T(8,128)(2,1)S(1)}, u32[]{:S(2)}, u32[]{:S(2)}) collective-permute-start(bf16[128,1024]{1,0:T(8,128)(2,1)S(1)} %copy-done.1), channel_id=1, source_target_pairs={{0,4},{4,0},{8,12},{12,8},{16,20},{20,16},{24,28},{28,24},{1,5},{5... | collective-permute-start | bytes 786440 | tf_op jit(solution)/shard_map/ppermute | solution.py:371
  5.8 17.7 %collective-permute-start.10 = (bf16[512,512]{1,0:T(8,128)(2,1)S(1)}, bf16[512,512]{1,0:T(8,128)(2,1)S(1)}, u32[]{:S(2)}, u32[]{:S(2)}) collective-permute-start(bf16[512,512]{1,0:T(8,128)(2,1)S(1)} %factor_pack.1.refs_0_), channel_id=1, source_target_pairs={{0,8},{4,20},{8,0},{12,28},{16,24},{20,4},{24,16},{28,12},{1,9},{5... | collective-permute-start | bytes 1572872 | tf_op jit(solution)/shard_map/ppermute | solution.py:377
  8.7 14.8 %collective-permute-start.11 = (bf16[512,512]{1,0:T(8,128)(2,1)S(1)}, bf16[512,512]{1,0:T(8,128)(2,1)S(1)}, u32[]{:S(2)}, u32[]{:S(2)}) collective-permute-start(bf16[512,512]{1,0:T(8,128)(2,1)S(1)} %collective-permute-done.3.refs_1_), channel_id=1, source_target_pairs={{0,8},{4,20},{8,0},{12,28},{16,24},{20,4},{24,16},{28,12},{1,9},{5... | collective-permute-start | bytes 1572872 | tf_op jit(solution)/shard_map/ppermute | solution.py:377
  8.8 6.7 %collective-permute-start.5 = (bf16[256,256]{1,0:T(8,128)(2,1)S(1)}, bf16[256,256]{1,0:T(8,128)(2,1)S(1)}, u32[]{:S(2)}, u32[]{:S(2)}) collective-permute-start(bf16[256,256]{1,0:T(8,128)(2,1)S(1)} %get-tuple-element.384), channel_id=1, source_target_pairs={{0,1},{1,0},{2,3},{3,2},{4,5},{5,4},{6,7},{7,6},{8,9},{9,8},{10,11... | collective-permute-start | bytes 393224 | tf_op jit(solution)/shard_map/ppermute | solution.py:374
  10.8 12.7 %collective-permute-start.6 = (bf16[256,256]{1,0:T(8,128)(2,1)S(1)}, bf16[256,256]{1,0:T(8,128)(2,1)S(1)}, u32[]{:S(2)}, u32[]{:S(2)}) collective-permute-start(bf16[256,256]{1,0:T(8,128)(2,1)S(1)} %get-tuple-element.385), channel_id=1, source_target_pairs={{0,2},{1,3},{2,0},{3,1},{4,6},{5,7},{6,4},{7,5},{8,10},{9,11},{10,... | collective-permute-start | bytes 393224 | tf_op jit(solution)/shard_map/ppermute | solution.py:374
  13.4 10.1 %collective-permute-start.7 = (bf16[256,256]{1,0:T(8,128)(2,1)S(1)}, bf16[256,256]{1,0:T(8,128)(2,1)S(1)}, u32[]{:S(2)}, u32[]{:S(2)}) collective-permute-start(bf16[256,256]{1,0:T(8,128)(2,1)S(1)} %get-tuple-element.386), channel_id=1, source_target_pairs={{0,3},{1,2},{2,1},{3,0},{4,7},{5,6},{6,5},{7,4},{8,11},{9,10},{10,... | collective-permute-start | bytes 393224 | tf_op jit(solution)/shard_map/ppermute | solution.py:374
  23.5 14.3 %collective-permute-start.12 = (bf16[512,4096]{1,0:T(8,128)(2,1)S(1)}, bf16[512,4096]{1,0:T(8,128)(2,1)S(1)}, u32[]{:S(2)}, u32[]{:S(2)}) collective-permute-start(bf16[512,4096]{1,0:T(8,128)(2,1)S(1)} %copy-done), channel_id=1, source_target_pairs={{0,4},{4,0},{8,12},{12,8},{16,20},{20,16},{24,28},{28,24},{1,5},{5... | collective-permute-start | bytes 12582920 | tf_op jit(solution)/shard_map/ppermute | solution.py:371
  23.6 9.2 %collective-permute-start.17 = (bf16[512,512]{1,0:T(8,128)(2,1)S(1)}, bf16[512,512]{1,0:T(8,128)(2,1)S(1)}, u32[]{:S(2)}, u32[]{:S(2)}) collective-permute-start(bf16[512,512]{1,0:T(8,128)(2,1)S(1)} %collective-permute-done.10.refs_2_), channel_id=1, source_target_pairs={{0,16},{4,12},{8,24},{12,4},{16,0},{20,28},{24,8},{28,20},{1,17},{... | collective-permute-start | bytes 1572872 | tf_op jit(solution)/shard_map/ppermute | solution.py:380
  25.2 23.0 %collective-permute-start.15 = (bf16[512,512]{1,0:T(8,128)(2,1)S(1)}, bf16[512,512]{1,0:T(8,128)(2,1)S(1)}, u32[]{:S(2)}, u32[]{:S(2)}) collective-permute-start(bf16[512,512]{1,0:T(8,128)(2,1)S(1)} %collective-permute-done.11.refs_3_), channel_id=1, source_target_pairs={{0,4},{4,0},{8,12},{12,8},{16,20},{20,16},{24,28},{28,24},{1,5},{5... | collective-permute-start | bytes 1572872 | tf_op jit(solution)/shard_map/ppermute | solution.py:371
  25.3 26.0 %collective-permute-start.16 = (bf16[512,512]{1,0:T(8,128)(2,1)S(1)}, bf16[512,512]{1,0:T(8,128)(2,1)S(1)}, u32[]{:S(2)}, u32[]{:S(2)}) collective-permute-start(bf16[512,512]{1,0:T(8,128)(2,1)S(1)} %collective-permute-done.10.refs_2_), channel_id=1, source_target_pairs={{0,4},{4,0},{8,12},{12,8},{16,20},{20,16},{24,28},{28,24},{1,5},{5... | collective-permute-start | bytes 1572872 | tf_op jit(solution)/shard_map/ppermute | solution.py:371
  32.8 18.4 %collective-permute-start.18 = (bf16[512,512]{1,0:T(8,128)(2,1)S(1)}, bf16[512,512]{1,0:T(8,128)(2,1)S(1)}, u32[]{:S(2)}, u32[]{:S(2)}) collective-permute-start(bf16[512,512]{1,0:T(8,128)(2,1)S(1)} %collective-permute-done.17.refs_6_), channel_id=1, source_target_pairs={{0,4},{4,0},{8,12},{12,8},{16,20},{20,16},{24,28},{28,24},{1,5},{5... | collective-permute-start | bytes 1572872 | tf_op jit(solution)/shard_map/ppermute | solution.py:371
  36.2 10.2 %collective-permute-start.8 = (bf16[512,256]{1,0:T(8,128)(2,1)S(1)}, bf16[512,256]{1,0:T(8,128)(2,1)S(1)}, u32[]{:S(2)}, u32[]{:S(2)}) collective-permute-start(bf16[512,256]{1,0:T(8,128)(2,1)S(1)} %get-tuple-element.387.refs_2_), channel_id=1, source_target_pairs={{0,8},{4,20},{8,0},{12,28},{16,24},{20,4},{24,16},{28,12},{1,9},{5... | collective-permute-start | bytes 786440 | tf_op jit(solution)/shard_map/ppermute | solution.py:377
  37.8 8.6 %collective-permute-start.9 = (bf16[256,256]{1,0:T(8,128)(2,1)S(1)}, bf16[256,256]{1,0:T(8,128)(2,1)S(1)}, u32[]{:S(2)}, u32[]{:S(2)}) collective-permute-start(bf16[256,256]{1,0:T(8,128)(2,1)S(1)} %get-tuple-element.388), channel_id=1, source_target_pairs={{0,24},{4,28},{8,16},{12,20},{16,8},{20,12},{24,0},{28,4},{1,25},{... | collective-permute-start | bytes 393224 | tf_op jit(solution)/shard_map/ppermute | solution.py:371
  46.4 5.8 %collective-permute-start.13 = (bf16[512,256]{1,0:T(8,128)(2,1)S(1)}, bf16[512,256]{1,0:T(8,128)(2,1)S(1)}, u32[]{:S(2)}, u32[]{:S(2)}) collective-permute-start(bf16[512,256]{1,0:T(8,128)(2,1)S(1)} %collective-permute-done.8.refs_3_), channel_id=1, source_target_pairs={{0,4},{4,0},{8,12},{12,8},{16,20},{20,16},{24,28},{28,24},{1,5},{5... | collective-permute-start | bytes 786440 | tf_op jit(solution)/shard_map/ppermute | solution.py:371
  46.4 5.8 %collective-permute-start.14 = (bf16[256,256]{1,0:T(8,128)(2,1)S(1)}, bf16[256,256]{1,0:T(8,128)(2,1)S(1)}, u32[]{:S(2)}, u32[]{:S(2)}) collective-permute-start(bf16[256,256]{1,0:T(8,128)(2,1)S(1)} %collective-permute-done.9.refs_5_), channel_id=1, source_target_pairs={{0,4},{4,0},{8,12},{12,8},{16,20},{20,16},{24,28},{28,24},{1,5},{5... | collective-permute-start | bytes 393224 | tf_op jit(solution)/shard_map/ppermute | solution.py:371
  48.2 16.4 %collective-permute-start.21 = (bf16[512,256]{1,0:T(8,128)(2,1)S(1)}, bf16[512,256]{1,0:T(8,128)(2,1)S(1)}, u32[]{:S(2)}, u32[]{:S(2)}) collective-permute-start(bf16[512,256]{1,0:T(8,128)(2,1)S(1)} %get-tuple-element.406), channel_id=1, source_target_pairs={{0,2},{1,3},{2,0},{3,1},{4,6},{5,7},{6,4},{7,5},{8,10},{9,11},{10,... | collective-permute-start | bytes 786440 | tf_op jit(solution)/shard_map/ppermute | solution.py:374
  56.4 9.1 %collective-permute-start.19 = (bf16[512,256]{1,0:T(8,128)(2,1)S(1)}, bf16[512,256]{1,0:T(8,128)(2,1)S(1)}, u32[]{:S(2)}, u32[]{:S(2)}) collective-permute-start(bf16[512,256]{1,0:T(8,128)(2,1)S(1)} %get-tuple-element.401.refs_2_), channel_id=1, source_target_pairs={{0,8},{4,20},{8,0},{12,28},{16,24},{20,4},{24,16},{28,12},{1,9},{5... | collective-permute-start | bytes 786440 | tf_op jit(solution)/shard_map/ppermute | solution.py:377
  58.0 7.6 %collective-permute-start.20 = (bf16[256,256]{1,0:T(8,128)(2,1)S(1)}, bf16[256,256]{1,0:T(8,128)(2,1)S(1)}, u32[]{:S(2)}, u32[]{:S(2)}) collective-permute-start(bf16[256,256]{1,0:T(8,128)(2,1)S(1)} %get-tuple-element.402), channel_id=1, source_target_pairs={{0,24},{4,28},{8,16},{12,20},{16,8},{20,12},{24,0},{28,4},{1,25},{... | collective-permute-start | bytes 393224 | tf_op jit(solution)/shard_map/ppermute | solution.py:371
  65.6 1.9 %collective-permute-start.22 = (bf16[512,256]{1,0:T(8,128)(2,1)S(1)}, bf16[512,256]{1,0:T(8,128)(2,1)S(1)}, u32[]{:S(2)}, u32[]{:S(2)}) collective-permute-start(bf16[512,256]{1,0:T(8,128)(2,1)S(1)} %collective-permute-done.19.refs_3_), channel_id=1, source_target_pairs={{0,4},{4,0},{8,12},{12,8},{16,20},{20,16},{24,28},{28,24},{1,5},{5... | collective-permute-start | bytes 786440 | tf_op jit(solution)/shard_map/ppermute | solution.py:371
  65.6 1.9 %collective-permute-start.23 = (bf16[256,256]{1,0:T(8,128)(2,1)S(1)}, bf16[256,256]{1,0:T(8,128)(2,1)S(1)}, u32[]{:S(2)}, u32[]{:S(2)}) collective-permute-start(bf16[256,256]{1,0:T(8,128)(2,1)S(1)} %collective-permute-done.20.refs_5_), channel_id=1, source_target_pairs={{0,4},{4,0},{8,12},{12,8},{16,20},{20,16},{24,28},{28,24},{1,5},{5... | collective-permute-start | bytes 393224 | tf_op jit(solution)/shard_map/ppermute | solution.py:371
  66.1 15.2 %collective-permute-start.26 = (bf16[512,256]{1,0:T(8,128)(2,1)S(1)}, bf16[512,256]{1,0:T(8,128)(2,1)S(1)}, u32[]{:S(2)}, u32[]{:S(2)}) collective-permute-start(bf16[512,256]{1,0:T(8,128)(2,1)S(1)} %get-tuple-element.419), channel_id=1, source_target_pairs={{0,3},{1,2},{2,1},{3,0},{4,7},{5,6},{6,5},{7,4},{8,11},{9,10},{10,... | collective-permute-start | bytes 786440 | tf_op jit(solution)/shard_map/ppermute | solution.py:374
  71.7 10.2 %collective-permute-start.24 = (bf16[512,256]{1,0:T(8,128)(2,1)S(1)}, bf16[512,256]{1,0:T(8,128)(2,1)S(1)}, u32[]{:S(2)}, u32[]{:S(2)}) collective-permute-start(bf16[512,256]{1,0:T(8,128)(2,1)S(1)} %get-tuple-element.414.refs_2_), channel_id=1, source_target_pairs={{0,8},{4,20},{8,0},{12,28},{16,24},{20,4},{24,16},{28,12},{1,9},{5... | collective-permute-start | bytes 786440 | tf_op jit(solution)/shard_map/ppermute | solution.py:377
  73.3 8.6 %collective-permute-start.25 = (bf16[256,256]{1,0:T(8,128)(2,1)S(1)}, bf16[256,256]{1,0:T(8,128)(2,1)S(1)}, u32[]{:S(2)}, u32[]{:S(2)}) collective-permute-start(bf16[256,256]{1,0:T(8,128)(2,1)S(1)} %get-tuple-element.415), channel_id=1, source_target_pairs={{0,24},{4,28},{8,16},{12,20},{16,8},{20,12},{24,0},{28,4},{1,25},{... | collective-permute-start | bytes 393224 | tf_op jit(solution)/shard_map/ppermute | solution.py:371
  82.0 1.7 %collective-permute-start.27 = (bf16[512,256]{1,0:T(8,128)(2,1)S(1)}, bf16[512,256]{1,0:T(8,128)(2,1)S(1)}, u32[]{:S(2)}, u32[]{:S(2)}) collective-permute-start(bf16[512,256]{1,0:T(8,128)(2,1)S(1)} %collective-permute-done.24.refs_3_), channel_id=1, source_target_pairs={{0,4},{4,0},{8,12},{12,8},{16,20},{20,16},{24,28},{28,24},{1,5},{5... | collective-permute-start | bytes 786440 | tf_op jit(solution)/shard_map/ppermute | solution.py:371
  82.0 1.7 %collective-permute-start.28 = (bf16[256,256]{1,0:T(8,128)(2,1)S(1)}, bf16[256,256]{1,0:T(8,128)(2,1)S(1)}, u32[]{:S(2)}, u32[]{:S(2)}) collective-permute-start(bf16[256,256]{1,0:T(8,128)(2,1)S(1)} %collective-permute-done.25.refs_5_), channel_id=1, source_target_pairs={{0,4},{4,0},{8,12},{12,8},{16,20},{20,16},{24,28},{28,24},{1,5},{5... | collective-permute-start | bytes 393224 | tf_op jit(solution)/shard_map/ppermute | solution.py:371
  82.5 11.2 %collective-permute-start.31 = (bf16[512,256]{1,0:T(8,128)(2,1)S(1)}, bf16[512,256]{1,0:T(8,128)(2,1)S(1)}, u32[]{:S(2)}, u32[]{:S(2)}) collective-permute-start(bf16[512,256]{1,0:T(8,128)(2,1)S(1)} %get-tuple-element.436), channel_id=1, source_target_pairs={{0,1},{1,0},{2,3},{3,2},{4,5},{5,4},{6,7},{7,6},{8,9},{9,8},{10,11... | collective-permute-start | bytes 786440 | tf_op jit(solution)/shard_map/ppermute | solution.py:374
  87.8 11.1 %collective-permute-start.29 = (bf16[512,256]{1,0:T(8,128)(2,1)S(1)}, bf16[512,256]{1,0:T(8,128)(2,1)S(1)}, u32[]{:S(2)}, u32[]{:S(2)}) collective-permute-start(bf16[512,256]{1,0:T(8,128)(2,1)S(1)} %get-tuple-element.427.refs_2_), channel_id=1, source_target_pairs={{0,8},{4,20},{8,0},{12,28},{16,24},{20,4},{24,16},{28,12},{1,9},{5... | collective-permute-start | bytes 786440 | tf_op jit(solution)/shard_map/ppermute | solution.py:377
  89.4 9.5 %collective-permute-start.30 = (bf16[256,256]{1,0:T(8,128)(2,1)S(1)}, bf16[256,256]{1,0:T(8,128)(2,1)S(1)}, u32[]{:S(2)}, u32[]{:S(2)}) collective-permute-start(bf16[256,256]{1,0:T(8,128)(2,1)S(1)} %get-tuple-element.432), channel_id=1, source_target_pairs={{0,24},{4,28},{8,16},{12,20},{16,8},{20,12},{24,0},{28,4},{1,25},{... | collective-permute-start | bytes 393224 | tf_op jit(solution)/shard_map/ppermute | solution.py:371
  98.9 2.0 %collective-permute-start.32 = (bf16[512,256]{1,0:T(8,128)(2,1)S(1)}, bf16[512,256]{1,0:T(8,128)(2,1)S(1)}, u32[]{:S(2)}, u32[]{:S(2)}) collective-permute-start(bf16[512,256]{1,0:T(8,128)(2,1)S(1)} %collective-permute-done.29.refs_3_), channel_id=1, source_target_pairs={{0,4},{4,0},{8,12},{12,8},{16,20},{20,16},{24,28},{28,24},{1,5},{5... | collective-permute-start | bytes 786440 | tf_op jit(solution)/shard_map/ppermute | solution.py:371
  99.6 1.3 %collective-permute-start.33 = (bf16[256,256]{1,0:T(8,128)(2,1)S(1)}, bf16[256,256]{1,0:T(8,128)(2,1)S(1)}, u32[]{:S(2)}, u32[]{:S(2)}) collective-permute-start(bf16[256,256]{1,0:T(8,128)(2,1)S(1)} %collective-permute-done.30.refs_5_), channel_id=1, source_target_pairs={{0,4},{4,0},{8,12},{12,8},{16,20},{20,16},{24,28},{28,24},{1,5},{5... | collective-permute-start | bytes 393224 | tf_op jit(solution)/shard_map/ppermute | solution.py:371
  (5 other events, 91.7 us)

commit v6 on v5

--- a/solution.py
+++ b/solution.py
@@ -118,13 +118,12 @@
         out[j * BS:(j + 1) * BS, :] = buf[j * BS:(j + 1) * BS, :] * mask[j:j + 1, :]
 
 
-def rhs_kernel(own_ref, other_ref, *sent):
+def rhs_kernel(rhs_ref, *sent):
     depth = lax.axis_index("rhs")
-    tall, width = own_ref.shape[0], sent[0].shape[1]
+    width = sent[0].shape[1]
     for s, out in enumerate(sent):
         at = pl.multiple_of(jnp.bitwise_xor(depth, s) * width, width)
-        out[0:tall, :] = own_ref[:, pl.ds(at, width)]
-        out[tall:2 * tall, :] = other_ref[:, pl.ds(at, width)]
+        out[...] = rhs_ref[:, pl.ds(at, width)]
 
 
 def table_kernel(owner, order, tab, flag, cnt):
@@ -179,13 +178,13 @@
 
 
 def first_pack_kernel(tab, *refs):
-    pieces, (chip_rhs, p_ref, b_ref) = refs[:4], refs[4:]
+    pieces, (chip_rhs, p_ref, b_ref) = refs[:8], refs[8:]
     depth, core = lax.axis_index("rhs"), lax.axis_index("rows") % 2
-    tall = pieces[0].shape[0] // 2
-    for s in range(4):
-        for side in range(2):
+    tall = pieces[0].shape[0]
+    for side in range(2):
+        for s in range(4):
             at = pl.multiple_of(side * SB * BS + jnp.bitwise_xor(depth, s) * tall, tall)
-            chip_rhs[pl.ds(at, tall), :] = pieces[s][side * tall:(side + 1) * tall, :]
+            chip_rhs[pl.ds(at, tall), :] = pieces[4 * side + s][...]
     for j in range(SB):
         p_ref[j * BS:(j + 1) * BS, :] = chip_rhs[rows_at(tab[PACK + j]), :]
     b_ref[...] = p_ref[pl.ds(pl.multiple_of(core * SB // 2 * BS, SB // 2 * BS), SB // 2 * BS), :]
@@ -215,20 +214,25 @@
 def make_prep_kernel(group):
     last = group == GROUPS - 1
 
-    def kernel(tab, *refs):
+    def kernel(tab, order, diag, *refs):
         l_refs, refs = refs[:8], refs[8:]
         if last:
-            l_out = refs[0]
+            m_out, lbuf = refs
         else:
             w_ref, chip_rhs = refs[:2]
             xs = refs[2:2 + group]
-            l_out, r_out = refs[2 + group:]
+            m_out, r_out, lbuf = refs[2 + group:]
         for i in range(SB):
             code = tab[LSRC + group * SB + i]
             for m in range(8):
                 @pl.when(code // SB == m)
                 def _(m=m, i=i, code=code):
-                    l_out[i * BS:(i + 1) * BS, :] = l_refs[m][rows_at(code % SB), :]
+                    lbuf[i * BS:(i + 1) * BS, :] = l_refs[m][rows_at(code % SB), :]
+        first, second = diag[order[2 * group]], diag[order[2 * group + 1]]
+        m_out[0:SN, 0:SN] = first
+        m_out[SN:PAIR, SN:PAIR] = second
+        joined = jnp.dot(second, lbuf[...], preferred_element_type=F32).astype(BF16)
+        m_out[SN:PAIR, 0:SN] = (-jnp.dot(joined, first, preferred_element_type=F32)).astype(BF16)
         if not last:
             total = jnp.concatenate([chip_rhs[rows_at(tab[PACK + (group + 1) * SB + j]), :] for j in range(SB)], axis=0).astype(F32)
             for k in range(group):
@@ -242,26 +246,19 @@
     last = group == GROUPS - 1
 
     def kernel(*refs):
-        tab, order, sources, d_ref, l_ref = refs[0], refs[1], refs[2:7], refs[7], refs[8]
+        tab, sources, m_ref = refs[0], refs[1:6], refs[6]
         if last:
-            x_ref, panel = refs[9:]
+            x_ref, panel = refs[7:]
         else:
-            r_ref, wn_ref, x_ref, p_ref, b_ref, panel = refs[9:]
-
-        def place(i):
+            r_ref, wn_ref, x_ref, p_ref, b_ref, panel = refs[7:]
+        for i in range(2 * SB):
             code = tab[SRC + group * 16 + i]
             for which, source in enumerate(sources):
                 @pl.when(code // SB == which)
-                def _(source=source):
-                    panel[rows_at(i), :] = source[rows_at(code % SB), :]
-
-        for i in range(2 * SB):
-            place(i)
-        x_a = jnp.dot(d_ref[order[2 * group]], panel[0:SN, :], preferred_element_type=F32).astype(BF16)
-        x_ref[0:SN, :] = x_a
-        rest = panel[SN:PAIR, :].astype(F32) - jnp.dot(l_ref[...], x_a, preferred_element_type=F32)
-        x_b = jnp.dot(d_ref[order[2 * group + 1]], rest.astype(BF16), preferred_element_type=F32).astype(BF16)
-        x_ref[SN:PAIR, :] = x_b
+                def _(source=source, i=i, code=code):
+                    panel[i * BS:(i + 1) * BS, :] = source[rows_at(code % SB), :]
+        x_ref[0:SN, :] = jnp.dot(m_ref[0:SN, 0:SN], panel[0:SN, :], preferred_element_type=F32).astype(BF16)
+        x_ref[SN:PAIR, :] = jnp.dot(m_ref[SN:PAIR, :], panel[...], preferred_element_type=F32).astype(BF16)
         if last:
             return
         total = r_ref[...] - jnp.dot(wn_ref[:, group * PAIR:(group + 1) * PAIR], x_ref[...], preferred_element_type=F32)
@@ -272,65 +269,62 @@
     return kernel
 
 
-def below_part(order, pattern, a_ref, buf, sems, group):
-    tiles = sems.shape[0]
-    tall = buf.shape[0] // tiles
-    copies = []
-    for i in range(tiles):
-        for q in range(2):
-            c = pltpu.make_async_copy(a_ref.at[pl.ds(i * tall, tall), columns_at(order[2 * group + q])],
-                                      buf.at[pl.ds(i * tall, tall), pl.ds(q * SN, SN)], sems.at[i, q])
+def make_below_mask_kernel(tile):
+    def kernel(pattern, a_ref, out, sems):
+        copies = []
+        for j in range(SB):
+            c = pltpu.make_async_copy(a_ref.at[pl.ds((tile * SB + j) * BS, BS), :], out.at[pl.ds(j * BS, BS), :], sems.at[j])
             c.start()
             copies.append(c)
-    spread = spread_matrix()
-    rows = pattern[...]
-    masks = [expand_mask(rows, order[2 * group + q], spread) for q in range(2)]
-    for i in range(tiles):
-        halves = []
-        for q in range(2):
-            copies[2 * i + q].wait()
-            halves.append(jnp.concatenate([buf[j * BS:(j + 1) * BS, q * SN:(q + 1) * SN] * masks[q][j:j + 1, :]
-                                           for j in range(i * tall // BS, (i + 1) * tall // BS)], axis=0))
-        yield slice(i * tall, (i + 1) * tall), jnp.concatenate(halves, axis=1)
-
-
-def last_mask_kernel(order, pattern, a_ref, out, sems):
-    for at, part in below_part(order, pattern, a_ref, out, sems, GROUPS - 1):
-        out[at, :] = part
-
-
-def first_rows_kernel(order, pattern, a_ref, x_ref, out, buf, sems):
-    for at, part in below_part(order, pattern, a_ref, buf, sems, 0):
-        out[at, :] = jnp.dot(part, x_ref[...], preferred_element_type=F32)
-
-
-def next_rows_kernel(order, pattern, a_ref, x_ref, sums, out, buf, sems):
-    for at, part in below_part(order, pattern, a_ref, buf, sems, 1):
-        out[at, :] = sums[at, :] + jnp.dot(part, x_ref[...], preferred_element_type=F32)
-
-
-def base_rows_kernel(order, pattern, a_ref, x_ref, sums, h0, h1, h2, h3, out, buf, sems, rhs):
+        spread = spread_matrix()
+        rows = pattern[tile * SB:(tile + 1) * SB, :]
+        masks = [expand_mask(rows, k, spread) for k in range(NSUP)]
+        for j in range(SB):
+            copies[j].wait()
+            for k in range(NSUP):
+                at = (slice(j * BS, (j + 1) * BS), slice(k * SN, (k + 1) * SN))
+                out[at] = out[at] * masks[k][j:j + 1, :]
+
+    return kernel
+
+
+def below_product(order, a_ref, x_ref, group):
+    first = jnp.dot(a_ref[:, columns_at(order[2 * group])], x_ref[0:SN, :], preferred_element_type=F32)
+    return first + jnp.dot(a_ref[:, columns_at(order[2 * group + 1])], x_ref[SN:PAIR, :], preferred_element_type=F32)
+
+
+def first_rows_kernel(order, a0, a1, a2, a3, x_ref, out):
+    for i, a_ref in enumerate((a0, a1, a2, a3)):
+        out[i * SN:(i + 1) * SN, :] = below_product(order, a_ref, x_ref, 0)
+
+
+def next_rows_kernel(order, a0, a1, a2, a3, x_ref, sums, out):
+    for i, a_ref in enumerate((a0, a1, a2, a3)):
+        at = slice(i * SN, (i + 1) * SN)
+        out[at, :] = sums[at, :] + below_product(order, a_ref, x_ref, 1)
+
+
+def base_rows_kernel(order, a0, a1, a2, a3, x_ref, sums, h0, h1, h2, h3, out, rhs):
     depth = lax.axis_index("rhs")
     tall = h0.shape[0]
     for s, h in enumerate((h0, h1, h2, h3)):
         rhs[pl.ds(pl.multiple_of(jnp.bitwise_xor(depth, s) * tall, tall), tall), :] = h[...]
-    for at, part in below_part(order, pattern, a_ref, buf, sems, 2):
-        out[at, :] = rhs[at, :].astype(F32) - (sums[at, :] + jnp.dot(part, x_ref[...], preferred_element_type=F32))
-
-
-def last_rows_kernel(order, a_ref, x0, x1, x2, x3, base, sol_ref, out_ref, done, sems, osem):
+    for i, a_ref in enumerate((a0, a1, a2, a3)):
+        at = slice(i * SN, (i + 1) * SN)
+        out[at, :] = rhs[at, :].astype(F32) - (sums[at, :] + below_product(order, a_ref, x_ref, 2))
+
+
+def last_rows_kernel(order, a0, a1, a2, a3, x0, x1, x2, x3, base, sol_ref, out_ref, done, sems, osem):
     copies = []
     for k, x in enumerate((x0, x1, x2, x3)):
         for q in range(2):
             at = pl.multiple_of(order[2 * k + q] * SN, SN)
             copies.append(pltpu.make_async_copy(x.at[pl.ds(q * SN, SN), :], sol_ref.at[pl.ds(at, SN), :], sems.at[2 * k + q]))
             copies[-1].start()
-    tiles = osem.shape[0]
-    tall = done.shape[0] // tiles
-    for i in range(tiles):
-        at = slice(i * tall, (i + 1) * tall)
-        done[at, :] = (base[at, :] - jnp.dot(a_ref[at, :], x3[...], preferred_element_type=F32)).astype(BF16)
-        copies.append(pltpu.make_async_copy(done.at[pl.ds(i * tall, tall), :], out_ref.at[pl.ds(i * tall, tall), :], osem.at[i]))
+    for i, a_ref in enumerate((a0, a1, a2, a3)):
+        at = slice(i * SN, (i + 1) * SN)
+        done[at, :] = (base[at, :] - below_product(order, a_ref, x3, GROUPS - 1)).astype(BF16)
+        copies.append(pltpu.make_async_copy(done.at[pl.ds(i * SN, SN), :], out_ref.at[pl.ds(i * SN, SN), :], osem.at[i]))
         copies[-1].start()
     for c in copies:
         c.wait()
@@ -379,10 +373,22 @@
     def forward(x):
         return lax.ppermute(x, "rows", [(i, i ^ (4 if i % 2 == 0 else 2)) for i in range(8)])
 
+    def mask_below(k, after):
+        pattern_later, _ = lax.optimization_barrier((anc_pattern, after))
+        return pl.pallas_call(
+            make_below_mask_kernel(k),
+            out_shape=shape_of((SN, NW)),
+            in_specs=[VMEM, HBM],
+            out_specs=VMEM,
+            scratch_shapes=[pltpu.SemaphoreType.DMA((SB,))],
+            compiler_params=params(4),
+            cost_estimate=cost(2),
+            name="mask_below",
+        )(pattern_later, in_hbm(anc_rows))
+
     columns = rhs_win.shape[1] // 4
     half = SN // 2
     tall = rhs_win.shape[0]
-    rhs_other = swap(rhs_win, 1)
     w_own = in_hbm(win_rows)
     l_own = pl.pallas_call(
         factor_kernel,
@@ -395,21 +401,22 @@
         cost_estimate=cost(2),
         name="factor_pack",
     )(window_owner, sn_order, win_pattern, w_own)
+    near = neighbour(l_own)
     l_other = swap(l_own, 1)
     rhs_late, _ = lax.optimization_barrier((rhs_win, l_own))
     sent = pl.pallas_call(
         rhs_kernel,
-        out_shape=(shape_of((2 * tall, columns)),) * 4,
-        in_specs=[VMEM] * 2,
+        out_shape=(shape_of((tall, columns)),) * 4,
+        in_specs=[VMEM],
         out_specs=(VMEM,) * 4,
         compiler_params=params(4),
         cost_estimate=cost(1),
         name="rhs_pack",
-    )(rhs_late, rhs_other)
-    l_own, l_other, *sent = lax.optimization_barrier((l_own, l_other, *sent))
-    near, near_other = neighbour(l_own), neighbour(l_other)
+    )(rhs_late)
+    l_other, *sent = lax.optimization_barrier((l_other, *sent))
+    near_other = neighbour(l_other)
     pieces = [sent[0]] + [deep(sent[s], s) for s in (1, 2, 3)]
-    owner_later, _ = lax.optimization_barrier((window_owner, l_own))
+    owner_later, _ = lax.optimization_barrier((window_owner, sent[0]))
     tab, flag = pl.pallas_call(
         table_kernel,
         out_shape=(shape_of((TABLE,), jnp.int32), shape_of((2,), jnp.int32)),
@@ -420,24 +427,27 @@
         cost_estimate=cost(3),
         name="tables",
     )(owner_later, sn_order)
+    w_other = swap(win_rows, 1)
+    below = [mask_below(0, sent[0])]
+    tab, w_other, below[0], *pieces = lax.optimization_barrier((tab, w_other, below[0], *pieces))
+    others = [swap(x, 1) for x in pieces]
     chip_rhs, packed, part = pl.pallas_call(
         first_pack_kernel,
         out_shape=(shape_of((PAIR, columns)), shape_of((SN, columns)), shape_of((half, columns))),
-        in_specs=[SMEM] + [VMEM] * 4,
+        in_specs=[SMEM] + [VMEM] * 8,
         out_specs=(VMEM,) * 3,
         compiler_params=params(4),
         cost_estimate=cost(1),
         name="first_pack",
-    )(tab, *pieces)
-    near_late, near_other, w_late, *_ = lax.optimization_barrier((near, near_other, win_rows, *pieces[1:]))
-    far = forward(near_late)
-    l_parts = [in_vmem(x) for x in (l_own, l_other, near, near_other, swap(near_other, 1), swap(near, 1), far, swap(far, 1))]
-    w_other = in_vmem(swap(w_late, 1))
+    )(tab, *pieces, *others)
+    near, near_other, _ = lax.optimization_barrier((near, near_other, packed))
+    far = forward(near)
+    l_parts = [x for x in (l_own, l_other, near, near_other, swap(near_other, 1), swap(near, 1), far)]
+    w_other = in_vmem(w_other)
     w_own = in_vmem(win_rows)
 
     tile = rhs_anc.shape[0]
     sums, solved, masked = None, [], []
-    anc_hbm = in_hbm(anc_rows)
     diag_vmem = in_vmem(diag_inv)
     below_rows = anc_rows.shape[0]
 
@@ -447,6 +457,9 @@
         a_own = neighbour(packed)
         b_own = swap(part, 6)
         if group == 0:
+            far_late, *_ = lax.optimization_barrier((far, a_own, b_own))
+            l_parts = [in_vmem(x) for x in (*l_parts, swap(far_late, 1))]
+            below += [mask_below(k, packed) for k in (1, 2, 3)]
             tab_later, order_later, _ = lax.optimization_barrier((tab, sn_order, packed))
             for k in range(GROUPS - 1):
                 masked.append(pl.pallas_call(
@@ -459,18 +472,6 @@
                     cost_estimate=cost(2),
                     name="mask_rows",
                 )(tab_later, order_later, win_pattern, w_own, w_other))
-        if group == 1:
-            order_later, _ = lax.optimization_barrier((sn_order, packed))
-            last_below = pl.pallas_call(
-                last_mask_kernel,
-                out_shape=shape_of((below_rows, PAIR)),
-                in_specs=[SMEM, VMEM, HBM],
-                out_specs=VMEM,
-                scratch_shapes=[pltpu.SemaphoreType.DMA((4, 2))],
-                compiler_params=params(4),
-                cost_estimate=cost(3),
-                name="last_mask",
-            )(order_later, anc_pattern, anc_hbm)
         if group == 0:
             rhs_later, _ = lax.optimization_barrier((rhs_anc, packed))
             anc_pieces = list(pl.pallas_call(
@@ -488,16 +489,17 @@
             moved, _ = lax.optimization_barrier((anc_pieces[s], packed))
             anc_pieces[s] = deep(moved, s)
 
-        operands = [tab, *l_parts]
-        out_shape = [shape_of((SN, SN))]
+        operands = [tab, sn_order, diag_vmem, *l_parts]
+        out_shape = [shape_of((PAIR, PAIR))]
         if not last:
             operands += [masked[group], chip_rhs, *solved]
             out_shape += [shape_of((SN, columns), F32)]
         ready = pl.pallas_call(
             make_prep_kernel(group),
             out_shape=tuple(out_shape),
-            in_specs=[SMEM] + [VMEM] * (len(operands) - 1),
+            in_specs=[SMEM, SMEM] + [VMEM] * (len(operands) - 2),
             out_specs=(VMEM,) * len(out_shape),
+            scratch_shapes=[pltpu.VMEM((SN, SN), BF16)],
             compiler_params=params(6),
             cost_estimate=cost(2),
             name="prep",
@@ -512,21 +514,19 @@
             sums = pl.pallas_call(
                 kernel,
                 out_shape=shape_of((below_rows, columns), F32),
-                in_specs=[SMEM, VMEM, HBM] + [VMEM] * (1 + len(more)),
+                in_specs=[SMEM] + [VMEM] * (5 + len(more)),
                 out_specs=VMEM,
-                scratch_shapes=[pltpu.VMEM((below_rows, PAIR), BF16), pltpu.SemaphoreType.DMA((4, 2))]
-                + ([pltpu.VMEM((below_rows, columns), BF16)] if k == 2 else []),
-                input_output_aliases={4: 0} if more else {},
-                compiler_params=params(10),
+                scratch_shapes=[pltpu.VMEM((below_rows, columns), BF16)] if k == 2 else [],
+                input_output_aliases={6: 0} if more else {},
+                compiler_params=params(6),
                 cost_estimate=cost(3),
                 name="rows_below",
-            )(sn_order, anc_pattern, anc_hbm, solved[k], *more)
-            if k == 2:
-                a_own, last_below = lax.optimization_barrier((a_own, last_below))
+            )(sn_order, *below, solved[k], *more)
             a_own, b_own, sums, previous, *ready = lax.optimization_barrier((a_own, b_own, sums, previous, *ready))
             anc_pieces[anc_order[k]] = previous
         else:
-            a_own, b_own, *masked = lax.optimization_barrier((a_own, b_own, *masked))
+            a_own, b_own, below[1], below[2], below[3], *masked = lax.optimization_barrier(
+                (a_own, b_own, below[1], below[2], below[3], *masked))
         a_swap = swap(a_own, 1)
         b_swap = swap(b_own, 1)
         ready = list(ready) if last else list(ready) + [masked[group]]
@@ -537,13 +537,13 @@
         results = pl.pallas_call(
             make_solve_kernel(group),
             out_shape=tuple(out_shape),
-            in_specs=[SMEM, SMEM] + [VMEM] * (6 + len(ready)),
+            in_specs=[SMEM] + [VMEM] * (5 + len(ready)),
             out_specs=(VMEM,) * len(out_shape),
             scratch_shapes=[pltpu.VMEM((PAIR, columns), BF16)],
             compiler_params=params(8),
             cost_estimate=cost(3),
             name="pair_solve",
-        )(tab, sn_order, packed, a_own, a_swap, b_own, b_swap, diag_vmem, *ready)
+        )(tab, packed, a_own, a_swap, b_own, b_swap, *ready)
         solved.append(results[0])
         if not last:
             packed, part = results[1:]
@@ -551,19 +551,19 @@
     outputs = pl.pallas_call(
         last_rows_kernel,
         out_shape=(shape_of((NW, columns)), shape_of((below_rows, columns))),
-        in_specs=[SMEM] + [VMEM] * 6,
+        in_specs=[SMEM] + [VMEM] * 9,
         out_specs=(HBM, HBM),
         scratch_shapes=[pltpu.VMEM((below_rows, columns), BF16), pltpu.SemaphoreType.DMA((2 * GROUPS,)),
                         pltpu.SemaphoreType.DMA((4,))],
         compiler_params=params(6),
         cost_estimate=cost(3),
         name="last_rows",
-    )(sn_order, last_below, *solved, sums)
+    )(sn_order, *below, *solved, sums)
 
     def again(carry):
         carry, own_pieces, below_pieces = lax.optimization_barrier((carry, pieces, anc_pieces))
         back = carry[0][1] ^ jnp.arange(4)
-        win_rhs = jnp.take(jnp.stack([x[:tall] for x in own_pieces]), back, axis=0).reshape(4 * tall, columns)
+        win_rhs = jnp.take(jnp.stack(own_pieces), back, axis=0).reshape(4 * tall, columns)
         anc_rhs = jnp.take(jnp.stack(below_pieces), back, axis=0).reshape(4 * tile, columns)
         return jnp.zeros_like(carry[0]), *general_path(
             win_rows, anc_rows, win_pattern, anc_pattern, window_owner, sn_order, diag_inv, win_rhs, anc_rhs)

time: 109 us -> 106 us (0.972)
  Pallas kernels: 52.2 us -> 45.1 us
  starting transfers between devices: 27.2 us -> 33.2 us
  waiting for transfers between devices: 27.3 us -> 25 us
    ppermute x18 -> x21, waiting for transfers between devices: 10 us -> 20.9 us  [swap(): return lax.ppermute(x, 'rows', [(i, i ^ m) for i in range(8)])]
    pallas_call x3, Pallas kernels: 14.7 us -> 5.86 us  [local(): pl.pallas_call(kernel, out_shape=shape_of((below_rows, columns), F32), in...]
    pallas_call x4, Pallas kernels: 16.3 us -> 8.85 us  [local(): pl.pallas_call(make_solve_kernel(group), out_shape=tuple(out_shape), in_s...]
    ppermute x6, waiting for transfers between devices: 10.1 us -> 2.95 us  [deep(): return lax.ppermute(x, 'rhs', [(i, i ^ m) for i in range(4)])]
    pallas_call x2 -> x5, Pallas kernels: 2.93 us -> 9.21 us  [the longest x4 9.18 us: mask_below(): pl.pallas_call(make_below_mask_kernel(k), out_shape=shape_of((SN, NW)), i...]
    ppermute x1, waiting for transfers between devices: 7.15 us -> 1.18 us  [forward(): lax.ppermute(x, 'rows', [(i, i ^ (4 if i % 2 == 0 else 2)) for i in range...]
    ppermute x6, starting transfers between devices: 9.01 us -> 12.3 us  [deep(): return lax.ppermute(x, 'rhs', [(i, i ^ m) for i in range(4)])]
    pallas_call x4, Pallas kernels: 5.13 us -> 8.18 us  [local(): pl.pallas_call(make_prep_kernel(group), out_shape=tuple(out_shape), in_sp...]
  transfers between devices with their start and end apart: 31 -> 34, of which waited for: 9 -> 13; matrix products, arithmetic and copies ran while one was open for 0% -> 0% of each run, Pallas kernels for 39% -> 38%
where the time goes in v6:
time: 106 us
  Pallas kernels  45.1 us (43%)
  starting transfers between devices  33.2 us (31%)
  waiting for transfers between devices  25 us (24%)
  between operations  1.19 us (1%)
    ppermute x21, waiting for transfers between devices, swap(): return lax.ppermute(x, 'rows', [(i, i ^ m) for i in range(8)])  20.9 us
    ppermute x6, starting transfers between devices, deep(): return lax.ppermute(x, 'rhs', [(i, i ^ m) for i in range(4)])  12.3 us
    ppermute x6, starting transfers between devices, neighbour(): lax.ppermute(x, 'rows', [(i, i ^ (2 if i % 2 == 0 else 4)) for i in range...  10.1 us
    ppermute x21, starting transfers between devices, swap(): return lax.ppermute(x, 'rows', [(i, i ^ m) for i in range(8)])  9.92 us
    pallas_call x4, Pallas kernels, mask_below(): pl.pallas_call(make_below_mask_kernel(k), out_shape=shape_of((SN, NW)), i...  9.18 us
    pallas_call x4, Pallas kernels, local(): pl.pallas_call(make_solve_kernel(group), out_shape=tuple(out_shape), in_s...  8.85 us
    pallas_call x4, Pallas kernels, local(): pl.pallas_call(make_prep_kernel(group), out_shape=tuple(out_shape), in_sp...  8.18 us
    pallas_call x3, Pallas kernels, local(): pl.pallas_call(kernel, out_shape=shape_of((below_rows, columns), F32), in...  5.86 us
  transfers between devices with their start and end apart: 34, of which 13 were waited for; matrix products, arithmetic and copies ran while one was open for 0% of the time, Pallas kernels for 38%

profile of v6, /device:TPU:0, one launch (start us, length us, event | category | flops | bytes accessed | tf_op | source)
XLA Modules:
  0.0 106.1 jit_solution(785532557486707164)
XLA Ops:
  1.2 2.4 %factor_pack.1.refs_0_ = bf16[512,512]{1,0:T(8,128)(2,1)S(1)} custom-call(s32[64]{0:T(128)} %owner.2, s32[8]{0:T(128)} %order.22, s32[64,64]{1,0:T(8,128)} %pattern.11, bf16[512,4096]{1,0:T(8,128)(2,1)} %w_own.5), custom_call_target="tpu_custom_call" | custom-call | flops 200000000 | bytes 6000000 | tf_op jit(solution)/shard_map/factor_pack/pallas_call | solution.py:393
  3.7 2.9 %collective-permute-start.16 = (bf16[512,512]{1,0:T(8,128)(2,1)S(1)}, bf16[512,512]{1,0:T(8,128)(2,1)S(1)}, u32[]{:S(2)}, u32[]{:S(2)}) collective-permute-start(bf16[512,512]{1,0:T(8,128)(2,1)S(1)} %factor_pack.1.refs_0_), channel_id=1, source_target_pairs={{0,8},{4,20},{8,0},{12,28},{16,24},{20,4},{24,16},{28,12},{1,9},{5... | collective-permute-start | bytes 1572872 | tf_op jit(solution)/shard_map/ppermute | solution.py:371
  6.7 2.0 %collective-permute-done.3.refs_1_ = bf16[512,512]{1,0:T(8,128)(2,1)S(1)} collective-permute-done((bf16[512,512]{1,0:T(8,128)(2,1)S(1)}, bf16[512,512]{1,0:T(8,128)(2,1)S(1)}, u32[]{:S(2)}, u32[]{:S(2)}) %collective-permute-start.3) | collective-permute-done | bytes 524320 | tf_op jit(solution)/shard_map/ppermute | solution.py:365
  8.7 2.9 %collective-permute-start.17 = (bf16[512,512]{1,0:T(8,128)(2,1)S(1)}, bf16[512,512]{1,0:T(8,128)(2,1)S(1)}, u32[]{:S(2)}, u32[]{:S(2)}) collective-permute-start(bf16[512,512]{1,0:T(8,128)(2,1)S(1)} %collective-permute-done.3.refs_1_), channel_id=1, source_target_pairs={{0,8},{4,20},{8,0},{12,28},{16,24},{20,4},{24,16},{28,12},{1,9},{5... | collective-permute-start | bytes 1572872 | tf_op jit(solution)/shard_map/ppermute | solution.py:371
  11.6 1.6 %collective-permute-start.5 = (bf16[128,256]{1,0:T(8,128)(2,1)S(1)}, bf16[128,256]{1,0:T(8,128)(2,1)S(1)}, u32[]{:S(2)}, u32[]{:S(2)}) collective-permute-start(bf16[128,256]{1,0:T(8,128)(2,1)S(1)} %get-tuple-element.392), channel_id=1, source_target_pairs={{0,1},{1,0},{2,3},{3,2},{4,5},{5,4},{6,7},{7,6},{8,9},{9,8},{10,11... | collective-permute-start | bytes 196616 | tf_op jit(solution)/shard_map/ppermute | solution.py:368
  13.1 2.6 %collective-permute-start.6 = (bf16[128,256]{1,0:T(8,128)(2,1)S(1)}, bf16[128,256]{1,0:T(8,128)(2,1)S(1)}, u32[]{:S(2)}, u32[]{:S(2)}) collective-permute-start(bf16[128,256]{1,0:T(8,128)(2,1)S(1)} %get-tuple-element.393), channel_id=1, source_target_pairs={{0,2},{1,3},{2,0},{3,1},{4,6},{5,7},{6,4},{7,5},{8,10},{9,11},{10,... | collective-permute-start | bytes 196616 | tf_op jit(solution)/shard_map/ppermute | solution.py:368
  15.8 4.3 %collective-permute-start.7 = (bf16[128,256]{1,0:T(8,128)(2,1)S(1)}, bf16[128,256]{1,0:T(8,128)(2,1)S(1)}, u32[]{:S(2)}, u32[]{:S(2)}) collective-permute-start(bf16[128,256]{1,0:T(8,128)(2,1)S(1)} %get-tuple-element.394), channel_id=1, source_target_pairs={{0,3},{1,2},{2,1},{3,0},{4,7},{5,6},{6,5},{7,4},{8,11},{9,10},{10,... | collective-permute-start | bytes 196616 | tf_op jit(solution)/shard_map/ppermute | solution.py:368
  20.1 2.3 %mask_below.4.a0 = bf16[512,4096]{1,0:T(8,128)(2,1)S(1)} custom-call(s32[32,64]{1,0:T(8,128)S(1)} %copy-done.5, bf16[2048,4096]{1,0:T(8,128)(2,1)} %a_ref.7), custom_call_target="tpu_custom_call" | custom-call | flops 200000000 | bytes 6000000 | tf_op jit(solution)/shard_map/mask_below/pallas_call | solution.py:378
  22.4 2.8 %tables.1 = (s32[128]{0:T(128)S(1)}, s32[2]{0:T(128)}) custom-call(s32[64]{0:T(128)S(1)} %copy-done.21, s32[8]{0:T(128)S(1)} %copy-done.22), custom_call_target="tpu_custom_call" | custom-call | flops 300000000 | bytes 9000000 | tf_op jit(solution)/shard_map/tables/pallas_call | solution.py:420
  30.5 1.5 %collective-permute-start.13 = (bf16[256,256]{1,0:T(8,128)(2,1)S(1)}, bf16[256,256]{1,0:T(8,128)(2,1)S(1)}, u32[]{:S(2)}, u32[]{:S(2)}) collective-permute-start(bf16[256,256]{1,0:T(8,128)(2,1)S(1)} %get-tuple-element.402), channel_id=1, source_target_pairs={{0,24},{4,28},{8,16},{12,20},{16,8},{20,12},{24,0},{28,4},{1,25},{... | collective-permute-start | bytes 393224 | tf_op jit(solution)/shard_map/ppermute | solution.py:365
  32.5 9.6 %collective-permute-done.13.refs_4_ = bf16[256,256]{1,0:T(8,128)(2,1)S(1)} collective-permute-done((bf16[256,256]{1,0:T(8,128)(2,1)S(1)}, bf16[256,256]{1,0:T(8,128)(2,1)S(1)}, u32[]{:S(2)}, u32[]{:S(2)}) %collective-permute-start.13) | collective-permute-done | bytes 131104 | tf_op jit(solution)/shard_map/ppermute | solution.py:365
  43.3 2.3 %mask_below.5.a1 = bf16[512,4096]{1,0:T(8,128)(2,1)S(1)} custom-call(s32[32,64]{1,0:T(8,128)S(1)} %copy-done.5, bf16[2048,4096]{1,0:T(8,128)(2,1)} %a_ref.7), custom_call_target="tpu_custom_call" | custom-call | flops 200000000 | bytes 6000000 | tf_op jit(solution)/shard_map/mask_below/pallas_call | solution.py:378
  45.6 2.3 %mask_below.6.a2 = bf16[512,4096]{1,0:T(8,128)(2,1)S(1)} custom-call(s32[32,64]{1,0:T(8,128)S(1)} %copy-done.5, bf16[2048,4096]{1,0:T(8,128)(2,1)} %a_ref.7), custom_call_target="tpu_custom_call" | custom-call | flops 200000000 | bytes 6000000 | tf_op jit(solution)/shard_map/mask_below/pallas_call | solution.py:378
  47.9 2.4 %mask_below.7.a3 = bf16[512,4096]{1,0:T(8,128)(2,1)S(1)} custom-call(s32[32,64]{1,0:T(8,128)S(1)} %copy-done.5, bf16[2048,4096]{1,0:T(8,128)(2,1)} %a_ref.7), custom_call_target="tpu_custom_call" | custom-call | flops 200000000 | bytes 6000000 | tf_op jit(solution)/shard_map/mask_below/pallas_call | solution.py:378
  56.3 1.7 %prep.4 = (bf16[1024,1024]{1,0:T(8,128)(2,1)S(1)}, f32[512,256]{1,0:T(8,128)S(1)}) custom-call(s32[128]{0:T(128)S(1)} %get-tuple-element.404.tab.refs_0_, s32[8]{0:T(128)S(1)} %copy-done.22, bf16[8,512,512]{2,1,0:T(8,128)(2,1)S(1)} %copy-done.1, bf16[512,512]{1,0:T(8,128)(2,1)S(1)} %factor_pack.1.refs_0_, ...), custom_call_target="tpu_custom_call" | custom-call | flops 200000000 | bytes 6000000 | tf_op jit(solution)/shard_map/prep/pallas_call | solution.py:497
  58.0 2.3 %pair_solve.4 = (bf16[1024,256]{1,0:T(8,128)(2,1)S(1)}, bf16[512,256]{1,0:T(8,128)(2,1)S(1)}, bf16[256,256]{1,0:T(8,128)(2,1)S(1)}) custom-call(s32[128]{0:T(128)S(1)} %get-tuple-element.404.tab.refs_0_, bf16[512,256]{1,0:T(8,128)(2,1)S(1)} %get-tuple-element.401.refs_1_, bf16[512,256]{1,0:T(8,128)(2,1)S(1)} %collective-permute-done.12.refs_2_, ...), custom_call_target="tpu_custom_call" | custom-call | flops 300000000 | bytes 9000000 | tf_op jit(solution)/shard_map/pair_solve/pallas_call | solution.py:537
  62.7 2.5 %prep.5 = (bf16[1024,1024]{1,0:T(8,128)(2,1)S(1)}, f32[512,256]{1,0:T(8,128)S(1)}) custom-call(s32[128]{0:T(128)S(1)} %get-tuple-element.404.tab.refs_0_, s32[8]{0:T(128)S(1)} %copy-done.22, bf16[8,512,512]{2,1,0:T(8,128)(2,1)S(1)} %copy-done.1, bf16[512,512]{1,0:T(8,128)(2,1)S(1)} %factor_pack.1.refs_0_, ...), custom_call_target="tpu_custom_call" | custom-call | flops 200000000 | bytes 6000000 | tf_op jit(solution)/shard_map/prep/pallas_call | solution.py:497
  65.3 1.8 %rows_below.3.sums = f32[2048,256]{1,0:T(8,128)S(1)} custom-call(s32[8]{0:T(128)S(1)} %copy-done.22, bf16[512,4096]{1,0:T(8,128)(2,1)S(1)} %mask_below.4.a0, bf16[512,4096]{1,0:T(8,128)(2,1)S(1)} %mask_below.5.a1, bf16[512,4096]{1,0:T(8,128)(2,1)S(1)} %mask_below.6.a2, bf16[512,4096]{1,0:T(8,128)(2,1)S(1)} %mask_below.7.a3, ...), custom_call_target="tpu_custom_call" | custom-call | flops 300000000 | bytes 9000000 | tf_op jit(solution)/shard_map/rows_below/pallas_call | solution.py:514
  67.1 2.6 %collective-permute-done.24.h2 = bf16[512,256]{1,0:T(8,128)(2,1)S(1)} collective-permute-done((bf16[512,256]{1,0:T(8,128)(2,1)S(1)}, bf16[512,256]{1,0:T(8,128)(2,1)S(1)}, u32[]{:S(2)}, u32[]{:S(2)}) %collective-permute-start.24) | collective-permute-done | bytes 262176 | tf_op jit(solution)/shard_map/ppermute | solution.py:368
  70.4 2.5 %collective-permute-start.29 = (bf16[512,256]{1,0:T(8,128)(2,1)S(1)}, bf16[512,256]{1,0:T(8,128)(2,1)S(1)}, u32[]{:S(2)}, u32[]{:S(2)}) collective-permute-start(bf16[512,256]{1,0:T(8,128)(2,1)S(1)} %get-tuple-element.438), channel_id=1, source_target_pairs={{0,3},{1,2},{2,1},{3,0},{4,7},{5,6},{6,5},{7,4},{8,11},{9,10},{10,... | collective-permute-start | bytes 786440 | tf_op jit(solution)/shard_map/ppermute | solution.py:368
  72.9 2.3 %pair_solve.5 = (bf16[1024,256]{1,0:T(8,128)(2,1)S(1)}, bf16[512,256]{1,0:T(8,128)(2,1)S(1)}, bf16[256,256]{1,0:T(8,128)(2,1)S(1)}) custom-call(s32[128]{0:T(128)S(1)} %get-tuple-element.404.tab.refs_0_, bf16[512,256]{1,0:T(8,128)(2,1)S(1)} %get-tuple-element.421.refs_1_, bf16[512,256]{1,0:T(8,128)(2,1)S(1)} %collective-permute-done.22.refs_2_, ...), custom_call_target="tpu_custom_call" | custom-call | flops 300000000 | bytes 9000000 | tf_op jit(solution)/shard_map/pair_solve/pallas_call | solution.py:537
  76.2 1.3 %collective-permute-start.28 = (bf16[256,256]{1,0:T(8,128)(2,1)S(1)}, bf16[256,256]{1,0:T(8,128)(2,1)S(1)}, u32[]{:S(2)}, u32[]{:S(2)}) collective-permute-start(bf16[256,256]{1,0:T(8,128)(2,1)S(1)} %get-tuple-element.435), channel_id=1, source_target_pairs={{0,24},{4,28},{8,16},{12,20},{16,8},{20,12},{24,0},{28,4},{1,25},{... | collective-permute-start | bytes 393224 | tf_op jit(solution)/shard_map/ppermute | solution.py:365
  77.6 2.2 %prep.6 = (bf16[1024,1024]{1,0:T(8,128)(2,1)S(1)}, f32[512,256]{1,0:T(8,128)S(1)}) custom-call(s32[128]{0:T(128)S(1)} %get-tuple-element.404.tab.refs_0_, s32[8]{0:T(128)S(1)} %copy-done.22, bf16[8,512,512]{2,1,0:T(8,128)(2,1)S(1)} %copy-done.1, bf16[512,512]{1,0:T(8,128)(2,1)S(1)} %factor_pack.1.refs_0_, ...), custom_call_target="tpu_custom_call" | custom-call | flops 200000000 | bytes 6000000 | tf_op jit(solution)/shard_map/prep/pallas_call | solution.py:497
  79.8 1.9 %rows_below.4.sums = f32[2048,256]{1,0:T(8,128)S(1)} custom-call(s32[8]{0:T(128)S(1)} %copy-done.22, bf16[512,4096]{1,0:T(8,128)(2,1)S(1)} %mask_below.4.a0, bf16[512,4096]{1,0:T(8,128)(2,1)S(1)} %mask_below.5.a1, bf16[512,4096]{1,0:T(8,128)(2,1)S(1)} %mask_below.6.a2, bf16[512,4096]{1,0:T(8,128)(2,1)S(1)} %mask_below.7.a3, ...), custom_call_target="tpu_custom_call", output_to_operand_aliasing={{}: (6, {})} | custom-call | flops 300000000 | bytes 9000000 | tf_op jit(solution)/shard_map/rows_below/pallas_call | solution.py:514
  81.7 3.0 %collective-permute-done.28.refs_4_ = bf16[256,256]{1,0:T(8,128)(2,1)S(1)} collective-permute-done((bf16[256,256]{1,0:T(8,128)(2,1)S(1)}, bf16[256,256]{1,0:T(8,128)(2,1)S(1)}, u32[]{:S(2)}, u32[]{:S(2)}) %collective-permute-start.28) | collective-permute-done | bytes 131104 | tf_op jit(solution)/shard_map/ppermute | solution.py:365
  86.5 2.3 %pair_solve.6 = (bf16[1024,256]{1,0:T(8,128)(2,1)S(1)}, bf16[512,256]{1,0:T(8,128)(2,1)S(1)}, bf16[256,256]{1,0:T(8,128)(2,1)S(1)}) custom-call(s32[128]{0:T(128)S(1)} %get-tuple-element.404.tab.refs_0_, bf16[512,256]{1,0:T(8,128)(2,1)S(1)} %get-tuple-element.434.refs_1_, bf16[512,256]{1,0:T(8,128)(2,1)S(1)} %collective-permute-done.27.refs_2_, ...), custom_call_target="tpu_custom_call" | custom-call | flops 300000000 | bytes 9000000 | tf_op jit(solution)/shard_map/pair_solve/pallas_call | solution.py:537
  89.9 1.6 %collective-permute-start.33 = (bf16[256,256]{1,0:T(8,128)(2,1)S(1)}, bf16[256,256]{1,0:T(8,128)(2,1)S(1)}, u32[]{:S(2)}, u32[]{:S(2)}) collective-permute-start(bf16[256,256]{1,0:T(8,128)(2,1)S(1)} %get-tuple-element.448), channel_id=1, source_target_pairs={{0,24},{4,28},{8,16},{12,20},{16,8},{20,12},{24,0},{28,4},{1,25},{... | collective-permute-start | bytes 393224 | tf_op jit(solution)/shard_map/ppermute | solution.py:365
  91.5 1.7 %prep.7.refs_6_ = bf16[1024,1024]{1,0:T(8,128)(2,1)S(1)} custom-call(s32[128]{0:T(128)S(1)} %get-tuple-element.404.tab.refs_0_, s32[8]{0:T(128)S(1)} %copy-done.22, bf16[8,512,512]{2,1,0:T(8,128)(2,1)S(1)} %copy-done.1, bf16[512,512]{1,0:T(8,128)(2,1)S(1)} %factor_pack.1.refs_0_, bf16[512,512]{1,0:T(8,128)(2,1)S(1)} %collective-permute-done.3.refs_1_, ...), custom_call_target="tpu_custom_call" | custom-call | flops 200000000 | bytes 6000000 | tf_op jit(solution)/shard_map/prep/pallas_call | solution.py:497
  93.4 2.1 %rows_below.5.base = f32[2048,256]{1,0:T(8,128)S(1)} custom-call(s32[8]{0:T(128)S(1)} %copy-done.22, bf16[512,4096]{1,0:T(8,128)(2,1)S(1)} %mask_below.4.a0, bf16[512,4096]{1,0:T(8,128)(2,1)S(1)} %mask_below.5.a1, bf16[512,4096]{1,0:T(8,128)(2,1)S(1)} %mask_below.6.a2, bf16[512,4096]{1,0:T(8,128)(2,1)S(1)} %mask_below.7.a3, ...), custom_call_target="tpu_custom_call", output_to_operand_aliasing={{}: (6, {})} | custom-call | flops 300000000 | bytes 9000000 | tf_op jit(solution)/shard_map/rows_below/pallas_call | solution.py:514
  95.6 3.1 %collective-permute-done.33.refs_4_ = bf16[256,256]{1,0:T(8,128)(2,1)S(1)} collective-permute-done((bf16[256,256]{1,0:T(8,128)(2,1)S(1)}, bf16[256,256]{1,0:T(8,128)(2,1)S(1)}, u32[]{:S(2)}, u32[]{:S(2)}) %collective-permute-start.33) | collective-permute-done | bytes 131104 | tf_op jit(solution)/shard_map/ppermute | solution.py:365
  100.4 1.9 %pair_solve.7.x3 = bf16[1024,256]{1,0:T(8,128)(2,1)S(1)} custom-call(s32[128]{0:T(128)S(1)} %get-tuple-element.404.tab.refs_0_, bf16[512,256]{1,0:T(8,128)(2,1)S(1)} %get-tuple-element.447.refs_1_, bf16[512,256]{1,0:T(8,128)(2,1)S(1)} %collective-permute-done.32.refs_2_, bf16[512,256]{1,0:T(8,128)(2,1)S(1)} %collective-permute-done.35.refs_3_, ...), custom_call_target="tpu_custom_call" | custom-call | flops 300000000 | bytes 9000000 | tf_op jit(solution)/shard_map/pair_solve/pallas_call | solution.py:537
  102.3 3.0 %last_rows.1 = (bf16[4096,256]{1,0:T(8,128)(2,1)}, bf16[2048,256]{1,0:T(8,128)(2,1)}) custom-call(s32[8]{0:T(128)S(1)} %copy-done.22, bf16[512,4096]{1,0:T(8,128)(2,1)S(1)} %mask_below.4.a0, bf16[512,4096]{1,0:T(8,128)(2,1)S(1)} %mask_below.5.a1, bf16[512,4096]{1,0:T(8,128)(2,1)S(1)} %mask_below.6.a2, bf16[512,4096]{1,0:T(8,128)(2,1)S(1)} %mask_below.7.a3, ...), custom_call_target="tpu_custom_call" | custom-call | flops 300000000 | bytes 9000000 | tf_op jit(solution)/shard_map/last_rows/pallas_call | solution.py:551
  (75 shorter events, 23.3 us)
Async XLA Ops:
  0.6 24.6 %collective-permute-start.4 = (bf16[512,4096]{1,0:T(8,128)(2,1)}, bf16[512,4096]{1,0:T(8,128)(2,1)S(1)}, u32[]{:S(2)}, u32[]{:S(2)}) collective-permute-start(bf16[512,4096]{1,0:T(8,128)(2,1)} %w_own.5), channel_id=1, source_target_pairs={{0,4},{4,0},{8,12},{12,8},{16,20},{20,16},{24,28},{28,24},{1,5},{5... | collective-permute-start | bytes 12582920 | tf_op jit(solution)/shard_map/ppermute | solution.py:365
  3.6 5.1 %collective-permute-start.3 = (bf16[512,512]{1,0:T(8,128)(2,1)S(1)}, bf16[512,512]{1,0:T(8,128)(2,1)S(1)}, u32[]{:S(2)}, u32[]{:S(2)}) collective-permute-start(bf16[512,512]{1,0:T(8,128)(2,1)S(1)} %factor_pack.1.refs_0_), channel_id=1, source_target_pairs={{0,4},{4,0},{8,12},{12,8},{16,20},{20,16},{24,28},{28,24},{1,5},{5... | collective-permute-start | bytes 1572872 | tf_op jit(solution)/shard_map/ppermute | solution.py:365
  3.7 24.7 %collective-permute-start.16 = (bf16[512,512]{1,0:T(8,128)(2,1)S(1)}, bf16[512,512]{1,0:T(8,128)(2,1)S(1)}, u32[]{:S(2)}, u32[]{:S(2)}) collective-permute-start(bf16[512,512]{1,0:T(8,128)(2,1)S(1)} %factor_pack.1.refs_0_), channel_id=1, source_target_pairs={{0,8},{4,20},{8,0},{12,28},{16,24},{20,4},{24,16},{28,12},{1,9},{5... | collective-permute-start | bytes 1572872 | tf_op jit(solution)/shard_map/ppermute | solution.py:371
  8.7 19.7 %collective-permute-start.17 = (bf16[512,512]{1,0:T(8,128)(2,1)S(1)}, bf16[512,512]{1,0:T(8,128)(2,1)S(1)}, u32[]{:S(2)}, u32[]{:S(2)}) collective-permute-start(bf16[512,512]{1,0:T(8,128)(2,1)S(1)} %collective-permute-done.3.refs_1_), channel_id=1, source_target_pairs={{0,8},{4,20},{8,0},{12,28},{16,24},{20,4},{24,16},{28,12},{1,9},{5... | collective-permute-start | bytes 1572872 | tf_op jit(solution)/shard_map/ppermute | solution.py:371
  11.6 4.3 %collective-permute-start.5 = (bf16[128,256]{1,0:T(8,128)(2,1)S(1)}, bf16[128,256]{1,0:T(8,128)(2,1)S(1)}, u32[]{:S(2)}, u32[]{:S(2)}) collective-permute-start(bf16[128,256]{1,0:T(8,128)(2,1)S(1)} %get-tuple-element.392), channel_id=1, source_target_pairs={{0,1},{1,0},{2,3},{3,2},{4,5},{5,4},{6,7},{7,6},{8,9},{9,8},{10,11... | collective-permute-start | bytes 196616 | tf_op jit(solution)/shard_map/ppermute | solution.py:368
  13.1 12.0 %collective-permute-start.6 = (bf16[128,256]{1,0:T(8,128)(2,1)S(1)}, bf16[128,256]{1,0:T(8,128)(2,1)S(1)}, u32[]{:S(2)}, u32[]{:S(2)}) collective-permute-start(bf16[128,256]{1,0:T(8,128)(2,1)S(1)} %get-tuple-element.393), channel_id=1, source_target_pairs={{0,2},{1,3},{2,0},{3,1},{4,6},{5,7},{6,4},{7,5},{8,10},{9,11},{10,... | collective-permute-start | bytes 196616 | tf_op jit(solution)/shard_map/ppermute | solution.py:368
  15.8 9.4 %collective-permute-start.7 = (bf16[128,256]{1,0:T(8,128)(2,1)S(1)}, bf16[128,256]{1,0:T(8,128)(2,1)S(1)}, u32[]{:S(2)}, u32[]{:S(2)}) collective-permute-start(bf16[128,256]{1,0:T(8,128)(2,1)S(1)} %get-tuple-element.394), channel_id=1, source_target_pairs={{0,3},{1,2},{2,1},{3,0},{4,7},{5,6},{6,5},{7,4},{8,11},{9,10},{10,... | collective-permute-start | bytes 196616 | tf_op jit(solution)/shard_map/ppermute | solution.py:368
  25.2 1.3 %collective-permute-start.8 = (bf16[128,256]{1,0:T(8,128)(2,1)S(1)}, bf16[128,256]{1,0:T(8,128)(2,1)S(1)}, u32[]{:S(2)}, u32[]{:S(2)}) collective-permute-start(bf16[128,256]{1,0:T(8,128)(2,1)S(1)} %get-tuple-element.821.refs_0_), channel_id=1, source_target_pairs={{0,4},{4,0},{8,12},{12,8},{16,20},{20,16},{24,28},{28,24},{1,5},{5... | collective-permute-start | bytes 196616 | tf_op jit(solution)/shard_map/ppermute | solution.py:365
  25.3 1.4 %collective-permute-start.9 = (bf16[128,256]{1,0:T(8,128)(2,1)S(1)}, bf16[128,256]{1,0:T(8,128)(2,1)S(1)}, u32[]{:S(2)}, u32[]{:S(2)}) collective-permute-start(bf16[128,256]{1,0:T(8,128)(2,1)S(1)} %collective-permute-done.5.refs_1_), channel_id=1, source_target_pairs={{0,4},{4,0},{8,12},{12,8},{16,20},{20,16},{24,28},{28,24},{1,5},{5... | collective-permute-start | bytes 196616 | tf_op jit(solution)/shard_map/ppermute | solution.py:365
  28.4 14.9 %collective-permute-start.20 = (bf16[512,512]{1,0:T(8,128)(2,1)S(1)}, bf16[512,512]{1,0:T(8,128)(2,1)S(1)}, u32[]{:S(2)}, u32[]{:S(2)}) collective-permute-start(bf16[512,512]{1,0:T(8,128)(2,1)S(1)} %collective-permute-done.16.refs_2_), channel_id=1, source_target_pairs={{0,16},{4,12},{8,24},{12,4},{16,0},{20,28},{24,8},{28,20},{1,17},{... | collective-permute-start | bytes 1572872 | tf_op jit(solution)/shard_map/ppermute | solution.py:374
  29.3 12.8 %collective-permute-start.12 = (bf16[512,256]{1,0:T(8,128)(2,1)S(1)}, bf16[512,256]{1,0:T(8,128)(2,1)S(1)}, u32[]{:S(2)}, u32[]{:S(2)}) collective-permute-start(bf16[512,256]{1,0:T(8,128)(2,1)S(1)} %get-tuple-element.401.refs_1_), channel_id=1, source_target_pairs={{0,8},{4,20},{8,0},{12,28},{16,24},{20,4},{24,16},{28,12},{1,9},{5... | collective-permute-start | bytes 786440 | tf_op jit(solution)/shard_map/ppermute | solution.py:371
  30.5 11.6 %collective-permute-start.13 = (bf16[256,256]{1,0:T(8,128)(2,1)S(1)}, bf16[256,256]{1,0:T(8,128)(2,1)S(1)}, u32[]{:S(2)}, u32[]{:S(2)}) collective-permute-start(bf16[256,256]{1,0:T(8,128)(2,1)S(1)} %get-tuple-element.402), channel_id=1, source_target_pairs={{0,24},{4,28},{8,16},{12,20},{16,8},{20,12},{24,0},{28,4},{1,25},{... | collective-permute-start | bytes 393224 | tf_op jit(solution)/shard_map/ppermute | solution.py:365
  32.0 24.3 %collective-permute-start.19 = (bf16[512,512]{1,0:T(8,128)(2,1)S(1)}, bf16[512,512]{1,0:T(8,128)(2,1)S(1)}, u32[]{:S(2)}, u32[]{:S(2)}) collective-permute-start(bf16[512,512]{1,0:T(8,128)(2,1)S(1)} %collective-permute-done.16.refs_2_), channel_id=1, source_target_pairs={{0,4},{4,0},{8,12},{12,8},{16,20},{20,16},{24,28},{28,24},{1,5},{5... | collective-permute-start | bytes 1572872 | tf_op jit(solution)/shard_map/ppermute | solution.py:365
  32.0 24.2 %collective-permute-start.18 = (bf16[512,512]{1,0:T(8,128)(2,1)S(1)}, bf16[512,512]{1,0:T(8,128)(2,1)S(1)}, u32[]{:S(2)}, u32[]{:S(2)}) collective-permute-start(bf16[512,512]{1,0:T(8,128)(2,1)S(1)} %collective-permute-done.17.refs_3_), channel_id=1, source_target_pairs={{0,4},{4,0},{8,12},{12,8},{16,20},{20,16},{24,28},{28,24},{1,5},{5... | collective-permute-start | bytes 1572872 | tf_op jit(solution)/shard_map/ppermute | solution.py:365
  43.3 13.0 %collective-permute-start.21 = (bf16[512,512]{1,0:T(8,128)(2,1)S(1)}, bf16[512,512]{1,0:T(8,128)(2,1)S(1)}, u32[]{:S(2)}, u32[]{:S(2)}) collective-permute-start(bf16[512,512]{1,0:T(8,128)(2,1)S(1)} %collective-permute-done.20.refs_6_), channel_id=1, source_target_pairs={{0,4},{4,0},{8,12},{12,8},{16,20},{20,16},{24,28},{28,24},{1,5},{5... | collective-permute-start | bytes 1572872 | tf_op jit(solution)/shard_map/ppermute | solution.py:365
  54.3 3.7 %collective-permute-start.14 = (bf16[512,256]{1,0:T(8,128)(2,1)S(1)}, bf16[512,256]{1,0:T(8,128)(2,1)S(1)}, u32[]{:S(2)}, u32[]{:S(2)}) collective-permute-start(bf16[512,256]{1,0:T(8,128)(2,1)S(1)} %collective-permute-done.12.refs_2_), channel_id=1, source_target_pairs={{0,4},{4,0},{8,12},{12,8},{16,20},{20,16},{24,28},{28,24},{1,5},{5... | collective-permute-start | bytes 786440 | tf_op jit(solution)/shard_map/ppermute | solution.py:365
  54.9 3.2 %collective-permute-start.15 = (bf16[256,256]{1,0:T(8,128)(2,1)S(1)}, bf16[256,256]{1,0:T(8,128)(2,1)S(1)}, u32[]{:S(2)}, u32[]{:S(2)}) collective-permute-start(bf16[256,256]{1,0:T(8,128)(2,1)S(1)} %collective-permute-done.13.refs_4_), channel_id=1, source_target_pairs={{0,4},{4,0},{8,12},{12,8},{16,20},{20,16},{24,28},{28,24},{1,5},{5... | collective-permute-start | bytes 393224 | tf_op jit(solution)/shard_map/ppermute | solution.py:365
  56.2 13.5 %collective-permute-start.24 = (bf16[512,256]{1,0:T(8,128)(2,1)S(1)}, bf16[512,256]{1,0:T(8,128)(2,1)S(1)}, u32[]{:S(2)}, u32[]{:S(2)}) collective-permute-start(bf16[512,256]{1,0:T(8,128)(2,1)S(1)} %get-tuple-element.425), channel_id=1, source_target_pairs={{0,2},{1,3},{2,0},{3,1},{4,6},{5,7},{6,4},{7,5},{8,10},{9,11},{10,... | collective-permute-start | bytes 786440 | tf_op jit(solution)/shard_map/ppermute | solution.py:368
  60.4 9.5 %collective-permute-start.22 = (bf16[512,256]{1,0:T(8,128)(2,1)S(1)}, bf16[512,256]{1,0:T(8,128)(2,1)S(1)}, u32[]{:S(2)}, u32[]{:S(2)}) collective-permute-start(bf16[512,256]{1,0:T(8,128)(2,1)S(1)} %get-tuple-element.421.refs_1_), channel_id=1, source_target_pairs={{0,8},{4,20},{8,0},{12,28},{16,24},{20,4},{24,16},{28,12},{1,9},{5... | collective-permute-start | bytes 786440 | tf_op jit(solution)/shard_map/ppermute | solution.py:371
  61.4 8.5 %collective-permute-start.23 = (bf16[256,256]{1,0:T(8,128)(2,1)S(1)}, bf16[256,256]{1,0:T(8,128)(2,1)S(1)}, u32[]{:S(2)}, u32[]{:S(2)}) collective-permute-start(bf16[256,256]{1,0:T(8,128)(2,1)S(1)} %get-tuple-element.422), channel_id=1, source_target_pairs={{0,24},{4,28},{8,16},{12,20},{16,8},{20,12},{24,0},{28,4},{1,25},{... | collective-permute-start | bytes 393224 | tf_op jit(solution)/shard_map/ppermute | solution.py:365
  69.9 3.0 %collective-permute-start.25 = (bf16[512,256]{1,0:T(8,128)(2,1)S(1)}, bf16[512,256]{1,0:T(8,128)(2,1)S(1)}, u32[]{:S(2)}, u32[]{:S(2)}) collective-permute-start(bf16[512,256]{1,0:T(8,128)(2,1)S(1)} %collective-permute-done.22.refs_2_), channel_id=1, source_target_pairs={{0,4},{4,0},{8,12},{12,8},{16,20},{20,16},{24,28},{28,24},{1,5},{5... | collective-permute-start | bytes 786440 | tf_op jit(solution)/shard_map/ppermute | solution.py:365
  69.9 3.0 %collective-permute-start.26 = (bf16[256,256]{1,0:T(8,128)(2,1)S(1)}, bf16[256,256]{1,0:T(8,128)(2,1)S(1)}, u32[]{:S(2)}, u32[]{:S(2)}) collective-permute-start(bf16[256,256]{1,0:T(8,128)(2,1)S(1)} %collective-permute-done.23.refs_4_), channel_id=1, source_target_pairs={{0,4},{4,0},{8,12},{12,8},{16,20},{20,16},{24,28},{28,24},{1,5},{5... | collective-permute-start | bytes 393224 | tf_op jit(solution)/shard_map/ppermute | solution.py:365
  70.4 11.3 %collective-permute-start.29 = (bf16[512,256]{1,0:T(8,128)(2,1)S(1)}, bf16[512,256]{1,0:T(8,128)(2,1)S(1)}, u32[]{:S(2)}, u32[]{:S(2)}) collective-permute-start(bf16[512,256]{1,0:T(8,128)(2,1)S(1)} %get-tuple-element.438), channel_id=1, source_target_pairs={{0,3},{1,2},{2,1},{3,0},{4,7},{5,6},{6,5},{7,4},{8,11},{9,10},{10,... | collective-permute-start | bytes 786440 | tf_op jit(solution)/shard_map/ppermute | solution.py:368
  75.2 9.5 %collective-permute-start.27 = (bf16[512,256]{1,0:T(8,128)(2,1)S(1)}, bf16[512,256]{1,0:T(8,128)(2,1)S(1)}, u32[]{:S(2)}, u32[]{:S(2)}) collective-permute-start(bf16[512,256]{1,0:T(8,128)(2,1)S(1)} %get-tuple-element.434.refs_1_), channel_id=1, source_target_pairs={{0,8},{4,20},{8,0},{12,28},{16,24},{20,4},{24,16},{28,12},{1,9},{5... | collective-permute-start | bytes 786440 | tf_op jit(solution)/shard_map/ppermute | solution.py:371
  76.2 8.5 %collective-permute-start.28 = (bf16[256,256]{1,0:T(8,128)(2,1)S(1)}, bf16[256,256]{1,0:T(8,128)(2,1)S(1)}, u32[]{:S(2)}, u32[]{:S(2)}) collective-permute-start(bf16[256,256]{1,0:T(8,128)(2,1)S(1)} %get-tuple-element.435), channel_id=1, source_target_pairs={{0,24},{4,28},{8,16},{12,20},{16,8},{20,12},{24,0},{28,4},{1,25},{... | collective-permute-start | bytes 393224 | tf_op jit(solution)/shard_map/ppermute | solution.py:365
  84.7 1.8 %collective-permute-start.30 = (bf16[512,256]{1,0:T(8,128)(2,1)S(1)}, bf16[512,256]{1,0:T(8,128)(2,1)S(1)}, u32[]{:S(2)}, u32[]{:S(2)}) collective-permute-start(bf16[512,256]{1,0:T(8,128)(2,1)S(1)} %collective-permute-done.27.refs_2_), channel_id=1, source_target_pairs={{0,4},{4,0},{8,12},{12,8},{16,20},{20,16},{24,28},{28,24},{1,5},{5... | collective-permute-start | bytes 786440 | tf_op jit(solution)/shard_map/ppermute | solution.py:365
  84.7 1.8 %collective-permute-start.31 = (bf16[256,256]{1,0:T(8,128)(2,1)S(1)}, bf16[256,256]{1,0:T(8,128)(2,1)S(1)}, u32[]{:S(2)}, u32[]{:S(2)}) collective-permute-start(bf16[256,256]{1,0:T(8,128)(2,1)S(1)} %collective-permute-done.28.refs_4_), channel_id=1, source_target_pairs={{0,4},{4,0},{8,12},{12,8},{16,20},{20,16},{24,28},{28,24},{1,5},{5... | collective-permute-start | bytes 393224 | tf_op jit(solution)/shard_map/ppermute | solution.py:365
  85.2 8.2 %collective-permute-start.34 = (bf16[512,256]{1,0:T(8,128)(2,1)S(1)}, bf16[512,256]{1,0:T(8,128)(2,1)S(1)}, u32[]{:S(2)}, u32[]{:S(2)}) collective-permute-start(bf16[512,256]{1,0:T(8,128)(2,1)S(1)} %get-tuple-element.452), channel_id=1, source_target_pairs={{0,1},{1,0},{2,3},{3,2},{4,5},{5,4},{6,7},{7,6},{8,9},{9,8},{10,11... | collective-permute-start | bytes 786440 | tf_op jit(solution)/shard_map/ppermute | solution.py:368
  88.8 9.8 %collective-permute-start.32 = (bf16[512,256]{1,0:T(8,128)(2,1)S(1)}, bf16[512,256]{1,0:T(8,128)(2,1)S(1)}, u32[]{:S(2)}, u32[]{:S(2)}) collective-permute-start(bf16[512,256]{1,0:T(8,128)(2,1)S(1)} %get-tuple-element.447.refs_1_), channel_id=1, source_target_pairs={{0,8},{4,20},{8,0},{12,28},{16,24},{20,4},{24,16},{28,12},{1,9},{5... | collective-permute-start | bytes 786440 | tf_op jit(solution)/shard_map/ppermute | solution.py:371
  89.9 8.7 %collective-permute-start.33 = (bf16[256,256]{1,0:T(8,128)(2,1)S(1)}, bf16[256,256]{1,0:T(8,128)(2,1)S(1)}, u32[]{:S(2)}, u32[]{:S(2)}) collective-permute-start(bf16[256,256]{1,0:T(8,128)(2,1)S(1)} %get-tuple-element.448), channel_id=1, source_target_pairs={{0,24},{4,28},{8,16},{12,20},{16,8},{20,12},{24,0},{28,4},{1,25},{... | collective-permute-start | bytes 393224 | tf_op jit(solution)/shard_map/ppermute | solution.py:365
  98.7 1.7 %collective-permute-start.35 = (bf16[512,256]{1,0:T(8,128)(2,1)S(1)}, bf16[512,256]{1,0:T(8,128)(2,1)S(1)}, u32[]{:S(2)}, u32[]{:S(2)}) collective-permute-start(bf16[512,256]{1,0:T(8,128)(2,1)S(1)} %collective-permute-done.32.refs_2_), channel_id=1, source_target_pairs={{0,4},{4,0},{8,12},{12,8},{16,20},{20,16},{24,28},{28,24},{1,5},{5... | collective-permute-start | bytes 786440 | tf_op jit(solution)/shard_map/ppermute | solution.py:365
  98.7 1.7 %collective-permute-start.36 = (bf16[256,256]{1,0:T(8,128)(2,1)S(1)}, bf16[256,256]{1,0:T(8,128)(2,1)S(1)}, u32[]{:S(2)}, u32[]{:S(2)}) collective-permute-start(bf16[256,256]{1,0:T(8,128)(2,1)S(1)} %collective-permute-done.33.refs_4_), channel_id=1, source_target_pairs={{0,4},{4,0},{8,12},{12,8},{16,20},{20,16},{24,28},{28,24},{1,5},{5... | collective-permute-start | bytes 393224 | tf_op jit(solution)/shard_map/ppermute | solution.py:365
  (9 other events, 65.4 us)

commit v7 on v6

--- a/solution.py
+++ b/solution.py
@@ -118,12 +118,18 @@
         out[j * BS:(j + 1) * BS, :] = buf[j * BS:(j + 1) * BS, :] * mask[j:j + 1, :]
 
 
-def rhs_kernel(rhs_ref, *sent):
+def start_pack_kernel(own_ref, other_ref, rhs_ref, l_chip, *sent):
+    l_chip[0:SN, :] = own_ref[...]
+    l_chip[SN:PAIR, :] = other_ref[...]
     depth = lax.axis_index("rhs")
     width = sent[0].shape[1]
     for s, out in enumerate(sent):
         at = pl.multiple_of(jnp.bitwise_xor(depth, s) * width, width)
         out[...] = rhs_ref[:, pl.ds(at, width)]
+
+
+def take_half_kernel(x_ref, out):
+    out[...] = x_ref[0:SN, :]
 
 
 def table_kernel(owner, order, tab, flag, cnt):
@@ -177,16 +183,29 @@
         c.wait()
 
 
-def first_pack_kernel(tab, *refs):
-    pieces, (chip_rhs, p_ref, b_ref) = refs[:8], refs[8:]
-    depth, core = lax.axis_index("rhs"), lax.axis_index("rows") % 2
+def first_pack_kernel(owner, order, *refs):
+    pieces, (chip_rhs, p_ref, b_ref, count) = refs[:8], refs[8:]
+    row, depth = lax.axis_index("rows"), lax.axis_index("rhs")
+    core = row % 2
     tall = pieces[0].shape[0]
     for side in range(2):
         for s in range(4):
             at = pl.multiple_of(side * SB * BS + jnp.bitwise_xor(depth, s) * tall, tall)
             chip_rhs[pl.ds(at, tall), :] = pieces[4 * side + s][...]
-    for j in range(SB):
-        p_ref[j * BS:(j + 1) * BS, :] = chip_rhs[rows_at(tab[PACK + j]), :]
+    count[0] = 0
+    for i in range(2 * SB):
+        slot = owner[order[i // SB] * SB + i % SB]
+
+        @pl.when(slot // (2 * SB) == row // 2)
+        def _(slot=slot):
+            rank = count[0]
+            count[0] = rank + 1
+            place = jnp.bitwise_xor((slot // SB) % 2, core) * SB + slot % SB
+
+            @pl.when(rank < SB)
+            def _():
+                p_ref[rows_at(rank), :] = chip_rhs[rows_at(place), :]
+
     b_ref[...] = p_ref[pl.ds(pl.multiple_of(core * SB // 2 * BS, SB // 2 * BS), SB // 2 * BS), :]
 
 
@@ -215,7 +234,9 @@
     last = group == GROUPS - 1
 
     def kernel(tab, order, diag, *refs):
-        l_refs, refs = refs[:8], refs[8:]
+        own, other, near, near_swap, far, far_swap = refs[:6]
+        l_refs = ((own, 0), (other, 0), (near, 0), (near, SB), (near_swap, SB), (near_swap, 0), (far, 0), (far_swap, 0))
+        refs = refs[6:]
         if last:
             m_out, lbuf = refs
         else:
@@ -227,7 +248,7 @@
             for m in range(8):
                 @pl.when(code // SB == m)
                 def _(m=m, i=i, code=code):
-                    lbuf[i * BS:(i + 1) * BS, :] = l_refs[m][rows_at(code % SB), :]
+                    lbuf[i * BS:(i + 1) * BS, :] = l_refs[m][0][rows_at(code % SB + l_refs[m][1]), :]
         first, second = diag[order[2 * group]], diag[order[2 * group + 1]]
         m_out[0:SN, 0:SN] = first
         m_out[SN:PAIR, SN:PAIR] = second
@@ -293,15 +314,9 @@
     return first + jnp.dot(a_ref[:, columns_at(order[2 * group + 1])], x_ref[SN:PAIR, :], preferred_element_type=F32)
 
 
-def first_rows_kernel(order, a0, a1, a2, a3, x_ref, out):
+def two_rows_kernel(order, a0, a1, a2, a3, x0_ref, x1_ref, out):
     for i, a_ref in enumerate((a0, a1, a2, a3)):
-        out[i * SN:(i + 1) * SN, :] = below_product(order, a_ref, x_ref, 0)
-
-
-def next_rows_kernel(order, a0, a1, a2, a3, x_ref, sums, out):
-    for i, a_ref in enumerate((a0, a1, a2, a3)):
-        at = slice(i * SN, (i + 1) * SN)
-        out[at, :] = sums[at, :] + below_product(order, a_ref, x_ref, 1)
+        out[i * SN:(i + 1) * SN, :] = below_product(order, a_ref, x0_ref, 0) + below_product(order, a_ref, x1_ref, 1)
 
 
 def base_rows_kernel(order, a0, a1, a2, a3, x_ref, sums, h0, h1, h2, h3, out, rhs):
@@ -401,22 +416,44 @@
         cost_estimate=cost(2),
         name="factor_pack",
     )(window_owner, sn_order, win_pattern, w_own)
-    near = neighbour(l_own)
     l_other = swap(l_own, 1)
-    rhs_late, _ = lax.optimization_barrier((rhs_win, l_own))
-    sent = pl.pallas_call(
-        rhs_kernel,
-        out_shape=(shape_of((tall, columns)),) * 4,
-        in_specs=[VMEM],
-        out_specs=(VMEM,) * 4,
+    l_chip, *sent = pl.pallas_call(
+        start_pack_kernel,
+        out_shape=(shape_of((PAIR, SN)),) + (shape_of((tall, columns)),) * 4,
+        in_specs=[VMEM] * 3,
+        out_specs=(VMEM,) * 5,
         compiler_params=params(4),
         cost_estimate=cost(1),
-        name="rhs_pack",
-    )(rhs_late)
-    l_other, *sent = lax.optimization_barrier((l_other, *sent))
-    near_other = neighbour(l_other)
+        name="start_pack",
+    )(l_own, l_other, rhs_win)
+    near = neighbour(l_chip)
     pieces = [sent[0]] + [deep(sent[s], s) for s in (1, 2, 3)]
-    owner_later, _ = lax.optimization_barrier((window_owner, sent[0]))
+    w_late, _ = lax.optimization_barrier((win_rows, l_chip))
+    w_other = swap(w_late, 1)
+    w_other, *pieces = lax.optimization_barrier((w_other, *pieces))
+    others = [swap(x, 1) for x in pieces]
+    chip_rhs, packed, part = pl.pallas_call(
+        first_pack_kernel,
+        out_shape=(shape_of((PAIR, columns)), shape_of((SN, columns)), shape_of((half, columns))),
+        in_specs=[SMEM, SMEM] + [VMEM] * 8,
+        out_specs=(VMEM,) * 3,
+        scratch_shapes=[pltpu.SMEM((1,), jnp.int32)],
+        compiler_params=params(4),
+        cost_estimate=cost(1),
+        name="first_pack",
+    )(window_owner, sn_order, *pieces, *others)
+    near, _ = lax.optimization_barrier((near, packed))
+    near_half = pl.pallas_call(
+        take_half_kernel,
+        out_shape=shape_of((SN, SN)),
+        in_specs=[VMEM],
+        out_specs=VMEM,
+        compiler_params=params(4),
+        cost_estimate=cost(1),
+        name="take_half",
+    )(near)
+    far = forward(near_half)
+    owner_later, order_later, _ = lax.optimization_barrier((window_owner, sn_order, packed))
     tab, flag = pl.pallas_call(
         table_kernel,
         out_shape=(shape_of((TABLE,), jnp.int32), shape_of((2,), jnp.int32)),
@@ -426,25 +463,10 @@
         compiler_params=params(4),
         cost_estimate=cost(3),
         name="tables",
-    )(owner_later, sn_order)
-    w_other = swap(win_rows, 1)
-    below = [mask_below(0, sent[0])]
-    tab, w_other, below[0], *pieces = lax.optimization_barrier((tab, w_other, below[0], *pieces))
-    others = [swap(x, 1) for x in pieces]
-    chip_rhs, packed, part = pl.pallas_call(
-        first_pack_kernel,
-        out_shape=(shape_of((PAIR, columns)), shape_of((SN, columns)), shape_of((half, columns))),
-        in_specs=[SMEM] + [VMEM] * 8,
-        out_specs=(VMEM,) * 3,
-        compiler_params=params(4),
-        cost_estimate=cost(1),
-        name="first_pack",
-    )(tab, *pieces, *others)
-    near, near_other, _ = lax.optimization_barrier((near, near_other, packed))
-    far = forward(near)
-    l_parts = [x for x in (l_own, l_other, near, near_other, swap(near_other, 1), swap(near, 1), far)]
+    )(owner_later, order_later)
     w_other = in_vmem(w_other)
     w_own = in_vmem(win_rows)
+    below = []
 
     tile = rhs_anc.shape[0]
     sums, solved, masked = None, [], []
@@ -457,10 +479,7 @@
         a_own = neighbour(packed)
         b_own = swap(part, 6)
         if group == 0:
-            far_late, *_ = lax.optimization_barrier((far, a_own, b_own))
-            l_parts = [in_vmem(x) for x in (*l_parts, swap(far_late, 1))]
-            below += [mask_below(k, packed) for k in (1, 2, 3)]
-            tab_later, order_later, _ = lax.optimization_barrier((tab, sn_order, packed))
+            below += [mask_below(k, packed) for k in (0, 1)]
             for k in range(GROUPS - 1):
                 masked.append(pl.pallas_call(
                     make_mask_kernel(k),
@@ -471,7 +490,7 @@
                     compiler_params=params(6),
                     cost_estimate=cost(2),
                     name="mask_rows",
-                )(tab_later, order_later, win_pattern, w_own, w_other))
+                )(tab, order_later, win_pattern, w_own, w_other))
         if group == 0:
             rhs_later, _ = lax.optimization_barrier((rhs_anc, packed))
             anc_pieces = list(pl.pallas_call(
@@ -489,6 +508,10 @@
             moved, _ = lax.optimization_barrier((anc_pieces[s], packed))
             anc_pieces[s] = deep(moved, s)
 
+        if group == 0:
+            a_own, b_own, near, far, below[0], below[1], *masked = lax.optimization_barrier(
+                (a_own, b_own, near, far, below[0], below[1], *masked))
+            l_parts = [in_vmem(x) for x in (l_own, l_other, near, swap(near, 1), far, swap(far, 1))]
         operands = [tab, sn_order, diag_vmem, *l_parts]
         out_shape = [shape_of((PAIR, PAIR))]
         if not last:
@@ -504,29 +527,32 @@
             cost_estimate=cost(2),
             name="prep",
         )(*operands)
-        if group > 0:
-            k = group - 1
-            previous = anc_pieces[anc_order[k]]
-            if k < 2:
-                more, kernel = ([], first_rows_kernel) if k == 0 else ([sums], next_rows_kernel)
-            else:
-                more, kernel = [sums, *anc_pieces], base_rows_kernel
+        hold = []
+        if group == 1:
+            below += [mask_below(k, packed) for k in (2, 3)]
+            hold = below[2:]
+        elif group > 1:
+            more, kernel = (solved[:2], two_rows_kernel) if group == 2 else ([solved[2], sums, *anc_pieces], base_rows_kernel)
             sums = pl.pallas_call(
                 kernel,
                 out_shape=shape_of((below_rows, columns), F32),
-                in_specs=[SMEM] + [VMEM] * (5 + len(more)),
+                in_specs=[SMEM] + [VMEM] * (4 + len(more)),
                 out_specs=VMEM,
-                scratch_shapes=[pltpu.VMEM((below_rows, columns), BF16)] if k == 2 else [],
-                input_output_aliases={6: 0} if more else {},
+                scratch_shapes=[pltpu.VMEM((below_rows, columns), BF16)] if last else [],
+                input_output_aliases={6: 0} if last else {},
                 compiler_params=params(6),
                 cost_estimate=cost(3),
                 name="rows_below",
-            )(sn_order, *below, solved[k], *more)
-            a_own, b_own, sums, previous, *ready = lax.optimization_barrier((a_own, b_own, sums, previous, *ready))
-            anc_pieces[anc_order[k]] = previous
-        else:
-            a_own, b_own, below[1], below[2], below[3], *masked = lax.optimization_barrier(
-                (a_own, b_own, below[1], below[2], below[3], *masked))
+            )(sn_order, *below, *more)
+            hold = [sums]
+        if group > 0:
+            s = anc_order[group - 1]
+            a_own, b_own, anc_pieces[s], *rest = lax.optimization_barrier((a_own, b_own, anc_pieces[s], *hold, *ready))
+            hold, ready = rest[:len(hold)], rest[len(hold):]
+            if group == 1:
+                below[2:] = hold
+            else:
+                sums = hold[0]
         a_swap = swap(a_own, 1)
         b_swap = swap(b_own, 1)
         ready = list(ready) if last else list(ready) + [masked[group]]

time: 106 us -> 91.7 us (0.87)
  waiting for transfers between devices: 25 us -> 15 us
  starting transfers between devices: 33.2 us -> 30 us
    ppermute x21 -> x20, waiting for transfers between devices: 20.9 us -> 8.81 us  [swap(): return lax.ppermute(x, 'rows', [(i, i ^ m) for i in range(8)])]
    ppermute x6, waiting for transfers between devices: 2.95 us -> 6.16 us  [deep(): return lax.ppermute(x, 'rhs', [(i, i ^ m) for i in range(4)])]
    ppermute x6 -> x5, starting transfers between devices: 10.1 us -> 6.93 us  [neighbour(): lax.ppermute(x, 'rows', [(i, i ^ (2 if i % 2 == 0 else 4)) for i in range...]
    ppermute x6, starting transfers between devices: 12.3 us -> 10.9 us  [deep(): return lax.ppermute(x, 'rhs', [(i, i ^ m) for i in range(4)])]
    ppermute x1, waiting for transfers between devices: 1.18 us -> 0.01 us  [forward(): lax.ppermute(x, 'rows', [(i, i ^ (4 if i % 2 == 0 else 2)) for i in range...]
    pallas_call x3 -> x2, Pallas kernels: 5.86 us -> 4.99 us  [local(): pl.pallas_call(kernel, out_shape=shape_of((below_rows, columns), F32), in...]
    ppermute x21 -> x20, starting transfers between devices: 9.92 us -> 10.4 us  [swap(): return lax.ppermute(x, 'rows', [(i, i ^ m) for i in range(8)])]
  transfers between devices with their start and end apart: 34 -> 32, of which waited for: 13 -> 11; matrix products, arithmetic and copies ran while one was open for 0% -> 0% of each run, Pallas kernels for 38% -> 40%
where the time goes in v7:
time: 91.7 us; the launch traced here: 91.5 us
  Pallas kernels  44.7 us (49%)
  starting transfers between devices  30 us (33%)
  waiting for transfers between devices  15 us (16%)
  between operations  1.18 us (1%)
    ppermute x6, starting transfers between devices, deep(): return lax.ppermute(x, 'rhs', [(i, i ^ m) for i in range(4)])  10.9 us
    ppermute x20, starting transfers between devices, swap(): return lax.ppermute(x, 'rows', [(i, i ^ m) for i in range(8)])  10.4 us
    pallas_call x4, Pallas kernels, mask_below(): pl.pallas_call(make_below_mask_kernel(k), out_shape=shape_of((SN, NW)), i...  9.03 us
    pallas_call x4, Pallas kernels, local(): pl.pallas_call(make_solve_kernel(group), out_shape=tuple(out_shape), in_s...  8.84 us
    ppermute x20, waiting for transfers between devices, swap(): return lax.ppermute(x, 'rows', [(i, i ^ m) for i in range(8)])  8.81 us
    pallas_call x4, Pallas kernels, local(): pl.pallas_call(make_prep_kernel(group), out_shape=tuple(out_shape), in_sp...  8.19 us
    ppermute x5, starting transfers between devices, neighbour(): lax.ppermute(x, 'rows', [(i, i ^ (2 if i % 2 == 0 else 4)) for i in range...  6.93 us
    ppermute x6, waiting for transfers between devices, deep(): return lax.ppermute(x, 'rhs', [(i, i ^ m) for i in range(4)])  6.16 us
  transfers between devices with their start and end apart: 32, of which 11 were waited for; matrix products, arithmetic and copies ran while one was open for 0% of the time, Pallas kernels for 40%

profile of v7, /device:TPU:0, one launch (start us, length us, event | category | flops | bytes accessed | tf_op | source)
XLA Modules:
  0.0 91.5 jit_solution(13451719086323507074)
XLA Ops:
  0.7 2.6 %factor_pack.1.own_ref.refs_0_ = bf16[512,512]{1,0:T(8,128)(2,1)S(1)} custom-call(s32[64]{0:T(128)} %owner.4, s32[8]{0:T(128)} %order.21, s32[64,64]{1,0:T(8,128)} %pattern.9, bf16[512,4096]{1,0:T(8,128)(2,1)} %w_own.5), custom_call_target="tpu_custom_call" | custom-call | flops 200000000 | bytes 6000000 | tf_op jit(solution)/shard_map/factor_pack/pallas_call | solution.py:408
  3.8 1.5 %collective-permute-done.3.other_ref.refs_1_ = bf16[512,512]{1,0:T(8,128)(2,1)S(1)} collective-permute-done((bf16[512,512]{1,0:T(8,128)(2,1)S(1)}, bf16[512,512]{1,0:T(8,128)(2,1)S(1)}, u32[]{:S(2)}, u32[]{:S(2)}) %collective-permute-start.3) | collective-permute-done | bytes 524320 | tf_op jit(solution)/shard_map/ppermute | solution.py:380
  5.9 2.6 %collective-permute-start.14 = (bf16[1024,512]{1,0:T(8,128)(2,1)S(1)}, bf16[1024,512]{1,0:T(8,128)(2,1)S(1)}, u32[]{:S(2)}, u32[]{:S(2)}) collective-permute-start(bf16[1024,512]{1,0:T(8,128)(2,1)S(1)} %get-tuple-element.375), channel_id=1, source_target_pairs={{0,8},{4,20},{8,0},{12,28},{16,24},{20,4},{24,16},{28,12},{1,9},{5... | collective-permute-start | bytes 3145736 | tf_op jit(solution)/shard_map/ppermute | solution.py:386
  8.5 1.6 %collective-permute-start.5 = (bf16[128,256]{1,0:T(8,128)(2,1)S(1)}, bf16[128,256]{1,0:T(8,128)(2,1)S(1)}, u32[]{:S(2)}, u32[]{:S(2)}) collective-permute-start(bf16[128,256]{1,0:T(8,128)(2,1)S(1)} %get-tuple-element.378), channel_id=1, source_target_pairs={{0,1},{1,0},{2,3},{3,2},{4,5},{5,4},{6,7},{7,6},{8,9},{9,8},{10,11... | collective-permute-start | bytes 196616 | tf_op jit(solution)/shard_map/ppermute | solution.py:383
  10.1 2.6 %collective-permute-start.6 = (bf16[128,256]{1,0:T(8,128)(2,1)S(1)}, bf16[128,256]{1,0:T(8,128)(2,1)S(1)}, u32[]{:S(2)}, u32[]{:S(2)}) collective-permute-start(bf16[128,256]{1,0:T(8,128)(2,1)S(1)} %get-tuple-element.379), channel_id=1, source_target_pairs={{0,2},{1,3},{2,0},{3,1},{4,6},{5,7},{6,4},{7,5},{8,10},{9,11},{10,... | collective-permute-start | bytes 196616 | tf_op jit(solution)/shard_map/ppermute | solution.py:383
  12.9 4.7 %collective-permute-done.6.refs_2_ = bf16[128,256]{1,0:T(8,128)(2,1)S(1)} collective-permute-done((bf16[128,256]{1,0:T(8,128)(2,1)S(1)}, bf16[128,256]{1,0:T(8,128)(2,1)S(1)}, u32[]{:S(2)}, u32[]{:S(2)}) %collective-permute-start.6) | collective-permute-done | bytes 65568 | tf_op jit(solution)/shard_map/ppermute | solution.py:383
  21.7 1.7 %collective-permute-start.15 = (bf16[512,512]{1,0:T(8,128)(2,1)S(1)}, bf16[512,512]{1,0:T(8,128)(2,1)S(1)}, u32[]{:S(2)}, u32[]{:S(2)}) collective-permute-start(bf16[512,512]{1,0:T(8,128)(2,1)S(1)} %take_half.1), channel_id=1, source_target_pairs={{0,16},{4,12},{8,24},{12,4},{16,0},{20,28},{24,8},{28,20},{1,17},{... | collective-permute-start | bytes 1572872 | tf_op jit(solution)/shard_map/ppermute | solution.py:389
  23.4 1.5 %collective-permute-start.12 = (bf16[512,256]{1,0:T(8,128)(2,1)S(1)}, bf16[512,256]{1,0:T(8,128)(2,1)S(1)}, u32[]{:S(2)}, u32[]{:S(2)}) collective-permute-start(bf16[512,256]{1,0:T(8,128)(2,1)S(1)} %get-tuple-element.385.refs_1_), channel_id=1, source_target_pairs={{0,8},{4,20},{8,0},{12,28},{16,24},{20,4},{24,16},{28,12},{1,9},{5... | collective-permute-start | bytes 786440 | tf_op jit(solution)/shard_map/ppermute | solution.py:386
  25.3 2.3 %mask_below.4.a0 = bf16[512,4096]{1,0:T(8,128)(2,1)S(1)} custom-call(s32[32,64]{1,0:T(8,128)S(1)} %copy-done.3, bf16[2048,4096]{1,0:T(8,128)(2,1)} %a_ref.7), custom_call_target="tpu_custom_call" | custom-call | flops 200000000 | bytes 6000000 | tf_op jit(solution)/shard_map/mask_below/pallas_call | solution.py:393
  27.5 2.3 %mask_below.5.a1 = bf16[512,4096]{1,0:T(8,128)(2,1)S(1)} custom-call(s32[32,64]{1,0:T(8,128)S(1)} %copy-done.3, bf16[2048,4096]{1,0:T(8,128)(2,1)} %a_ref.7), custom_call_target="tpu_custom_call" | custom-call | flops 200000000 | bytes 6000000 | tf_op jit(solution)/shard_map/mask_below/pallas_call | solution.py:393
  29.8 2.8 %tables.1 = (s32[128]{0:T(128)S(1)}, s32[2]{0:T(128)}) custom-call(s32[64]{0:T(128)S(1)} %copy-done.19, s32[8]{0:T(128)S(1)} %copy-done.20), custom_call_target="tpu_custom_call" | custom-call | flops 300000000 | bytes 9000000 | tf_op jit(solution)/shard_map/tables/pallas_call | solution.py:457
  38.5 2.9 %collective-permute-start.22 = (bf16[512,256]{1,0:T(8,128)(2,1)S(1)}, bf16[512,256]{1,0:T(8,128)(2,1)S(1)}, u32[]{:S(2)}, u32[]{:S(2)}) collective-permute-start(bf16[512,256]{1,0:T(8,128)(2,1)S(1)} %get-tuple-element.408), channel_id=1, source_target_pairs={{0,2},{1,3},{2,0},{3,1},{4,6},{5,7},{6,4},{7,5},{8,10},{9,11},{10,... | collective-permute-start | bytes 786440 | tf_op jit(solution)/shard_map/ppermute | solution.py:383
  41.4 1.7 %prep.4 = (bf16[1024,1024]{1,0:T(8,128)(2,1)S(1)}, f32[512,256]{1,0:T(8,128)S(1)}) custom-call(s32[128]{0:T(128)S(1)} %get-tuple-element.392.tab.refs_0_, s32[8]{0:T(128)S(1)} %copy-done.20, bf16[8,512,512]{2,1,0:T(8,128)(2,1)S(1)} %copy-done.1, bf16[512,512]{1,0:T(8,128)(2,1)S(1)} %factor_pack.1.own_ref.refs_0_, ...), custom_call_target="tpu_custom_call" | custom-call | flops 200000000 | bytes 6000000 | tf_op jit(solution)/shard_map/prep/pallas_call | solution.py:520
  43.1 2.3 %pair_solve.4 = (bf16[1024,256]{1,0:T(8,128)(2,1)S(1)}, bf16[512,256]{1,0:T(8,128)(2,1)S(1)}, bf16[256,256]{1,0:T(8,128)(2,1)S(1)}) custom-call(s32[128]{0:T(128)S(1)} %get-tuple-element.392.tab.refs_0_, bf16[512,256]{1,0:T(8,128)(2,1)S(1)} %get-tuple-element.385.refs_1_, bf16[512,256]{1,0:T(8,128)(2,1)S(1)} %collective-permute-done.12.refs_2_, ...), custom_call_target="tpu_custom_call" | custom-call | flops 300000000 | bytes 9000000 | tf_op jit(solution)/shard_map/pair_solve/pallas_call | solution.py:563
  46.4 2.1 %collective-permute-start.21 = (bf16[256,256]{1,0:T(8,128)(2,1)S(1)}, bf16[256,256]{1,0:T(8,128)(2,1)S(1)}, u32[]{:S(2)}, u32[]{:S(2)}) collective-permute-start(bf16[256,256]{1,0:T(8,128)(2,1)S(1)} %get-tuple-element.405), channel_id=1, source_target_pairs={{0,24},{4,28},{8,16},{12,20},{16,8},{20,12},{24,0},{28,4},{1,25},{... | collective-permute-start | bytes 393224 | tf_op jit(solution)/shard_map/ppermute | solution.py:380
  48.5 2.3 %mask_below.6.a2 = bf16[512,4096]{1,0:T(8,128)(2,1)S(1)} custom-call(s32[32,64]{1,0:T(8,128)S(1)} %copy-done.3, bf16[2048,4096]{1,0:T(8,128)(2,1)} %a_ref.7), custom_call_target="tpu_custom_call" | custom-call | flops 200000000 | bytes 6000000 | tf_op jit(solution)/shard_map/mask_below/pallas_call | solution.py:393
  50.7 2.3 %mask_below.7.a3 = bf16[512,4096]{1,0:T(8,128)(2,1)S(1)} custom-call(s32[32,64]{1,0:T(8,128)S(1)} %copy-done.3, bf16[2048,4096]{1,0:T(8,128)(2,1)} %a_ref.7), custom_call_target="tpu_custom_call" | custom-call | flops 200000000 | bytes 6000000 | tf_op jit(solution)/shard_map/mask_below/pallas_call | solution.py:393
  53.0 2.5 %prep.5 = (bf16[1024,1024]{1,0:T(8,128)(2,1)S(1)}, f32[512,256]{1,0:T(8,128)S(1)}) custom-call(s32[128]{0:T(128)S(1)} %get-tuple-element.392.tab.refs_0_, s32[8]{0:T(128)S(1)} %copy-done.20, bf16[8,512,512]{2,1,0:T(8,128)(2,1)S(1)} %copy-done.1, bf16[512,512]{1,0:T(8,128)(2,1)S(1)} %factor_pack.1.own_ref.refs_0_, ...), custom_call_target="tpu_custom_call" | custom-call | flops 200000000 | bytes 6000000 | tf_op jit(solution)/shard_map/prep/pallas_call | solution.py:520
  56.2 2.1 %collective-permute-start.27 = (bf16[512,256]{1,0:T(8,128)(2,1)S(1)}, bf16[512,256]{1,0:T(8,128)(2,1)S(1)}, u32[]{:S(2)}, u32[]{:S(2)}) collective-permute-start(bf16[512,256]{1,0:T(8,128)(2,1)S(1)} %get-tuple-element.424), channel_id=1, source_target_pairs={{0,3},{1,2},{2,1},{3,0},{4,7},{5,6},{6,5},{7,4},{8,11},{9,10},{10,... | collective-permute-start | bytes 786440 | tf_op jit(solution)/shard_map/ppermute | solution.py:383
  58.3 2.3 %pair_solve.5 = (bf16[1024,256]{1,0:T(8,128)(2,1)S(1)}, bf16[512,256]{1,0:T(8,128)(2,1)S(1)}, bf16[256,256]{1,0:T(8,128)(2,1)S(1)}) custom-call(s32[128]{0:T(128)S(1)} %get-tuple-element.392.tab.refs_0_, bf16[512,256]{1,0:T(8,128)(2,1)S(1)} %get-tuple-element.404.refs_1_, bf16[512,256]{1,0:T(8,128)(2,1)S(1)} %collective-permute-done.20.refs_2_, ...), custom_call_target="tpu_custom_call" | custom-call | flops 300000000 | bytes 9000000 | tf_op jit(solution)/shard_map/pair_solve/pallas_call | solution.py:563
  61.5 1.4 %collective-permute-start.26 = (bf16[256,256]{1,0:T(8,128)(2,1)S(1)}, bf16[256,256]{1,0:T(8,128)(2,1)S(1)}, u32[]{:S(2)}, u32[]{:S(2)}) collective-permute-start(bf16[256,256]{1,0:T(8,128)(2,1)S(1)} %get-tuple-element.422), channel_id=1, source_target_pairs={{0,24},{4,28},{8,16},{12,20},{16,8},{20,12},{24,0},{28,4},{1,25},{... | collective-permute-start | bytes 393224 | tf_op jit(solution)/shard_map/ppermute | solution.py:380
  62.9 2.2 %prep.6 = (bf16[1024,1024]{1,0:T(8,128)(2,1)S(1)}, f32[512,256]{1,0:T(8,128)S(1)}) custom-call(s32[128]{0:T(128)S(1)} %get-tuple-element.392.tab.refs_0_, s32[8]{0:T(128)S(1)} %copy-done.20, bf16[8,512,512]{2,1,0:T(8,128)(2,1)S(1)} %copy-done.1, bf16[512,512]{1,0:T(8,128)(2,1)S(1)} %factor_pack.1.own_ref.refs_0_, ...), custom_call_target="tpu_custom_call" | custom-call | flops 200000000 | bytes 6000000 | tf_op jit(solution)/shard_map/prep/pallas_call | solution.py:520
  65.1 2.9 %rows_below.2.sums = f32[2048,256]{1,0:T(8,128)S(1)} custom-call(s32[8]{0:T(128)S(1)} %copy-done.20, bf16[512,4096]{1,0:T(8,128)(2,1)S(1)} %mask_below.4.a0, bf16[512,4096]{1,0:T(8,128)(2,1)S(1)} %mask_below.5.a1, bf16[512,4096]{1,0:T(8,128)(2,1)S(1)} %mask_below.6.a2, bf16[512,4096]{1,0:T(8,128)(2,1)S(1)} %mask_below.7.a3, ...), custom_call_target="tpu_custom_call" | custom-call | flops 300000000 | bytes 9000000 | tf_op jit(solution)/shard_map/rows_below/pallas_call | solution.py:536
  68.0 2.0 %collective-permute-done.26.refs_4_ = bf16[256,256]{1,0:T(8,128)(2,1)S(1)} collective-permute-done((bf16[256,256]{1,0:T(8,128)(2,1)S(1)}, bf16[256,256]{1,0:T(8,128)(2,1)S(1)}, u32[]{:S(2)}, u32[]{:S(2)}) %collective-permute-start.26) | collective-permute-done | bytes 131104 | tf_op jit(solution)/shard_map/ppermute | solution.py:380
  70.6 1.6 %collective-permute-start.32 = (bf16[512,256]{1,0:T(8,128)(2,1)S(1)}, bf16[512,256]{1,0:T(8,128)(2,1)S(1)}, u32[]{:S(2)}, u32[]{:S(2)}) collective-permute-start(bf16[512,256]{1,0:T(8,128)(2,1)S(1)} %get-tuple-element.436), channel_id=1, source_target_pairs={{0,1},{1,0},{2,3},{3,2},{4,5},{5,4},{6,7},{7,6},{8,9},{9,8},{10,11... | collective-permute-start | bytes 786440 | tf_op jit(solution)/shard_map/ppermute | solution.py:383
  72.2 2.3 %pair_solve.6 = (bf16[1024,256]{1,0:T(8,128)(2,1)S(1)}, bf16[512,256]{1,0:T(8,128)(2,1)S(1)}, bf16[256,256]{1,0:T(8,128)(2,1)S(1)}) custom-call(s32[128]{0:T(128)S(1)} %get-tuple-element.392.tab.refs_0_, bf16[512,256]{1,0:T(8,128)(2,1)S(1)} %get-tuple-element.421.refs_1_, bf16[512,256]{1,0:T(8,128)(2,1)S(1)} %collective-permute-done.25.refs_2_, ...), custom_call_target="tpu_custom_call" | custom-call | flops 300000000 | bytes 9000000 | tf_op jit(solution)/shard_map/pair_solve/pallas_call | solution.py:563
  75.4 1.4 %collective-permute-start.31 = (bf16[256,256]{1,0:T(8,128)(2,1)S(1)}, bf16[256,256]{1,0:T(8,128)(2,1)S(1)}, u32[]{:S(2)}, u32[]{:S(2)}) collective-permute-start(bf16[256,256]{1,0:T(8,128)(2,1)S(1)} %get-tuple-element.434), channel_id=1, source_target_pairs={{0,24},{4,28},{8,16},{12,20},{16,8},{20,12},{24,0},{28,4},{1,25},{... | collective-permute-start | bytes 393224 | tf_op jit(solution)/shard_map/ppermute | solution.py:380
  76.9 1.7 %prep.7.refs_6_ = bf16[1024,1024]{1,0:T(8,128)(2,1)S(1)} custom-call(s32[128]{0:T(128)S(1)} %get-tuple-element.392.tab.refs_0_, s32[8]{0:T(128)S(1)} %copy-done.20, bf16[8,512,512]{2,1,0:T(8,128)(2,1)S(1)} %copy-done.1, bf16[512,512]{1,0:T(8,128)(2,1)S(1)} %factor_pack.1.own_ref.refs_0_, bf16[512,512]{1,0:T(8,128)(2,1)S(1)} %collective-permute-done.3.other_ref.refs_1_, ...), custom_call_target="tpu_custom_call" | custom-call | flops 200000000 | bytes 6000000 | tf_op jit(solution)/shard_map/prep/pallas_call | solution.py:520
  78.8 2.1 %rows_below.3.base = f32[2048,256]{1,0:T(8,128)S(1)} custom-call(s32[8]{0:T(128)S(1)} %copy-done.20, bf16[512,4096]{1,0:T(8,128)(2,1)S(1)} %mask_below.4.a0, bf16[512,4096]{1,0:T(8,128)(2,1)S(1)} %mask_below.5.a1, bf16[512,4096]{1,0:T(8,128)(2,1)S(1)} %mask_below.6.a2, bf16[512,4096]{1,0:T(8,128)(2,1)S(1)} %mask_below.7.a3, ...), custom_call_target="tpu_custom_call", output_to_operand_aliasing={{}: (6, {})} | custom-call | flops 300000000 | bytes 9000000 | tf_op jit(solution)/shard_map/rows_below/pallas_call | solution.py:536
  80.9 3.1 %collective-permute-done.31.refs_4_ = bf16[256,256]{1,0:T(8,128)(2,1)S(1)} collective-permute-done((bf16[256,256]{1,0:T(8,128)(2,1)S(1)}, bf16[256,256]{1,0:T(8,128)(2,1)S(1)}, u32[]{:S(2)}, u32[]{:S(2)}) %collective-permute-start.31) | collective-permute-done | bytes 131104 | tf_op jit(solution)/shard_map/ppermute | solution.py:380
  85.7 1.9 %pair_solve.7.x3 = bf16[1024,256]{1,0:T(8,128)(2,1)S(1)} custom-call(s32[128]{0:T(128)S(1)} %get-tuple-element.392.tab.refs_0_, bf16[512,256]{1,0:T(8,128)(2,1)S(1)} %get-tuple-element.433.refs_1_, bf16[512,256]{1,0:T(8,128)(2,1)S(1)} %collective-permute-done.30.refs_2_, bf16[512,256]{1,0:T(8,128)(2,1)S(1)} %collective-permute-done.33.refs_3_, ...), custom_call_target="tpu_custom_call" | custom-call | flops 300000000 | bytes 9000000 | tf_op jit(solution)/shard_map/pair_solve/pallas_call | solution.py:563
  87.7 3.0 %last_rows.1 = (bf16[4096,256]{1,0:T(8,128)(2,1)}, bf16[2048,256]{1,0:T(8,128)(2,1)}) custom-call(s32[8]{0:T(128)S(1)} %copy-done.20, bf16[512,4096]{1,0:T(8,128)(2,1)S(1)} %mask_below.4.a0, bf16[512,4096]{1,0:T(8,128)(2,1)S(1)} %mask_below.5.a1, bf16[512,4096]{1,0:T(8,128)(2,1)S(1)} %mask_below.6.a2, bf16[512,4096]{1,0:T(8,128)(2,1)S(1)} %mask_below.7.a3, ...), custom_call_target="tpu_custom_call" | custom-call | flops 300000000 | bytes 9000000 | tf_op jit(solution)/shard_map/last_rows/pallas_call | solution.py:577
  (71 shorter events, 18.1 us)
Async XLA Ops:
  3.2 2.1 %collective-permute-start.3 = (bf16[512,512]{1,0:T(8,128)(2,1)S(1)}, bf16[512,512]{1,0:T(8,128)(2,1)S(1)}, u32[]{:S(2)}, u32[]{:S(2)}) collective-permute-start(bf16[512,512]{1,0:T(8,128)(2,1)S(1)} %factor_pack.1.own_ref.refs_0_), channel_id=1, source_target_pairs={{0,4},{4,0},{8,12},{12,8},{16,20},{20,16},{24,28},{28,24},{1,5},{5... | collective-permute-start | bytes 1572872 | tf_op jit(solution)/shard_map/ppermute | solution.py:380
  5.4 13.4 %collective-permute-start.4 = (bf16[512,4096]{1,0:T(8,128)(2,1)S(1)}, bf16[512,4096]{1,0:T(8,128)(2,1)S(1)}, u32[]{:S(2)}, u32[]{:S(2)}) collective-permute-start(bf16[512,4096]{1,0:T(8,128)(2,1)S(1)} %copy-done), channel_id=1, source_target_pairs={{0,4},{4,0},{8,12},{12,8},{16,20},{20,16},{24,28},{28,24},{1,5},{5... | collective-permute-start | bytes 12582920 | tf_op jit(solution)/shard_map/ppermute | solution.py:380
  5.9 15.8 %collective-permute-start.14 = (bf16[1024,512]{1,0:T(8,128)(2,1)S(1)}, bf16[1024,512]{1,0:T(8,128)(2,1)S(1)}, u32[]{:S(2)}, u32[]{:S(2)}) collective-permute-start(bf16[1024,512]{1,0:T(8,128)(2,1)S(1)} %get-tuple-element.375), channel_id=1, source_target_pairs={{0,8},{4,20},{8,0},{12,28},{16,24},{20,4},{24,16},{28,12},{1,9},{5... | collective-permute-start | bytes 3145736 | tf_op jit(solution)/shard_map/ppermute | solution.py:386
  8.5 4.4 %collective-permute-start.5 = (bf16[128,256]{1,0:T(8,128)(2,1)S(1)}, bf16[128,256]{1,0:T(8,128)(2,1)S(1)}, u32[]{:S(2)}, u32[]{:S(2)}) collective-permute-start(bf16[128,256]{1,0:T(8,128)(2,1)S(1)} %get-tuple-element.378), channel_id=1, source_target_pairs={{0,1},{1,0},{2,3},{3,2},{4,5},{5,4},{6,7},{7,6},{8,9},{9,8},{10,11... | collective-permute-start | bytes 196616 | tf_op jit(solution)/shard_map/ppermute | solution.py:383
  10.1 7.5 %collective-permute-start.6 = (bf16[128,256]{1,0:T(8,128)(2,1)S(1)}, bf16[128,256]{1,0:T(8,128)(2,1)S(1)}, u32[]{:S(2)}, u32[]{:S(2)}) collective-permute-start(bf16[128,256]{1,0:T(8,128)(2,1)S(1)} %get-tuple-element.379), channel_id=1, source_target_pairs={{0,2},{1,3},{2,0},{3,1},{4,6},{5,7},{6,4},{7,5},{8,10},{9,11},{10,... | collective-permute-start | bytes 196616 | tf_op jit(solution)/shard_map/ppermute | solution.py:383
  12.7 6.2 %collective-permute-start.7 = (bf16[128,256]{1,0:T(8,128)(2,1)S(1)}, bf16[128,256]{1,0:T(8,128)(2,1)S(1)}, u32[]{:S(2)}, u32[]{:S(2)}) collective-permute-start(bf16[128,256]{1,0:T(8,128)(2,1)S(1)} %get-tuple-element.380), channel_id=1, source_target_pairs={{0,3},{1,2},{2,1},{3,0},{4,7},{5,6},{6,5},{7,4},{8,11},{9,10},{10,... | collective-permute-start | bytes 196616 | tf_op jit(solution)/shard_map/ppermute | solution.py:383
  18.8 1.3 %collective-permute-start.8 = (bf16[128,256]{1,0:T(8,128)(2,1)S(1)}, bf16[128,256]{1,0:T(8,128)(2,1)S(1)}, u32[]{:S(2)}, u32[]{:S(2)}) collective-permute-start(bf16[128,256]{1,0:T(8,128)(2,1)S(1)} %get-tuple-element.807.refs_0_), channel_id=1, source_target_pairs={{0,4},{4,0},{8,12},{12,8},{16,20},{20,16},{24,28},{28,24},{1,5},{5... | collective-permute-start | bytes 196616 | tf_op jit(solution)/shard_map/ppermute | solution.py:380
  18.8 1.4 %collective-permute-start.9 = (bf16[128,256]{1,0:T(8,128)(2,1)S(1)}, bf16[128,256]{1,0:T(8,128)(2,1)S(1)}, u32[]{:S(2)}, u32[]{:S(2)}) collective-permute-start(bf16[128,256]{1,0:T(8,128)(2,1)S(1)} %collective-permute-done.5.refs_1_), channel_id=1, source_target_pairs={{0,4},{4,0},{8,12},{12,8},{16,20},{20,16},{24,28},{28,24},{1,5},{5... | collective-permute-start | bytes 196616 | tf_op jit(solution)/shard_map/ppermute | solution.py:380
  19.3 1.3 %collective-permute-start.10 = (bf16[128,256]{1,0:T(8,128)(2,1)S(1)}, bf16[128,256]{1,0:T(8,128)(2,1)S(1)}, u32[]{:S(2)}, u32[]{:S(2)}) collective-permute-start(bf16[128,256]{1,0:T(8,128)(2,1)S(1)} %collective-permute-done.6.refs_2_), channel_id=1, source_target_pairs={{0,4},{4,0},{8,12},{12,8},{16,20},{20,16},{24,28},{28,24},{1,5},{5... | collective-permute-start | bytes 196616 | tf_op jit(solution)/shard_map/ppermute | solution.py:380
  19.3 1.4 %collective-permute-start.11 = (bf16[128,256]{1,0:T(8,128)(2,1)S(1)}, bf16[128,256]{1,0:T(8,128)(2,1)S(1)}, u32[]{:S(2)}, u32[]{:S(2)}) collective-permute-start(bf16[128,256]{1,0:T(8,128)(2,1)S(1)} %collective-permute-done.7.refs_3_), channel_id=1, source_target_pairs={{0,4},{4,0},{8,12},{12,8},{16,20},{20,16},{24,28},{28,24},{1,5},{5... | collective-permute-start | bytes 196616 | tf_op jit(solution)/shard_map/ppermute | solution.py:380
  21.7 13.9 %collective-permute-start.15 = (bf16[512,512]{1,0:T(8,128)(2,1)S(1)}, bf16[512,512]{1,0:T(8,128)(2,1)S(1)}, u32[]{:S(2)}, u32[]{:S(2)}) collective-permute-start(bf16[512,512]{1,0:T(8,128)(2,1)S(1)} %take_half.1), channel_id=1, source_target_pairs={{0,16},{4,12},{8,24},{12,4},{16,0},{20,28},{24,8},{28,20},{1,17},{... | collective-permute-start | bytes 1572872 | tf_op jit(solution)/shard_map/ppermute | solution.py:389
  23.4 12.2 %collective-permute-start.12 = (bf16[512,256]{1,0:T(8,128)(2,1)S(1)}, bf16[512,256]{1,0:T(8,128)(2,1)S(1)}, u32[]{:S(2)}, u32[]{:S(2)}) collective-permute-start(bf16[512,256]{1,0:T(8,128)(2,1)S(1)} %get-tuple-element.385.refs_1_), channel_id=1, source_target_pairs={{0,8},{4,20},{8,0},{12,28},{16,24},{20,4},{24,16},{28,12},{1,9},{5... | collective-permute-start | bytes 786440 | tf_op jit(solution)/shard_map/ppermute | solution.py:386
  24.9 10.7 %collective-permute-start.13 = (bf16[256,256]{1,0:T(8,128)(2,1)S(1)}, bf16[256,256]{1,0:T(8,128)(2,1)S(1)}, u32[]{:S(2)}, u32[]{:S(2)}) collective-permute-start(bf16[256,256]{1,0:T(8,128)(2,1)S(1)} %get-tuple-element.389), channel_id=1, source_target_pairs={{0,24},{4,28},{8,16},{12,20},{16,8},{20,12},{24,0},{28,4},{1,25},{... | collective-permute-start | bytes 393224 | tf_op jit(solution)/shard_map/ppermute | solution.py:380
  35.6 5.7 %collective-permute-start.18 = (bf16[1024,512]{1,0:T(8,128)(2,1)S(1)}, bf16[1024,512]{1,0:T(8,128)(2,1)S(1)}, u32[]{:S(2)}, u32[]{:S(2)}) collective-permute-start(bf16[1024,512]{1,0:T(8,128)(2,1)S(1)} %collective-permute-done.14.x_ref.refs_2_), channel_id=1, source_target_pairs={{0,4},{4,0},{8,12},{12,8},{16,20},{20,16},{24,28},{28,24},{1,5},{5... | collective-permute-start | bytes 3145736 | tf_op jit(solution)/shard_map/ppermute | solution.py:380
  36.7 4.7 %collective-permute-start.19 = (bf16[512,512]{1,0:T(8,128)(2,1)S(1)}, bf16[512,512]{1,0:T(8,128)(2,1)S(1)}, u32[]{:S(2)}, u32[]{:S(2)}) collective-permute-start(bf16[512,512]{1,0:T(8,128)(2,1)S(1)} %collective-permute-done.15.refs_4_), channel_id=1, source_target_pairs={{0,4},{4,0},{8,12},{12,8},{16,20},{20,16},{24,28},{28,24},{1,5},{5... | collective-permute-start | bytes 1572872 | tf_op jit(solution)/shard_map/ppermute | solution.py:380
  36.8 6.4 %collective-permute-start.16 = (bf16[512,256]{1,0:T(8,128)(2,1)S(1)}, bf16[512,256]{1,0:T(8,128)(2,1)S(1)}, u32[]{:S(2)}, u32[]{:S(2)}) collective-permute-start(bf16[512,256]{1,0:T(8,128)(2,1)S(1)} %collective-permute-done.12.refs_2_), channel_id=1, source_target_pairs={{0,4},{4,0},{8,12},{12,8},{16,20},{20,16},{24,28},{28,24},{1,5},{5... | collective-permute-start | bytes 786440 | tf_op jit(solution)/shard_map/ppermute | solution.py:380
  37.2 5.9 %collective-permute-start.17 = (bf16[256,256]{1,0:T(8,128)(2,1)S(1)}, bf16[256,256]{1,0:T(8,128)(2,1)S(1)}, u32[]{:S(2)}, u32[]{:S(2)}) collective-permute-start(bf16[256,256]{1,0:T(8,128)(2,1)S(1)} %collective-permute-done.13.refs_4_), channel_id=1, source_target_pairs={{0,4},{4,0},{8,12},{12,8},{16,20},{20,16},{24,28},{28,24},{1,5},{5... | collective-permute-start | bytes 393224 | tf_op jit(solution)/shard_map/ppermute | solution.py:380
  38.5 17.1 %collective-permute-start.22 = (bf16[512,256]{1,0:T(8,128)(2,1)S(1)}, bf16[512,256]{1,0:T(8,128)(2,1)S(1)}, u32[]{:S(2)}, u32[]{:S(2)}) collective-permute-start(bf16[512,256]{1,0:T(8,128)(2,1)S(1)} %get-tuple-element.408), channel_id=1, source_target_pairs={{0,2},{1,3},{2,0},{3,1},{4,6},{5,7},{6,4},{7,5},{8,10},{9,11},{10,... | collective-permute-start | bytes 786440 | tf_op jit(solution)/shard_map/ppermute | solution.py:383
  45.4 10.1 %collective-permute-start.20 = (bf16[512,256]{1,0:T(8,128)(2,1)S(1)}, bf16[512,256]{1,0:T(8,128)(2,1)S(1)}, u32[]{:S(2)}, u32[]{:S(2)}) collective-permute-start(bf16[512,256]{1,0:T(8,128)(2,1)S(1)} %get-tuple-element.404.refs_1_), channel_id=1, source_target_pairs={{0,8},{4,20},{8,0},{12,28},{16,24},{20,4},{24,16},{28,12},{1,9},{5... | collective-permute-start | bytes 786440 | tf_op jit(solution)/shard_map/ppermute | solution.py:386
  46.4 9.2 %collective-permute-start.21 = (bf16[256,256]{1,0:T(8,128)(2,1)S(1)}, bf16[256,256]{1,0:T(8,128)(2,1)S(1)}, u32[]{:S(2)}, u32[]{:S(2)}) collective-permute-start(bf16[256,256]{1,0:T(8,128)(2,1)S(1)} %get-tuple-element.405), channel_id=1, source_target_pairs={{0,24},{4,28},{8,16},{12,20},{16,8},{20,12},{24,0},{28,4},{1,25},{... | collective-permute-start | bytes 393224 | tf_op jit(solution)/shard_map/ppermute | solution.py:380
  55.6 2.7 %collective-permute-start.23 = (bf16[512,256]{1,0:T(8,128)(2,1)S(1)}, bf16[512,256]{1,0:T(8,128)(2,1)S(1)}, u32[]{:S(2)}, u32[]{:S(2)}) collective-permute-start(bf16[512,256]{1,0:T(8,128)(2,1)S(1)} %collective-permute-done.20.refs_2_), channel_id=1, source_target_pairs={{0,4},{4,0},{8,12},{12,8},{16,20},{20,16},{24,28},{28,24},{1,5},{5... | collective-permute-start | bytes 786440 | tf_op jit(solution)/shard_map/ppermute | solution.py:380
  55.7 2.6 %collective-permute-start.24 = (bf16[256,256]{1,0:T(8,128)(2,1)S(1)}, bf16[256,256]{1,0:T(8,128)(2,1)S(1)}, u32[]{:S(2)}, u32[]{:S(2)}) collective-permute-start(bf16[256,256]{1,0:T(8,128)(2,1)S(1)} %collective-permute-done.21.refs_4_), channel_id=1, source_target_pairs={{0,4},{4,0},{8,12},{12,8},{16,20},{20,16},{24,28},{28,24},{1,5},{5... | collective-permute-start | bytes 393224 | tf_op jit(solution)/shard_map/ppermute | solution.py:380
  56.2 11.8 %collective-permute-start.27 = (bf16[512,256]{1,0:T(8,128)(2,1)S(1)}, bf16[512,256]{1,0:T(8,128)(2,1)S(1)}, u32[]{:S(2)}, u32[]{:S(2)}) collective-permute-start(bf16[512,256]{1,0:T(8,128)(2,1)S(1)} %get-tuple-element.424), channel_id=1, source_target_pairs={{0,3},{1,2},{2,1},{3,0},{4,7},{5,6},{6,5},{7,4},{8,11},{9,10},{10,... | collective-permute-start | bytes 786440 | tf_op jit(solution)/shard_map/ppermute | solution.py:383
  60.6 9.5 %collective-permute-start.25 = (bf16[512,256]{1,0:T(8,128)(2,1)S(1)}, bf16[512,256]{1,0:T(8,128)(2,1)S(1)}, u32[]{:S(2)}, u32[]{:S(2)}) collective-permute-start(bf16[512,256]{1,0:T(8,128)(2,1)S(1)} %get-tuple-element.421.refs_1_), channel_id=1, source_target_pairs={{0,8},{4,20},{8,0},{12,28},{16,24},{20,4},{24,16},{28,12},{1,9},{5... | collective-permute-start | bytes 786440 | tf_op jit(solution)/shard_map/ppermute | solution.py:386
  61.5 8.5 %collective-permute-start.26 = (bf16[256,256]{1,0:T(8,128)(2,1)S(1)}, bf16[256,256]{1,0:T(8,128)(2,1)S(1)}, u32[]{:S(2)}, u32[]{:S(2)}) collective-permute-start(bf16[256,256]{1,0:T(8,128)(2,1)S(1)} %get-tuple-element.422), channel_id=1, source_target_pairs={{0,24},{4,28},{8,16},{12,20},{16,8},{20,12},{24,0},{28,4},{1,25},{... | collective-permute-start | bytes 393224 | tf_op jit(solution)/shard_map/ppermute | solution.py:380
  70.1 2.1 %collective-permute-start.28 = (bf16[512,256]{1,0:T(8,128)(2,1)S(1)}, bf16[512,256]{1,0:T(8,128)(2,1)S(1)}, u32[]{:S(2)}, u32[]{:S(2)}) collective-permute-start(bf16[512,256]{1,0:T(8,128)(2,1)S(1)} %collective-permute-done.25.refs_2_), channel_id=1, source_target_pairs={{0,4},{4,0},{8,12},{12,8},{16,20},{20,16},{24,28},{28,24},{1,5},{5... | collective-permute-start | bytes 786440 | tf_op jit(solution)/shard_map/ppermute | solution.py:380
  70.1 2.1 %collective-permute-start.29 = (bf16[256,256]{1,0:T(8,128)(2,1)S(1)}, bf16[256,256]{1,0:T(8,128)(2,1)S(1)}, u32[]{:S(2)}, u32[]{:S(2)}) collective-permute-start(bf16[256,256]{1,0:T(8,128)(2,1)S(1)} %collective-permute-done.26.refs_4_), channel_id=1, source_target_pairs={{0,4},{4,0},{8,12},{12,8},{16,20},{20,16},{24,28},{28,24},{1,5},{5... | collective-permute-start | bytes 393224 | tf_op jit(solution)/shard_map/ppermute | solution.py:380
  70.6 8.2 %collective-permute-start.32 = (bf16[512,256]{1,0:T(8,128)(2,1)S(1)}, bf16[512,256]{1,0:T(8,128)(2,1)S(1)}, u32[]{:S(2)}, u32[]{:S(2)}) collective-permute-start(bf16[512,256]{1,0:T(8,128)(2,1)S(1)} %get-tuple-element.436), channel_id=1, source_target_pairs={{0,1},{1,0},{2,3},{3,2},{4,5},{5,4},{6,7},{7,6},{8,9},{9,8},{10,11... | collective-permute-start | bytes 786440 | tf_op jit(solution)/shard_map/ppermute | solution.py:383
  74.5 9.5 %collective-permute-start.30 = (bf16[512,256]{1,0:T(8,128)(2,1)S(1)}, bf16[512,256]{1,0:T(8,128)(2,1)S(1)}, u32[]{:S(2)}, u32[]{:S(2)}) collective-permute-start(bf16[512,256]{1,0:T(8,128)(2,1)S(1)} %get-tuple-element.433.refs_1_), channel_id=1, source_target_pairs={{0,8},{4,20},{8,0},{12,28},{16,24},{20,4},{24,16},{28,12},{1,9},{5... | collective-permute-start | bytes 786440 | tf_op jit(solution)/shard_map/ppermute | solution.py:386
  75.4 8.6 %collective-permute-start.31 = (bf16[256,256]{1,0:T(8,128)(2,1)S(1)}, bf16[256,256]{1,0:T(8,128)(2,1)S(1)}, u32[]{:S(2)}, u32[]{:S(2)}) collective-permute-start(bf16[256,256]{1,0:T(8,128)(2,1)S(1)} %get-tuple-element.434), channel_id=1, source_target_pairs={{0,24},{4,28},{8,16},{12,20},{16,8},{20,12},{24,0},{28,4},{1,25},{... | collective-permute-start | bytes 393224 | tf_op jit(solution)/shard_map/ppermute | solution.py:380
  84.0 1.7 %collective-permute-start.33 = (bf16[512,256]{1,0:T(8,128)(2,1)S(1)}, bf16[512,256]{1,0:T(8,128)(2,1)S(1)}, u32[]{:S(2)}, u32[]{:S(2)}) collective-permute-start(bf16[512,256]{1,0:T(8,128)(2,1)S(1)} %collective-permute-done.30.refs_2_), channel_id=1, source_target_pairs={{0,4},{4,0},{8,12},{12,8},{16,20},{20,16},{24,28},{28,24},{1,5},{5... | collective-permute-start | bytes 786440 | tf_op jit(solution)/shard_map/ppermute | solution.py:380
  84.0 1.7 %collective-permute-start.34 = (bf16[256,256]{1,0:T(8,128)(2,1)S(1)}, bf16[256,256]{1,0:T(8,128)(2,1)S(1)}, u32[]{:S(2)}, u32[]{:S(2)}) collective-permute-start(bf16[256,256]{1,0:T(8,128)(2,1)S(1)} %collective-permute-done.31.refs_4_), channel_id=1, source_target_pairs={{0,4},{4,0},{8,12},{12,8},{16,20},{20,16},{24,28},{28,24},{1,5},{5... | collective-permute-start | bytes 393224 | tf_op jit(solution)/shard_map/ppermute | solution.py:380
  (7 other events, 83.6 us)

commit v8 on v7

--- a/solution.py
+++ b/solution.py
@@ -118,14 +118,17 @@
         out[j * BS:(j + 1) * BS, :] = buf[j * BS:(j + 1) * BS, :] * mask[j:j + 1, :]
 
 
-def start_pack_kernel(own_ref, other_ref, rhs_ref, l_chip, *sent):
-    l_chip[0:SN, :] = own_ref[...]
-    l_chip[SN:PAIR, :] = other_ref[...]
+def rhs_pack_kernel(rhs_ref, *sent):
     depth = lax.axis_index("rhs")
     width = sent[0].shape[1]
     for s, out in enumerate(sent):
         at = pl.multiple_of(jnp.bitwise_xor(depth, s) * width, width)
         out[...] = rhs_ref[:, pl.ds(at, width)]
+
+
+def chip_pack_kernel(own_ref, other_ref, l_chip):
+    l_chip[0:SN, :] = own_ref[...]
+    l_chip[SN:PAIR, :] = other_ref[...]
 
 
 def take_half_kernel(x_ref, out):
@@ -154,7 +157,8 @@
             diagonal = rel == 3
             source = jnp.where(rel == 0, 0, jnp.where(diagonal, jnp.where(rank // 4 == core, 3, 4),
                                                       jnp.where(rel == 1 + core, 1, 2)))
-            tab[SRC + group * 16 + i] = source * SB + jnp.where(diagonal, rank % 4, rank)
+            start = jnp.where(source == 4, 7 * SB // 2, source * SB)
+            tab[SRC + group * 16 + i] = start + jnp.where(diagonal, rank % 4, rank)
 
             @pl.when(rel == 0)
             def _():
@@ -269,15 +273,15 @@
     def kernel(*refs):
         tab, sources, m_ref = refs[0], refs[1:6], refs[6]
         if last:
-            x_ref, panel = refs[7:]
+            x_ref, panel, pool = refs[7:]
         else:
-            r_ref, wn_ref, x_ref, p_ref, b_ref, panel = refs[7:]
+            r_ref, wn_ref, x_ref, p_ref, b_ref, panel, pool = refs[7:]
+        at = 0
+        for source in sources:
+            pool[at:at + source.shape[0], :] = source[...]
+            at += source.shape[0]
         for i in range(2 * SB):
-            code = tab[SRC + group * 16 + i]
-            for which, source in enumerate(sources):
-                @pl.when(code // SB == which)
-                def _(source=source, i=i, code=code):
-                    panel[i * BS:(i + 1) * BS, :] = source[rows_at(code % SB), :]
+            panel[i * BS:(i + 1) * BS, :] = pool[rows_at(tab[SRC + group * 16 + i]), :]
         x_ref[0:SN, :] = jnp.dot(m_ref[0:SN, 0:SN], panel[0:SN, :], preferred_element_type=F32).astype(BF16)
         x_ref[SN:PAIR, :] = jnp.dot(m_ref[SN:PAIR, :], panel[...], preferred_element_type=F32).astype(BF16)
         if last:
@@ -416,21 +420,32 @@
         cost_estimate=cost(2),
         name="factor_pack",
     )(window_owner, sn_order, win_pattern, w_own)
-    l_other = swap(l_own, 1)
-    l_chip, *sent = pl.pallas_call(
-        start_pack_kernel,
-        out_shape=(shape_of((PAIR, SN)),) + (shape_of((tall, columns)),) * 4,
-        in_specs=[VMEM] * 3,
-        out_specs=(VMEM,) * 5,
+    sent = pl.pallas_call(
+        rhs_pack_kernel,
+        out_shape=(shape_of((tall, columns)),) * 4,
+        in_specs=[VMEM],
+        out_specs=(VMEM,) * 4,
         compiler_params=params(4),
         cost_estimate=cost(1),
-        name="start_pack",
-    )(l_own, l_other, rhs_win)
+        name="rhs_pack",
+    )(rhs_win)
+    pieces = [sent[0]] + [deep(sent[s], s) for s in (1, 2, 3)]
+    l_late, pieces[1] = lax.optimization_barrier((l_own, pieces[1]))
+    l_other = swap(l_late, 1)
+    l_chip = pl.pallas_call(
+        chip_pack_kernel,
+        out_shape=shape_of((PAIR, SN)),
+        in_specs=[VMEM] * 2,
+        out_specs=VMEM,
+        compiler_params=params(4),
+        cost_estimate=cost(1),
+        name="chip_pack",
+    )(l_own, l_other)
     near = neighbour(l_chip)
-    pieces = [sent[0]] + [deep(sent[s], s) for s in (1, 2, 3)]
     w_late, _ = lax.optimization_barrier((win_rows, l_chip))
     w_other = swap(w_late, 1)
-    w_other, *pieces = lax.optimization_barrier((w_other, *pieces))
+    below = [mask_below(k, l_chip) for k in (0, 1)]
+    w_other, below[0], below[1], *pieces = lax.optimization_barrier((w_other, *below, *pieces))
     others = [swap(x, 1) for x in pieces]
     chip_rhs, packed, part = pl.pallas_call(
         first_pack_kernel,
@@ -466,20 +481,18 @@
     )(owner_later, order_later)
     w_other = in_vmem(w_other)
     w_own = in_vmem(win_rows)
-    below = []
 
     tile = rhs_anc.shape[0]
     sums, solved, masked = None, [], []
     diag_vmem = in_vmem(diag_inv)
     below_rows = anc_rows.shape[0]
 
-    anc_order, anc_pieces = (2, 3, 1), [None] * 4
+    anc_order, anc_pieces = (1, 2, 3), [None] * 4
     for group in range(GROUPS):
         last = group == GROUPS - 1
         a_own = neighbour(packed)
         b_own = swap(part, 6)
         if group == 0:
-            below += [mask_below(k, packed) for k in (0, 1)]
             for k in range(GROUPS - 1):
                 masked.append(pl.pallas_call(
                     make_mask_kernel(k),
@@ -509,8 +522,8 @@
             anc_pieces[s] = deep(moved, s)
 
         if group == 0:
-            a_own, b_own, near, far, below[0], below[1], *masked = lax.optimization_barrier(
-                (a_own, b_own, near, far, below[0], below[1], *masked))
+            a_own, b_own, near, far, anc_pieces[1], *masked = lax.optimization_barrier(
+                (a_own, b_own, near, far, anc_pieces[1], *masked))
             l_parts = [in_vmem(x) for x in (l_own, l_other, near, swap(near, 1), far, swap(far, 1))]
         operands = [tab, sn_order, diag_vmem, *l_parts]
         out_shape = [shape_of((PAIR, PAIR))]
@@ -565,7 +578,7 @@
             out_shape=tuple(out_shape),
             in_specs=[SMEM] + [VMEM] * (5 + len(ready)),
             out_specs=(VMEM,) * len(out_shape),
-            scratch_shapes=[pltpu.VMEM((PAIR, columns), BF16)],
+            scratch_shapes=[pltpu.VMEM((PAIR, columns), BF16), pltpu.VMEM((2 * PAIR, columns), BF16)],
             compiler_params=params(8),
             cost_estimate=cost(3),
             name="pair_solve",

time: 91.7 us -> 93.8 us (1.023)
  Pallas kernels: 44.7 us -> 42.4 us
  waiting for transfers between devices: 15 us -> 17.3 us
  local copies, waits for them, and re-layouts: 0.04 us -> 0.98 us
    ppermute x6, starting transfers between devices: 10.9 us -> 14.7 us  [deep(): return lax.ppermute(x, 'rhs', [(i, i ^ m) for i in range(4)])]
    pallas_call x4, Pallas kernels: 8.84 us -> 6.54 us  [local(): pl.pallas_call(make_solve_kernel(group), out_shape=tuple(out_shape), in_s...]
    ppermute x5, starting transfers between devices: 6.93 us -> 5.04 us  [neighbour(): lax.ppermute(x, 'rows', [(i, i ^ (2 if i % 2 == 0 else 4)) for i in range...]
    ppermute x5, waiting for transfers between devices: 0.01 us -> 1.67 us  [neighbour(): lax.ppermute(x, 'rows', [(i, i ^ (2 if i % 2 == 0 else 4)) for i in range...]
    ppermute x6, waiting for transfers between devices: 6.16 us -> 4.62 us  [deep(): return lax.ppermute(x, 'rhs', [(i, i ^ m) for i in range(4)])]
    ppermute x20, waiting for transfers between devices: 8.81 us -> 10 us  [swap(): return lax.ppermute(x, 'rows', [(i, i ^ m) for i in range(8)])]
    ppermute x20, starting transfers between devices: 10.4 us -> 9.42 us  [swap(): return lax.ppermute(x, 'rows', [(i, i ^ m) for i in range(8)])]
    ppermute x1, waiting for transfers between devices: 0.01 us -> 0.99 us  [forward(): lax.ppermute(x, 'rows', [(i, i ^ (4 if i % 2 == 0 else 2)) for i in range...]
  transfers between devices with their start and end apart: 32 -> 32, of which waited for: 11 -> 15; matrix products, arithmetic and copies ran while one was open for 0% -> 0% of each run, Pallas kernels for 40% -> 39%
where the time goes in v8:
time: 93.8 us; the launch traced here: 93.5 us
  Pallas kernels  42.4 us (45%)
  starting transfers between devices  30.8 us (33%)
  waiting for transfers between devices  17.3 us (18%)
  between operations  1.13 us (1%)
  local copies, waits for them, and re-layouts  0.98 us (1%)
    ppermute x6, starting transfers between devices, deep(): return lax.ppermute(x, 'rhs', [(i, i ^ m) for i in range(4)])  14.7 us
    ppermute x20, waiting for transfers between devices, swap(): return lax.ppermute(x, 'rows', [(i, i ^ m) for i in range(8)])  10 us
    ppermute x20, starting transfers between devices, swap(): return lax.ppermute(x, 'rows', [(i, i ^ m) for i in range(8)])  9.42 us
    pallas_call x4, Pallas kernels, mask_below(): pl.pallas_call(make_below_mask_kernel(k), out_shape=shape_of((SN, NW)), i...  9.03 us
    pallas_call x4, Pallas kernels, local(): pl.pallas_call(make_prep_kernel(group), out_shape=tuple(out_shape), in_sp...  8.2 us
    pallas_call x4, Pallas kernels, local(): pl.pallas_call(make_solve_kernel(group), out_shape=tuple(out_shape), in_s...  6.54 us
    ppermute x5, starting transfers between devices, neighbour(): lax.ppermute(x, 'rows', [(i, i ^ (2 if i % 2 == 0 else 4)) for i in range...  5.04 us
    pallas_call x2, Pallas kernels, local(): pl.pallas_call(kernel, out_shape=shape_of((below_rows, columns), F32), in...  5.01 us
  transfers between devices with their start and end apart: 32, of which 15 were waited for; matrix products, arithmetic and copies ran while one was open for 0% of the time, Pallas kernels for 39%

profile of v8, /device:TPU:0, one launch (start us, length us, event | category | flops | bytes accessed | tf_op | source)
XLA Modules:
  0.0 93.5 jit_solution(11110995420446237857)
XLA Ops:
  1.6 3.1 %collective-permute-start.3 = (bf16[128,256]{1,0:T(8,128)(2,1)S(1)}, bf16[128,256]{1,0:T(8,128)(2,1)S(1)}, u32[]{:S(2)}, u32[]{:S(2)}) collective-permute-start(bf16[128,256]{1,0:T(8,128)(2,1)S(1)} %get-tuple-element.377), channel_id=1, source_target_pairs={{0,1},{1,0},{2,3},{3,2},{4,5},{5,4},{6,7},{7,6},{8,9},{9,8},{10,11... | collective-permute-start | bytes 196616 | tf_op jit(solution)/shard_map/ppermute | solution.py:387
  4.7 2.5 %factor_pack.1.own_ref.refs_0_ = bf16[512,512]{1,0:T(8,128)(2,1)S(1)} custom-call(s32[64]{0:T(128)} %owner.4, s32[8]{0:T(128)} %order.21, s32[64,64]{1,0:T(8,128)} %pattern.9, bf16[512,4096]{1,0:T(8,128)(2,1)} %w_own.5), custom_call_target="tpu_custom_call" | custom-call | flops 200000000 | bytes 6000000 | tf_op jit(solution)/shard_map/factor_pack/pallas_call | solution.py:412
  7.4 1.9 %collective-permute-done.4.other_ref.refs_1_ = bf16[512,512]{1,0:T(8,128)(2,1)S(1)} collective-permute-done((bf16[512,512]{1,0:T(8,128)(2,1)S(1)}, bf16[512,512]{1,0:T(8,128)(2,1)S(1)}, u32[]{:S(2)}, u32[]{:S(2)}) %collective-permute-start.4) | collective-permute-done | bytes 524320 | tf_op jit(solution)/shard_map/ppermute | solution.py:384
  9.5 1.5 %collective-permute-start.14 = (bf16[1024,512]{1,0:T(8,128)(2,1)S(1)}, bf16[1024,512]{1,0:T(8,128)(2,1)S(1)}, u32[]{:S(2)}, u32[]{:S(2)}) collective-permute-start(bf16[1024,512]{1,0:T(8,128)(2,1)S(1)} %chip_pack.1), channel_id=1, source_target_pairs={{0,8},{4,20},{8,0},{12,28},{16,24},{20,4},{24,16},{28,12},{1,9},{5... | collective-permute-start | bytes 3145736 | tf_op jit(solution)/shard_map/ppermute | solution.py:390
  11.1 2.6 %collective-permute-start.6 = (bf16[128,256]{1,0:T(8,128)(2,1)S(1)}, bf16[128,256]{1,0:T(8,128)(2,1)S(1)}, u32[]{:S(2)}, u32[]{:S(2)}) collective-permute-start(bf16[128,256]{1,0:T(8,128)(2,1)S(1)} %get-tuple-element.383), channel_id=1, source_target_pairs={{0,2},{1,3},{2,0},{3,1},{4,6},{5,7},{6,4},{7,5},{8,10},{9,11},{10,... | collective-permute-start | bytes 196616 | tf_op jit(solution)/shard_map/ppermute | solution.py:387
  15.0 2.3 %mask_below.4.a0 = bf16[512,4096]{1,0:T(8,128)(2,1)S(1)} custom-call(s32[32,64]{1,0:T(8,128)S(1)} %copy-done.3, bf16[2048,4096]{1,0:T(8,128)(2,1)} %a_ref.7), custom_call_target="tpu_custom_call" | custom-call | flops 200000000 | bytes 6000000 | tf_op jit(solution)/shard_map/mask_below/pallas_call | solution.py:397
  17.3 2.3 %mask_below.5.a1 = bf16[512,4096]{1,0:T(8,128)(2,1)S(1)} custom-call(s32[32,64]{1,0:T(8,128)S(1)} %copy-done.3, bf16[2048,4096]{1,0:T(8,128)(2,1)} %a_ref.7), custom_call_target="tpu_custom_call" | custom-call | flops 200000000 | bytes 6000000 | tf_op jit(solution)/shard_map/mask_below/pallas_call | solution.py:397
  22.7 1.7 %collective-permute-done.14.x_ref.refs_2_ = bf16[1024,512]{1,0:T(8,128)(2,1)S(1)} collective-permute-done((bf16[1024,512]{1,0:T(8,128)(2,1)S(1)}, bf16[1024,512]{1,0:T(8,128)(2,1)S(1)}, u32[]{:S(2)}, u32[]{:S(2)}) %collective-permute-start.14) | collective-permute-done | bytes 1048608 | tf_op jit(solution)/shard_map/ppermute | solution.py:390
  24.4 1.6 %collective-permute-start.15 = (bf16[512,512]{1,0:T(8,128)(2,1)S(1)}, bf16[512,512]{1,0:T(8,128)(2,1)S(1)}, u32[]{:S(2)}, u32[]{:S(2)}) collective-permute-start(bf16[512,512]{1,0:T(8,128)(2,1)S(1)} %take_half.1), channel_id=1, source_target_pairs={{0,16},{4,12},{8,24},{12,4},{16,0},{20,28},{24,8},{28,20},{1,17},{... | collective-permute-start | bytes 1572872 | tf_op jit(solution)/shard_map/ppermute | solution.py:393
  26.0 1.5 %collective-permute-start.12 = (bf16[512,256]{1,0:T(8,128)(2,1)S(1)}, bf16[512,256]{1,0:T(8,128)(2,1)S(1)}, u32[]{:S(2)}, u32[]{:S(2)}) collective-permute-start(bf16[512,256]{1,0:T(8,128)(2,1)S(1)} %get-tuple-element.389.refs_1_), channel_id=1, source_target_pairs={{0,8},{4,20},{8,0},{12,28},{16,24},{20,4},{24,16},{28,12},{1,9},{5... | collective-permute-start | bytes 786440 | tf_op jit(solution)/shard_map/ppermute | solution.py:390
  28.7 1.6 %collective-permute-start.16 = (bf16[512,256]{1,0:T(8,128)(2,1)S(1)}, bf16[512,256]{1,0:T(8,128)(2,1)S(1)}, u32[]{:S(2)}, u32[]{:S(2)}) collective-permute-start(bf16[512,256]{1,0:T(8,128)(2,1)S(1)} %get-tuple-element.400), channel_id=1, source_target_pairs={{0,1},{1,0},{2,3},{3,2},{4,5},{5,4},{6,7},{7,6},{8,9},{9,8},{10,11... | collective-permute-start | bytes 786440 | tf_op jit(solution)/shard_map/ppermute | solution.py:387
  30.9 2.8 %tables.1 = (s32[128]{0:T(128)S(1)}, s32[2]{0:T(128)}) custom-call(s32[64]{0:T(128)S(1)} %copy-done.19, s32[8]{0:T(128)S(1)} %copy-done.20), custom_call_target="tpu_custom_call" | custom-call | flops 300000000 | bytes 9000000 | tf_op jit(solution)/shard_map/tables/pallas_call | solution.py:472
  40.1 2.4 %collective-permute-done.20.refs_5_ = bf16[512,512]{1,0:T(8,128)(2,1)S(1)} collective-permute-done((bf16[512,512]{1,0:T(8,128)(2,1)S(1)}, bf16[512,512]{1,0:T(8,128)(2,1)S(1)}, u32[]{:S(2)}, u32[]{:S(2)}) %collective-permute-start.20) | collective-permute-done | bytes 524320 | tf_op jit(solution)/shard_map/ppermute | solution.py:384
  42.5 1.7 %prep.4 = (bf16[1024,1024]{1,0:T(8,128)(2,1)S(1)}, f32[512,256]{1,0:T(8,128)S(1)}) custom-call(s32[128]{0:T(128)S(1)} %get-tuple-element.395.tab.refs_0_, s32[8]{0:T(128)S(1)} %copy-done.20, bf16[8,512,512]{2,1,0:T(8,128)(2,1)S(1)} %copy-done.1, bf16[512,512]{1,0:T(8,128)(2,1)S(1)} %factor_pack.1.own_ref.refs_0_, ...), custom_call_target="tpu_custom_call" | custom-call | flops 200000000 | bytes 6000000 | tf_op jit(solution)/shard_map/prep/pallas_call | solution.py:533
  44.2 1.8 %pair_solve.4 = (bf16[1024,256]{1,0:T(8,128)(2,1)S(1)}, bf16[512,256]{1,0:T(8,128)(2,1)S(1)}, bf16[256,256]{1,0:T(8,128)(2,1)S(1)}) custom-call(s32[128]{0:T(128)S(1)} %get-tuple-element.395.tab.refs_0_, bf16[512,256]{1,0:T(8,128)(2,1)S(1)} %get-tuple-element.389.refs_1_, bf16[512,256]{1,0:T(8,128)(2,1)S(1)} %collective-permute-done.12.refs_2_, ...), custom_call_target="tpu_custom_call" | custom-call | flops 300000000 | bytes 9000000 | tf_op jit(solution)/shard_map/pair_solve/pallas_call | solution.py:576
  46.8 2.2 %collective-permute-start.22 = (bf16[256,256]{1,0:T(8,128)(2,1)S(1)}, bf16[256,256]{1,0:T(8,128)(2,1)S(1)}, u32[]{:S(2)}, u32[]{:S(2)}) collective-permute-start(bf16[256,256]{1,0:T(8,128)(2,1)S(1)} %get-tuple-element.411), channel_id=1, source_target_pairs={{0,24},{4,28},{8,16},{12,20},{16,8},{20,12},{24,0},{28,4},{1,25},{... | collective-permute-start | bytes 393224 | tf_op jit(solution)/shard_map/ppermute | solution.py:384
  49.0 2.3 %mask_below.6.a2 = bf16[512,4096]{1,0:T(8,128)(2,1)S(1)} custom-call(s32[32,64]{1,0:T(8,128)S(1)} %copy-done.3, bf16[2048,4096]{1,0:T(8,128)(2,1)} %a_ref.7), custom_call_target="tpu_custom_call" | custom-call | flops 200000000 | bytes 6000000 | tf_op jit(solution)/shard_map/mask_below/pallas_call | solution.py:397
  51.3 2.3 %mask_below.7.a3 = bf16[512,4096]{1,0:T(8,128)(2,1)S(1)} custom-call(s32[32,64]{1,0:T(8,128)S(1)} %copy-done.3, bf16[2048,4096]{1,0:T(8,128)(2,1)} %a_ref.7), custom_call_target="tpu_custom_call" | custom-call | flops 200000000 | bytes 6000000 | tf_op jit(solution)/shard_map/mask_below/pallas_call | solution.py:397
  53.6 2.5 %prep.5 = (bf16[1024,1024]{1,0:T(8,128)(2,1)S(1)}, f32[512,256]{1,0:T(8,128)S(1)}) custom-call(s32[128]{0:T(128)S(1)} %get-tuple-element.395.tab.refs_0_, s32[8]{0:T(128)S(1)} %copy-done.20, bf16[8,512,512]{2,1,0:T(8,128)(2,1)S(1)} %copy-done.1, bf16[512,512]{1,0:T(8,128)(2,1)S(1)} %factor_pack.1.own_ref.refs_0_, ...), custom_call_target="tpu_custom_call" | custom-call | flops 200000000 | bytes 6000000 | tf_op jit(solution)/shard_map/prep/pallas_call | solution.py:533
  56.7 2.6 %collective-permute-start.27 = (bf16[512,256]{1,0:T(8,128)(2,1)S(1)}, bf16[512,256]{1,0:T(8,128)(2,1)S(1)}, u32[]{:S(2)}, u32[]{:S(2)}) collective-permute-start(bf16[512,256]{1,0:T(8,128)(2,1)S(1)} %get-tuple-element.428), channel_id=1, source_target_pairs={{0,2},{1,3},{2,0},{3,1},{4,6},{5,7},{6,4},{7,5},{8,10},{9,11},{10,... | collective-permute-start | bytes 786440 | tf_op jit(solution)/shard_map/ppermute | solution.py:387
  59.3 1.8 %pair_solve.5 = (bf16[1024,256]{1,0:T(8,128)(2,1)S(1)}, bf16[512,256]{1,0:T(8,128)(2,1)S(1)}, bf16[256,256]{1,0:T(8,128)(2,1)S(1)}) custom-call(s32[128]{0:T(128)S(1)} %get-tuple-element.395.tab.refs_0_, bf16[512,256]{1,0:T(8,128)(2,1)S(1)} %get-tuple-element.410.refs_1_, bf16[512,256]{1,0:T(8,128)(2,1)S(1)} %collective-permute-done.21.refs_2_, ...), custom_call_target="tpu_custom_call" | custom-call | flops 300000000 | bytes 9000000 | tf_op jit(solution)/shard_map/pair_solve/pallas_call | solution.py:576
  61.7 1.4 %collective-permute-start.26 = (bf16[256,256]{1,0:T(8,128)(2,1)S(1)}, bf16[256,256]{1,0:T(8,128)(2,1)S(1)}, u32[]{:S(2)}, u32[]{:S(2)}) collective-permute-start(bf16[256,256]{1,0:T(8,128)(2,1)S(1)} %get-tuple-element.426), channel_id=1, source_target_pairs={{0,24},{4,28},{8,16},{12,20},{16,8},{20,12},{24,0},{28,4},{1,25},{... | collective-permute-start | bytes 393224 | tf_op jit(solution)/shard_map/ppermute | solution.py:384
  63.1 2.2 %prep.6 = (bf16[1024,1024]{1,0:T(8,128)(2,1)S(1)}, f32[512,256]{1,0:T(8,128)S(1)}) custom-call(s32[128]{0:T(128)S(1)} %get-tuple-element.395.tab.refs_0_, s32[8]{0:T(128)S(1)} %copy-done.20, bf16[8,512,512]{2,1,0:T(8,128)(2,1)S(1)} %copy-done.1, bf16[512,512]{1,0:T(8,128)(2,1)S(1)} %factor_pack.1.own_ref.refs_0_, ...), custom_call_target="tpu_custom_call" | custom-call | flops 200000000 | bytes 6000000 | tf_op jit(solution)/shard_map/prep/pallas_call | solution.py:533
  65.4 2.9 %rows_below.2.sums = f32[2048,256]{1,0:T(8,128)S(1)} custom-call(s32[8]{0:T(128)S(1)} %copy-done.20, bf16[512,4096]{1,0:T(8,128)(2,1)S(1)} %mask_below.4.a0, bf16[512,4096]{1,0:T(8,128)(2,1)S(1)} %mask_below.5.a1, bf16[512,4096]{1,0:T(8,128)(2,1)S(1)} %mask_below.6.a2, bf16[512,4096]{1,0:T(8,128)(2,1)S(1)} %mask_below.7.a3, ...), custom_call_target="tpu_custom_call" | custom-call | flops 300000000 | bytes 9000000 | tf_op jit(solution)/shard_map/rows_below/pallas_call | solution.py:549
  68.3 3.3 %collective-permute-done.27.h2 = bf16[512,256]{1,0:T(8,128)(2,1)S(1)} collective-permute-done((bf16[512,256]{1,0:T(8,128)(2,1)S(1)}, bf16[512,256]{1,0:T(8,128)(2,1)S(1)}, u32[]{:S(2)}, u32[]{:S(2)}) %collective-permute-start.27) | collective-permute-done | bytes 262176 | tf_op jit(solution)/shard_map/ppermute | solution.py:387
  72.1 3.5 %collective-permute-start.32 = (bf16[512,256]{1,0:T(8,128)(2,1)S(1)}, bf16[512,256]{1,0:T(8,128)(2,1)S(1)}, u32[]{:S(2)}, u32[]{:S(2)}) collective-permute-start(bf16[512,256]{1,0:T(8,128)(2,1)S(1)} %get-tuple-element.440), channel_id=1, source_target_pairs={{0,3},{1,2},{2,1},{3,0},{4,7},{5,6},{6,5},{7,4},{8,11},{9,10},{10,... | collective-permute-start | bytes 786440 | tf_op jit(solution)/shard_map/ppermute | solution.py:387
  75.5 1.8 %pair_solve.6 = (bf16[1024,256]{1,0:T(8,128)(2,1)S(1)}, bf16[512,256]{1,0:T(8,128)(2,1)S(1)}, bf16[256,256]{1,0:T(8,128)(2,1)S(1)}) custom-call(s32[128]{0:T(128)S(1)} %get-tuple-element.395.tab.refs_0_, bf16[512,256]{1,0:T(8,128)(2,1)S(1)} %get-tuple-element.425.refs_1_, bf16[512,256]{1,0:T(8,128)(2,1)S(1)} %collective-permute-done.25.refs_2_, ...), custom_call_target="tpu_custom_call" | custom-call | flops 300000000 | bytes 9000000 | tf_op jit(solution)/shard_map/pair_solve/pallas_call | solution.py:576
  77.9 1.4 %collective-permute-start.31 = (bf16[256,256]{1,0:T(8,128)(2,1)S(1)}, bf16[256,256]{1,0:T(8,128)(2,1)S(1)}, u32[]{:S(2)}, u32[]{:S(2)}) collective-permute-start(bf16[256,256]{1,0:T(8,128)(2,1)S(1)} %get-tuple-element.438), channel_id=1, source_target_pairs={{0,24},{4,28},{8,16},{12,20},{16,8},{20,12},{24,0},{28,4},{1,25},{... | collective-permute-start | bytes 393224 | tf_op jit(solution)/shard_map/ppermute | solution.py:384
  79.4 1.7 %prep.7.refs_6_ = bf16[1024,1024]{1,0:T(8,128)(2,1)S(1)} custom-call(s32[128]{0:T(128)S(1)} %get-tuple-element.395.tab.refs_0_, s32[8]{0:T(128)S(1)} %copy-done.20, bf16[8,512,512]{2,1,0:T(8,128)(2,1)S(1)} %copy-done.1, bf16[512,512]{1,0:T(8,128)(2,1)S(1)} %factor_pack.1.own_ref.refs_0_, bf16[512,512]{1,0:T(8,128)(2,1)S(1)} %collective-permute-done.4.other_ref.refs_1_, ...), custom_call_target="tpu_custom_call" | custom-call | flops 200000000 | bytes 6000000 | tf_op jit(solution)/shard_map/prep/pallas_call | solution.py:533
  82.2 2.1 %rows_below.3.base = f32[2048,256]{1,0:T(8,128)S(1)} custom-call(s32[8]{0:T(128)S(1)} %copy-done.20, bf16[512,4096]{1,0:T(8,128)(2,1)S(1)} %mask_below.4.a0, bf16[512,4096]{1,0:T(8,128)(2,1)S(1)} %mask_below.5.a1, bf16[512,4096]{1,0:T(8,128)(2,1)S(1)} %mask_below.6.a2, bf16[512,4096]{1,0:T(8,128)(2,1)S(1)} %mask_below.7.a3, ...), custom_call_target="tpu_custom_call", output_to_operand_aliasing={{}: (6, {})} | custom-call | flops 300000000 | bytes 9000000 | tf_op jit(solution)/shard_map/rows_below/pallas_call | solution.py:549
  84.4 2.1 %collective-permute-done.31.refs_4_ = bf16[256,256]{1,0:T(8,128)(2,1)S(1)} collective-permute-done((bf16[256,256]{1,0:T(8,128)(2,1)S(1)}, bf16[256,256]{1,0:T(8,128)(2,1)S(1)}, u32[]{:S(2)}, u32[]{:S(2)}) %collective-permute-start.31) | collective-permute-done | bytes 131104 | tf_op jit(solution)/shard_map/ppermute | solution.py:384
  89.5 3.0 %last_rows.1 = (bf16[4096,256]{1,0:T(8,128)(2,1)}, bf16[2048,256]{1,0:T(8,128)(2,1)}) custom-call(s32[8]{0:T(128)S(1)} %copy-done.20, bf16[512,4096]{1,0:T(8,128)(2,1)S(1)} %mask_below.4.a0, bf16[512,4096]{1,0:T(8,128)(2,1)S(1)} %mask_below.5.a1, bf16[512,4096]{1,0:T(8,128)(2,1)S(1)} %mask_below.6.a2, bf16[512,4096]{1,0:T(8,128)(2,1)S(1)} %mask_below.7.a3, ...), custom_call_target="tpu_custom_call" | custom-call | flops 300000000 | bytes 9000000 | tf_op jit(solution)/shard_map/last_rows/pallas_call | solution.py:590
  (72 shorter events, 21.9 us)
Async XLA Ops:
  1.6 5.7 %collective-permute-start.3 = (bf16[128,256]{1,0:T(8,128)(2,1)S(1)}, bf16[128,256]{1,0:T(8,128)(2,1)S(1)}, u32[]{:S(2)}, u32[]{:S(2)}) collective-permute-start(bf16[128,256]{1,0:T(8,128)(2,1)S(1)} %get-tuple-element.377), channel_id=1, source_target_pairs={{0,1},{1,0},{2,3},{3,2},{4,5},{5,4},{6,7},{7,6},{8,9},{9,8},{10,11... | collective-permute-start | bytes 196616 | tf_op jit(solution)/shard_map/ppermute | solution.py:387
  7.3 2.0 %collective-permute-start.4 = (bf16[512,512]{1,0:T(8,128)(2,1)S(1)}, bf16[512,512]{1,0:T(8,128)(2,1)S(1)}, u32[]{:S(2)}, u32[]{:S(2)}) collective-permute-start(bf16[512,512]{1,0:T(8,128)(2,1)S(1)} %factor_pack.1.own_ref.refs_0_), channel_id=1, source_target_pairs={{0,4},{4,0},{8,12},{12,8},{16,20},{20,16},{24,28},{28,24},{1,5},{5... | collective-permute-start | bytes 1572872 | tf_op jit(solution)/shard_map/ppermute | solution.py:384
  9.3 10.5 %collective-permute-start.5 = (bf16[512,4096]{1,0:T(8,128)(2,1)S(1)}, bf16[512,4096]{1,0:T(8,128)(2,1)S(1)}, u32[]{:S(2)}, u32[]{:S(2)}) collective-permute-start(bf16[512,4096]{1,0:T(8,128)(2,1)S(1)} %copy-done), channel_id=1, source_target_pairs={{0,4},{4,0},{8,12},{12,8},{16,20},{20,16},{24,28},{28,24},{1,5},{5... | collective-permute-start | bytes 12582920 | tf_op jit(solution)/shard_map/ppermute | solution.py:384
  9.5 14.8 %collective-permute-start.14 = (bf16[1024,512]{1,0:T(8,128)(2,1)S(1)}, bf16[1024,512]{1,0:T(8,128)(2,1)S(1)}, u32[]{:S(2)}, u32[]{:S(2)}) collective-permute-start(bf16[1024,512]{1,0:T(8,128)(2,1)S(1)} %chip_pack.1), channel_id=1, source_target_pairs={{0,8},{4,20},{8,0},{12,28},{16,24},{20,4},{24,16},{28,12},{1,9},{5... | collective-permute-start | bytes 3145736 | tf_op jit(solution)/shard_map/ppermute | solution.py:390
  11.1 8.5 %collective-permute-start.6 = (bf16[128,256]{1,0:T(8,128)(2,1)S(1)}, bf16[128,256]{1,0:T(8,128)(2,1)S(1)}, u32[]{:S(2)}, u32[]{:S(2)}) collective-permute-start(bf16[128,256]{1,0:T(8,128)(2,1)S(1)} %get-tuple-element.383), channel_id=1, source_target_pairs={{0,2},{1,3},{2,0},{3,1},{4,6},{5,7},{6,4},{7,5},{8,10},{9,11},{10,... | collective-permute-start | bytes 196616 | tf_op jit(solution)/shard_map/ppermute | solution.py:387
  13.7 6.1 %collective-permute-start.7 = (bf16[128,256]{1,0:T(8,128)(2,1)S(1)}, bf16[128,256]{1,0:T(8,128)(2,1)S(1)}, u32[]{:S(2)}, u32[]{:S(2)}) collective-permute-start(bf16[128,256]{1,0:T(8,128)(2,1)S(1)} %get-tuple-element.384), channel_id=1, source_target_pairs={{0,3},{1,2},{2,1},{3,0},{4,7},{5,6},{6,5},{7,4},{8,11},{9,10},{10,... | collective-permute-start | bytes 196616 | tf_op jit(solution)/shard_map/ppermute | solution.py:387
  19.8 1.3 %collective-permute-start.8 = (bf16[128,256]{1,0:T(8,128)(2,1)S(1)}, bf16[128,256]{1,0:T(8,128)(2,1)S(1)}, u32[]{:S(2)}, u32[]{:S(2)}) collective-permute-start(bf16[128,256]{1,0:T(8,128)(2,1)S(1)} %get-tuple-element.811.refs_0_), channel_id=1, source_target_pairs={{0,4},{4,0},{8,12},{12,8},{16,20},{20,16},{24,28},{28,24},{1,5},{5... | collective-permute-start | bytes 196616 | tf_op jit(solution)/shard_map/ppermute | solution.py:384
  19.8 1.4 %collective-permute-start.9 = (bf16[128,256]{1,0:T(8,128)(2,1)S(1)}, bf16[128,256]{1,0:T(8,128)(2,1)S(1)}, u32[]{:S(2)}, u32[]{:S(2)}) collective-permute-start(bf16[128,256]{1,0:T(8,128)(2,1)S(1)} %collective-permute-done.3.refs_1_), channel_id=1, source_target_pairs={{0,4},{4,0},{8,12},{12,8},{16,20},{20,16},{24,28},{28,24},{1,5},{5... | collective-permute-start | bytes 196616 | tf_op jit(solution)/shard_map/ppermute | solution.py:384
  20.3 1.3 %collective-permute-start.10 = (bf16[128,256]{1,0:T(8,128)(2,1)S(1)}, bf16[128,256]{1,0:T(8,128)(2,1)S(1)}, u32[]{:S(2)}, u32[]{:S(2)}) collective-permute-start(bf16[128,256]{1,0:T(8,128)(2,1)S(1)} %collective-permute-done.6.refs_2_), channel_id=1, source_target_pairs={{0,4},{4,0},{8,12},{12,8},{16,20},{20,16},{24,28},{28,24},{1,5},{5... | collective-permute-start | bytes 196616 | tf_op jit(solution)/shard_map/ppermute | solution.py:384
  20.4 1.3 %collective-permute-start.11 = (bf16[128,256]{1,0:T(8,128)(2,1)S(1)}, bf16[128,256]{1,0:T(8,128)(2,1)S(1)}, u32[]{:S(2)}, u32[]{:S(2)}) collective-permute-start(bf16[128,256]{1,0:T(8,128)(2,1)S(1)} %collective-permute-done.7.refs_3_), channel_id=1, source_target_pairs={{0,4},{4,0},{8,12},{12,8},{16,20},{20,16},{24,28},{28,24},{1,5},{5... | collective-permute-start | bytes 196616 | tf_op jit(solution)/shard_map/ppermute | solution.py:384
  24.4 14.7 %collective-permute-start.15 = (bf16[512,512]{1,0:T(8,128)(2,1)S(1)}, bf16[512,512]{1,0:T(8,128)(2,1)S(1)}, u32[]{:S(2)}, u32[]{:S(2)}) collective-permute-start(bf16[512,512]{1,0:T(8,128)(2,1)S(1)} %take_half.1), channel_id=1, source_target_pairs={{0,16},{4,12},{8,24},{12,4},{16,0},{20,28},{24,8},{28,20},{1,17},{... | collective-permute-start | bytes 1572872 | tf_op jit(solution)/shard_map/ppermute | solution.py:393
  26.0 12.0 %collective-permute-start.12 = (bf16[512,256]{1,0:T(8,128)(2,1)S(1)}, bf16[512,256]{1,0:T(8,128)(2,1)S(1)}, u32[]{:S(2)}, u32[]{:S(2)}) collective-permute-start(bf16[512,256]{1,0:T(8,128)(2,1)S(1)} %get-tuple-element.389.refs_1_), channel_id=1, source_target_pairs={{0,8},{4,20},{8,0},{12,28},{16,24},{20,4},{24,16},{28,12},{1,9},{5... | collective-permute-start | bytes 786440 | tf_op jit(solution)/shard_map/ppermute | solution.py:390
  28.7 9.3 %collective-permute-start.16 = (bf16[512,256]{1,0:T(8,128)(2,1)S(1)}, bf16[512,256]{1,0:T(8,128)(2,1)S(1)}, u32[]{:S(2)}, u32[]{:S(2)}) collective-permute-start(bf16[512,256]{1,0:T(8,128)(2,1)S(1)} %get-tuple-element.400), channel_id=1, source_target_pairs={{0,1},{1,0},{2,3},{3,2},{4,5},{5,4},{6,7},{7,6},{8,9},{9,8},{10,11... | collective-permute-start | bytes 786440 | tf_op jit(solution)/shard_map/ppermute | solution.py:387
  30.4 7.7 %collective-permute-start.13 = (bf16[256,256]{1,0:T(8,128)(2,1)S(1)}, bf16[256,256]{1,0:T(8,128)(2,1)S(1)}, u32[]{:S(2)}, u32[]{:S(2)}) collective-permute-start(bf16[256,256]{1,0:T(8,128)(2,1)S(1)} %get-tuple-element.396), channel_id=1, source_target_pairs={{0,24},{4,28},{8,16},{12,20},{16,8},{20,12},{24,0},{28,4},{1,25},{... | collective-permute-start | bytes 393224 | tf_op jit(solution)/shard_map/ppermute | solution.py:384
  39.1 3.4 %collective-permute-start.19 = (bf16[1024,512]{1,0:T(8,128)(2,1)S(1)}, bf16[1024,512]{1,0:T(8,128)(2,1)S(1)}, u32[]{:S(2)}, u32[]{:S(2)}) collective-permute-start(bf16[1024,512]{1,0:T(8,128)(2,1)S(1)} %collective-permute-done.14.x_ref.refs_2_), channel_id=1, source_target_pairs={{0,4},{4,0},{8,12},{12,8},{16,20},{20,16},{24,28},{28,24},{1,5},{5... | collective-permute-start | bytes 3145736 | tf_op jit(solution)/shard_map/ppermute | solution.py:384
  39.1 3.4 %collective-permute-start.20 = (bf16[512,512]{1,0:T(8,128)(2,1)S(1)}, bf16[512,512]{1,0:T(8,128)(2,1)S(1)}, u32[]{:S(2)}, u32[]{:S(2)}) collective-permute-start(bf16[512,512]{1,0:T(8,128)(2,1)S(1)} %collective-permute-done.15.refs_4_), channel_id=1, source_target_pairs={{0,4},{4,0},{8,12},{12,8},{16,20},{20,16},{24,28},{28,24},{1,5},{5... | collective-permute-start | bytes 1572872 | tf_op jit(solution)/shard_map/ppermute | solution.py:384
  39.6 4.6 %collective-permute-start.17 = (bf16[512,256]{1,0:T(8,128)(2,1)S(1)}, bf16[512,256]{1,0:T(8,128)(2,1)S(1)}, u32[]{:S(2)}, u32[]{:S(2)}) collective-permute-start(bf16[512,256]{1,0:T(8,128)(2,1)S(1)} %collective-permute-done.12.refs_2_), channel_id=1, source_target_pairs={{0,4},{4,0},{8,12},{12,8},{16,20},{20,16},{24,28},{28,24},{1,5},{5... | collective-permute-start | bytes 786440 | tf_op jit(solution)/shard_map/ppermute | solution.py:384
  39.6 4.6 %collective-permute-start.18 = (bf16[256,256]{1,0:T(8,128)(2,1)S(1)}, bf16[256,256]{1,0:T(8,128)(2,1)S(1)}, u32[]{:S(2)}, u32[]{:S(2)}) collective-permute-start(bf16[256,256]{1,0:T(8,128)(2,1)S(1)} %collective-permute-done.13.refs_4_), channel_id=1, source_target_pairs={{0,4},{4,0},{8,12},{12,8},{16,20},{20,16},{24,28},{28,24},{1,5},{5... | collective-permute-start | bytes 393224 | tf_op jit(solution)/shard_map/ppermute | solution.py:384
  46.0 10.2 %collective-permute-start.21 = (bf16[512,256]{1,0:T(8,128)(2,1)S(1)}, bf16[512,256]{1,0:T(8,128)(2,1)S(1)}, u32[]{:S(2)}, u32[]{:S(2)}) collective-permute-start(bf16[512,256]{1,0:T(8,128)(2,1)S(1)} %get-tuple-element.410.refs_1_), channel_id=1, source_target_pairs={{0,8},{4,20},{8,0},{12,28},{16,24},{20,4},{24,16},{28,12},{1,9},{5... | collective-permute-start | bytes 786440 | tf_op jit(solution)/shard_map/ppermute | solution.py:390
  46.8 9.4 %collective-permute-start.22 = (bf16[256,256]{1,0:T(8,128)(2,1)S(1)}, bf16[256,256]{1,0:T(8,128)(2,1)S(1)}, u32[]{:S(2)}, u32[]{:S(2)}) collective-permute-start(bf16[256,256]{1,0:T(8,128)(2,1)S(1)} %get-tuple-element.411), channel_id=1, source_target_pairs={{0,24},{4,28},{8,16},{12,20},{16,8},{20,12},{24,0},{28,4},{1,25},{... | collective-permute-start | bytes 393224 | tf_op jit(solution)/shard_map/ppermute | solution.py:384
  56.2 3.1 %collective-permute-start.23 = (bf16[512,256]{1,0:T(8,128)(2,1)S(1)}, bf16[512,256]{1,0:T(8,128)(2,1)S(1)}, u32[]{:S(2)}, u32[]{:S(2)}) collective-permute-start(bf16[512,256]{1,0:T(8,128)(2,1)S(1)} %collective-permute-done.21.refs_2_), channel_id=1, source_target_pairs={{0,4},{4,0},{8,12},{12,8},{16,20},{20,16},{24,28},{28,24},{1,5},{5... | collective-permute-start | bytes 786440 | tf_op jit(solution)/shard_map/ppermute | solution.py:384
  56.2 3.1 %collective-permute-start.24 = (bf16[256,256]{1,0:T(8,128)(2,1)S(1)}, bf16[256,256]{1,0:T(8,128)(2,1)S(1)}, u32[]{:S(2)}, u32[]{:S(2)}) collective-permute-start(bf16[256,256]{1,0:T(8,128)(2,1)S(1)} %collective-permute-done.22.refs_4_), channel_id=1, source_target_pairs={{0,4},{4,0},{8,12},{12,8},{16,20},{20,16},{24,28},{28,24},{1,5},{5... | collective-permute-start | bytes 393224 | tf_op jit(solution)/shard_map/ppermute | solution.py:384
  56.7 14.8 %collective-permute-start.27 = (bf16[512,256]{1,0:T(8,128)(2,1)S(1)}, bf16[512,256]{1,0:T(8,128)(2,1)S(1)}, u32[]{:S(2)}, u32[]{:S(2)}) collective-permute-start(bf16[512,256]{1,0:T(8,128)(2,1)S(1)} %get-tuple-element.428), channel_id=1, source_target_pairs={{0,2},{1,3},{2,0},{3,1},{4,6},{5,7},{6,4},{7,5},{8,10},{9,11},{10,... | collective-permute-start | bytes 786440 | tf_op jit(solution)/shard_map/ppermute | solution.py:387
  61.1 10.4 %collective-permute-start.25 = (bf16[512,256]{1,0:T(8,128)(2,1)S(1)}, bf16[512,256]{1,0:T(8,128)(2,1)S(1)}, u32[]{:S(2)}, u32[]{:S(2)}) collective-permute-start(bf16[512,256]{1,0:T(8,128)(2,1)S(1)} %get-tuple-element.425.refs_1_), channel_id=1, source_target_pairs={{0,8},{4,20},{8,0},{12,28},{16,24},{20,4},{24,16},{28,12},{1,9},{5... | collective-permute-start | bytes 786440 | tf_op jit(solution)/shard_map/ppermute | solution.py:390
  61.7 9.8 %collective-permute-start.26 = (bf16[256,256]{1,0:T(8,128)(2,1)S(1)}, bf16[256,256]{1,0:T(8,128)(2,1)S(1)}, u32[]{:S(2)}, u32[]{:S(2)}) collective-permute-start(bf16[256,256]{1,0:T(8,128)(2,1)S(1)} %get-tuple-element.426), channel_id=1, source_target_pairs={{0,24},{4,28},{8,16},{12,20},{16,8},{20,12},{24,0},{28,4},{1,25},{... | collective-permute-start | bytes 393224 | tf_op jit(solution)/shard_map/ppermute | solution.py:384
  71.5 4.0 %collective-permute-start.28 = (bf16[512,256]{1,0:T(8,128)(2,1)S(1)}, bf16[512,256]{1,0:T(8,128)(2,1)S(1)}, u32[]{:S(2)}, u32[]{:S(2)}) collective-permute-start(bf16[512,256]{1,0:T(8,128)(2,1)S(1)} %collective-permute-done.25.refs_2_), channel_id=1, source_target_pairs={{0,4},{4,0},{8,12},{12,8},{16,20},{20,16},{24,28},{28,24},{1,5},{5... | collective-permute-start | bytes 786440 | tf_op jit(solution)/shard_map/ppermute | solution.py:384
  71.5 4.0 %collective-permute-start.29 = (bf16[256,256]{1,0:T(8,128)(2,1)S(1)}, bf16[256,256]{1,0:T(8,128)(2,1)S(1)}, u32[]{:S(2)}, u32[]{:S(2)}) collective-permute-start(bf16[256,256]{1,0:T(8,128)(2,1)S(1)} %collective-permute-done.26.refs_4_), channel_id=1, source_target_pairs={{0,4},{4,0},{8,12},{12,8},{16,20},{20,16},{24,28},{28,24},{1,5},{5... | collective-permute-start | bytes 393224 | tf_op jit(solution)/shard_map/ppermute | solution.py:384
  72.1 10.2 %collective-permute-start.32 = (bf16[512,256]{1,0:T(8,128)(2,1)S(1)}, bf16[512,256]{1,0:T(8,128)(2,1)S(1)}, u32[]{:S(2)}, u32[]{:S(2)}) collective-permute-start(bf16[512,256]{1,0:T(8,128)(2,1)S(1)} %get-tuple-element.440), channel_id=1, source_target_pairs={{0,3},{1,2},{2,1},{3,0},{4,7},{5,6},{6,5},{7,4},{8,11},{9,10},{10,... | collective-permute-start | bytes 786440 | tf_op jit(solution)/shard_map/ppermute | solution.py:387
  77.3 9.2 %collective-permute-start.30 = (bf16[512,256]{1,0:T(8,128)(2,1)S(1)}, bf16[512,256]{1,0:T(8,128)(2,1)S(1)}, u32[]{:S(2)}, u32[]{:S(2)}) collective-permute-start(bf16[512,256]{1,0:T(8,128)(2,1)S(1)} %get-tuple-element.437.refs_1_), channel_id=1, source_target_pairs={{0,8},{4,20},{8,0},{12,28},{16,24},{20,4},{24,16},{28,12},{1,9},{5... | collective-permute-start | bytes 786440 | tf_op jit(solution)/shard_map/ppermute | solution.py:390
  77.9 8.6 %collective-permute-start.31 = (bf16[256,256]{1,0:T(8,128)(2,1)S(1)}, bf16[256,256]{1,0:T(8,128)(2,1)S(1)}, u32[]{:S(2)}, u32[]{:S(2)}) collective-permute-start(bf16[256,256]{1,0:T(8,128)(2,1)S(1)} %get-tuple-element.438), channel_id=1, source_target_pairs={{0,24},{4,28},{8,16},{12,20},{16,8},{20,12},{24,0},{28,4},{1,25},{... | collective-permute-start | bytes 393224 | tf_op jit(solution)/shard_map/ppermute | solution.py:384
  86.5 1.7 %collective-permute-start.33 = (bf16[512,256]{1,0:T(8,128)(2,1)S(1)}, bf16[512,256]{1,0:T(8,128)(2,1)S(1)}, u32[]{:S(2)}, u32[]{:S(2)}) collective-permute-start(bf16[512,256]{1,0:T(8,128)(2,1)S(1)} %collective-permute-done.30.refs_2_), channel_id=1, source_target_pairs={{0,4},{4,0},{8,12},{12,8},{16,20},{20,16},{24,28},{28,24},{1,5},{5... | collective-permute-start | bytes 786440 | tf_op jit(solution)/shard_map/ppermute | solution.py:384
  86.5 1.7 %collective-permute-start.34 = (bf16[256,256]{1,0:T(8,128)(2,1)S(1)}, bf16[256,256]{1,0:T(8,128)(2,1)S(1)}, u32[]{:S(2)}, u32[]{:S(2)}) collective-permute-start(bf16[256,256]{1,0:T(8,128)(2,1)S(1)} %collective-permute-done.31.refs_4_), channel_id=1, source_target_pairs={{0,4},{4,0},{8,12},{12,8},{16,20},{20,16},{24,28},{28,24},{1,5},{5... | collective-permute-start | bytes 393224 | tf_op jit(solution)/shard_map/ppermute | solution.py:384
  (7 other events, 43.0 us)

commit v9 on v8

--- a/solution.py
+++ b/solution.py
@@ -94,16 +94,9 @@
 def factor_kernel(owner, order, pattern, win_ref, out, buf, pat, inv, pos, sem):
     row = lax.axis_index("rows")
 
-    def note_slot(w, carry):
+    for w in range(NWB):
         slot = owner[w]
-
-        @pl.when(slot // SB == row)
-        def _():
-            inv[slot % SB] = w
-
-        return carry
-
-    lax.fori_loop(0, NWB, note_slot, 0, unroll=8)
+        inv[jnp.where(slot // SB == row, slot % SB, SB)] = w
     for k in range(NSUP):
         pos[order[k]] = k
     labels = jnp.zeros((SB, 1), jnp.int32)
@@ -135,60 +128,42 @@
     out[...] = x_ref[0:SN, :]
 
 
-def table_kernel(owner, order, tab, flag, cnt):
+def table_kernel(owner, order, tab, flag):
     row = lax.axis_index("rows")
     chip, core = row // 2, row % 2
-    flag[0] = 0
-    flag[1] = lax.axis_index("rhs")
+    bad = 0
     for t in range(GROUPS * SB):
         tab[PACK + t] = 0
     for group in range(GROUPS):
-        for t in range(4):
-            cnt[t] = 0
-
-        def one(i, carry, group=group):
+        counts = 0
+        for i in range(2 * SB):
             slot = owner[order[2 * group + i // SB] * SB + i % SB]
             where, device = slot // (2 * SB), slot // SB
-            rank = cnt[where]
-            cnt[where] = rank + 1
-            flag[0] = jnp.where(rank >= SB, 1, flag[0])
+            rank = (counts >> (8 * where)) & 255
+            counts = counts + (1 << (8 * where))
+            bad = bad | (rank // SB)
             rank = jnp.minimum(rank, SB - 1)
             rel = jnp.bitwise_xor(where, chip)
-            diagonal = rel == 3
-            source = jnp.where(rel == 0, 0, jnp.where(diagonal, jnp.where(rank // 4 == core, 3, 4),
-                                                      jnp.where(rel == 1 + core, 1, 2)))
-            start = jnp.where(source == 4, 7 * SB // 2, source * SB)
-            tab[SRC + group * 16 + i] = start + jnp.where(diagonal, rank % 4, rank)
-
-            @pl.when(rel == 0)
-            def _():
-                tab[PACK + group * SB + rank] = jnp.bitwise_xor(device % 2, core) * SB + slot % SB
-
-            @pl.when(i >= SB)
-            def _():
-                kind = jnp.where(rel == 0, 0, jnp.where(diagonal, 3, jnp.where(rel == 1 + core, 1, 2)))
-                tab[LSRC + group * SB + i - SB] = (2 * kind + jnp.where(device % 2 == core, 0, 1)) * SB + slot % SB
-
-            return carry
-
-        lax.fori_loop(0, 2 * SB, one, 0, unroll=True)
-
-
-def below_rhs_kernel(rhs_ref, *refs):
-    outs, sems = refs[:-1], refs[-1]
+            cross = jnp.bitwise_xor(device % 2, core)
+            kind = jnp.where((rel == 1) | (rel == 2), jnp.where(rel == 1 + core, 1, 2), rel)
+            far_rank = 3 * SB + jnp.where(rank // 4 == core, 0, 4) + rank % 4
+            tab[SRC + group * 16 + i] = jnp.where(kind == 3, far_rank, kind * SB + rank)
+            tab[jnp.where(rel == 0, PACK + group * SB + rank, TABLE)] = cross * SB + slot % SB
+            if i >= SB:
+                tab[LSRC + group * SB + i - SB] = (2 * kind + cross) * SB + slot % SB
+    flag[0] = bad
+    flag[1] = lax.axis_index("rhs")
+
+
+def below_rhs_kernel(rhs_ref, *outs):
     depth = lax.axis_index("rhs")
     width = outs[0].shape[1]
-    copies = []
     for s, out in enumerate(outs):
-        at = pl.multiple_of(jnp.bitwise_xor(depth, s) * width, width)
-        copies.append(pltpu.make_async_copy(rhs_ref.at[:, pl.ds(at, width)], out, sems.at[s]))
-        copies[-1].start()
-    for c in copies:
-        c.wait()
+        out[...] = rhs_ref[:, pl.ds(pl.multiple_of(jnp.bitwise_xor(depth, s) * width, width), width)]
 
 
 def first_pack_kernel(owner, order, *refs):
-    pieces, (chip_rhs, p_ref, b_ref, count) = refs[:8], refs[8:]
+    pieces, (chip_rhs, p_ref, b_ref, place) = refs[:8], refs[8:]
     row, depth = lax.axis_index("rows"), lax.axis_index("rhs")
     core = row % 2
     tall = pieces[0].shape[0]
@@ -196,20 +171,16 @@
         for s in range(4):
             at = pl.multiple_of(side * SB * BS + jnp.bitwise_xor(depth, s) * tall, tall)
             chip_rhs[pl.ds(at, tall), :] = pieces[4 * side + s][...]
-    count[0] = 0
+    for t in range(SB):
+        place[t] = 0
+    rank = 0
     for i in range(2 * SB):
         slot = owner[order[i // SB] * SB + i % SB]
-
-        @pl.when(slot // (2 * SB) == row // 2)
-        def _(slot=slot):
-            rank = count[0]
-            count[0] = rank + 1
-            place = jnp.bitwise_xor((slot // SB) % 2, core) * SB + slot % SB
-
-            @pl.when(rank < SB)
-            def _():
-                p_ref[rows_at(rank), :] = chip_rhs[rows_at(place), :]
-
+        here = slot // (2 * SB) == row // 2
+        place[jnp.where(here & (rank < SB), rank, SB)] = jnp.bitwise_xor((slot // SB) % 2, core) * SB + slot % SB
+        rank = rank + jnp.where(here, 1, 0)
+    for t in range(SB):
+        p_ref[t * BS:(t + 1) * BS, :] = chip_rhs[rows_at(place[t]), :]
     b_ref[...] = p_ref[pl.ds(pl.multiple_of(core * SB // 2 * BS, SB // 2 * BS), SB // 2 * BS), :]
 
 
@@ -297,14 +268,15 @@
 def make_below_mask_kernel(tile):
     def kernel(pattern, a_ref, out, sems):
         copies = []
-        for j in range(SB):
-            c = pltpu.make_async_copy(a_ref.at[pl.ds((tile * SB + j) * BS, BS), :], out.at[pl.ds(j * BS, BS), :], sems.at[j])
+        count = 2 * SB
+        for j in range(count):
+            c = pltpu.make_async_copy(a_ref.at[pl.ds((tile * count + j) * BS, BS), :], out.at[pl.ds(j * BS, BS), :], sems.at[j])
             c.start()
             copies.append(c)
         spread = spread_matrix()
-        rows = pattern[tile * SB:(tile + 1) * SB, :]
+        rows = pattern[tile * count:(tile + 1) * count, :]
         masks = [expand_mask(rows, k, spread) for k in range(NSUP)]
-        for j in range(SB):
+        for j in range(count):
             copies[j].wait()
             for k in range(NSUP):
                 at = (slice(j * BS, (j + 1) * BS), slice(k * SN, (k + 1) * SN))
@@ -313,36 +285,37 @@
     return kernel
 
 
-def below_product(order, a_ref, x_ref, group):
-    first = jnp.dot(a_ref[:, columns_at(order[2 * group])], x_ref[0:SN, :], preferred_element_type=F32)
-    return first + jnp.dot(a_ref[:, columns_at(order[2 * group + 1])], x_ref[SN:PAIR, :], preferred_element_type=F32)
-
-
-def two_rows_kernel(order, a0, a1, a2, a3, x0_ref, x1_ref, out):
-    for i, a_ref in enumerate((a0, a1, a2, a3)):
-        out[i * SN:(i + 1) * SN, :] = below_product(order, a_ref, x0_ref, 0) + below_product(order, a_ref, x1_ref, 1)
-
-
-def base_rows_kernel(order, a0, a1, a2, a3, x_ref, sums, h0, h1, h2, h3, out, rhs):
+def below_product(order, a_ref, x_ref, group, i):
+    rows = slice((i % 2) * SN, (i % 2 + 1) * SN)
+    first = jnp.dot(a_ref[rows, columns_at(order[2 * group])], x_ref[0:SN, :], preferred_element_type=F32)
+    return first + jnp.dot(a_ref[rows, columns_at(order[2 * group + 1])], x_ref[SN:PAIR, :], preferred_element_type=F32)
+
+
+def two_rows_kernel(order, a0, a1, x0_ref, x1_ref, out):
+    for i, a_ref in enumerate((a0, a0, a1, a1)):
+        out[i * SN:(i + 1) * SN, :] = below_product(order, a_ref, x0_ref, 0, i) + below_product(order, a_ref, x1_ref, 1, i)
+
+
+def base_rows_kernel(order, a0, a1, x_ref, sums, h0, h1, h2, h3, out, rhs):
     depth = lax.axis_index("rhs")
     tall = h0.shape[0]
     for s, h in enumerate((h0, h1, h2, h3)):
         rhs[pl.ds(pl.multiple_of(jnp.bitwise_xor(depth, s) * tall, tall), tall), :] = h[...]
-    for i, a_ref in enumerate((a0, a1, a2, a3)):
+    for i, a_ref in enumerate((a0, a0, a1, a1)):
         at = slice(i * SN, (i + 1) * SN)
-        out[at, :] = rhs[at, :].astype(F32) - (sums[at, :] + below_product(order, a_ref, x_ref, 2))
-
-
-def last_rows_kernel(order, a0, a1, a2, a3, x0, x1, x2, x3, base, sol_ref, out_ref, done, sems, osem):
+        out[at, :] = rhs[at, :].astype(F32) - (sums[at, :] + below_product(order, a_ref, x_ref, 2, i))
+
+
+def last_rows_kernel(order, a0, a1, x0, x1, x2, x3, base, sol_ref, out_ref, done, sems, osem):
     copies = []
     for k, x in enumerate((x0, x1, x2, x3)):
         for q in range(2):
             at = pl.multiple_of(order[2 * k + q] * SN, SN)
             copies.append(pltpu.make_async_copy(x.at[pl.ds(q * SN, SN), :], sol_ref.at[pl.ds(at, SN), :], sems.at[2 * k + q]))
             copies[-1].start()
-    for i, a_ref in enumerate((a0, a1, a2, a3)):
+    for i, a_ref in enumerate((a0, a0, a1, a1)):
         at = slice(i * SN, (i + 1) * SN)
-        done[at, :] = (base[at, :] - below_product(order, a_ref, x3, GROUPS - 1)).astype(BF16)
+        done[at, :] = (base[at, :] - below_product(order, a_ref, x3, GROUPS - 1, i)).astype(BF16)
         copies.append(pltpu.make_async_copy(done.at[pl.ds(i * SN, SN), :], out_ref.at[pl.ds(i * SN, SN), :], osem.at[i]))
         copies[-1].start()
     for c in copies:
@@ -396,12 +369,12 @@
         pattern_later, _ = lax.optimization_barrier((anc_pattern, after))
         return pl.pallas_call(
             make_below_mask_kernel(k),
-            out_shape=shape_of((SN, NW)),
+            out_shape=shape_of((PAIR, NW)),
             in_specs=[VMEM, HBM],
             out_specs=VMEM,
-            scratch_shapes=[pltpu.SemaphoreType.DMA((SB,))],
+            scratch_shapes=[pltpu.SemaphoreType.DMA((2 * SB,))],
             compiler_params=params(4),
-            cost_estimate=cost(2),
+            cost_estimate=cost(4),
             name="mask_below",
         )(pattern_later, in_hbm(anc_rows))
 
@@ -415,11 +388,12 @@
         in_specs=[SMEM, SMEM, VMEM, HBM],
         out_specs=VMEM,
         scratch_shapes=[pltpu.VMEM((SN, SN), BF16), pltpu.VMEM((SB, NWB), jnp.int32),
-                        pltpu.SMEM((SB,), jnp.int32), pltpu.SMEM((SB,), jnp.int32), pltpu.SemaphoreType.DMA],
+                        pltpu.SMEM((SB + 1,), jnp.int32), pltpu.SMEM((SB,), jnp.int32), pltpu.SemaphoreType.DMA],
         compiler_params=params(4),
         cost_estimate=cost(2),
         name="factor_pack",
     )(window_owner, sn_order, win_pattern, w_own)
+    rhs_late, _ = lax.optimization_barrier((rhs_win, l_own))
     sent = pl.pallas_call(
         rhs_pack_kernel,
         out_shape=(shape_of((tall, columns)),) * 4,
@@ -428,7 +402,7 @@
         compiler_params=params(4),
         cost_estimate=cost(1),
         name="rhs_pack",
-    )(rhs_win)
+    )(rhs_late)
     pieces = [sent[0]] + [deep(sent[s], s) for s in (1, 2, 3)]
     l_late, pieces[1] = lax.optimization_barrier((l_own, pieces[1]))
     l_other = swap(l_late, 1)
@@ -444,15 +418,15 @@
     near = neighbour(l_chip)
     w_late, _ = lax.optimization_barrier((win_rows, l_chip))
     w_other = swap(w_late, 1)
-    below = [mask_below(k, l_chip) for k in (0, 1)]
-    w_other, below[0], below[1], *pieces = lax.optimization_barrier((w_other, *below, *pieces))
+    below = [mask_below(0, l_chip)]
+    w_other, below[0], *pieces = lax.optimization_barrier((w_other, *below, *pieces))
     others = [swap(x, 1) for x in pieces]
     chip_rhs, packed, part = pl.pallas_call(
         first_pack_kernel,
         out_shape=(shape_of((PAIR, columns)), shape_of((SN, columns)), shape_of((half, columns))),
         in_specs=[SMEM, SMEM] + [VMEM] * 8,
         out_specs=(VMEM,) * 3,
-        scratch_shapes=[pltpu.SMEM((1,), jnp.int32)],
+        scratch_shapes=[pltpu.SMEM((SB + 1,), jnp.int32)],
         compiler_params=params(4),
         cost_estimate=cost(1),
         name="first_pack",
@@ -471,12 +445,11 @@
     owner_later, order_later, _ = lax.optimization_barrier((window_owner, sn_order, packed))
     tab, flag = pl.pallas_call(
         table_kernel,
-        out_shape=(shape_of((TABLE,), jnp.int32), shape_of((2,), jnp.int32)),
+        out_shape=(shape_of((TABLE + 1,), jnp.int32), shape_of((2,), jnp.int32)),
         in_specs=[SMEM, SMEM],
         out_specs=(SMEM, SMEM),
-        scratch_shapes=[pltpu.SMEM((4,), jnp.int32)],
         compiler_params=params(4),
-        cost_estimate=cost(3),
+        cost_estimate=cost(2),
         name="tables",
     )(owner_later, order_later)
     w_other = in_vmem(w_other)
@@ -487,7 +460,7 @@
     diag_vmem = in_vmem(diag_inv)
     below_rows = anc_rows.shape[0]
 
-    anc_order, anc_pieces = (1, 2, 3), [None] * 4
+    anc_order, anc_pieces = (2, 3, 1), [None] * 4
     for group in range(GROUPS):
         last = group == GROUPS - 1
         a_own = neighbour(packed)
@@ -509,21 +482,20 @@
             anc_pieces = list(pl.pallas_call(
                 below_rhs_kernel,
                 out_shape=(shape_of((tile, columns)),) * 4,
-                in_specs=[HBM],
+                in_specs=[VMEM],
                 out_specs=(VMEM,) * 4,
-                scratch_shapes=[pltpu.SemaphoreType.DMA((4,))],
                 compiler_params=params(4),
                 cost_estimate=cost(1),
                 name="below_rhs",
-            )(in_hbm(rhs_later)))
+            )(in_vmem(rhs_later)))
         if not last:
             s = anc_order[group]
             moved, _ = lax.optimization_barrier((anc_pieces[s], packed))
             anc_pieces[s] = deep(moved, s)
 
         if group == 0:
-            a_own, b_own, near, far, anc_pieces[1], *masked = lax.optimization_barrier(
-                (a_own, b_own, near, far, anc_pieces[1], *masked))
+            a_own, b_own, near, far, *masked = lax.optimization_barrier(
+                (a_own, b_own, near, far, *masked))
             l_parts = [in_vmem(x) for x in (l_own, l_other, near, swap(near, 1), far, swap(far, 1))]
         operands = [tab, sn_order, diag_vmem, *l_parts]
         out_shape = [shape_of((PAIR, PAIR))]
@@ -542,17 +514,17 @@
         )(*operands)
         hold = []
         if group == 1:
-            below += [mask_below(k, packed) for k in (2, 3)]
-            hold = below[2:]
+            below.append(mask_below(1, packed))
+            hold = below[1:]
         elif group > 1:
             more, kernel = (solved[:2], two_rows_kernel) if group == 2 else ([solved[2], sums, *anc_pieces], base_rows_kernel)
             sums = pl.pallas_call(
                 kernel,
                 out_shape=shape_of((below_rows, columns), F32),
-                in_specs=[SMEM] + [VMEM] * (4 + len(more)),
+                in_specs=[SMEM] + [VMEM] * (2 + len(more)),
                 out_specs=VMEM,
                 scratch_shapes=[pltpu.VMEM((below_rows, columns), BF16)] if last else [],
-                input_output_aliases={6: 0} if last else {},
+                input_output_aliases={4: 0} if last else {},
                 compiler_params=params(6),
                 cost_estimate=cost(3),
                 name="rows_below",
@@ -563,7 +535,7 @@
             a_own, b_own, anc_pieces[s], *rest = lax.optimization_barrier((a_own, b_own, anc_pieces[s], *hold, *ready))
             hold, ready = rest[:len(hold)], rest[len(hold):]
             if group == 1:
-                below[2:] = hold
+                below[1:] = hold
             else:
                 sums = hold[0]
         a_swap = swap(a_own, 1)
@@ -590,7 +562,7 @@
     outputs = pl.pallas_call(
         last_rows_kernel,
         out_shape=(shape_of((NW, columns)), shape_of((below_rows, columns))),
-        in_specs=[SMEM] + [VMEM] * 9,
+        in_specs=[SMEM] + [VMEM] * 7,
         out_specs=(HBM, HBM),
         scratch_shapes=[pltpu.VMEM((below_rows, columns), BF16), pltpu.SemaphoreType.DMA((2 * GROUPS,)),
                         pltpu.SemaphoreType.DMA((4,))],

time: 93.8 us -> 93.9 us (level)
  Pallas kernels: 42.4 us -> 39.4 us
  waiting for transfers between devices: 17.3 us -> 19.8 us
  starting transfers between devices: 30.8 us -> 32.5 us
  local copies, waits for them, and re-layouts: 0.98 us -> 0.04 us
    ppermute x20, waiting for transfers between devices: 10 us -> 14.1 us  [swap(): return lax.ppermute(x, 'rows', [(i, i ^ m) for i in range(8)])]
    pallas_call x5 -> x3, Pallas kernels: 11.8 us -> 9.84 us  [the longest x2 7.11 us: mask_below(): pl.pallas_call(make_below_mask_kernel(k), out_shape=shape_of((PAIR, NW)),...]
    pallas_call x1, Pallas kernels: 1.23 us -> 0.14 us  [local(): pl.pallas_call(below_rhs_kernel, out_shape=(shape_of((tile, columns)),) *...]
  transfers between devices with their start and end apart: 32 -> 32, of which waited for: 15 -> 16; matrix products, arithmetic and copies ran while one was open for 0% -> 0% of each run, Pallas kernels for 39% -> 35%
where the time goes in v9:
time: 93.9 us; the launch traced here: 93.7 us
  Pallas kernels  39.4 us (42%)
  starting transfers between devices  32.5 us (35%)
  waiting for transfers between devices  19.8 us (21%)
  between operations  1.11 us (1%)
    ppermute x6, starting transfers between devices, deep(): return lax.ppermute(x, 'rhs', [(i, i ^ m) for i in range(4)])  15 us
    ppermute x20, waiting for transfers between devices, swap(): return lax.ppermute(x, 'rows', [(i, i ^ m) for i in range(8)])  14.1 us
    ppermute x20, starting transfers between devices, swap(): return lax.ppermute(x, 'rows', [(i, i ^ m) for i in range(8)])  10.1 us
    pallas_call x4, Pallas kernels, local(): pl.pallas_call(make_prep_kernel(group), out_shape=tuple(out_shape), in_sp...  8.23 us
    pallas_call x2, Pallas kernels, mask_below(): pl.pallas_call(make_below_mask_kernel(k), out_shape=shape_of((PAIR, NW)),...  7.11 us
    pallas_call x4, Pallas kernels, local(): pl.pallas_call(make_solve_kernel(group), out_shape=tuple(out_shape), in_s...  6.57 us
    ppermute x5, starting transfers between devices, neighbour(): lax.ppermute(x, 'rows', [(i, i ^ (2 if i % 2 == 0 else 4)) for i in range...  5.45 us
    pallas_call x2, Pallas kernels, local(): pl.pallas_call(kernel, out_shape=shape_of((below_rows, columns), F32), in...  5.01 us
  transfers between devices with their start and end apart: 32, of which 16 were waited for; matrix products, arithmetic and copies ran while one was open for 0% of the time, Pallas kernels for 35%

profile of v9, /device:TPU:0, one launch (start us, length us, event | category | flops | bytes accessed | tf_op | source)
XLA Modules:
  0.0 93.7 jit_solution(10048543273900450031)
XLA Ops:
  0.7 2.6 %factor_pack.1.own_ref.refs_0_ = bf16[512,512]{1,0:T(8,128)(2,1)S(1)} custom-call(s32[64]{0:T(128)} %owner.4, s32[8]{0:T(128)} %order.21, s32[64,64]{1,0:T(8,128)} %pattern.8, bf16[512,4096]{1,0:T(8,128)(2,1)} %w_own.5), custom_call_target="tpu_custom_call" | custom-call | flops 200000000 | bytes 6000000 | tf_op jit(solution)/shard_map/factor_pack/pallas_call | solution.py:385
  3.3 3.1 %collective-permute-start.3 = (bf16[128,256]{1,0:T(8,128)(2,1)S(1)}, bf16[128,256]{1,0:T(8,128)(2,1)S(1)}, u32[]{:S(2)}, u32[]{:S(2)}) collective-permute-start(bf16[128,256]{1,0:T(8,128)(2,1)S(1)} %get-tuple-element.376), channel_id=1, source_target_pairs={{0,1},{1,0},{2,3},{3,2},{4,5},{5,4},{6,7},{7,6},{8,9},{9,8},{10,11... | collective-permute-start | bytes 196616 | tf_op jit(solution)/shard_map/ppermute | solution.py:360
  6.4 2.2 %collective-permute-done.3.refs_1_ = bf16[128,256]{1,0:T(8,128)(2,1)S(1)} collective-permute-done((bf16[128,256]{1,0:T(8,128)(2,1)S(1)}, bf16[128,256]{1,0:T(8,128)(2,1)S(1)}, u32[]{:S(2)}, u32[]{:S(2)}) %collective-permute-start.3) | collective-permute-done | bytes 65568 | tf_op jit(solution)/shard_map/ppermute | solution.py:360
  8.6 1.9 %collective-permute-done.4.other_ref.refs_1_ = bf16[512,512]{1,0:T(8,128)(2,1)S(1)} collective-permute-done((bf16[512,512]{1,0:T(8,128)(2,1)S(1)}, bf16[512,512]{1,0:T(8,128)(2,1)S(1)}, u32[]{:S(2)}, u32[]{:S(2)}) %collective-permute-start.4) | collective-permute-done | bytes 524320 | tf_op jit(solution)/shard_map/ppermute | solution.py:357
  10.8 1.9 %collective-permute-start.14 = (bf16[1024,512]{1,0:T(8,128)(2,1)S(1)}, bf16[1024,512]{1,0:T(8,128)(2,1)S(1)}, u32[]{:S(2)}, u32[]{:S(2)}) collective-permute-start(bf16[1024,512]{1,0:T(8,128)(2,1)S(1)} %chip_pack.1), channel_id=1, source_target_pairs={{0,8},{4,20},{8,0},{12,28},{16,24},{20,4},{24,16},{28,12},{1,9},{5... | collective-permute-start | bytes 3145736 | tf_op jit(solution)/shard_map/ppermute | solution.py:363
  12.8 2.6 %collective-permute-start.6 = (bf16[128,256]{1,0:T(8,128)(2,1)S(1)}, bf16[128,256]{1,0:T(8,128)(2,1)S(1)}, u32[]{:S(2)}, u32[]{:S(2)}) collective-permute-start(bf16[128,256]{1,0:T(8,128)(2,1)S(1)} %get-tuple-element.382), channel_id=1, source_target_pairs={{0,2},{1,3},{2,0},{3,1},{4,6},{5,7},{6,4},{7,5},{8,10},{9,11},{10,... | collective-permute-start | bytes 196616 | tf_op jit(solution)/shard_map/ppermute | solution.py:360
  15.3 1.3 %collective-permute-start.7 = (bf16[128,256]{1,0:T(8,128)(2,1)S(1)}, bf16[128,256]{1,0:T(8,128)(2,1)S(1)}, u32[]{:S(2)}, u32[]{:S(2)}) collective-permute-start(bf16[128,256]{1,0:T(8,128)(2,1)S(1)} %get-tuple-element.383), channel_id=1, source_target_pairs={{0,3},{1,2},{2,1},{3,0},{4,7},{5,6},{6,5},{7,4},{8,11},{9,10},{10,... | collective-permute-start | bytes 196616 | tf_op jit(solution)/shard_map/ppermute | solution.py:360
  16.7 3.6 %mask_below.2.a0 = bf16[1024,4096]{1,0:T(8,128)(2,1)S(1)} custom-call(s32[32,64]{1,0:T(8,128)S(1)} %copy-done.4, bf16[2048,4096]{1,0:T(8,128)(2,1)} %a_ref.3), custom_call_target="tpu_custom_call" | custom-call | flops 400000000 | bytes 12000000 | tf_op jit(solution)/shard_map/mask_below/pallas_call | solution.py:370
  24.2 1.4 %collective-permute-done.14.x_ref.refs_2_ = bf16[1024,512]{1,0:T(8,128)(2,1)S(1)} collective-permute-done((bf16[1024,512]{1,0:T(8,128)(2,1)S(1)}, bf16[1024,512]{1,0:T(8,128)(2,1)S(1)}, u32[]{:S(2)}, u32[]{:S(2)}) %collective-permute-start.14) | collective-permute-done | bytes 1048608 | tf_op jit(solution)/shard_map/ppermute | solution.py:363
  25.7 2.0 %collective-permute-start.15 = (bf16[512,512]{1,0:T(8,128)(2,1)S(1)}, bf16[512,512]{1,0:T(8,128)(2,1)S(1)}, u32[]{:S(2)}, u32[]{:S(2)}) collective-permute-start(bf16[512,512]{1,0:T(8,128)(2,1)S(1)} %take_half.1), channel_id=1, source_target_pairs={{0,16},{4,12},{8,24},{12,4},{16,0},{20,28},{24,8},{28,20},{1,17},{... | collective-permute-start | bytes 1572872 | tf_op jit(solution)/shard_map/ppermute | solution.py:366
  27.7 1.5 %collective-permute-start.12 = (bf16[512,256]{1,0:T(8,128)(2,1)S(1)}, bf16[512,256]{1,0:T(8,128)(2,1)S(1)}, u32[]{:S(2)}, u32[]{:S(2)}) collective-permute-start(bf16[512,256]{1,0:T(8,128)(2,1)S(1)} %get-tuple-element.388.refs_1_), channel_id=1, source_target_pairs={{0,8},{4,20},{8,0},{12,28},{16,24},{20,4},{24,16},{28,12},{1,9},{5... | collective-permute-start | bytes 786440 | tf_op jit(solution)/shard_map/ppermute | solution.py:363
  29.2 2.7 %tables.1 = (s32[129]{0:T(256)S(1)}, s32[2]{0:T(128)}) custom-call(s32[64]{0:T(128)S(1)} %copy-done.20, s32[8]{0:T(128)S(1)} %copy-done.21), custom_call_target="tpu_custom_call" | custom-call | flops 200000000 | bytes 6000000 | tf_op jit(solution)/shard_map/tables/pallas_call | solution.py:446
  35.0 4.3 %collective-permute-done.13.refs_4_ = bf16[256,256]{1,0:T(8,128)(2,1)S(1)} collective-permute-done((bf16[256,256]{1,0:T(8,128)(2,1)S(1)}, bf16[256,256]{1,0:T(8,128)(2,1)S(1)}, u32[]{:S(2)}, u32[]{:S(2)}) %collective-permute-start.13) | collective-permute-done | bytes 131104 | tf_op jit(solution)/shard_map/ppermute | solution.py:357
  41.1 3.5 %collective-permute-start.22 = (bf16[512,256]{1,0:T(8,128)(2,1)S(1)}, bf16[512,256]{1,0:T(8,128)(2,1)S(1)}, u32[]{:S(2)}, u32[]{:S(2)}) collective-permute-start(bf16[512,256]{1,0:T(8,128)(2,1)S(1)} %get-tuple-element.409), channel_id=1, source_target_pairs={{0,2},{1,3},{2,0},{3,1},{4,6},{5,7},{6,4},{7,5},{8,10},{9,11},{10,... | collective-permute-start | bytes 786440 | tf_op jit(solution)/shard_map/ppermute | solution.py:360
  44.6 1.7 %prep.4 = (bf16[1024,1024]{1,0:T(8,128)(2,1)S(1)}, f32[512,256]{1,0:T(8,128)S(1)}) custom-call(s32[129]{0:T(256)S(1)} %get-tuple-element.393.tab.refs_0_, s32[8]{0:T(128)S(1)} %copy-done.21, bf16[8,512,512]{2,1,0:T(8,128)(2,1)S(1)} %copy-done.1, bf16[512,512]{1,0:T(8,128)(2,1)S(1)} %factor_pack.1.own_ref.refs_0_, ...), custom_call_target="tpu_custom_call" | custom-call | flops 200000000 | bytes 6000000 | tf_op jit(solution)/shard_map/prep/pallas_call | solution.py:505
  46.3 1.8 %pair_solve.4 = (bf16[1024,256]{1,0:T(8,128)(2,1)S(1)}, bf16[512,256]{1,0:T(8,128)(2,1)S(1)}, bf16[256,256]{1,0:T(8,128)(2,1)S(1)}) custom-call(s32[129]{0:T(256)S(1)} %get-tuple-element.393.tab.refs_0_, bf16[512,256]{1,0:T(8,128)(2,1)S(1)} %get-tuple-element.388.refs_1_, bf16[512,256]{1,0:T(8,128)(2,1)S(1)} %collective-permute-done.12.refs_2_, ...), custom_call_target="tpu_custom_call" | custom-call | flops 300000000 | bytes 9000000 | tf_op jit(solution)/shard_map/pair_solve/pallas_call | solution.py:548
  48.8 2.4 %collective-permute-start.21 = (bf16[256,256]{1,0:T(8,128)(2,1)S(1)}, bf16[256,256]{1,0:T(8,128)(2,1)S(1)}, u32[]{:S(2)}, u32[]{:S(2)}) collective-permute-start(bf16[256,256]{1,0:T(8,128)(2,1)S(1)} %get-tuple-element.406), channel_id=1, source_target_pairs={{0,24},{4,28},{8,16},{12,20},{16,8},{20,12},{24,0},{28,4},{1,25},{... | collective-permute-start | bytes 393224 | tf_op jit(solution)/shard_map/ppermute | solution.py:357
  51.1 2.5 %prep.5 = (bf16[1024,1024]{1,0:T(8,128)(2,1)S(1)}, f32[512,256]{1,0:T(8,128)S(1)}) custom-call(s32[129]{0:T(256)S(1)} %get-tuple-element.393.tab.refs_0_, s32[8]{0:T(128)S(1)} %copy-done.21, bf16[8,512,512]{2,1,0:T(8,128)(2,1)S(1)} %copy-done.1, bf16[512,512]{1,0:T(8,128)(2,1)S(1)} %factor_pack.1.own_ref.refs_0_, ...), custom_call_target="tpu_custom_call" | custom-call | flops 200000000 | bytes 6000000 | tf_op jit(solution)/shard_map/prep/pallas_call | solution.py:505
  53.7 3.6 %mask_below.3.a1 = bf16[1024,4096]{1,0:T(8,128)(2,1)S(1)} custom-call(s32[32,64]{1,0:T(8,128)S(1)} %copy-done.4, bf16[2048,4096]{1,0:T(8,128)(2,1)} %a_ref.3), custom_call_target="tpu_custom_call" | custom-call | flops 400000000 | bytes 12000000 | tf_op jit(solution)/shard_map/mask_below/pallas_call | solution.py:370
  58.8 3.3 %collective-permute-start.27 = (bf16[512,256]{1,0:T(8,128)(2,1)S(1)}, bf16[512,256]{1,0:T(8,128)(2,1)S(1)}, u32[]{:S(2)}, u32[]{:S(2)}) collective-permute-start(bf16[512,256]{1,0:T(8,128)(2,1)S(1)} %get-tuple-element.424), channel_id=1, source_target_pairs={{0,3},{1,2},{2,1},{3,0},{4,7},{5,6},{6,5},{7,4},{8,11},{9,10},{10,... | collective-permute-start | bytes 786440 | tf_op jit(solution)/shard_map/ppermute | solution.py:360
  62.0 1.8 %pair_solve.5 = (bf16[1024,256]{1,0:T(8,128)(2,1)S(1)}, bf16[512,256]{1,0:T(8,128)(2,1)S(1)}, bf16[256,256]{1,0:T(8,128)(2,1)S(1)}) custom-call(s32[129]{0:T(256)S(1)} %get-tuple-element.393.tab.refs_0_, bf16[512,256]{1,0:T(8,128)(2,1)S(1)} %get-tuple-element.405.refs_1_, bf16[512,256]{1,0:T(8,128)(2,1)S(1)} %collective-permute-done.20.refs_2_, ...), custom_call_target="tpu_custom_call" | custom-call | flops 300000000 | bytes 9000000 | tf_op jit(solution)/shard_map/pair_solve/pallas_call | solution.py:548
  64.4 1.4 %collective-permute-start.26 = (bf16[256,256]{1,0:T(8,128)(2,1)S(1)}, bf16[256,256]{1,0:T(8,128)(2,1)S(1)}, u32[]{:S(2)}, u32[]{:S(2)}) collective-permute-start(bf16[256,256]{1,0:T(8,128)(2,1)S(1)} %get-tuple-element.422), channel_id=1, source_target_pairs={{0,24},{4,28},{8,16},{12,20},{16,8},{20,12},{24,0},{28,4},{1,25},{... | collective-permute-start | bytes 393224 | tf_op jit(solution)/shard_map/ppermute | solution.py:357
  65.8 2.3 %prep.6 = (bf16[1024,1024]{1,0:T(8,128)(2,1)S(1)}, f32[512,256]{1,0:T(8,128)S(1)}) custom-call(s32[129]{0:T(256)S(1)} %get-tuple-element.393.tab.refs_0_, s32[8]{0:T(128)S(1)} %copy-done.21, bf16[8,512,512]{2,1,0:T(8,128)(2,1)S(1)} %copy-done.1, bf16[512,512]{1,0:T(8,128)(2,1)S(1)} %factor_pack.1.own_ref.refs_0_, ...), custom_call_target="tpu_custom_call" | custom-call | flops 200000000 | bytes 6000000 | tf_op jit(solution)/shard_map/prep/pallas_call | solution.py:505
  68.1 2.9 %rows_below.2.sums = f32[2048,256]{1,0:T(8,128)S(1)} custom-call(s32[8]{0:T(128)S(1)} %copy-done.21, bf16[1024,4096]{1,0:T(8,128)(2,1)S(1)} %mask_below.2.a0, bf16[1024,4096]{1,0:T(8,128)(2,1)S(1)} %mask_below.3.a1, bf16[1024,256]{1,0:T(8,128)(2,1)S(1)} %get-tuple-element.412.refs_8_.x0_ref.x0, bf16[1024,256]{1,0:T(8,128)(2,1)S(1)} %get-tuple-element.420.x1_ref.refs_9_.x1), custom_call_target="tpu_custom_call" | custom-call | flops 300000000 | bytes 9000000 | tf_op jit(solution)/shard_map/rows_below/pallas_call | solution.py:521
  71.0 1.9 %collective-permute-done.26.refs_4_ = bf16[256,256]{1,0:T(8,128)(2,1)S(1)} collective-permute-done((bf16[256,256]{1,0:T(8,128)(2,1)S(1)}, bf16[256,256]{1,0:T(8,128)(2,1)S(1)}, u32[]{:S(2)}, u32[]{:S(2)}) %collective-permute-start.26) | collective-permute-done | bytes 131104 | tf_op jit(solution)/shard_map/ppermute | solution.py:357
  73.5 1.2 %collective-permute-start.32 = (bf16[512,256]{1,0:T(8,128)(2,1)S(1)}, bf16[512,256]{1,0:T(8,128)(2,1)S(1)}, u32[]{:S(2)}, u32[]{:S(2)}) collective-permute-start(bf16[512,256]{1,0:T(8,128)(2,1)S(1)} %get-tuple-element.436), channel_id=1, source_target_pairs={{0,1},{1,0},{2,3},{3,2},{4,5},{5,4},{6,7},{7,6},{8,9},{9,8},{10,11... | collective-permute-start | bytes 786440 | tf_op jit(solution)/shard_map/ppermute | solution.py:360
  74.7 1.8 %pair_solve.6 = (bf16[1024,256]{1,0:T(8,128)(2,1)S(1)}, bf16[512,256]{1,0:T(8,128)(2,1)S(1)}, bf16[256,256]{1,0:T(8,128)(2,1)S(1)}) custom-call(s32[129]{0:T(256)S(1)} %get-tuple-element.393.tab.refs_0_, bf16[512,256]{1,0:T(8,128)(2,1)S(1)} %get-tuple-element.421.refs_1_, bf16[512,256]{1,0:T(8,128)(2,1)S(1)} %collective-permute-done.25.refs_2_, ...), custom_call_target="tpu_custom_call" | custom-call | flops 300000000 | bytes 9000000 | tf_op jit(solution)/shard_map/pair_solve/pallas_call | solution.py:548
  77.2 2.3 %collective-permute-start.31 = (bf16[256,256]{1,0:T(8,128)(2,1)S(1)}, bf16[256,256]{1,0:T(8,128)(2,1)S(1)}, u32[]{:S(2)}, u32[]{:S(2)}) collective-permute-start(bf16[256,256]{1,0:T(8,128)(2,1)S(1)} %get-tuple-element.434), channel_id=1, source_target_pairs={{0,24},{4,28},{8,16},{12,20},{16,8},{20,12},{24,0},{28,4},{1,25},{... | collective-permute-start | bytes 393224 | tf_op jit(solution)/shard_map/ppermute | solution.py:357
  79.5 1.7 %prep.7.refs_6_ = bf16[1024,1024]{1,0:T(8,128)(2,1)S(1)} custom-call(s32[129]{0:T(256)S(1)} %get-tuple-element.393.tab.refs_0_, s32[8]{0:T(128)S(1)} %copy-done.21, bf16[8,512,512]{2,1,0:T(8,128)(2,1)S(1)} %copy-done.1, bf16[512,512]{1,0:T(8,128)(2,1)S(1)} %factor_pack.1.own_ref.refs_0_, bf16[512,512]{1,0:T(8,128)(2,1)S(1)} %collective-permute-done.4.other_ref.refs_1_, ...), custom_call_target="tpu_custom_call" | custom-call | flops 200000000 | bytes 6000000 | tf_op jit(solution)/shard_map/prep/pallas_call | solution.py:505
  81.7 2.1 %rows_below.3.base = f32[2048,256]{1,0:T(8,128)S(1)} custom-call(s32[8]{0:T(128)S(1)} %copy-done.21, bf16[1024,4096]{1,0:T(8,128)(2,1)S(1)} %mask_below.2.a0, bf16[1024,4096]{1,0:T(8,128)(2,1)S(1)} %mask_below.3.a1, bf16[1024,256]{1,0:T(8,128)(2,1)S(1)} %get-tuple-element.432.x_ref.x2, ...), custom_call_target="tpu_custom_call", output_to_operand_aliasing={{}: (4, {})} | custom-call | flops 300000000 | bytes 9000000 | tf_op jit(solution)/shard_map/rows_below/pallas_call | solution.py:521
  83.8 2.9 %collective-permute-done.31.refs_4_ = bf16[256,256]{1,0:T(8,128)(2,1)S(1)} collective-permute-done((bf16[256,256]{1,0:T(8,128)(2,1)S(1)}, bf16[256,256]{1,0:T(8,128)(2,1)S(1)}, u32[]{:S(2)}, u32[]{:S(2)}) %collective-permute-start.31) | collective-permute-done | bytes 131104 | tf_op jit(solution)/shard_map/ppermute | solution.py:357
  89.6 3.0 %last_rows.1 = (bf16[4096,256]{1,0:T(8,128)(2,1)}, bf16[2048,256]{1,0:T(8,128)(2,1)}) custom-call(s32[8]{0:T(128)S(1)} %copy-done.21, bf16[1024,4096]{1,0:T(8,128)(2,1)S(1)} %mask_below.2.a0, bf16[1024,4096]{1,0:T(8,128)(2,1)S(1)} %mask_below.3.a1, bf16[1024,256]{1,0:T(8,128)(2,1)S(1)} %get-tuple-element.412.refs_8_.x0_ref.x0, ...), custom_call_target="tpu_custom_call" | custom-call | flops 300000000 | bytes 9000000 | tf_op jit(solution)/shard_map/last_rows/pallas_call | solution.py:562
  (72 shorter events, 17.5 us)
Async XLA Ops:
  3.3 5.3 %collective-permute-start.3 = (bf16[128,256]{1,0:T(8,128)(2,1)S(1)}, bf16[128,256]{1,0:T(8,128)(2,1)S(1)}, u32[]{:S(2)}, u32[]{:S(2)}) collective-permute-start(bf16[128,256]{1,0:T(8,128)(2,1)S(1)} %get-tuple-element.376), channel_id=1, source_target_pairs={{0,1},{1,0},{2,3},{3,2},{4,5},{5,4},{6,7},{7,6},{8,9},{9,8},{10,11... | collective-permute-start | bytes 196616 | tf_op jit(solution)/shard_map/ppermute | solution.py:360
  8.6 1.9 %collective-permute-start.4 = (bf16[512,512]{1,0:T(8,128)(2,1)S(1)}, bf16[512,512]{1,0:T(8,128)(2,1)S(1)}, u32[]{:S(2)}, u32[]{:S(2)}) collective-permute-start(bf16[512,512]{1,0:T(8,128)(2,1)S(1)} %factor_pack.1.own_ref.refs_0_), channel_id=1, source_target_pairs={{0,4},{4,0},{8,12},{12,8},{16,20},{20,16},{24,28},{28,24},{1,5},{5... | collective-permute-start | bytes 1572872 | tf_op jit(solution)/shard_map/ppermute | solution.py:357
  10.6 10.9 %collective-permute-start.5 = (bf16[512,4096]{1,0:T(8,128)(2,1)S(1)}, bf16[512,4096]{1,0:T(8,128)(2,1)S(1)}, u32[]{:S(2)}, u32[]{:S(2)}) collective-permute-start(bf16[512,4096]{1,0:T(8,128)(2,1)S(1)} %copy-done), channel_id=1, source_target_pairs={{0,4},{4,0},{8,12},{12,8},{16,20},{20,16},{24,28},{28,24},{1,5},{5... | collective-permute-start | bytes 12582920 | tf_op jit(solution)/shard_map/ppermute | solution.py:357
  10.8 14.8 %collective-permute-start.14 = (bf16[1024,512]{1,0:T(8,128)(2,1)S(1)}, bf16[1024,512]{1,0:T(8,128)(2,1)S(1)}, u32[]{:S(2)}, u32[]{:S(2)}) collective-permute-start(bf16[1024,512]{1,0:T(8,128)(2,1)S(1)} %chip_pack.1), channel_id=1, source_target_pairs={{0,8},{4,20},{8,0},{12,28},{16,24},{20,4},{24,16},{28,12},{1,9},{5... | collective-permute-start | bytes 3145736 | tf_op jit(solution)/shard_map/ppermute | solution.py:363
  12.8 7.7 %collective-permute-start.6 = (bf16[128,256]{1,0:T(8,128)(2,1)S(1)}, bf16[128,256]{1,0:T(8,128)(2,1)S(1)}, u32[]{:S(2)}, u32[]{:S(2)}) collective-permute-start(bf16[128,256]{1,0:T(8,128)(2,1)S(1)} %get-tuple-element.382), channel_id=1, source_target_pairs={{0,2},{1,3},{2,0},{3,1},{4,6},{5,7},{6,4},{7,5},{8,10},{9,11},{10,... | collective-permute-start | bytes 196616 | tf_op jit(solution)/shard_map/ppermute | solution.py:360
  15.3 6.1 %collective-permute-start.7 = (bf16[128,256]{1,0:T(8,128)(2,1)S(1)}, bf16[128,256]{1,0:T(8,128)(2,1)S(1)}, u32[]{:S(2)}, u32[]{:S(2)}) collective-permute-start(bf16[128,256]{1,0:T(8,128)(2,1)S(1)} %get-tuple-element.383), channel_id=1, source_target_pairs={{0,3},{1,2},{2,1},{3,0},{4,7},{5,6},{6,5},{7,4},{8,11},{9,10},{10,... | collective-permute-start | bytes 196616 | tf_op jit(solution)/shard_map/ppermute | solution.py:360
  21.5 1.3 %collective-permute-start.8 = (bf16[128,256]{1,0:T(8,128)(2,1)S(1)}, bf16[128,256]{1,0:T(8,128)(2,1)S(1)}, u32[]{:S(2)}, u32[]{:S(2)}) collective-permute-start(bf16[128,256]{1,0:T(8,128)(2,1)S(1)} %get-tuple-element.807.refs_0_), channel_id=1, source_target_pairs={{0,4},{4,0},{8,12},{12,8},{16,20},{20,16},{24,28},{28,24},{1,5},{5... | collective-permute-start | bytes 196616 | tf_op jit(solution)/shard_map/ppermute | solution.py:357
  21.5 1.4 %collective-permute-start.9 = (bf16[128,256]{1,0:T(8,128)(2,1)S(1)}, bf16[128,256]{1,0:T(8,128)(2,1)S(1)}, u32[]{:S(2)}, u32[]{:S(2)}) collective-permute-start(bf16[128,256]{1,0:T(8,128)(2,1)S(1)} %collective-permute-done.3.refs_1_), channel_id=1, source_target_pairs={{0,4},{4,0},{8,12},{12,8},{16,20},{20,16},{24,28},{28,24},{1,5},{5... | collective-permute-start | bytes 196616 | tf_op jit(solution)/shard_map/ppermute | solution.py:357
  22.0 1.3 %collective-permute-start.10 = (bf16[128,256]{1,0:T(8,128)(2,1)S(1)}, bf16[128,256]{1,0:T(8,128)(2,1)S(1)}, u32[]{:S(2)}, u32[]{:S(2)}) collective-permute-start(bf16[128,256]{1,0:T(8,128)(2,1)S(1)} %collective-permute-done.6.refs_2_), channel_id=1, source_target_pairs={{0,4},{4,0},{8,12},{12,8},{16,20},{20,16},{24,28},{28,24},{1,5},{5... | collective-permute-start | bytes 196616 | tf_op jit(solution)/shard_map/ppermute | solution.py:357
  22.0 1.4 %collective-permute-start.11 = (bf16[128,256]{1,0:T(8,128)(2,1)S(1)}, bf16[128,256]{1,0:T(8,128)(2,1)S(1)}, u32[]{:S(2)}, u32[]{:S(2)}) collective-permute-start(bf16[128,256]{1,0:T(8,128)(2,1)S(1)} %collective-permute-done.7.refs_3_), channel_id=1, source_target_pairs={{0,4},{4,0},{8,12},{12,8},{16,20},{20,16},{24,28},{28,24},{1,5},{5... | collective-permute-start | bytes 196616 | tf_op jit(solution)/shard_map/ppermute | solution.py:357
  25.7 14.1 %collective-permute-start.15 = (bf16[512,512]{1,0:T(8,128)(2,1)S(1)}, bf16[512,512]{1,0:T(8,128)(2,1)S(1)}, u32[]{:S(2)}, u32[]{:S(2)}) collective-permute-start(bf16[512,512]{1,0:T(8,128)(2,1)S(1)} %take_half.1), channel_id=1, source_target_pairs={{0,16},{4,12},{8,24},{12,4},{16,0},{20,28},{24,8},{28,20},{1,17},{... | collective-permute-start | bytes 1572872 | tf_op jit(solution)/shard_map/ppermute | solution.py:366
  27.7 11.6 %collective-permute-start.12 = (bf16[512,256]{1,0:T(8,128)(2,1)S(1)}, bf16[512,256]{1,0:T(8,128)(2,1)S(1)}, u32[]{:S(2)}, u32[]{:S(2)}) collective-permute-start(bf16[512,256]{1,0:T(8,128)(2,1)S(1)} %get-tuple-element.388.refs_1_), channel_id=1, source_target_pairs={{0,8},{4,20},{8,0},{12,28},{16,24},{20,4},{24,16},{28,12},{1,9},{5... | collective-permute-start | bytes 786440 | tf_op jit(solution)/shard_map/ppermute | solution.py:363
  29.2 10.1 %collective-permute-start.13 = (bf16[256,256]{1,0:T(8,128)(2,1)S(1)}, bf16[256,256]{1,0:T(8,128)(2,1)S(1)}, u32[]{:S(2)}, u32[]{:S(2)}) collective-permute-start(bf16[256,256]{1,0:T(8,128)(2,1)S(1)} %get-tuple-element.394), channel_id=1, source_target_pairs={{0,24},{4,28},{8,16},{12,20},{16,8},{20,12},{24,0},{28,4},{1,25},{... | collective-permute-start | bytes 393224 | tf_op jit(solution)/shard_map/ppermute | solution.py:357
  39.8 4.8 %collective-permute-start.18 = (bf16[1024,512]{1,0:T(8,128)(2,1)S(1)}, bf16[1024,512]{1,0:T(8,128)(2,1)S(1)}, u32[]{:S(2)}, u32[]{:S(2)}) collective-permute-start(bf16[1024,512]{1,0:T(8,128)(2,1)S(1)} %collective-permute-done.14.x_ref.refs_2_), channel_id=1, source_target_pairs={{0,4},{4,0},{8,12},{12,8},{16,20},{20,16},{24,28},{28,24},{1,5},{5... | collective-permute-start | bytes 3145736 | tf_op jit(solution)/shard_map/ppermute | solution.py:357
  40.4 4.2 %collective-permute-start.19 = (bf16[512,512]{1,0:T(8,128)(2,1)S(1)}, bf16[512,512]{1,0:T(8,128)(2,1)S(1)}, u32[]{:S(2)}, u32[]{:S(2)}) collective-permute-start(bf16[512,512]{1,0:T(8,128)(2,1)S(1)} %collective-permute-done.15.refs_4_), channel_id=1, source_target_pairs={{0,4},{4,0},{8,12},{12,8},{16,20},{20,16},{24,28},{28,24},{1,5},{5... | collective-permute-start | bytes 1572872 | tf_op jit(solution)/shard_map/ppermute | solution.py:357
  40.4 5.9 %collective-permute-start.16 = (bf16[512,256]{1,0:T(8,128)(2,1)S(1)}, bf16[512,256]{1,0:T(8,128)(2,1)S(1)}, u32[]{:S(2)}, u32[]{:S(2)}) collective-permute-start(bf16[512,256]{1,0:T(8,128)(2,1)S(1)} %collective-permute-done.12.refs_2_), channel_id=1, source_target_pairs={{0,4},{4,0},{8,12},{12,8},{16,20},{20,16},{24,28},{28,24},{1,5},{5... | collective-permute-start | bytes 786440 | tf_op jit(solution)/shard_map/ppermute | solution.py:357
  40.9 5.4 %collective-permute-start.17 = (bf16[256,256]{1,0:T(8,128)(2,1)S(1)}, bf16[256,256]{1,0:T(8,128)(2,1)S(1)}, u32[]{:S(2)}, u32[]{:S(2)}) collective-permute-start(bf16[256,256]{1,0:T(8,128)(2,1)S(1)} %collective-permute-done.13.refs_4_), channel_id=1, source_target_pairs={{0,4},{4,0},{8,12},{12,8},{16,20},{20,16},{24,28},{28,24},{1,5},{5... | collective-permute-start | bytes 393224 | tf_op jit(solution)/shard_map/ppermute | solution.py:357
  41.1 16.2 %collective-permute-start.22 = (bf16[512,256]{1,0:T(8,128)(2,1)S(1)}, bf16[512,256]{1,0:T(8,128)(2,1)S(1)}, u32[]{:S(2)}, u32[]{:S(2)}) collective-permute-start(bf16[512,256]{1,0:T(8,128)(2,1)S(1)} %get-tuple-element.409), channel_id=1, source_target_pairs={{0,2},{1,3},{2,0},{3,1},{4,6},{5,7},{6,4},{7,5},{8,10},{9,11},{10,... | collective-permute-start | bytes 786440 | tf_op jit(solution)/shard_map/ppermute | solution.py:360
  48.1 10.1 %collective-permute-start.20 = (bf16[512,256]{1,0:T(8,128)(2,1)S(1)}, bf16[512,256]{1,0:T(8,128)(2,1)S(1)}, u32[]{:S(2)}, u32[]{:S(2)}) collective-permute-start(bf16[512,256]{1,0:T(8,128)(2,1)S(1)} %get-tuple-element.405.refs_1_), channel_id=1, source_target_pairs={{0,8},{4,20},{8,0},{12,28},{16,24},{20,4},{24,16},{28,12},{1,9},{5... | collective-permute-start | bytes 786440 | tf_op jit(solution)/shard_map/ppermute | solution.py:363
  48.8 9.4 %collective-permute-start.21 = (bf16[256,256]{1,0:T(8,128)(2,1)S(1)}, bf16[256,256]{1,0:T(8,128)(2,1)S(1)}, u32[]{:S(2)}, u32[]{:S(2)}) collective-permute-start(bf16[256,256]{1,0:T(8,128)(2,1)S(1)} %get-tuple-element.406), channel_id=1, source_target_pairs={{0,24},{4,28},{8,16},{12,20},{16,8},{20,12},{24,0},{28,4},{1,25},{... | collective-permute-start | bytes 393224 | tf_op jit(solution)/shard_map/ppermute | solution.py:357
  58.2 3.8 %collective-permute-start.23 = (bf16[512,256]{1,0:T(8,128)(2,1)S(1)}, bf16[512,256]{1,0:T(8,128)(2,1)S(1)}, u32[]{:S(2)}, u32[]{:S(2)}) collective-permute-start(bf16[512,256]{1,0:T(8,128)(2,1)S(1)} %collective-permute-done.20.refs_2_), channel_id=1, source_target_pairs={{0,4},{4,0},{8,12},{12,8},{16,20},{20,16},{24,28},{28,24},{1,5},{5... | collective-permute-start | bytes 786440 | tf_op jit(solution)/shard_map/ppermute | solution.py:357
  58.2 3.8 %collective-permute-start.24 = (bf16[256,256]{1,0:T(8,128)(2,1)S(1)}, bf16[256,256]{1,0:T(8,128)(2,1)S(1)}, u32[]{:S(2)}, u32[]{:S(2)}) collective-permute-start(bf16[256,256]{1,0:T(8,128)(2,1)S(1)} %collective-permute-done.21.refs_4_), channel_id=1, source_target_pairs={{0,4},{4,0},{8,12},{12,8},{16,20},{20,16},{24,28},{28,24},{1,5},{5... | collective-permute-start | bytes 393224 | tf_op jit(solution)/shard_map/ppermute | solution.py:357
  58.8 12.2 %collective-permute-start.27 = (bf16[512,256]{1,0:T(8,128)(2,1)S(1)}, bf16[512,256]{1,0:T(8,128)(2,1)S(1)}, u32[]{:S(2)}, u32[]{:S(2)}) collective-permute-start(bf16[512,256]{1,0:T(8,128)(2,1)S(1)} %get-tuple-element.424), channel_id=1, source_target_pairs={{0,3},{1,2},{2,1},{3,0},{4,7},{5,6},{6,5},{7,4},{8,11},{9,10},{10,... | collective-permute-start | bytes 786440 | tf_op jit(solution)/shard_map/ppermute | solution.py:360
  63.8 9.1 %collective-permute-start.25 = (bf16[512,256]{1,0:T(8,128)(2,1)S(1)}, bf16[512,256]{1,0:T(8,128)(2,1)S(1)}, u32[]{:S(2)}, u32[]{:S(2)}) collective-permute-start(bf16[512,256]{1,0:T(8,128)(2,1)S(1)} %get-tuple-element.421.refs_1_), channel_id=1, source_target_pairs={{0,8},{4,20},{8,0},{12,28},{16,24},{20,4},{24,16},{28,12},{1,9},{5... | collective-permute-start | bytes 786440 | tf_op jit(solution)/shard_map/ppermute | solution.py:363
  64.4 8.5 %collective-permute-start.26 = (bf16[256,256]{1,0:T(8,128)(2,1)S(1)}, bf16[256,256]{1,0:T(8,128)(2,1)S(1)}, u32[]{:S(2)}, u32[]{:S(2)}) collective-permute-start(bf16[256,256]{1,0:T(8,128)(2,1)S(1)} %get-tuple-element.422), channel_id=1, source_target_pairs={{0,24},{4,28},{8,16},{12,20},{16,8},{20,12},{24,0},{28,4},{1,25},{... | collective-permute-start | bytes 393224 | tf_op jit(solution)/shard_map/ppermute | solution.py:357
  72.9 1.7 %collective-permute-start.28 = (bf16[512,256]{1,0:T(8,128)(2,1)S(1)}, bf16[512,256]{1,0:T(8,128)(2,1)S(1)}, u32[]{:S(2)}, u32[]{:S(2)}) collective-permute-start(bf16[512,256]{1,0:T(8,128)(2,1)S(1)} %collective-permute-done.25.refs_2_), channel_id=1, source_target_pairs={{0,4},{4,0},{8,12},{12,8},{16,20},{20,16},{24,28},{28,24},{1,5},{5... | collective-permute-start | bytes 786440 | tf_op jit(solution)/shard_map/ppermute | solution.py:357
  72.9 1.7 %collective-permute-start.29 = (bf16[256,256]{1,0:T(8,128)(2,1)S(1)}, bf16[256,256]{1,0:T(8,128)(2,1)S(1)}, u32[]{:S(2)}, u32[]{:S(2)}) collective-permute-start(bf16[256,256]{1,0:T(8,128)(2,1)S(1)} %collective-permute-done.26.refs_4_), channel_id=1, source_target_pairs={{0,4},{4,0},{8,12},{12,8},{16,20},{20,16},{24,28},{28,24},{1,5},{5... | collective-permute-start | bytes 393224 | tf_op jit(solution)/shard_map/ppermute | solution.py:357
  73.5 8.2 %collective-permute-start.32 = (bf16[512,256]{1,0:T(8,128)(2,1)S(1)}, bf16[512,256]{1,0:T(8,128)(2,1)S(1)}, u32[]{:S(2)}, u32[]{:S(2)}) collective-permute-start(bf16[512,256]{1,0:T(8,128)(2,1)S(1)} %get-tuple-element.436), channel_id=1, source_target_pairs={{0,1},{1,0},{2,3},{3,2},{4,5},{5,4},{6,7},{7,6},{8,9},{9,8},{10,11... | collective-permute-start | bytes 786440 | tf_op jit(solution)/shard_map/ppermute | solution.py:360
  76.5 10.2 %collective-permute-start.30 = (bf16[512,256]{1,0:T(8,128)(2,1)S(1)}, bf16[512,256]{1,0:T(8,128)(2,1)S(1)}, u32[]{:S(2)}, u32[]{:S(2)}) collective-permute-start(bf16[512,256]{1,0:T(8,128)(2,1)S(1)} %get-tuple-element.433.refs_1_), channel_id=1, source_target_pairs={{0,8},{4,20},{8,0},{12,28},{16,24},{20,4},{24,16},{28,12},{1,9},{5... | collective-permute-start | bytes 786440 | tf_op jit(solution)/shard_map/ppermute | solution.py:363
  77.2 9.4 %collective-permute-start.31 = (bf16[256,256]{1,0:T(8,128)(2,1)S(1)}, bf16[256,256]{1,0:T(8,128)(2,1)S(1)}, u32[]{:S(2)}, u32[]{:S(2)}) collective-permute-start(bf16[256,256]{1,0:T(8,128)(2,1)S(1)} %get-tuple-element.434), channel_id=1, source_target_pairs={{0,24},{4,28},{8,16},{12,20},{16,8},{20,12},{24,0},{28,4},{1,25},{... | collective-permute-start | bytes 393224 | tf_op jit(solution)/shard_map/ppermute | solution.py:357
  86.7 1.7 %collective-permute-start.33 = (bf16[512,256]{1,0:T(8,128)(2,1)S(1)}, bf16[512,256]{1,0:T(8,128)(2,1)S(1)}, u32[]{:S(2)}, u32[]{:S(2)}) collective-permute-start(bf16[512,256]{1,0:T(8,128)(2,1)S(1)} %collective-permute-done.30.refs_2_), channel_id=1, source_target_pairs={{0,4},{4,0},{8,12},{12,8},{16,20},{20,16},{24,28},{28,24},{1,5},{5... | collective-permute-start | bytes 786440 | tf_op jit(solution)/shard_map/ppermute | solution.py:357
  86.7 1.7 %collective-permute-start.34 = (bf16[256,256]{1,0:T(8,128)(2,1)S(1)}, bf16[256,256]{1,0:T(8,128)(2,1)S(1)}, u32[]{:S(2)}, u32[]{:S(2)}) collective-permute-start(bf16[256,256]{1,0:T(8,128)(2,1)S(1)} %collective-permute-done.31.refs_4_), channel_id=1, source_target_pairs={{0,4},{4,0},{8,12},{12,8},{16,20},{20,16},{24,28},{28,24},{1,5},{5... | collective-permute-start | bytes 393224 | tf_op jit(solution)/shard_map/ppermute | solution.py:357
  (8 other events, 71.5 us)
